TPU v7x, 128 devices: a whole 4x4x4 slice. The times are simulated.
128 devices in a mesh: req: 16 (over z, x_hi, core), mdl: 8 (over x_lo, y).
Axes of the slice: x: 4 (x_hi: 2, x_lo: 2; x = x_hi * 2 + x_lo), y: 4, z: 4, core: 2. Of those that a mesh axis runs over, the one named last changes fastest.
Arguments:
- tokens: bfloat16 [16384, 2048], P('req'), may hold values from -6 to 6
- doc_ids: int32 [16384], P('req'), may hold values from 0 to 16383, as said below
- positions: int32 [16384], P('req'), may hold values from 0 to 1023, as said below
- attn_gain: float32 [2048], replicated, may hold values from 0.5 to 1.5
- mlp_gain: float32 [2048], replicated, may hold values from 0.5 to 1.5
- q_gain: float32 [128], replicated, may hold values from 0.5 to 48
- key_norm_gain: float32 [128], replicated, may hold values from 0.5 to 1.5
- q_weight: float32 [2048, 2048], P('req', 'mdl'), may hold values from -0.125 to 0.125
- key_matrix: float32 [2048, 1024], P('req', 'mdl'), may hold values from -0.125 to 0.125
- value_matrix: float32 [2048, 1024], P('req', 'mdl'), may hold values from -0.125 to 0.125
- o_weight: float32 [2048, 2048], P('mdl', 'req'), may hold values from -0.125 to 0.125
- gate_weight: float32 [2048, 6144], P('mdl', 'req'), may hold values from -0.125 to 0.125
- up_weight: float32 [2048, 6144], P('mdl', 'req'), may hold values from -0.125 to 0.125
- down_weight: float32 [6144, 2048], P('req', 'mdl'), may hold values from -0.078125 to 0.078125
Outputs:
- layer_out: bfloat16 [16384, 2048], P(('req', 'mdl'))
- key_value_cache: bfloat16 [2, 16384, 1024], P(None, 'req', 'mdl')
Inputs may be any that keep to these rules, and one draw needn't show every extreme that they name: `doc_ids`: A row's prompt number is the index of its prompt's first row among all packed rows, so it never falls along the rows; a prompt holds at most 1024 rows, every aligned block of 1024 rows has a prompt start in its second half, every block but the first begins inside the prompt that the block before it ends with, and the last row starts a prompt. `positions`: positions count from 0 at each prompt's first row.
All inputs are finite; a program needn't handle non-finite values.
Results may differ from a plain program's by a relative error of at most 0.02.
The roundings to bfloat16 on the way count: a program that leaves them out, or rounds other values in their place, can miss the bound.
Values may be sent and summed in bfloat16 or wider, within the bound.
No kernel may reach another device: no remote copies, remote signals or barrier semaphores. Data moves between devices by JAX's collectives and lax.ppermute only.
A program may use at most 128 MiB of HBM per device.

v0:
```python
import math

import jax
import jax.numpy as jnp
from jax import lax
from jax.sharding import PartitionSpec as P

HEAD_SIZE = 128


def passed_along(block, axis, distance):
    devices = range(lax.axis_size(axis))
    route = [(i - distance, i) for i in devices if i - distance in devices]
    return lax.ppermute(block, axis, route)


def root_mean_scale(values, gain):
    return values * lax.rsqrt(jnp.mean(values * values, axis=-1, keepdims=True) + 1e-06) * gain


def apply_rotary(tensor, position):
    half = tensor.shape[-1] // 2
    freq = jnp.exp(
        jnp.arange(half, dtype=jnp.float32) * (-2.0 * math.log(1000000.0) / tensor.shape[-1])
    )
    angle = position.astype(jnp.float32)[:, None] * freq[None, :]
    cosine = jnp.cos(angle)[:, None, :]
    sine = jnp.sin(angle)[:, None, :]
    front = tensor[..., :half]
    back = tensor[..., half:]
    return jnp.concatenate([front * cosine - back * sine, back * cosine + front * sine], axis=-1)


def per_device(
    tokens,
    doc_ids,
    positions,
    attn_gain,
    mlp_gain,
    q_gain,
    key_norm_gain,
    q_weight,
    key_matrix,
    value_matrix,
    o_weight,
    gate_weight,
    up_weight,
    down_weight,
):
    rows_here = tokens.shape[0]
    normed = root_mean_scale(tokens.astype(jnp.float32), attn_gain).astype(jnp.bfloat16)
    query_cols = q_weight.shape[1]
    kv_cols = key_matrix.shape[1]
    pieces = (
        lax.all_gather(q_weight.astype(jnp.bfloat16), "req", axis=0, tiled=True),
        lax.all_gather(key_matrix.astype(jnp.bfloat16), "req", axis=0, tiled=True),
        lax.all_gather(value_matrix.astype(jnp.bfloat16), "req", axis=0, tiled=True),
    )
    query_raw, unnormed_keys, unnormed_values = tuple(
        (jnp.dot(normed, piece, preferred_element_type=jnp.float32) for piece in pieces)
    )
    q_heads = query_cols // HEAD_SIZE
    kv_heads = kv_cols // HEAD_SIZE
    head_groups = q_heads // kv_heads
    query_rows = apply_rotary(
        root_mean_scale(query_raw.reshape(rows_here, q_heads, HEAD_SIZE), q_gain), positions
    ).astype(jnp.bfloat16)
    rotated_keys = (
        apply_rotary(
            root_mean_scale(unnormed_keys.reshape(rows_here, kv_heads, HEAD_SIZE), key_norm_gain),
            positions,
        )
        .astype(jnp.bfloat16)
        .reshape(rows_here, kv_cols)
    )
    projected_values = unnormed_values.astype(jnp.bfloat16)
    key_value_cache = jnp.stack([rotated_keys, projected_values])
    prior_keys, prior_values = passed_along((rotated_keys, projected_values), "req", 1)
    all_keys = jnp.concatenate([prior_keys, rotated_keys], axis=0).reshape(-1, kv_heads, HEAD_SIZE)
    all_values = jnp.concatenate([prior_values, projected_values], axis=0).reshape(
        -1, kv_heads, HEAD_SIZE
    )
    prior_index = jnp.arange(prior_keys.shape[0], dtype=jnp.int32)
    prior_live = prior_index >= rows_here - positions[0]
    grouped_queries = query_rows.reshape(rows_here, kv_heads, head_groups, HEAD_SIZE)
    block_rows = min(512, rows_here)
    scale = HEAD_SIZE ** (-0.5)
    outputs = []
    for block_index in range(rows_here // block_rows):
        lower = block_index * block_rows
        block_q = grouped_queries[lower : lower + block_rows]
        block_doc = doc_ids[lower : lower + block_rows]
        block_pos = positions[lower : lower + block_rows]
        scores = (
            jnp.einsum("qkrd,skd->krqs", block_q, all_keys, preferred_element_type=jnp.float32)
            * scale
        )
        earlier = (block_doc == doc_ids[0])[:, None] & prior_live[None, :]
        current = (doc_ids[None, :] == block_doc[:, None]) & (
            positions[None, :] <= block_pos[:, None]
        )
        allowed = jnp.concatenate([earlier, current], axis=1)
        scores = jnp.where(allowed[None, None], scores, -jnp.inf)
        top = jnp.max(scores, axis=-1, keepdims=True)
        expo = jnp.exp(scores - top)
        probs = (expo / jnp.sum(expo, axis=-1, keepdims=True)).astype(jnp.bfloat16)
        context_block = jnp.einsum(
            "krqs,skd->qkrd", probs, all_values, preferred_element_type=jnp.float32
        )
        outputs.append(context_block.astype(jnp.bfloat16).reshape(block_rows, q_heads * HEAD_SIZE))
    context = jnp.concatenate(outputs, axis=0)
    head_terms = jnp.dot(
        context,
        lax.all_gather(o_weight.astype(jnp.bfloat16), "req", axis=1, tiled=True),
        preferred_element_type=jnp.float32,
    )
    attn_rows = lax.psum_scatter(
        head_terms.astype(jnp.bfloat16), "mdl", scatter_dimension=0, tiled=True
    ).astype(jnp.float32)
    share = rows_here // lax.axis_size("mdl")
    own_rows = lax.dynamic_slice_in_dim(tokens, lax.axis_index("mdl") * share, share, 0)
    resid = lax.optimization_barrier(
        (own_rows.astype(jnp.float32) + attn_rows).astype(jnp.bfloat16)
    ).astype(jnp.float32)
    mlp_in = root_mean_scale(resid, mlp_gain).astype(jnp.bfloat16)
    gate_local = gate_weight.astype(jnp.bfloat16)
    up_local = up_weight.astype(jnp.bfloat16)
    down_local = down_weight.astype(jnp.bfloat16)
    gate_whole, up_whole = (
        lax.all_gather(gate_local, "req", axis=1, tiled=True),
        lax.all_gather(up_local, "req", axis=1, tiled=True),
    )
    down_whole = lax.all_gather(down_local, "req", axis=0, tiled=True)
    gate_server, up_server = (
        lax.all_to_all(gate_whole, "mdl", split_axis=1, concat_axis=0, tiled=True),
        lax.all_to_all(up_whole, "mdl", split_axis=1, concat_axis=0, tiled=True),
    )
    down_server = lax.all_to_all(down_whole, "mdl", split_axis=0, concat_axis=1, tiled=True)
    piece = lax.all_gather(mlp_in, "mdl", axis=0, tiled=True)
    gate = jnp.dot(piece, gate_server, preferred_element_type=jnp.float32)
    upper = jnp.dot(piece, up_server, preferred_element_type=jnp.float32)
    hidden = (jax.nn.silu(gate) * upper).astype(jnp.bfloat16)
    unit_terms = jnp.dot(hidden, down_server, preferred_element_type=jnp.float32)
    mlp_rows = lax.psum_scatter(
        unit_terms.astype(jnp.bfloat16), "mdl", scatter_dimension=0, tiled=True
    ).astype(jnp.float32)
    layer_out = (resid + mlp_rows).astype(jnp.bfloat16)
    return (layer_out, key_value_cache)


def solution(mesh):
    in_specs = (
        P("req", None),
        P("req"),
        P("req"),
        P(),
        P(),
        P(),
        P(),
        P("req", "mdl"),
        P("req", "mdl"),
        P("req", "mdl"),
        P("mdl", "req"),
        P("mdl", "req"),
        P("mdl", "req"),
        P("req", "mdl"),
    )
    out_specs = (P(("req", "mdl"), None), P(None, "req", "mdl"))
    return jax.shard_map(
        per_device, mesh=mesh, in_specs=in_specs, out_specs=out_specs, check_vma=False
    )
```

profile of v0, /device:TPU:32, one launch (start us, length us, event | category | flops | bytes accessed | tf_op | source)
XLA Modules:
  0.0 520.0 jit_solution(16136902884525856238)
XLA Ops:
  7.2 1.5 convert_element_type.107
  8.8 1.5 convert_element_type.116
  10.5 3.2 fusion
  13.9 1.0 fusion.2
  15.0 26.0 %all_gather.25 = bf16[2048,128]{1,0:T(8,128)(2,1)S(1)} all-gather(bf16[128,128]{1,0:T(8,128)(2,1)S(1)} %convert_element_type.105), channel_id=1, replica_groups=mesh['req'=16,'mdl'=8] {'req'}, dimensions={0}, use_global_device_ids=true | all-gather | bytes 557056 | tf_op jit(solution)/shard_map/all_gather | solution.py:56
  40.9 1.5 multiply_reduce_fusion.1
  42.9 2.4 fusion.26
  46.0 0.8 pad_maximum_fusion.3
  46.9 2.2 collective-permute-start.1
  49.2 23.3 %all_gather.24 = bf16[2048,128]{1,0:T(8,128)(2,1)S(1)} all-gather(bf16[128,128]{1,0:T(8,128)(2,1)S(1)} %convert_element_type.103), channel_id=1, replica_groups=mesh['req'=16,'mdl'=8] {'req'}, dimensions={0}, use_global_device_ids=true | all-gather | bytes 557056 | tf_op jit(solution)/shard_map/all_gather | solution.py:57
  72.4 4.1 convolution_convert_fusion.2
  76.6 2.3 collective-permute-start
  78.9 0.8 copy.34
  81.0 3.0 multiply_cosine_fusion
  85.8 1.2 compare_and_fusion.1
  87.0 0.8 pad_add_fusion
  87.8 4.9 multiply_reduce_fusion
  92.7 1.5 copy.29
  94.6 1.7 subtract_convert_fusion
  96.3 2.9 fusion.5
  99.3 2.9 fusion.6
  102.2 2.0 fusion.3
  104.2 2.2 fusion.4
  106.4 3.9 fusion.11
  110.3 3.9 fusion.14
  114.3 4.5 convolution_convert_fusion
  118.9 0.8 copy.36
  119.8 0.7 convert_element_type.125
  120.5 34.6 %all-gather.13.cloned.1.call-done = bf16[256,6144]{0,1:T(8,128)(2,1)} async-done(((bf16[256,384]{0,1:T(8,128)(2,1)}), bf16[256,6144]{0,1:T(8,128)(2,1)}) %all-gather.13.cloned.1.call-update) | async-done | bytes 3145744 | tf_op jit(solution)/shard_map/all_gather | solution.py:130
  155.1 4.4 all-to-all-start
  159.5 81.8 %reduce-scatter.3.cloned.1.call-done = bf16[128,2048]{1,0:T(8,128)(2,1)} async-done(((bf16[1024,2048]{1,0:T(8,128)(2,1)}), bf16[128,2048]{1,0:T(8,128)(2,1)}) %reduce-scatter.3.cloned.1.call-update) | async-done | bytes 524304 | tf_op jit(solution)/shard_map/reduce_scatter | solution.py:117
  241.4 1.3 add_convert_fusion
  243.5 1.0 fusion.19
  244.5 48.5 %all-gather.15.cloned.1.call-done = bf16[256,6144]{0,1:T(8,128)(2,1)} async-done(((bf16[256,384]{0,1:T(8,128)(2,1)}), bf16[256,6144]{0,1:T(8,128)(2,1)}) %all-gather.15.cloned.1.call-update) | async-done | bytes 3145744 | tf_op jit(solution)/shard_map/all_gather | solution.py:131
  293.0 4.5 all-to-all-start.1
  297.5 54.4 %all-gather.17.cloned.1.call-done = bf16[6144,256]{1,0:T(8,128)(2,1)} async-done(((bf16[384,256]{1,0:T(8,128)(2,1)}), bf16[6144,256]{1,0:T(8,128)(2,1)}) %all-gather.17.cloned.1.call-update) | async-done | bytes 3145744 | tf_op jit(solution)/shard_map/all_gather | solution.py:133
  351.8 4.8 all-to-all-start.2
  356.7 3.1 copy.35
  359.7 3.2 copy.37
  362.9 54.4 %all-to-all-done.2 = bf16[8,768,256]{2,1,0:T(8,128)(2,1)} async-done(((bf16[8,768,256]{2,1,0:T(8,128)(2,1)}), bf16[8,768,256]{2,1,0:T(8,128)(2,1)}, u32[]{:S(2)}, u32[]{:S(2)}) %all-to-all-start.2) | async-done | bytes 3145760 | tf_op jit(solution)/shard_map/all_to_all | solution.py:138
  417.4 4.7 copy.38
  422.1 16.0 %all-gather.11.cloned.1.call-done = bf16[1024,2048]{1,0:T(8,128)(2,1)} async-done(((bf16[128,2048]{1,0:T(8,128)(2,1)}), bf16[1024,2048]{1,0:T(8,128)(2,1)}) %all-gather.11.cloned.1.call-update) | async-done | bytes 4194320 | tf_op jit(solution)/shard_map/all_gather | solution.py:139
  438.1 8.2 %fusion.49 = f32[1024,768]{1,0:T(8,128)} fusion(bf16[1024,2048]{1,0:T(8,128)(2,1)} %all-gather.11.cloned.1.call-done, bf16[2048,768]{1,0:T(8,128)(2,1)} %bitcast.100), kind=kOutput, calls=%fused_computation.91 | convolution fusion | flops 3221225472 | bytes 10485760 | tf_op jit(solution)/shard_map/dot_general | solution.py:140
  446.3 12.2 %convolution_convert_fusion.1 = bf16[1024,2048]{1,0:T(8,128)(2,1)} fusion(bf16[768,2048]{0,1:T(8,128)(2,1)} %bitcast.101, f32[1024,768]{1,0:T(8,128)} %fusion.49, bf16[1024,2048]{1,0:T(8,128)(2,1)} %all-gather.11.cloned.1.call-done, bf16[2048,768]{1,0:T(8,128)(2,1)S(1)} %bitcast.99), kind=kOutput, calls=%fused_computation.22 | convolution fusion | flops 6449266688 | bytes 17825792 | tf_op jit(solution)/shard_map/dot_general | solution.py:143
  458.6 0.9 copy-done.6
  459.5 1.9 pad_maximum_fusion
  461.4 49.8 %reduce-scatter.5.cloned.1.call-done = bf16[128,2048]{1,0:T(8,128)(2,1)} async-done(((bf16[1024,2048]{1,0:T(8,128)(2,1)}), bf16[128,2048]{1,0:T(8,128)(2,1)}) %reduce-scatter.5.cloned.1.call-update) | async-done | bytes 524304 | tf_op jit(solution)/shard_map/reduce_scatter | solution.py:144
  511.2 2.0 fusion.20
  (76 shorter events, 5.4 us)
Async XLA Ops:
  7.2 6.5 %copy-start.10 = (f32[128,128]{1,0:T(8,128)S(1)}, f32[128,128]{1,0:T(8,128)}, u32[]{:S(2)}) copy-start(f32[128,128]{1,0:T(8,128)} %param.22) | copy-start | bytes 196612
  7.2 6.6 %copy-start.14 = (f32[2048]{0:T(1024)S(1)}, f32[2048]{0:T(1024)}, u32[]{:S(2)}) copy-start(f32[2048]{0:T(1024)} %param.17) | copy-start | bytes 24580
  7.2 80.6 %all-gather.7.cloned.1.call-start = ((), (), s32[]{:S(2)}) async-start(), calls=%async_computation.5 | async-start | bytes 1114112 | tf_op jit(solution)/shard_map/all_gather | solution.py:55
  8.8 105.4 %all-gather.9.cloned.1.call-start = ((), (), s32[]{:S(2)}) async-start(), calls=%async_computation.6 | async-start | bytes 1114112 | tf_op jit(solution)/shard_map/all_gather | solution.py:114
  10.4 144.7 %all-gather.13.cloned.1.call-start = ((), (), s32[]{:S(2)}) async-start(), calls=%async_computation.9 | async-start | bytes 3342336 | tf_op jit(solution)/shard_map/all_gather | solution.py:130
  10.4 3.5 copy-start
  14.9 26.0 %copy-start.1 = (bf16[1024,2048]{1,0:T(8,128)(2,1)}, bf16[1024,2048]{1,0:T(8,128)(2,1)S(1)}, u32[]{:S(2)}) copy-start(bf16[1024,2048]{1,0:T(8,128)(2,1)S(1)} %fusion.2) | copy-start | bytes 12582916
  14.9 27.7 %copy-start.12 = (s32[1024]{0:T(1024)S(1)}, s32[1024]{0:T(1024)}, u32[]{:S(2)}) copy-start(s32[1024]{0:T(1024)} %param.16) | copy-start | bytes 12292
  15.0 27.8 %copy-start.16 = (f32[128]{0:T(128)S(1)}, f32[128]{0:T(128)}, u32[]{:S(2)}) copy-start(f32[128]{0:T(128)} %param.20) | copy-start | bytes 1540
  40.9 8.2 %copy-start.11 = (f32[128,128]{1,0:T(8,128)S(1)}, f32[128,128]{1,0:T(8,128)}, u32[]{:S(2)}) copy-start(f32[128,128]{1,0:T(8,128)} %param.23) | copy-start | bytes 196612
  45.4 0.7 copy-start.4
  45.4 33.5 %copy-start.7 = (f32[256,384]{1,0:T(8,128)S(1)}, f32[256,384]{1,0:T(8,128)}, u32[]{:S(2)}) copy-start(f32[256,384]{1,0:T(8,128)} %param.25) | copy-start | bytes 1179652
  46.0 33.9 %copy-start.13 = (s32[1024]{0:T(1024)S(1)}, s32[1024]{0:T(1024)}, u32[]{:S(2)}) copy-start(s32[1024]{0:T(1024)} %param.15) | copy-start | bytes 12292
  46.9 49.4 %collective-permute-start.1 = (bf16[1024,128]{1,0:T(8,128)(2,1)}, bf16[1024,128]{1,0:T(8,128)(2,1)}, u32[]{:S(2)}, u32[]{:S(2)}) collective-permute-start(bf16[1024,128]{1,0:T(8,128)(2,1)} %pad_maximum_fusion.3), channel_id=1, source_target_pairs={{0,8},{8,16},{16,24},{24,32},{32,40},{40,48},{48,56},{56,64},{64,7... | collective-permute-start | bytes 786440 | tf_op jit(solution)/shard_map/ppermute | solution.py:14
  76.6 29.8 %collective-permute-start = (bf16[1024,128]{1,0:T(8,128)(2,1)}, bf16[1024,128]{1,0:T(8,128)(2,1)}, u32[]{:S(2)}, u32[]{:S(2)}) collective-permute-start(bf16[1024,128]{1,0:T(8,128)(2,1)} %convolution_convert_fusion.2), channel_id=1, source_target_pairs={{0,8},{8,16},{16,24},{24,32},{32,40},{40,48},{48,56},{56,64},{64,7... | collective-permute-start | bytes 786440 | tf_op jit(solution)/shard_map/ppermute | solution.py:14
  79.7 161.7 %reduce-scatter.3.cloned.1.call-start = ((), (), s32[]{:S(2)}) async-start(), calls=%async_computation.7 | async-start | bytes 4718592 | tf_op jit(solution)/shard_map/reduce_scatter | solution.py:117
  87.7 6.5 %copy-start.17 = (f32[128]{0:T(128)S(1)}, f32[128]{0:T(128)}, u32[]{:S(2)}) copy-start(f32[128]{0:T(128)} %param.19) | copy-start | bytes 1540
  94.2 2.1 copy-start.5
  114.2 4.6 copy-start.8
  118.8 1.0 copy-start.9
  118.8 174.2 %all-gather.15.cloned.1.call-start = ((), (), s32[]{:S(2)}) async-start(), calls=%async_computation.10 | async-start | bytes 3342336 | tf_op jit(solution)/shard_map/all_gather | solution.py:131
  119.7 232.1 %all-gather.17.cloned.1.call-start = ((), (), s32[]{:S(2)}) async-start(), calls=%async_computation.11 | async-start | bytes 3342336 | tf_op jit(solution)/shard_map/all_gather | solution.py:133
  155.1 88.5 %copy-start.15 = (f32[2048]{0:T(1024)S(1)}, f32[2048]{0:T(1024)}, u32[]{:S(2)}) copy-start(f32[2048]{0:T(1024)} %param.18) | copy-start | bytes 24580
  155.1 138.0 %all-to-all-start = ((bf16[256,8,768]{0,2,1:T(8,128)(2,1)}), bf16[256,8,768]{0,2,1:T(8,128)(2,1)S(1)}, u32[]{:S(2)}, u32[]{:S(2)}) async-start(bf16[256,8,768]{0,2,1:T(8,128)(2,1)} %bitcast.96), calls=%async_computation.1 | async-start | bytes 6291456 | tf_op jit(solution)/shard_map/all_to_all | solution.py:135
  159.5 278.6 %all-gather.11.cloned.1.call-start = ((), (), s32[]{:S(2)}) async-start(), calls=%async_computation.8 | async-start | bytes 4718592 | tf_op jit(solution)/shard_map/all_gather | solution.py:139
  242.7 0.8 copy-start.2
  293.0 58.8 %all-to-all-start.1 = ((bf16[256,8,768]{0,2,1:T(8,128)(2,1)}), bf16[256,8,768]{0,2,1:T(8,128)(2,1)}, u32[]{:S(2)}, u32[]{:S(2)}) async-start(bf16[256,8,768]{0,2,1:T(8,128)(2,1)} %bitcast.98), calls=%async_computation.2 | async-start | bytes 6291456 | tf_op jit(solution)/shard_map/all_to_all | solution.py:136
  351.8 65.5 %all-to-all-start.2 = ((bf16[8,768,256]{2,1,0:T(8,128)(2,1)}), bf16[8,768,256]{2,1,0:T(8,128)(2,1)}, u32[]{:S(2)}, u32[]{:S(2)}) async-start(bf16[8,768,256]{2,1,0:T(8,128)(2,1)} %bitcast.97), calls=%async_computation.3 | async-start | bytes 6291456 | tf_op jit(solution)/shard_map/all_to_all | solution.py:138
  356.6 154.6 %reduce-scatter.5.cloned.1.call-start = ((), (), s32[]{:S(2)}) async-start(), calls=%async_computation.12 | async-start | bytes 4718592 | tf_op jit(solution)/shard_map/reduce_scatter | solution.py:144
  458.5 0.9 copy-start.6
  458.5 52.7 %copy-start.3 = (bf16[128,2048]{1,0:T(8,128)(2,1)S(1)}, bf16[128,2048]{1,0:T(8,128)(2,1)}, u32[]{:S(2)}) copy-start(bf16[128,2048]{1,0:T(8,128)(2,1)} %copy-done.2) | copy-start | bytes 1572868
Sparse Core Ops, SparseCore 0:
  10.5 48.8 all-gather.6
  61.7 38.9 all-gather.8
  103.2 51.8 all-gather.12
  157.3 84.0 reduce-scatter.2
  243.7 49.2 all-gather.14
  295.3 56.4 all-gather.16
  354.1 83.9 all-gather.10
  458.7 52.4 reduce-scatter.4
where the time goes:
time: 522 us; the launch traced here: 520 us
  waiting for transfers between devices  340 us (65%)
  blocking collectives  49.2 us (9%)
  matrix products  49.2 us (9%)
  other arithmetic  30.2 us (6%)
  starting transfers between devices  18.7 us (4%)
  local copies, waits for them, and re-layouts  17.8 us (3%)
  between operations  15.2 us (3%)
    reduce_scatter x1, waiting for transfers between devices, per_device(): lax.psum_scatter(head_terms.astype(jnp.bfloat16), 'mdl', scatter_dimensio...  81.8 us
    all_to_all x1, waiting for transfers between devices, per_device(): lax.all_to_all(down_whole, 'mdl', split_axis=0, concat_axis=1, tiled=True)  54.4 us
    all_gather x1, waiting for transfers between devices, per_device(): down_whole = lax.all_gather(down_local, 'req', axis=0, tiled=True)  54.4 us
    reduce_scatter x1, waiting for transfers between devices, per_device(): lax.psum_scatter(unit_terms.astype(jnp.bfloat16), 'mdl', scatter_dimensio...  49.8 us
    all_gather x1, waiting for transfers between devices, per_device(): lax.all_gather(up_local, 'req', axis=1, tiled=True)  48.5 us
    all_gather x1, waiting for transfers between devices, per_device(): lax.all_gather(gate_local, 'req', axis=1, tiled=True)  34.6 us
    all_gather x1, blocking collectives, per_device(): lax.all_gather(key_matrix.astype(jnp.bfloat16), 'req', axis=0, tiled=True)  26 us
    all_gather x1, blocking collectives, per_device(): lax.all_gather(value_matrix.astype(jnp.bfloat16), 'req', axis=0, tiled=True)  23.3 us
  transfers between devices with their start and end apart: 13, of which 7 were waited for; matrix products, arithmetic and copies ran while one was open for 14% of the time, Pallas kernels for 0%

commit v1 on v0

v1 whole, which is shorter than its diff:
```python
import math

import jax
import jax.numpy as jnp
from jax import lax
from jax.experimental import pallas as pl
from jax.experimental.pallas import tpu as pltpu
from jax.sharding import Mesh
from jax.sharding import PartitionSpec as P

HEAD = 128
BF = jnp.bfloat16
F32 = jnp.float32
REQ = ("z", "xh", "core")
MDL = ("xl", "y")


def ring(step):
    return [(i, (i + step) % 4) for i in range(4)]


def spread(block, axes):
    count = lax.axis_size(axes)
    wide = jnp.broadcast_to(block[None], (count,) + block.shape)
    return lax.all_to_all(wide, axes, split_axis=0, concat_axis=0, tiled=True)


def swap(block, axis):
    return lax.ppermute(block, axis, [(0, 1), (1, 0)])


def qkv_kernel(core_ref, x_ref, own_ref, oth_ref, gain_ref, qg_ref, kg_ref, cs_ref, q_ref, kv_ref, w_ref):
    core = core_ref[0]

    @pl.when(pl.program_id(0) == 0)
    def _():
        for i in range(8):
            w_ref[pl.ds(pl.multiple_of((2 * i + core) * 128, 128), 128), :] = own_ref[i]
            w_ref[pl.ds(pl.multiple_of((2 * i + 1 - core) * 128, 128), 128), :] = oth_ref[i]

    x = x_ref[...].astype(F32)
    scale = lax.rsqrt(jnp.mean(x * x, axis=-1, keepdims=True) + 1e-06)
    normed = (x * scale * gain_ref[...]).astype(BF)
    raw = jnp.dot(normed, w_ref[...], preferred_element_type=F32)
    cs = cs_ref[...]
    turned = pltpu.roll(cs, 64, 1)
    low = lax.broadcasted_iota(jnp.int32, cs.shape, 1) < 64
    cosine = jnp.where(low, cs, turned)
    sine = jnp.where(low, -turned, cs)

    def head(t, gain):
        t = t * lax.rsqrt(jnp.mean(t * t, axis=-1, keepdims=True) + 1e-06) * gain
        return (t * cosine + pltpu.roll(t, 64, 1) * sine).astype(BF)

    q_ref[:, :128] = head(raw[:, :128], qg_ref[...])
    q_ref[:, 128:] = head(raw[:, 128:256], qg_ref[...])
    kv_ref[0] = head(raw[:, 256:384], kg_ref[...])
    kv_ref[1] = raw[:, 384:].astype(BF)


def project(core, tokens, own, oth, attn_gain, q_gain, key_gain, cs):
    rows = tokens.shape[0]
    tile = 256
    fixed = lambda *shape: pl.BlockSpec(shape, lambda i, c: (0,) * len(shape))
    return pl.pallas_call(
        qkv_kernel,
        grid_spec=pltpu.PrefetchScalarGridSpec(
            num_scalar_prefetch=1,
            grid=(rows // tile,),
            in_specs=[
                pl.BlockSpec((tile, 2048), lambda i, c: (i, 0)),
                fixed(8, 128, 512),
                fixed(8, 128, 512),
                fixed(1, 2048),
                fixed(1, 128),
                fixed(1, 128),
                pl.BlockSpec((tile, 128), lambda i, c: (i, 0)),
            ],
            out_specs=[
                pl.BlockSpec((tile, 256), lambda i, c: (i, 0)),
                pl.BlockSpec((2, tile, 128), lambda i, c: (0, i, 0)),
            ],
            scratch_shapes=[pltpu.VMEM((2048, 512), BF)],
        ),
        out_shape=(
            jax.ShapeDtypeStruct((rows, 256), BF),
            jax.ShapeDtypeStruct((2, rows, 128), BF),
        ),
        compiler_params=pltpu.CompilerParams(vmem_limit_bytes=40 << 20),
        name="qkv",
    )(core, tokens, own, oth, attn_gain[None], q_gain[None], key_gain[None], cs)


def attend_kernel(q_ref, kv_ref, prior_ref, lo_ref, out_ref):
    factor = HEAD ** (-0.5) * math.log2(math.e)
    nt = (((1,), (1,)), ((), ()))
    for i in range(4):
        first = i * 256
        skip = 256 if i == 3 else 0
        count = first + 256
        lo = lo_ref[first : first + 256, :]
        row = lax.broadcasted_iota(jnp.int32, (256, count), 0) + first
        col = lax.broadcasted_iota(jnp.int32, (256, count), 1)
        near = (col >= lo) & (col <= row)
        prior_col = lax.broadcasted_iota(jnp.int32, (256, 512 - skip), 1) + (skip - 512)
        far = prior_col >= lo
        for h in range(2):
            q = q_ref[first : first + 256, h * 128 : h * 128 + 128]
            s1 = lax.dot_general(q, kv_ref[0, :count], nt, preferred_element_type=F32)
            s0 = lax.dot_general(q, prior_ref[0, skip:], nt, preferred_element_type=F32)
            s1 = jnp.where(near, s1, -1e30)
            s0 = jnp.where(far, s0, -1e30)
            top = jnp.maximum(jnp.max(s1, -1, keepdims=True), jnp.max(s0, -1, keepdims=True))
            e1 = jnp.exp2((s1 - top) * factor)
            e0 = jnp.exp2((s0 - top) * factor)
            inv = 1.0 / (jnp.sum(e1, -1, keepdims=True) + jnp.sum(e0, -1, keepdims=True))
            p1 = (e1 * inv).astype(BF)
            p0 = (e0 * inv).astype(BF)
            o = jnp.dot(p1, kv_ref[1, :count], preferred_element_type=F32)
            o = o + jnp.dot(p0, prior_ref[1, skip:], preferred_element_type=F32)
            o = o.astype(BF)
            for part in range(2):
                block = 2 * i + part
                out_ref[block % 4, block // 4, :, h * 128 : h * 128 + 128] = o[part * 128 : part * 128 + 128]


def attend(q, kv, prior, lo):
    return pl.pallas_call(
        attend_kernel,
        out_shape=jax.ShapeDtypeStruct((4, 2, 128, 256), BF),
        compiler_params=pltpu.CompilerParams(vmem_limit_bytes=40 << 20),
        name="attend",
    )(q, kv, prior, lo)


def out_kernel(at_ref, ctx_ref, own_ref, oth_ref, keep_ref, send_ref):
    core = at_ref[0]
    xl = at_ref[1]

    def body(even, odd):
        left = [jnp.concatenate([ctx_ref[s, xl], ctx_ref[s, 1 - xl]], axis=0) for s in range(4)]
        for i in range(8):
            total = None
            for s in range(4):
                w = jnp.concatenate([even[s, i], odd[s, i]], axis=1)
                term = jnp.dot(left[s], w, preferred_element_type=F32)
                total = term if total is None else total + term
            keep_ref[:, i * 256 : i * 256 + 256] = total[:128]
            send_ref[:, i * 256 : i * 256 + 256] = total[128:].astype(BF)

    @pl.when(core == 0)
    def _():
        body(own_ref, oth_ref)

    @pl.when(core == 1)
    def _():
        body(oth_ref, own_ref)


def out_project(at, ctx, own, oth):
    vm = pl.BlockSpec(memory_space=pltpu.VMEM)
    return pl.pallas_call(
        out_kernel,
        in_specs=[pl.BlockSpec(memory_space=pltpu.SMEM), vm, vm, vm],
        out_shape=(
            jax.ShapeDtypeStruct((128, 2048), F32),
            jax.ShapeDtypeStruct((128, 2048), BF),
        ),
        compiler_params=pltpu.CompilerParams(vmem_limit_bytes=40 << 20),
        name="oproj",
    )(at, ctx, own, oth)


def mlp_kernel(x0_ref, x1_ref, x2_ref, x3_ref, x4_ref, own_ref, oth_ref, keep_ref, left_ref, right_ref, far_ref,
               w_ref, x_ref, hid_ref, sems):
    nt = (((1,), (1,)), ((), ()))
    copies = {}
    for g, c in ((0, 0), (1, 0), (0, 1), (1, 1), (2, 0), (2, 1)):
        src = own_ref if c == 0 else oth_ref
        for m in range(8):
            copies[g, c, m] = pltpu.make_async_copy(
                src.at[:, m // 4, m % 4, g * 96 : g * 96 + 96, :],
                w_ref.at[g, c, :, :, m * 256 : m * 256 + 256],
                sems.at[g, c, m],
            )
            copies[g, c, m].start()
    x_ref[0:128] = x0_ref[...]
    x_ref[128:256] = x1_ref[...]
    x_ref[256:384] = x2_ref[...]
    x_ref[384:448] = x3_ref[...]
    x_ref[448:512] = x4_ref[...]
    x = x_ref[...]
    for c in range(2):
        for g in range(2):
            for m in range(8):
                copies[g, c, m].wait()
        gate_w = w_ref[0, c].reshape(768, 2048)
        up_w = w_ref[1, c].reshape(768, 2048)
        for t in range(3):
            gate = lax.dot_general(x, gate_w[t * 256 : t * 256 + 256], nt, preferred_element_type=F32)
            upper = lax.dot_general(x, up_w[t * 256 : t * 256 + 256], nt, preferred_element_type=F32)
            hidden = gate / (1.0 + jnp.exp(-gate)) * upper
            at = c * 768 + t * 256
            hid_ref[:, at : at + 256] = hidden.astype(BF)
    for c in range(2):
        for m in range(8):
            copies[2, c, m].wait()
    hid = hid_ref[...]
    down = w_ref[2].reshape(1536, 2048)
    for n in range(8):
        at = slice(n * 256, n * 256 + 256)
        out = jnp.dot(hid, down[:, at], preferred_element_type=F32)
        keep_ref[:, at] = out[:128]
        left_ref[:, at] = out[128:256].astype(BF)
        right_ref[:, at] = out[256:384].astype(BF)
        far_ref[:, at] = out[384:].astype(BF)


def feed_forward(pieces, own, oth):
    vm = pl.BlockSpec(memory_space=pltpu.VMEM)
    hbm = pl.BlockSpec(memory_space=pl.ANY)
    part = jax.ShapeDtypeStruct((128, 2048), BF)
    return pl.pallas_call(
        mlp_kernel,
        in_specs=[vm] * 5 + [hbm] * 2,
        out_shape=(jax.ShapeDtypeStruct((128, 2048), F32), part, part, part),
        scratch_shapes=[
            pltpu.VMEM((3, 2, 8, 96, 2048), BF),
            pltpu.VMEM((512, 2048), BF),
            pltpu.VMEM((512, 1536), BF),
            pltpu.SemaphoreType.DMA((3, 2, 8)),
        ],
        compiler_params=pltpu.CompilerParams(vmem_limit_bytes=56 << 20),
        name="mlp",
    )(*pieces, own, oth)


def per_device(
    tokens,
    doc_ids,
    positions,
    attn_gain,
    mlp_gain,
    q_gain,
    key_norm_gain,
    q_weight,
    key_matrix,
    value_matrix,
    o_weight,
    gate_weight,
    up_weight,
    down_weight,
):
    rows = tokens.shape[0]
    core = lax.axis_index("core").astype(jnp.int32)
    xl = lax.axis_index("xl").astype(jnp.int32)
    m = lax.axis_index(MDL).astype(jnp.int32)

    qkv_local = jnp.concatenate([q_weight, key_matrix, value_matrix], axis=1).astype(BF)
    qkv_own = spread(qkv_local, ("z", "xh"))
    qkv_oth = swap(qkv_own, "core")

    o_cols = spread(o_weight.astype(BF), ("z", "xh"))
    o_own = spread(o_cols, "y")
    o_oth = swap(o_own, "core")

    mlp_local = jnp.stack([gate_weight.T, up_weight.T, down_weight]).astype(BF)
    mlp_local = mlp_local.reshape(3, 4, 96, 256).transpose(1, 0, 2, 3).reshape(4, 288, 256)
    mlp_group = lax.all_to_all(mlp_local, "y", split_axis=0, concat_axis=0, tiled=True)
    mlp_own = lax.all_gather(mlp_group, ("z", "xh", "xl"), axis=0, tiled=False)
    mlp_own = mlp_own.reshape(8, 2, 4, 288, 256)
    mlp_oth = swap(mlp_own, "core")

    half = HEAD // 2
    freq = jnp.exp(jnp.arange(half, dtype=F32) * (-2.0 * math.log(1000000.0) / HEAD))
    angle = positions.astype(F32)[:, None] * freq[None, :]
    cs = jnp.concatenate([jnp.cos(angle), jnp.sin(angle)], axis=1)
    lo = (jnp.arange(rows, dtype=jnp.int32) - positions)[:, None]

    q, cache = project(core[None], tokens, qkv_own, qkv_oth, attn_gain, q_gain, key_norm_gain, cs)
    prior = lax.ppermute(cache[:, rows // 2 :], REQ, [(i - 1, i) for i in range(1, 16)])
    ctx = attend(q, cache, prior, lo)
    ctx = lax.all_to_all(ctx, "y", split_axis=0, concat_axis=0, tiled=True)
    keep, send = out_project(jnp.stack([core, xl]), ctx, o_own, o_oth)
    got = swap(send, "xl")

    own_rows = lax.dynamic_slice_in_dim(tokens, m * 128, 128, 0).astype(F32)
    resid = (own_rows + (keep + got.astype(F32))).astype(BF)
    resid = lax.optimization_barrier(resid).astype(F32)
    scale = lax.rsqrt(jnp.mean(resid * resid, axis=-1, keepdims=True) + 1e-06)
    mlp_in = (resid * scale * mlp_gain).astype(BF)

    left = lax.ppermute(mlp_in, "y", ring(1))
    right = lax.ppermute(mlp_in, "y", ring(3))
    far_top = lax.ppermute(left[:64], "y", ring(1))
    far_bottom = lax.ppermute(right[64:], "y", ring(3))
    keep, to_left, to_right, to_far = feed_forward((mlp_in, left, right, far_top, far_bottom), mlp_own, mlp_oth)
    via_left = lax.ppermute(to_far[:64], "y", ring(1))
    via_right = lax.ppermute(to_far[64:], "y", ring(3))
    to_right = jnp.concatenate([(to_right[:64].astype(F32) + via_left.astype(F32)).astype(BF), to_right[64:]])
    to_left = jnp.concatenate([to_left[:64], (to_left[64:].astype(F32) + via_right.astype(F32)).astype(BF)])
    from_left = lax.ppermute(to_right, "y", ring(1))
    from_right = lax.ppermute(to_left, "y", ring(3))
    total = keep + from_left.astype(F32) + from_right.astype(F32)
    return ((resid + total).astype(BF), cache)


def solution(mesh):
    fine = Mesh(mesh.devices.reshape(4, 2, 2, 2, 4), REQ + MDL)
    rows = P(REQ)
    in_specs = (
        P(REQ, None),
        rows,
        rows,
        P(),
        P(),
        P(),
        P(),
        P(REQ, MDL),
        P(REQ, MDL),
        P(REQ, MDL),
        P(MDL, REQ),
        P(MDL, REQ),
        P(MDL, REQ),
        P(REQ, MDL),
    )
    out_specs = (P(REQ + MDL, None), P(None, REQ, MDL))
    return jax.shard_map(per_device, mesh=fine, in_specs=in_specs, out_specs=out_specs, check_vma=False)
```

time: 522 us -> 306 us (0.59)
  the two profiles are of different devices: /device:TPU:32 before, /device:TPU:0 now
where the time goes in v1:
time: 306 us; the launch traced here: 305 us
  waiting for transfers between devices  179 us (58%)
  Pallas kernels  32.6 us (11%)
  blocking collectives  32 us (10%)
  starting transfers between devices  23.2 us (8%)
  local copies, waits for them, and re-layouts  15.7 us (5%)
  between operations  14.4 us (5%)
  other arithmetic  8.45 us (3%)
    all_gather x1, waiting for transfers between devices, per_device(): mlp_own = lax.all_gather(mlp_group, ('z', 'xh', 'xl'), axis=0, tiled=False)  76.4 us
    all_to_all x2, waiting for transfers between devices, spread(): return lax.all_to_all(wide, axes, split_axis=0, concat_axis=0, tiled=True)  41.5 us
    all_to_all x1, blocking collectives, spread(): return lax.all_to_all(wide, axes, split_axis=0, concat_axis=0, tiled=True)  17.3 us
    pallas_call x1, Pallas kernels, feed_forward(): pl.pallas_call(mlp_kernel, in_specs=[vm] * 5 + [hbm] * 2, out_shape=(jax....  16.5 us
    all_to_all x1, blocking collectives, per_device(): lax.all_to_all(mlp_local, 'y', split_axis=0, concat_axis=0, tiled=True)  14.6 us
    ppermute x4, waiting for transfers between devices, swap(): return lax.ppermute(block, axis, [(0, 1), (1, 0)])  13.9 us
    ppermute x1, waiting for transfers between devices, per_device(): right = lax.ppermute(mlp_in, 'y', ring(3))  12.5 us
    all_to_all x1, waiting for transfers between devices, per_device(): ctx = lax.all_to_all(ctx, 'y', split_axis=0, concat_axis=0, tiled=True)  8.7 us
  transfers between devices with their start and end apart: 17, of which 14 were waited for; matrix products, arithmetic and copies ran while one was open for 4% of the time, Pallas kernels for 5%

profile of v1, /device:TPU:0, one launch (start us, length us, event | category | flops | bytes accessed | tf_op | source)
XLA Modules:
  0.0 305.4 jit_solution(5668933929909207611)
XLA Ops:
  7.2 1.2 copy.26
  8.4 1.1 copy.27
  9.5 1.0 convert.28
  10.7 14.6 %all_to_all.25 = bf16[4,288,256]{2,1,0:T(8,128)(2,1)} all-to-all(bf16[4,288,256]{2,1,0:T(8,128)(2,1)S(1)} %bitcast.22), channel_id=1, replica_groups=mesh['z'=4,'xh'=2,'core'=2,'xl'=2,'y'=4] {'y'}, dimensions={0} | all-to-all | bytes 1179648 | tf_op jit(solution)/shard_map/all_to_all | solution.py:269
  25.3 76.4 %all-gather.3.cloned.1.call-done = bf16[64,288,256]{2,1,0:T(8,128)(2,1)} async-done(((bf16[4,288,256]{2,1,0:T(8,128)(2,1)}), bf16[64,288,256]{2,1,0:T(8,128)(2,1)}) %all-gather.3.cloned.1.call-update) | async-done | bytes 9437200 | tf_op jit(solution)/shard_map/all_gather | solution.py:270
  101.8 17.3 %all_to_all.26 = bf16[8,256,128]{2,1,0:T(8,128)(2,1)S(1)} all-to-all(bf16[8,256,128]{2,1,0:T(8,128)(2,1)S(1)} %broadcast_in_dim.19), channel_id=1, replica_groups=mesh['z'=4,'xh'=2,'core'=2,'xl'=2,'y'=4] {'z','xh'}, dimensions={0} | all-to-all | bytes 1048576 | tf_op jit(solution)/shard_map/all_to_all | solution.py:25
  119.2 1.8 broadcast_in_dim.20
  121.0 4.4 %all-to-all-start.3 = ((bf16[4,8,256,128]{3,2,1,0:T(8,128)(2,1)}), bf16[4,8,256,128]{3,2,1,0:T(8,128)(2,1)S(1)}, u32[]{:S(2)}, u32[]{:S(2)}) async-start(bf16[4,8,256,128]{3,2,1,0:T(8,128)(2,1)} %broadcast_in_dim.20), calls=%async_computation.3 | async-start | bytes 4194304 | tf_op jit(solution)/shard_map/all_to_all | solution.py:25
  125.5 25.8 %all-to-all-done.3.own_ref = bf16[4,8,256,128]{3,2,1,0:T(8,128)(2,1)S(1)} async-done(((bf16[4,8,256,128]{3,2,1,0:T(8,128)(2,1)}), bf16[4,8,256,128]{3,2,1,0:T(8,128)(2,1)S(1)}, u32[]{:S(2)}, u32[]{:S(2)}) %all-to-all-start.3) | async-done | bytes 2097184 | tf_op jit(solution)/shard_map/all_to_all | solution.py:25
  151.3 1.1 broadcast_in_dim.14
  152.4 3.6 %all-to-all-start = ((bf16[8,128,512]{2,1,0:T(8,128)(2,1)}), bf16[8,128,512]{2,1,0:T(8,128)(2,1)S(1)}, u32[]{:S(2)}, u32[]{:S(2)}) async-start(bf16[8,128,512]{2,1,0:T(8,128)(2,1)} %broadcast_in_dim.14), calls=%async_computation | async-start | bytes 2097152 | tf_op jit(solution)/shard_map/all_to_all | solution.py:25
  156.0 15.7 %all-to-all-done.own_ref = bf16[8,128,512]{2,1,0:T(8,128)(2,1)S(1)} async-done(((bf16[8,128,512]{2,1,0:T(8,128)(2,1)}), bf16[8,128,512]{2,1,0:T(8,128)(2,1)S(1)}, u32[]{:S(2)}, u32[]{:S(2)}) %all-to-all-start) | async-done | bytes 1048608 | tf_op jit(solution)/shard_map/all_to_all | solution.py:25
  171.8 1.9 multiply_cosine_fusion
  173.9 0.7 collective-permute-done.oth_ref
  174.6 2.2 copy-done
  176.7 6.7 %qkv.1 = (bf16[1024,256]{1,0:T(8,128)(2,1)S(1)}, bf16[2,1024,128]{2,1,0:T(8,128)(2,1)}) custom-call(s32[1]{0:T(128)} %bitcast.core_ref, bf16[1024,2048]{1,0:T(8,128)(2,1)S(1)} %copy-done, bf16[8,128,512]{2,1,0:T(8,128)(2,1)S(1)} %all-to-all-done.own_ref, bf16[8,128,512]{2,1,0:T(8,128)(2,1)} %collective-permute-done.oth_ref, f32[1,2048]{1,0:T(1,128)S(1)} %bitcast.17, ...), custom_call_target="tpu_custom_call" | custom-call | tf_op jit(solution)/shard_map/qkv/pallas_call | solution.py:65
  183.4 1.1 slice.27
  184.5 2.1 collective-permute-start.1
  186.8 0.9 collective-permute-done.1.prior_ref
  187.7 1.0 copy-done.1
  188.8 1.0 copy-done.4
  189.8 6.4 %attend.1 = bf16[4,2,128,256]{3,2,1,0:T(8,128)(2,1)} custom-call(bf16[1024,256]{1,0:T(8,128)(2,1)S(1)} %copy-done.4, bf16[2,1024,128]{2,1,0:T(8,128)(2,1)S(1)} %copy-done.1, bf16[2,512,128]{2,1,0:T(8,128)(2,1)S(1)} %collective-permute-done.1.prior_ref, s32[1024,1]{1,0:T(8,128)S(1)} %copy.25.lo_ref), custom_call_target="tpu_custom_call" | custom-call | tf_op jit(solution)/shard_map/attend/pallas_call | solution.py:128
  196.2 3.5 %all-to-all-start.1 = ((bf16[4,2,128,256]{3,2,1,0:T(8,128)(2,1)}), bf16[4,2,128,256]{3,2,1,0:T(8,128)(2,1)S(1)}, u32[]{:S(2)}, u32[]{:S(2)}) async-start(bf16[4,2,128,256]{3,2,1,0:T(8,128)(2,1)} %attend.1), calls=%async_computation.1 | async-start | bytes 1048576 | tf_op jit(solution)/shard_map/all_to_all | solution.py:283
  199.8 8.7 %all-to-all-done.1.ctx_ref = bf16[4,2,128,256]{3,2,1,0:T(8,128)(2,1)S(1)} async-done(((bf16[4,2,128,256]{3,2,1,0:T(8,128)(2,1)}), bf16[4,2,128,256]{3,2,1,0:T(8,128)(2,1)S(1)}, u32[]{:S(2)}, u32[]{:S(2)}) %all-to-all-start.1) | async-done | bytes 524320 | tf_op jit(solution)/shard_map/all_to_all | solution.py:283
  208.5 3.0 oproj.1
  211.6 1.0 copy-done.2
  212.5 0.6 collective-permute-start.3
  213.2 13.2 %collective-permute-done.3 = bf16[128,2048]{1,0:T(8,128)(2,1)S(1)} collective-permute-done((bf16[128,2048]{1,0:T(8,128)(2,1)S(1)}, bf16[128,2048]{1,0:T(8,128)(2,1)S(1)}, u32[]{:S(2)}, u32[]{:S(2)}) %collective-permute-start.3) | collective-permute-done | bytes 524320 | tf_op jit(solution)/shard_map/ppermute | solution.py:29
  226.4 1.5 add_convert_fusion
  228.4 1.3 collective-permute-start.5
  229.6 0.8 collective-permute-start.4
  230.5 12.5 %collective-permute-done.5.x2_ref = bf16[128,2048]{1,0:T(8,128)(2,1)S(1)} collective-permute-done((bf16[128,2048]{1,0:T(8,128)(2,1)S(1)}, bf16[128,2048]{1,0:T(8,128)(2,1)S(1)}, u32[]{:S(2)}, u32[]{:S(2)}) %collective-permute-start.5) | collective-permute-done | bytes 524320 | tf_op jit(solution)/shard_map/ppermute | solution.py:294
  243.0 2.5 collective-permute-start.7
  245.6 5.6 %collective-permute-done.7.x4_ref = bf16[64,2048]{1,0:T(8,128)(2,1)S(1)} collective-permute-done((bf16[64,2048]{1,0:T(8,128)(2,1)S(1)}, bf16[64,2048]{1,0:T(8,128)(2,1)S(1)}, u32[]{:S(2)}, u32[]{:S(2)}) %collective-permute-start.7) | collective-permute-done | bytes 262176 | tf_op jit(solution)/shard_map/ppermute | solution.py:296
  251.2 3.4 %collective-permute-done.6.x3_ref = bf16[64,2048]{1,0:T(8,128)(2,1)S(1)} collective-permute-done((bf16[64,2048]{1,0:T(8,128)(2,1)S(1)}, bf16[64,2048]{1,0:T(8,128)(2,1)S(1)}, u32[]{:S(2)}, u32[]{:S(2)}) %collective-permute-start.6) | collective-permute-done | bytes 262176 | tf_op jit(solution)/shard_map/ppermute | solution.py:295
  254.6 0.7 copy-done.13
  255.3 16.5 %mlp.1 = (f32[128,2048]{1,0:T(8,128)}, bf16[128,2048]{1,0:T(8,128)(2,1)}, bf16[128,2048]{1,0:T(8,128)(2,1)}, bf16[128,2048]{1,0:T(8,128)(2,1)}) custom-call(bf16[128,2048]{1,0:T(8,128)(2,1)} %copy-done.8, bf16[128,2048]{1,0:T(8,128)(2,1)} %copy-done.10, bf16[128,2048]{1,0:T(8,128)(2,1)} %copy-done.9, bf16[64,2048]{1,0:T(8,128)(2,1)} %copy-done.13, ...), custom_call_target="tpu_custom_call" | custom-call | tf_op jit(solution)/shard_map/mlp/pallas_call | solution.py:223
  271.8 1.2 fusion.4
  273.3 1.0 slice.32
  274.3 1.0 slice.33
  275.3 1.8 collective-permute-start.9
  277.1 2.9 collective-permute-done.11
  279.9 1.0 add_convert_fusion.1
  281.0 1.9 collective-permute-start.12
  283.5 1.0 add_convert_fusion.2
  284.8 7.8 %collective-permute-done.12 = bf16[128,2048]{1,0:T(8,128)(2,1)S(1)} collective-permute-done((bf16[128,2048]{1,0:T(8,128)(2,1)S(1)}, bf16[128,2048]{1,0:T(8,128)(2,1)S(1)}, u32[]{:S(2)}, u32[]{:S(2)}) %collective-permute-start.12) | collective-permute-done | bytes 524320 | tf_op jit(solution)/shard_map/ppermute | solution.py:303
  292.7 4.8 %collective-permute-done.10 = bf16[128,2048]{1,0:T(8,128)(2,1)S(1)} collective-permute-done((bf16[128,2048]{1,0:T(8,128)(2,1)S(1)}, bf16[128,2048]{1,0:T(8,128)(2,1)S(1)}, u32[]{:S(2)}, u32[]{:S(2)}) %collective-permute-start.10) | collective-permute-done | bytes 524320 | tf_op jit(solution)/shard_map/ppermute | solution.py:302
  297.5 1.1 fusion.3
  (67 shorter events, 2.8 us)
Async XLA Ops:
  7.2 94.5 %copy-start.14 = (f32[256,128]{1,0:T(8,128)S(1)}, f32[256,128]{1,0:T(8,128)}, u32[]{:S(2)}) copy-start(f32[256,128]{1,0:T(8,128)} %param.23) | copy-start | bytes 393220
  7.2 94.5 %all-gather.3.cloned.1.call-start = ((), (), s32[]{:S(2)}) async-start(), calls=%async_computation.5 | async-start | bytes 10027008 | tf_op jit(solution)/shard_map/all_gather | solution.py:270
  101.7 152.9 %collective-permute-start.8 = (bf16[8,2,4,288,256]{4,3,2,1,0:T(8,128)(2,1)}, bf16[8,2,4,288,256]{4,3,2,1,0:T(8,128)(2,1)}, u32[]{:S(2)}, u32[]{:S(2)}) collective-permute-start(bf16[8,2,4,288,256]{4,3,2,1,0:T(8,128)(2,1)} %bitcast.20), channel_id=1, source_target_pairs={{0,8},{8,0},{1,9},{9,1},{2,10},{10,2},{3,11},{11,3},{4,12},{12,4},... | collective-permute-start | bytes 28311560 | tf_op jit(solution)/shard_map/ppermute | solution.py:29
  101.7 23.7 %copy-start.16 = (f32[128,128]{1,0:T(8,128)S(1)}, f32[128,128]{1,0:T(8,128)}, u32[]{:S(2)}) copy-start(f32[128,128]{1,0:T(8,128)} %param.21) | copy-start | bytes 196612
  101.7 23.7 %copy-start.17 = (f32[128,128]{1,0:T(8,128)S(1)}, f32[128,128]{1,0:T(8,128)}, u32[]{:S(2)}) copy-start(f32[128,128]{1,0:T(8,128)} %param.22) | copy-start | bytes 196612
  101.7 23.7 %copy-start.15 = (f32[128,256]{1,0:T(8,128)S(1)}, f32[128,256]{1,0:T(8,128)}, u32[]{:S(2)}) copy-start(f32[128,256]{1,0:T(8,128)} %param.20) | copy-start | bytes 393220
  121.0 50.8 %copy-start.19 = (s32[1024]{0:T(1024)S(1)}, s32[1024]{0:T(1024)}, u32[]{:S(2)}) copy-start(s32[1024]{0:T(1024)} %param.15) | copy-start | bytes 12292
  121.0 30.3 %all-to-all-start.3 = ((bf16[4,8,256,128]{3,2,1,0:T(8,128)(2,1)}), bf16[4,8,256,128]{3,2,1,0:T(8,128)(2,1)S(1)}, u32[]{:S(2)}, u32[]{:S(2)}) async-start(bf16[4,8,256,128]{3,2,1,0:T(8,128)(2,1)} %broadcast_in_dim.20), calls=%async_computation.3 | async-start | bytes 4194304 | tf_op jit(solution)/shard_map/all_to_all | solution.py:25
  125.4 49.1 %copy-start.5 = (f32[2048]{0:T(1024)S(1)}, f32[2048]{0:T(1024)}, u32[]{:S(2)}) copy-start(f32[2048]{0:T(1024)} %param.16) | copy-start | bytes 24580
  125.4 49.1 %copy-start.6 = (f32[128]{0:T(128)S(1)}, f32[128]{0:T(128)}, u32[]{:S(2)}) copy-start(f32[128]{0:T(128)} %param.18) | copy-start | bytes 1540
  125.4 49.1 %copy-start.7 = (f32[128]{0:T(128)S(1)}, f32[128]{0:T(128)}, u32[]{:S(2)}) copy-start(f32[128]{0:T(128)} %param.19) | copy-start | bytes 1540
  152.4 19.4 %all-to-all-start = ((bf16[8,128,512]{2,1,0:T(8,128)(2,1)}), bf16[8,128,512]{2,1,0:T(8,128)(2,1)S(1)}, u32[]{:S(2)}, u32[]{:S(2)}) async-start(bf16[8,128,512]{2,1,0:T(8,128)(2,1)} %broadcast_in_dim.14), calls=%async_computation | async-start | bytes 2097152 | tf_op jit(solution)/shard_map/all_to_all | solution.py:25
  155.9 52.6 %collective-permute-start.2 = (bf16[4,8,256,128]{3,2,1,0:T(8,128)(2,1)S(1)}, bf16[4,8,256,128]{3,2,1,0:T(8,128)(2,1)}, u32[]{:S(2)}, u32[]{:S(2)}) collective-permute-start(bf16[4,8,256,128]{3,2,1,0:T(8,128)(2,1)S(1)} %all-to-all-done.3.own_ref), channel_id=1, source_target_pairs={{0,8},{8,0},{1,9},{9,1},{2,10},{10,2},{3,11},{11,3},{4,12},{12,4},... | collective-permute-start | bytes 6291464 | tf_op jit(solution)/shard_map/ppermute | solution.py:29
  171.7 2.8 collective-permute-start
  174.5 2.2 copy-start
  183.4 3.2 %copy-start.3 = (bf16[1024,256]{1,0:T(8,128)(2,1)}, bf16[1024,256]{1,0:T(8,128)(2,1)S(1)}, u32[]{:S(2)}) copy-start(bf16[1024,256]{1,0:T(8,128)(2,1)S(1)} %get-tuple-element.10.q_ref) | copy-start | bytes 1572868
  184.5 3.2 %collective-permute-start.1 = (bf16[2,512,128]{2,1,0:T(8,128)(2,1)S(1)}, bf16[2,512,128]{2,1,0:T(8,128)(2,1)S(1)}, u32[]{:S(2)}, u32[]{:S(2)}) collective-permute-start(bf16[2,512,128]{2,1,0:T(8,128)(2,1)S(1)} %slice.27), channel_id=1, source_target_pairs={{0,8},{8,16},{16,24},{24,32},{32,40},{40,48},{48,56},{56,64},{64,7... | collective-permute-start | bytes 786440 | tf_op jit(solution)/shard_map/ppermute | solution.py:281
  187.7 1.0 copy-start.1
  188.8 1.0 copy-start.4
  196.2 12.3 %all-to-all-start.1 = ((bf16[4,2,128,256]{3,2,1,0:T(8,128)(2,1)}), bf16[4,2,128,256]{3,2,1,0:T(8,128)(2,1)S(1)}, u32[]{:S(2)}, u32[]{:S(2)}) async-start(bf16[4,2,128,256]{3,2,1,0:T(8,128)(2,1)} %attend.1), calls=%async_computation.1 | async-start | bytes 1048576 | tf_op jit(solution)/shard_map/all_to_all | solution.py:283
  199.7 28.5 %copy-start.18 = (f32[2048]{0:T(1024)S(1)}, f32[2048]{0:T(1024)}, u32[]{:S(2)}) copy-start(f32[2048]{0:T(1024)} %param.17) | copy-start | bytes 24580
  211.6 1.0 copy-start.2
  212.5 13.9 %collective-permute-start.3 = (bf16[128,2048]{1,0:T(8,128)(2,1)S(1)}, bf16[128,2048]{1,0:T(8,128)(2,1)S(1)}, u32[]{:S(2)}, u32[]{:S(2)}) collective-permute-start(bf16[128,2048]{1,0:T(8,128)(2,1)S(1)} %get-tuple-element.13), channel_id=1, source_target_pairs={{0,4},{4,0},{1,5},{5,1},{2,6},{6,2},{3,7},{7,3},{8,12},{12,8},{9,1... | collective-permute-start | bytes 1572872 | tf_op jit(solution)/shard_map/ppermute | solution.py:29
  228.4 26.2 %copy-start.8 = (bf16[128,2048]{1,0:T(8,128)(2,1)}, bf16[128,2048]{1,0:T(8,128)(2,1)S(1)}, u32[]{:S(2)}) copy-start(bf16[128,2048]{1,0:T(8,128)(2,1)S(1)} %fusion.2.x0_ref) | copy-start | bytes 1572868
  228.4 14.6 %collective-permute-start.5 = (bf16[128,2048]{1,0:T(8,128)(2,1)S(1)}, bf16[128,2048]{1,0:T(8,128)(2,1)S(1)}, u32[]{:S(2)}, u32[]{:S(2)}) collective-permute-start(bf16[128,2048]{1,0:T(8,128)(2,1)S(1)} %fusion.2.x0_ref), channel_id=1, source_target_pairs={{0,3},{1,0},{2,1},{3,2},{4,7},{5,4},{6,5},{7,6},{8,11},{9,8},{10,9... | collective-permute-start | bytes 1572872 | tf_op jit(solution)/shard_map/ppermute | solution.py:294
  229.6 15.9 %collective-permute-start.4 = (bf16[128,2048]{1,0:T(8,128)(2,1)S(1)}, bf16[128,2048]{1,0:T(8,128)(2,1)S(1)}, u32[]{:S(2)}, u32[]{:S(2)}) collective-permute-start(bf16[128,2048]{1,0:T(8,128)(2,1)S(1)} %fusion.2.x0_ref), channel_id=1, source_target_pairs={{0,1},{1,2},{2,3},{3,0},{4,5},{5,6},{6,7},{7,4},{8,9},{9,10},{10,1... | collective-permute-start | bytes 1572872 | tf_op jit(solution)/shard_map/ppermute | solution.py:293
  243.0 11.6 %copy-start.9 = (bf16[128,2048]{1,0:T(8,128)(2,1)}, bf16[128,2048]{1,0:T(8,128)(2,1)S(1)}, u32[]{:S(2)}) copy-start(bf16[128,2048]{1,0:T(8,128)(2,1)S(1)} %collective-permute-done.5.x2_ref) | copy-start | bytes 1572868
  243.0 8.2 %collective-permute-start.7 = (bf16[64,2048]{1,0:T(8,128)(2,1)S(1)}, bf16[64,2048]{1,0:T(8,128)(2,1)S(1)}, u32[]{:S(2)}, u32[]{:S(2)}) collective-permute-start(bf16[64,2048]{1,0:T(8,128)(2,1)S(1)} %slice.37), channel_id=1, source_target_pairs={{0,3},{1,0},{2,1},{3,2},{4,7},{5,4},{6,5},{7,6},{8,11},{9,8},{10,9... | collective-permute-start | bytes 786440 | tf_op jit(solution)/shard_map/ppermute | solution.py:296
  245.5 9.1 %copy-start.10 = (bf16[128,2048]{1,0:T(8,128)(2,1)}, bf16[128,2048]{1,0:T(8,128)(2,1)S(1)}, u32[]{:S(2)}) copy-start(bf16[128,2048]{1,0:T(8,128)(2,1)S(1)} %collective-permute-done.4.x1_ref) | copy-start | bytes 1572868
  245.5 9.1 %collective-permute-start.6 = (bf16[64,2048]{1,0:T(8,128)(2,1)S(1)}, bf16[64,2048]{1,0:T(8,128)(2,1)S(1)}, u32[]{:S(2)}, u32[]{:S(2)}) collective-permute-start(bf16[64,2048]{1,0:T(8,128)(2,1)S(1)} %slice.36), channel_id=1, source_target_pairs={{0,1},{1,2},{2,3},{3,0},{4,5},{5,6},{6,7},{7,4},{8,9},{9,10},{10,1... | collective-permute-start | bytes 786440 | tf_op jit(solution)/shard_map/ppermute | solution.py:295
  251.2 3.4 %copy-start.12 = (bf16[64,2048]{1,0:T(8,128)(2,1)}, bf16[64,2048]{1,0:T(8,128)(2,1)S(1)}, u32[]{:S(2)}) copy-start(bf16[64,2048]{1,0:T(8,128)(2,1)S(1)} %collective-permute-done.7.x4_ref) | copy-start | bytes 786436
  254.6 0.7 copy-start.13
  271.8 25.7 %copy-start.11 = (f32[128,2048]{1,0:T(8,128)S(1)}, f32[128,2048]{1,0:T(8,128)}, u32[]{:S(2)}) copy-start(f32[128,2048]{1,0:T(8,128)} %get-tuple-element.14) | copy-start | bytes 3145732
  273.0 7.0 %collective-permute-start.11 = (bf16[64,2048]{1,0:T(8,128)(2,1)S(1)}, bf16[64,2048]{1,0:T(8,128)(2,1)S(1)}, u32[]{:S(2)}, u32[]{:S(2)}) collective-permute-start(bf16[64,2048]{1,0:T(8,128)(2,1)S(1)} %get-tuple-element.19), channel_id=1, source_target_pairs={{0,3},{1,0},{2,1},{3,2},{4,7},{5,4},{6,5},{7,6},{8,11},{9,8},{10,9... | collective-permute-start | bytes 786440 | tf_op jit(solution)/shard_map/ppermute | solution.py:299
  275.3 8.2 %collective-permute-start.9 = (bf16[64,2048]{1,0:T(8,128)(2,1)S(1)}, bf16[64,2048]{1,0:T(8,128)(2,1)S(1)}, u32[]{:S(2)}, u32[]{:S(2)}) collective-permute-start(bf16[64,2048]{1,0:T(8,128)(2,1)S(1)} %get-tuple-element.18), channel_id=1, source_target_pairs={{0,1},{1,2},{2,3},{3,0},{4,5},{5,6},{6,7},{7,4},{8,9},{9,10},{10,1... | collective-permute-start | bytes 786440 | tf_op jit(solution)/shard_map/ppermute | solution.py:298
  281.0 11.7 %collective-permute-start.12 = (bf16[128,2048]{1,0:T(8,128)(2,1)S(1)}, bf16[128,2048]{1,0:T(8,128)(2,1)S(1)}, u32[]{:S(2)}, u32[]{:S(2)}) collective-permute-start(bf16[128,2048]{1,0:T(8,128)(2,1)S(1)} %pad_maximum_fusion.2), channel_id=1, source_target_pairs={{0,3},{1,0},{2,1},{3,2},{4,7},{5,4},{6,5},{7,6},{8,11},{9,8},{10,9... | collective-permute-start | bytes 1572872 | tf_op jit(solution)/shard_map/ppermute | solution.py:303
  284.6 12.9 %collective-permute-start.10 = (bf16[128,2048]{1,0:T(8,128)(2,1)S(1)}, bf16[128,2048]{1,0:T(8,128)(2,1)S(1)}, u32[]{:S(2)}, u32[]{:S(2)}) collective-permute-start(bf16[128,2048]{1,0:T(8,128)(2,1)S(1)} %pad_maximum_fusion.1), channel_id=1, source_target_pairs={{0,1},{1,2},{2,3},{3,0},{4,5},{5,6},{6,7},{7,4},{8,9},{9,10},{10,1... | collective-permute-start | bytes 1572872 | tf_op jit(solution)/shard_map/ppermute | solution.py:302
Sparse Core Ops, SparseCore 0:
  25.4 76.1 all-gather.2

commit v2 on v1

v2 whole, which is shorter than its diff:
```python
import math

import jax
import jax.numpy as jnp
from jax import lax
from jax.experimental import pallas as pl
from jax.experimental.pallas import tpu as pltpu
from jax.sharding import Mesh
from jax.sharding import PartitionSpec as P

HEAD = 128
BF = jnp.bfloat16
F32 = jnp.float32
REQ = ("z", "xh", "core")
MDL = ("xl", "y")


def ring(step):
    return [(i, (i + step) % 4) for i in range(4)]


def swap(block, axis):
    return lax.ppermute(block, axis, [(0, 1), (1, 0)])


def shard(at_ref, e, side):
    z, xh, core = at_ref[0], at_ref[1], at_ref[2]
    return lax.rem(z + lax.div(jnp.int32(e), 2), 4) * 4 + lax.rem(xh + lax.rem(jnp.int32(e), 2), 2) * 2 + (core if side == 0 else 1 - core)


PLACES = ((0, 0, 2), (1, 2, 2), (2, 4, 1), (3, 5, 1), (4, 6, 2))


def qkv_kernel(at_ref, x_ref, *refs):
    pieces, (gain_ref, qg_ref, kg_ref, cs_ref, q_ref, kv_ref, w_ref) = refs[:10], refs[10:]

    @pl.when(pl.program_id(0) == 0)
    def _():
        for n, first, count in PLACES:
            for side in range(2):
                for i in range(count):
                    at = pl.multiple_of(shard(at_ref, first + i, side) * 128, 128)
                    w_ref[pl.ds(at, 128), :] = pieces[2 * n + side][i, :128]

    x = x_ref[...].astype(F32)
    scale = lax.rsqrt(jnp.mean(x * x, axis=-1, keepdims=True) + 1e-06)
    normed = (x * scale * gain_ref[...]).astype(BF)
    raw = jnp.dot(normed, w_ref[...], preferred_element_type=F32)
    cs = cs_ref[...]
    turned = pltpu.roll(cs, 64, 1)
    low = lax.broadcasted_iota(jnp.int32, cs.shape, 1) < 64
    cosine = jnp.where(low, cs, turned)
    sine = jnp.where(low, -turned, cs)

    def head(t, gain):
        t = t * lax.rsqrt(jnp.mean(t * t, axis=-1, keepdims=True) + 1e-06) * gain
        return (t * cosine + pltpu.roll(t, 64, 1) * sine).astype(BF)

    q_ref[:, :128] = head(raw[:, :128], qg_ref[...])
    q_ref[:, 128:] = head(raw[:, 128:256], qg_ref[...])
    kv_ref[0] = head(raw[:, 256:384], kg_ref[...])
    kv_ref[1] = raw[:, 384:].astype(BF)


def project(at, tokens, pieces, attn_gain, q_gain, key_gain, cs):
    rows = tokens.shape[0]
    tile = 256
    fixed = lambda *shape: pl.BlockSpec(shape, lambda i, c: (0,) * len(shape))
    return pl.pallas_call(
        qkv_kernel,
        grid_spec=pltpu.PrefetchScalarGridSpec(
            num_scalar_prefetch=1,
            grid=(rows // tile,),
            in_specs=[
                pl.BlockSpec((tile, 2048), lambda i, c: (i, 0)),
                *(fixed(count, 192, 512) for _, _, count in PLACES for _ in range(2)),
                fixed(1, 2048),
                fixed(1, 128),
                fixed(1, 128),
                pl.BlockSpec((tile, 128), lambda i, c: (i, 0)),
            ],
            out_specs=[
                pl.BlockSpec((tile, 256), lambda i, c: (i, 0)),
                pl.BlockSpec((2, tile, 128), lambda i, c: (0, i, 0)),
            ],
            scratch_shapes=[pltpu.VMEM((2048, 512), BF)],
        ),
        out_shape=(
            jax.ShapeDtypeStruct((rows, 256), BF),
            jax.ShapeDtypeStruct((2, rows, 128), BF),
        ),
        compiler_params=pltpu.CompilerParams(vmem_limit_bytes=40 << 20),
        name="qkv",
    )(at, tokens, *pieces, attn_gain[None], q_gain[None], key_gain[None], cs)


def attend_kernel(y_ref, q_ref, kv_ref, prior_ref, lo_ref, *refs):
    out_ref = refs[4]
    factor = HEAD ** (-0.5) * math.log2(math.e)
    nt = (((1,), (1,)), ((), ()))
    for i in range(4):
        first = i * 256
        skip = 256 if i == 3 else 0
        count = first + 256
        lo = lo_ref[first : first + 256, :]
        row = lax.broadcasted_iota(jnp.int32, (256, count), 0) + first
        col = lax.broadcasted_iota(jnp.int32, (256, count), 1)
        near = (col >= lo) & (col <= row)
        prior_col = lax.broadcasted_iota(jnp.int32, (256, 512 - skip), 1) + (skip - 512)
        far = prior_col >= lo
        for h in range(2):
            q = q_ref[first : first + 256, h * 128 : h * 128 + 128]
            s1 = lax.dot_general(q, kv_ref[0, :count], nt, preferred_element_type=F32)
            s0 = lax.dot_general(q, prior_ref[0, skip:], nt, preferred_element_type=F32)
            s1 = jnp.where(near, s1, -1e30)
            s0 = jnp.where(far, s0, -1e30)
            top = jnp.maximum(jnp.max(s1, -1, keepdims=True), jnp.max(s0, -1, keepdims=True))
            e1 = jnp.exp2((s1 - top) * factor)
            e0 = jnp.exp2((s0 - top) * factor)
            inv = 1.0 / (jnp.sum(e1, -1, keepdims=True) + jnp.sum(e0, -1, keepdims=True))
            p1 = (e1 * inv).astype(BF)
            p0 = (e0 * inv).astype(BF)
            o = jnp.dot(p1, kv_ref[1, :count], preferred_element_type=F32)
            o = o + jnp.dot(p0, prior_ref[1, skip:], preferred_element_type=F32)
            o = o.astype(BF)
            for part in range(2):
                block = 2 * i + part
                out_ref[block % 4, block // 4, :, h * 128 : h * 128 + 128] = o[part * 128 : part * 128 + 128]
    for k in range(4):
        refs[k][...] = out_ref[lax.rem(y_ref[0] + k, 4)]


def attend(y, q, kv, prior, lo):
    vm = pl.BlockSpec(memory_space=pltpu.VMEM)
    return pl.pallas_call(
        attend_kernel,
        in_specs=[pl.BlockSpec(memory_space=pltpu.SMEM)] + [vm] * 4,
        out_shape=[jax.ShapeDtypeStruct((2, 128, 256), BF)] * 4,
        scratch_shapes=[pltpu.VMEM((4, 2, 128, 256), BF)],
        compiler_params=pltpu.CompilerParams(vmem_limit_bytes=40 << 20),
        name="attend",
    )(y, q, kv, prior, lo)


def out_kernel(at_ref, c0_ref, c1_ref, c2_ref, c3_ref, *refs):
    near, far, (keep_ref, send_ref, w_ref, x_ref, sems) = refs[:10], refs[10:18], refs[18:]
    xl = at_ref[3]

    def each(act):
        sources = [(0, first, count, 128, near[2 * n : 2 * n + 2]) for n, first, count in PLACES]
        for n, (s, first, count) in enumerate(((1, 0, 8), (2, 0, 4), (2, 4, 4), (3, 0, 8))):
            sources.append((s, first, count, 0, far[2 * n : 2 * n + 2]))
        for s, first, count, offset, pair in sources:
            for side in range(2):

                def step(i, carry, s=s, first=first, offset=offset, src=pair[side], side=side):
                    at = pl.ds(pl.multiple_of(shard(at_ref, first + i, side) * 128, 128), 128)
                    for k in range(4):
                        act(pltpu.make_async_copy(
                            src.at[i, offset : offset + 64, k * 128 : k * 128 + 128],
                            w_ref.at[s * 256 + k * 64 : s * 256 + k * 64 + 64, at],
                            sems.at[side, s, first + i, k],
                        ))
                    return carry

                lax.fori_loop(0, count, step, 0)

    each(lambda c: c.start())
    for s, c in enumerate((c0_ref, c1_ref, c2_ref, c3_ref)):
        x_ref[:128, s * 256 : s * 256 + 256] = c[xl]
        x_ref[128:, s * 256 : s * 256 + 256] = c[1 - xl]
    each(lambda c: c.wait())
    x = x_ref[...]

    def column(n, carry):
        at = pl.ds(pl.multiple_of(n * 512, 512), 512)
        total = jnp.dot(x, w_ref[:, at], preferred_element_type=F32)
        keep_ref[:, at] = total[:128]
        send_ref[:, at] = total[128:].astype(BF)
        return carry

    lax.fori_loop(0, 4, column, 0)


def out_project(at, ctx, near, far):
    vm = pl.BlockSpec(memory_space=pltpu.VMEM)
    anywhere = pl.BlockSpec(memory_space=pl.ANY)
    return pl.pallas_call(
        out_kernel,
        in_specs=[pl.BlockSpec(memory_space=pltpu.SMEM)] + [vm] * 4 + [anywhere] * 18,
        out_shape=(
            jax.ShapeDtypeStruct((128, 2048), F32),
            jax.ShapeDtypeStruct((128, 2048), BF),
        ),
        scratch_shapes=[
            pltpu.VMEM((1024, 2048), BF),
            pltpu.VMEM((256, 1024), BF),
            pltpu.SemaphoreType.DMA((2, 4, 8, 4)),
        ],
        compiler_params=pltpu.CompilerParams(vmem_limit_bytes=40 << 20),
        name="oproj",
    )(at, *ctx, *near, *far)


def fetcher(own_ref, oth_ref, w_ref, sems, y):
    def copy(c, g, m):
        src = own_ref if c == 0 else oth_ref
        at = pl.multiple_of(((m // 4) * 4 + lax.rem(y + lax.rem(m, 4), 4)) * 256, 256)
        return pltpu.make_async_copy(
            src.at[:, m // 4, lax.rem(m, 4), g * 96 : g * 96 + 96, :],
            w_ref.at[g, c * 8 : c * 8 + 8, :, pl.ds(at, 256)],
            sems.at[g, c, m],
        )

    def each(c, groups, act):
        def step(m, carry):
            for g in range(groups):
                act(copy(c, g, m))
            return carry

        lax.fori_loop(0, 8, step, 0)

    return each


def gate_kernel(y_ref, x0_ref, x1_ref, x2_ref, x3_ref, x4_ref, own_ref, oth_ref, hid_ref, w_ref, x_ref, sems):
    nt = (((1,), (1,)), ((), ()))
    each = fetcher(own_ref, oth_ref, w_ref, sems, y_ref[0])
    each(0, 2, lambda c: c.start())
    each(1, 2, lambda c: c.start())
    x_ref[0:128] = x0_ref[...]
    x_ref[128:256] = x1_ref[...]
    x_ref[256:384] = x2_ref[...]
    x_ref[384:448] = x3_ref[...]
    x_ref[448:512] = x4_ref[...]
    x = x_ref[...]

    for c in range(2):
        each(c, 2, lambda copy: copy.wait())
        gate_w = w_ref[0, c * 8 : c * 8 + 8].reshape(768, 2048)
        up_w = w_ref[1, c * 8 : c * 8 + 8].reshape(768, 2048)
        for t in range(3):
            gate = lax.dot_general(x, gate_w[t * 256 : t * 256 + 256], nt, preferred_element_type=F32)
            upper = lax.dot_general(x, up_w[t * 256 : t * 256 + 256], nt, preferred_element_type=F32)
            hidden = gate / (1.0 + jnp.exp(-gate)) * upper
            at = c * 768 + t * 256
            hid_ref[:, at : at + 256] = hidden.astype(BF)


def down_kernel(y_ref, hid_ref, own_ref, oth_ref, keep_ref, left_ref, right_ref, far_ref, w_ref, sems):
    each = fetcher(own_ref, oth_ref, w_ref, sems, y_ref[0])
    for c in range(2):
        each(c, 1, lambda copy: copy.start())
    for c in range(2):
        each(c, 1, lambda copy: copy.wait())
    hid = hid_ref[...]

    def column(n, carry):
        at = pl.ds(pl.multiple_of(n * 512, 512), 512)
        out = jnp.dot(hid, w_ref[0, :, :, at].reshape(1536, 512), preferred_element_type=F32)
        keep_ref[:, at] = out[:128]
        left_ref[:, at] = out[128:256].astype(BF)
        right_ref[:, at] = out[256:384].astype(BF)
        far_ref[:, at] = out[384:].astype(BF)
        return carry

    lax.fori_loop(0, 4, column, 0)


def gate_up(y, pieces, own, oth):
    vm = pl.BlockSpec(memory_space=pltpu.VMEM)
    hbm = pl.BlockSpec(memory_space=pltpu.HBM)
    return pl.pallas_call(
        gate_kernel,
        in_specs=[pl.BlockSpec(memory_space=pltpu.SMEM)] + [vm] * 5 + [hbm] * 2,
        out_shape=jax.ShapeDtypeStruct((512, 1536), BF),
        scratch_shapes=[
            pltpu.VMEM((2, 16, 96, 2048), BF),
            pltpu.VMEM((512, 2048), BF),
            pltpu.SemaphoreType.DMA((2, 2, 8)),
        ],
        compiler_params=pltpu.CompilerParams(vmem_limit_bytes=40 << 20),
        name="gate_up",
    )(y, *pieces, own, oth)


def down(y, hidden, own, oth):
    vm = pl.BlockSpec(memory_space=pltpu.VMEM)
    hbm = pl.BlockSpec(memory_space=pltpu.HBM)
    part = jax.ShapeDtypeStruct((128, 2048), BF)
    return pl.pallas_call(
        down_kernel,
        in_specs=[pl.BlockSpec(memory_space=pltpu.SMEM), vm] + [hbm] * 2,
        out_shape=(jax.ShapeDtypeStruct((128, 2048), F32), part, part, part),
        scratch_shapes=[
            pltpu.VMEM((1, 16, 96, 2048), BF),
            pltpu.SemaphoreType.DMA((1, 2, 8)),
        ],
        compiler_params=pltpu.CompilerParams(vmem_limit_bytes=40 << 20),
        name="down",
    )(y, hidden, own, oth)


def pack_kernel(q_ref, k_ref, v_ref, o_ref, out_ref):
    out_ref[:128, :256] = q_ref[...].astype(BF)
    out_ref[:128, 256:384] = k_ref[...].astype(BF)
    out_ref[:128, 384:] = v_ref[...].astype(BF)
    for k in range(4):
        out_ref[128:, k * 128 : k * 128 + 128] = o_ref[k * 64 : k * 64 + 64].astype(BF)


def pack(q, k, v, o):
    return pl.pallas_call(
        pack_kernel,
        out_shape=jax.ShapeDtypeStruct((192, 512), BF),
        name="pack",
    )(q, k, v, o)


def prep_kernel(y_ref, gate_ref, up_ref, down_ref, p0_ref, p1_ref, p2_ref, p3_ref, g_ref, u_ref):
    g_ref[...] = gate_ref[...].T
    u_ref[...] = up_ref[...].T
    for k, out_ref in enumerate((p0_ref, p1_ref, p2_ref, p3_ref)):
        at = pl.ds(pl.multiple_of(lax.rem(y_ref[0] + k, 4) * 96, 96), 96)
        out_ref[:96] = g_ref[at, :].astype(BF)
        out_ref[96:192] = u_ref[at, :].astype(BF)
        out_ref[192:] = down_ref[at, :].astype(BF)


def prepare(y, gate, up, down):
    vm = pl.BlockSpec(memory_space=pltpu.VMEM)
    return pl.pallas_call(
        prep_kernel,
        in_specs=[pl.BlockSpec(memory_space=pltpu.SMEM)] + [vm] * 3,
        out_shape=[jax.ShapeDtypeStruct((288, 256), BF)] * 4,
        scratch_shapes=[pltpu.VMEM((384, 256), F32), pltpu.VMEM((384, 256), F32)],
        name="prep",
    )(y, gate, up, down)


def join_kernel(p0_ref, p1_ref, p2_ref, p3_ref, gu_ref, d_ref):
    for k, ref in enumerate((p0_ref, p1_ref, p2_ref, p3_ref)):
        gu_ref[k] = ref[:192]
        d_ref[k] = ref[192:]


def join(parts):
    return pl.pallas_call(
        join_kernel,
        out_shape=(jax.ShapeDtypeStruct((4, 192, 256), BF), jax.ShapeDtypeStruct((4, 96, 256), BF)),
        name="join",
    )(*parts)


def trade(parts):
    return [parts[0]] + [lax.ppermute(parts[4 - k], "y", ring(4 - k)) for k in (1, 2, 3)]


def per_device(
    tokens,
    doc_ids,
    positions,
    attn_gain,
    mlp_gain,
    q_gain,
    key_norm_gain,
    q_weight,
    key_matrix,
    value_matrix,
    o_weight,
    gate_weight,
    up_weight,
    down_weight,
):
    rows = tokens.shape[0]
    at = jnp.stack([lax.axis_index(name).astype(jnp.int32) for name in ("z", "xh", "core", "xl")])
    xl = lax.axis_index("xl").astype(jnp.int32)
    y = lax.axis_index("y").astype(jnp.int32)
    hold = lax.optimization_barrier

    packed = pack(q_weight, key_matrix, value_matrix, o_weight)
    packed_xh = swap(packed, "xh")

    parts = trade(prepare(y[None], gate_weight, up_weight, down_weight))
    half = HEAD // 2
    freq = jnp.exp(jnp.arange(half, dtype=F32) * (-2.0 * math.log(1000000.0) / HEAD))
    angle = positions.astype(F32)[:, None] * freq[None, :]
    cs = jnp.concatenate([jnp.cos(angle), jnp.sin(angle)], axis=1)
    cs, packed_xh, *parts = hold((cs, packed_xh, *parts))
    gu_group, d_group = join(parts)
    gu_own = lax.all_gather(gu_group, ("z", "xh", "xl"), axis=0, tiled=False).reshape(8, 2, 4, 192, 256)
    d_own = lax.all_gather(d_group, ("z", "xh", "xl"), axis=0, tiled=False).reshape(8, 2, 4, 96, 256)

    lo = (jnp.arange(rows, dtype=jnp.int32) - positions)[:, None]

    here = jnp.stack([packed, packed_xh])
    up = lax.ppermute(here, "z", ring(3))
    under = lax.ppermute(here, "z", ring(1))
    across = [lax.ppermute(up[:1], "z", ring(3)), lax.ppermute(under[1:], "z", ring(1))]
    near = []
    for piece in (here, up, *across, under):
        near += [piece, swap(piece, "core")]

    o_here = jnp.concatenate([piece[:, 128:] for piece in near[::2]])
    o_up = lax.ppermute(o_here, "y", ring(3))
    o_down = lax.ppermute(o_here, "y", ring(1))
    o_far = [lax.ppermute(o_up[:4], "y", ring(3)), lax.ppermute(o_down[4:], "y", ring(1))]
    far = []
    for piece in (o_up, *o_far, o_down):
        far += [piece, swap(piece, "core")]

    q, cache = project(at, tokens, near, attn_gain, q_gain, key_norm_gain, cs)
    prior = lax.ppermute(cache[:, rows // 2 :], REQ, [(i - 1, i) for i in range(1, 16)])
    ctx = trade(attend(y[None], q, cache, prior, lo))
    keep, send = out_project(at, ctx, near, far)
    got = swap(send, "xl")

    own_rows = lax.dynamic_slice_in_dim(tokens, (xl * 4 + y) * 128, 128, 0).astype(F32)
    resid = (own_rows + (keep + got.astype(F32))).astype(BF)
    resid = hold(resid).astype(F32)
    scale = lax.rsqrt(jnp.mean(resid * resid, axis=-1, keepdims=True) + 1e-06)
    mlp_in = (resid * scale * mlp_gain).astype(BF)

    gu_own, mlp_in = hold((gu_own, mlp_in))
    gu_oth = swap(gu_own, "core")
    left = lax.ppermute(mlp_in, "y", ring(1))
    right = lax.ppermute(mlp_in, "y", ring(3))
    far_top = lax.ppermute(left[:64], "y", ring(1))
    far_bottom = lax.ppermute(right[64:], "y", ring(3))
    d_own, left, right, far_top, far_bottom = hold((d_own, left, right, far_top, far_bottom))
    d_oth = swap(d_own, "core")
    hidden = gate_up(y[None], (mlp_in, left, right, far_top, far_bottom), gu_own, gu_oth)
    keep, to_left, to_right, to_far = down(y[None], hidden, d_own, d_oth)
    via_left = lax.ppermute(to_far[:64], "y", ring(1))
    via_right = lax.ppermute(to_far[64:], "y", ring(3))
    to_right = jnp.concatenate([(to_right[:64].astype(F32) + via_left.astype(F32)).astype(BF), to_right[64:]])
    to_left = jnp.concatenate([to_left[:64], (to_left[64:].astype(F32) + via_right.astype(F32)).astype(BF)])
    from_left = lax.ppermute(to_right, "y", ring(1))
    from_right = lax.ppermute(to_left, "y", ring(3))
    total = keep + from_left.astype(F32) + from_right.astype(F32)
    return ((resid + total).astype(BF), cache)


def solution(mesh):
    fine = Mesh(mesh.devices.reshape(4, 2, 2, 2, 4), REQ + MDL)
    rows = P(REQ)
    in_specs = (
        P(REQ, None),
        rows,
        rows,
        P(),
        P(),
        P(),
        P(),
        P(REQ, MDL),
        P(REQ, MDL),
        P(REQ, MDL),
        P(MDL, REQ),
        P(MDL, REQ),
        P(MDL, REQ),
        P(REQ, MDL),
    )
    out_specs = (P(REQ + MDL, None), P(None, REQ, MDL))
    return jax.shard_map(per_device, mesh=fine, in_specs=in_specs, out_specs=out_specs, check_vma=False)
```

time: 306 us -> 225 us (0.74)
  the two profiles are of different devices: /device:TPU:0 before, /device:TPU:32 now
where the time goes in v2:
time: 225 us; the launch traced here: 222 us
  waiting for transfers between devices  96 us (43%)
  starting transfers between devices  43.8 us (19%)
  Pallas kernels  41.5 us (18%)
  local copies, waits for them, and re-layouts  18 us (8%)
  between operations  14.5 us (6%)
  other arithmetic  7.8 us (3%)
    ppermute x13, waiting for transfers between devices, swap(): return lax.ppermute(block, axis, [(0, 1), (1, 0)])  22.8 us
    ppermute x6, waiting for transfers between devices, trade(): lax.ppermute(parts[4 - k], 'y', ring(4 - k))  13.2 us
    unnamed x39, local copies, waits for them, and re-layouts  12.7 us
    ppermute x1, waiting for transfers between devices, per_device(): left = lax.ppermute(mlp_in, 'y', ring(1))  12.2 us
    ppermute x1, waiting for transfers between devices, per_device(): from_left = lax.ppermute(to_right, 'y', ring(1))  11.4 us
    ppermute x6, starting transfers between devices, trade(): lax.ppermute(parts[4 - k], 'y', ring(4 - k))  11.2 us
    pallas_call x1, Pallas kernels, gate_up(): pl.pallas_call(gate_kernel, in_specs=[pl.BlockSpec(memory_space=pltpu.SME...  8.54 us
    ppermute x1, waiting for transfers between devices, per_device(): up = lax.ppermute(here, 'z', ring(3))  8.48 us
  transfers between devices with their start and end apart: 38, of which 15 were waited for; matrix products, arithmetic and copies ran while one was open for 7% of the time, Pallas kernels for 14%

profile of v2, /device:TPU:32, one launch (start us, length us, event | category | flops | bytes accessed | tf_op | source)
XLA Modules:
  0.0 221.7 jit_solution(12277153069246636791)
XLA Ops:
  7.2 2.4 %prep.1 = (bf16[288,256]{1,0:T(8,128)(2,1)}, bf16[288,256]{1,0:T(8,128)(2,1)}, bf16[288,256]{1,0:T(8,128)(2,1)}, bf16[288,256]{1,0:T(8,128)(2,1)}) custom-call(s32[1]{0:T(128)} %bitcast.4.y_ref, f32[256,384]{1,0:T(8,128)} %gate_ref.1, f32[256,384]{1,0:T(8,128)} %up_ref.1, f32[384,256]{1,0:T(8,128)} %down_ref.1), custom_call_target="tpu_custom_call" | custom-call | tf_op jit(solution)/shard_map/prep/pallas_call | solution.py:332
  9.6 3.0 %collective-permute-start.1 = (bf16[288,256]{1,0:T(8,128)(2,1)}, bf16[288,256]{1,0:T(8,128)(2,1)S(1)}, u32[]{:S(2)}, u32[]{:S(2)}) collective-permute-start(bf16[288,256]{1,0:T(8,128)(2,1)} %get-tuple-element.34), channel_id=1, source_target_pairs={{0,3},{1,0},{2,1},{3,2},{4,7},{5,4},{6,5},{7,6},{8,11},{9,8},{10,9... | collective-permute-start | bytes 442376 | tf_op jit(solution)/shard_map/ppermute | solution.py:356
  13.3 1.0 collective-permute-start.3
  14.2 1.7 pack.1
  16.0 3.0 %collective-permute-start = (bf16[192,512]{1,0:T(8,128)(2,1)}, bf16[192,512]{1,0:T(8,128)(2,1)S(1)}, u32[]{:S(2)}, u32[]{:S(2)}) collective-permute-start(bf16[192,512]{1,0:T(8,128)(2,1)} %pack.1), channel_id=1, source_target_pairs={{0,16},{16,0},{1,17},{17,1},{2,18},{18,2},{3,19},{19,3},{4,20},{20... | collective-permute-start | bytes 589832 | tf_op jit(solution)/shard_map/ppermute | solution.py:23
  19.8 1.9 multiply_cosine_fusion
  23.5 2.0 join.1
  25.6 1.0 pad_maximum_fusion.3.refs_0_
  26.7 1.9 collective-permute-start.9
  29.3 8.5 %collective-permute-done.5.refs_2_ = bf16[2,192,512]{2,1,0:T(8,128)(2,1)S(1)} collective-permute-done((bf16[2,192,512]{2,1,0:T(8,128)(2,1)S(1)}, bf16[2,192,512]{2,1,0:T(8,128)(2,1)S(1)}, u32[]{:S(2)}, u32[]{:S(2)}) %collective-permute-start.5) | collective-permute-done | bytes 393248 | tf_op jit(solution)/shard_map/ppermute | solution.py:397
  37.8 3.6 %collective-permute-start.7 = (bf16[1,192,512]{2,1,0:T(8,128)(2,1)S(1)}, bf16[1,192,512]{2,1,0:T(8,128)(2,1)S(1)}, u32[]{:S(2)}, u32[]{:S(2)}) collective-permute-start(bf16[1,192,512]{2,1,0:T(8,128)(2,1)S(1)} %slice.72), channel_id=1, source_target_pairs={{0,96},{32,0},{64,32},{96,64},{1,97},{33,1},{65,33},{97,65},{2,98}... | collective-permute-start | bytes 589832 | tf_op jit(solution)/shard_map/ppermute | solution.py:399
  43.2 7.7 %collective-permute-done.10.refs_6_ = bf16[1,192,512]{2,1,0:T(8,128)(2,1)} collective-permute-done((bf16[1,192,512]{2,1,0:T(8,128)(2,1)S(1)}, bf16[1,192,512]{2,1,0:T(8,128)(2,1)}, u32[]{:S(2)}, u32[]{:S(2)}) %collective-permute-start.10) | collective-permute-done | bytes 196640 | tf_op jit(solution)/shard_map/ppermute | solution.py:399
  51.6 1.5 slice_dynamic-update-slice_fusion.2
  53.7 2.0 collective-permute-start.21
  56.0 1.7 collective-permute-done.8.refs_5_
  57.7 2.2 copy-done.1
  60.8 7.2 %qkv.1 = (bf16[1024,256]{1,0:T(8,128)(2,1)S(1)}, bf16[2,1024,128]{2,1,0:T(8,128)(2,1)}) custom-call(s32[4]{0:T(128)S(1)} %pad_add_fusion.at_ref, bf16[1024,2048]{1,0:T(8,128)(2,1)S(1)} %copy-done.1, bf16[2,192,512]{2,1,0:T(8,128)(2,1)S(1)} %pad_maximum_fusion.3.refs_0_, bf16[2,192,512]{2,1,0:T(8,128)(2,1)S(1)} %collective-permute-done.4.refs_1_, ...), custom_call_target="tpu_custom_call" | custom-call | tf_op jit(solution)/shard_map/qkv/pallas_call | solution.py:69
  68.0 1.8 slice.56
  69.8 2.1 collective-permute-start.13
  72.7 1.5 collective-permute-start.19
  74.2 1.7 slice.81
  76.4 3.0 %collective-permute-start.18 = (bf16[8,64,512]{2,1,0:T(8,128)(2,1)S(1)}, bf16[8,64,512]{2,1,0:T(8,128)(2,1)}, u32[]{:S(2)}, u32[]{:S(2)}) collective-permute-start(bf16[8,64,512]{2,1,0:T(8,128)(2,1)S(1)} %collective-permute-done.17.refs_10_), channel_id=1, source_target_pairs={{0,8},{8,0},{1,9},{9,1},{2,10},{10,2},{3,11},{11,3},{4,12},{12,4},... | collective-permute-start | bytes 1572872 | tf_op jit(solution)/shard_map/ppermute | solution.py:23
  79.6 7.3 %collective-permute-done.13.prior_ref = bf16[2,512,128]{2,1,0:T(8,128)(2,1)} collective-permute-done((bf16[2,512,128]{2,1,0:T(8,128)(2,1)}, bf16[2,512,128]{2,1,0:T(8,128)(2,1)}, u32[]{:S(2)}, u32[]{:S(2)}) %collective-permute-start.13) | collective-permute-done | bytes 262176 | tf_op jit(solution)/shard_map/ppermute | solution.py:413
  86.9 1.0 copy-done.3
  87.9 1.0 copy-done.9
  88.9 6.6 %attend.1 = (bf16[2,128,256]{2,1,0:T(8,128)(2,1)S(1)}, bf16[2,128,256]{2,1,0:T(8,128)(2,1)S(1)}, bf16[2,128,256]{2,1,0:T(8,128)(2,1)S(1)}, bf16[2,128,256]{2,1,0:T(8,128)(2,1)S(1)}) custom-call(s32[1]{0:T(128)} %bitcast.4.y_ref, bf16[1024,256]{1,0:T(8,128)(2,1)S(1)} %copy-done.9, bf16[2,1024,128]{2,1,0:T(8,128)(2,1)S(1)} %copy-done.3, ...), custom_call_target="tpu_custom_call" | custom-call | tf_op jit(solution)/shard_map/attend/pallas_call | solution.py:135
  95.6 2.4 %collective-permute-start.14 = (bf16[2,128,256]{2,1,0:T(8,128)(2,1)S(1)}, bf16[2,128,256]{2,1,0:T(8,128)(2,1)S(1)}, u32[]{:S(2)}, u32[]{:S(2)}) collective-permute-start(bf16[2,128,256]{2,1,0:T(8,128)(2,1)S(1)} %get-tuple-element.42), channel_id=1, source_target_pairs={{0,3},{1,0},{2,1},{3,2},{4,7},{5,4},{6,5},{7,6},{8,11},{9,8},{10,9... | collective-permute-start | bytes 393224 | tf_op jit(solution)/shard_map/ppermute | solution.py:356
  98.0 2.6 %collective-permute-done.14.c1_ref = bf16[2,128,256]{2,1,0:T(8,128)(2,1)S(1)} collective-permute-done((bf16[2,128,256]{2,1,0:T(8,128)(2,1)S(1)}, bf16[2,128,256]{2,1,0:T(8,128)(2,1)S(1)}, u32[]{:S(2)}, u32[]{:S(2)}) %collective-permute-start.14) | collective-permute-done | bytes 131104 | tf_op jit(solution)/shard_map/ppermute | solution.py:356
  100.6 1.9 collective-permute-start.15
  103.0 4.1 %collective-permute-done.15.c2_ref = bf16[2,128,256]{2,1,0:T(8,128)(2,1)S(1)} collective-permute-done((bf16[2,128,256]{2,1,0:T(8,128)(2,1)S(1)}, bf16[2,128,256]{2,1,0:T(8,128)(2,1)S(1)}, u32[]{:S(2)}, u32[]{:S(2)}) %collective-permute-start.15) | collective-permute-done | bytes 131104 | tf_op jit(solution)/shard_map/ppermute | solution.py:356
  107.1 2.3 %collective-permute-start.16 = (bf16[2,128,256]{2,1,0:T(8,128)(2,1)S(1)}, bf16[2,128,256]{2,1,0:T(8,128)(2,1)S(1)}, u32[]{:S(2)}, u32[]{:S(2)}) collective-permute-start(bf16[2,128,256]{2,1,0:T(8,128)(2,1)S(1)} %get-tuple-element.44), channel_id=1, source_target_pairs={{0,1},{1,2},{2,3},{3,0},{4,5},{5,6},{6,7},{7,4},{8,9},{9,10},{10,1... | collective-permute-start | bytes 393224 | tf_op jit(solution)/shard_map/ppermute | solution.py:356
  109.4 5.6 %collective-permute-done.16.c3_ref = bf16[2,128,256]{2,1,0:T(8,128)(2,1)S(1)} collective-permute-done((bf16[2,128,256]{2,1,0:T(8,128)(2,1)S(1)}, bf16[2,128,256]{2,1,0:T(8,128)(2,1)S(1)}, u32[]{:S(2)}, u32[]{:S(2)}) %collective-permute-start.16) | collective-permute-done | bytes 131104 | tf_op jit(solution)/shard_map/ppermute | solution.py:356
  115.9 7.9 %oproj.1 = (f32[128,2048]{1,0:T(8,128)S(1)}, bf16[128,2048]{1,0:T(8,128)(2,1)}) custom-call(s32[4]{0:T(128)S(1)} %pad_add_fusion.at_ref, bf16[2,128,256]{2,1,0:T(8,128)(2,1)S(1)} %get-tuple-element.41.c0_ref, bf16[2,128,256]{2,1,0:T(8,128)(2,1)S(1)} %collective-permute-done.14.c1_ref, bf16[2,128,256]{2,1,0:T(8,128)(2,1)S(1)} %collective-permute-done.15.c2_ref, ...), custom_call_target="tpu_custom_call" | custom-call | tf_op jit(solution)/shard_map/oproj/pallas_call | solution.py:188
  123.9 1.0 copy-done.7
  124.9 20.4 %collective-permute-done.25 = bf16[128,2048]{1,0:T(8,128)(2,1)S(1)} collective-permute-done((bf16[128,2048]{1,0:T(8,128)(2,1)}, bf16[128,2048]{1,0:T(8,128)(2,1)S(1)}, u32[]{:S(2)}, u32[]{:S(2)}) %collective-permute-start.25) | collective-permute-done | bytes 524320 | tf_op jit(solution)/shard_map/ppermute | solution.py:23
  145.2 1.5 add_convert_fusion
  148.2 2.4 %collective-permute-start.27 = (bf16[128,2048]{1,0:T(8,128)(2,1)S(1)}, bf16[128,2048]{1,0:T(8,128)(2,1)S(1)}, u32[]{:S(2)}, u32[]{:S(2)}) collective-permute-start(bf16[128,2048]{1,0:T(8,128)(2,1)S(1)} %fusion.2.x0_ref), channel_id=1, source_target_pairs={{0,3},{1,0},{2,1},{3,2},{4,7},{5,4},{6,5},{7,6},{8,11},{9,8},{10,9... | collective-permute-start | bytes 1572872 | tf_op jit(solution)/shard_map/ppermute | solution.py:427
  150.6 12.2 %collective-permute-done.26.x1_ref = bf16[128,2048]{1,0:T(8,128)(2,1)S(1)} collective-permute-done((bf16[128,2048]{1,0:T(8,128)(2,1)S(1)}, bf16[128,2048]{1,0:T(8,128)(2,1)S(1)}, u32[]{:S(2)}, u32[]{:S(2)}) %collective-permute-start.26) | collective-permute-done | bytes 524320 | tf_op jit(solution)/shard_map/ppermute | solution.py:426
  163.0 3.3 %collective-permute-start.29 = (bf16[64,2048]{1,0:T(8,128)(2,1)S(1)}, bf16[64,2048]{1,0:T(8,128)(2,1)S(1)}, u32[]{:S(2)}, u32[]{:S(2)}) collective-permute-start(bf16[64,2048]{1,0:T(8,128)(2,1)S(1)} %slice.83), channel_id=1, source_target_pairs={{0,3},{1,0},{2,1},{3,2},{4,7},{5,4},{6,5},{7,6},{8,11},{9,8},{10,9... | collective-permute-start | bytes 786440 | tf_op jit(solution)/shard_map/ppermute | solution.py:429
  166.3 5.7 %collective-permute-done.28.x3_ref = bf16[64,2048]{1,0:T(8,128)(2,1)S(1)} collective-permute-done((bf16[64,2048]{1,0:T(8,128)(2,1)S(1)}, bf16[64,2048]{1,0:T(8,128)(2,1)S(1)}, u32[]{:S(2)}, u32[]{:S(2)}) %collective-permute-start.28) | collective-permute-done | bytes 262176 | tf_op jit(solution)/shard_map/ppermute | solution.py:428
  172.1 2.8 %copy-done = bf16[64,192,256]{2,1,0:T(8,128)(2,1)S(1)} copy-done((bf16[64,192,256]{2,1,0:T(8,128)(2,1)S(1)}, bf16[64,192,256]{2,1,0:T(8,128)(2,1)}, u32[]{:S(2)}) %copy-start) | copy-done | bytes 6291480
  174.8 8.5 %gate_up.1.hid_ref = bf16[512,1536]{1,0:T(8,128)(2,1)S(1)} custom-call(s32[1]{0:T(128)} %bitcast.4.y_ref, bf16[128,2048]{1,0:T(8,128)(2,1)S(1)} %fusion.2.x0_ref, bf16[128,2048]{1,0:T(8,128)(2,1)S(1)} %collective-permute-done.26.x1_ref, bf16[128,2048]{1,0:T(8,128)(2,1)S(1)} %collective-permute-done.27.x2_ref, ...), custom_call_target="tpu_custom_call" | custom-call | tf_op jit(solution)/shard_map/gate_up/pallas_call | solution.py:273
  183.4 5.2 %down.1 = (f32[128,2048]{1,0:T(8,128)S(1)}, bf16[128,2048]{1,0:T(8,128)(2,1)S(1)}, bf16[128,2048]{1,0:T(8,128)(2,1)S(1)}, bf16[128,2048]{1,0:T(8,128)(2,1)S(1)}) custom-call(s32[1]{0:T(128)} %bitcast.4.y_ref, bf16[512,1536]{1,0:T(8,128)(2,1)S(1)} %gate_up.1.hid_ref, bf16[8,2,4,96,256]{4,3,2,1,0:T(8,128)(2,1)S(1)} %bitcast.16, ...), custom_call_target="tpu_custom_call" | custom-call | tf_op jit(solution)/shard_map/down/pallas_call | solution.py:291
  188.8 3.3 %collective-permute-start.34 = (bf16[64,2048]{1,0:T(8,128)(2,1)S(1)}, bf16[64,2048]{1,0:T(8,128)(2,1)S(1)}, u32[]{:S(2)}, u32[]{:S(2)}) collective-permute-start(bf16[64,2048]{1,0:T(8,128)(2,1)S(1)} %get-tuple-element.65), channel_id=1, source_target_pairs={{0,3},{1,0},{2,1},{3,2},{4,7},{5,4},{6,5},{7,6},{8,11},{9,8},{10,9... | collective-permute-start | bytes 786440 | tf_op jit(solution)/shard_map/ppermute | solution.py:435
  192.1 6.7 %collective-permute-done.32 = bf16[64,2048]{1,0:T(8,128)(2,1)S(1)} collective-permute-done((bf16[64,2048]{1,0:T(8,128)(2,1)S(1)}, bf16[64,2048]{1,0:T(8,128)(2,1)S(1)}, u32[]{:S(2)}, u32[]{:S(2)}) %collective-permute-start.32) | collective-permute-done | bytes 262176 | tf_op jit(solution)/shard_map/ppermute | solution.py:434
  199.1 3.3 %collective-permute-start.35 = (bf16[128,2048]{1,0:T(8,128)(2,1)S(1)}, bf16[128,2048]{1,0:T(8,128)(2,1)S(1)}, u32[]{:S(2)}, u32[]{:S(2)}) collective-permute-start(bf16[128,2048]{1,0:T(8,128)(2,1)S(1)} %pad_maximum_fusion.2), channel_id=1, source_target_pairs={{0,3},{1,0},{2,1},{3,2},{4,7},{5,4},{6,5},{7,6},{8,11},{9,8},{10,9... | collective-permute-start | bytes 1572872 | tf_op jit(solution)/shard_map/ppermute | solution.py:439
  202.3 11.4 %collective-permute-done.33 = bf16[128,2048]{1,0:T(8,128)(2,1)S(1)} collective-permute-done((bf16[128,2048]{1,0:T(8,128)(2,1)S(1)}, bf16[128,2048]{1,0:T(8,128)(2,1)S(1)}, u32[]{:S(2)}, u32[]{:S(2)}) %collective-permute-start.33) | collective-permute-done | bytes 524320 | tf_op jit(solution)/shard_map/ppermute | solution.py:438
  213.8 1.1 fusion.3
  (105 shorter events, 13.3 us)
Async XLA Ops:
  7.2 140.1 %all-gather.5.cloned.1.call-start = ((), (), s32[]{:S(2)}) async-start(), calls=%async_computation | async-start | bytes 6684672 | tf_op jit(solution)/shard_map/all_gather | solution.py:391
  7.2 50.4 %copy-start.10 = (f32[2048]{0:T(1024)S(1)}, f32[2048]{0:T(1024)}, u32[]{:S(2)}) copy-start(f32[2048]{0:T(1024)} %param.16) | copy-start | bytes 24580
  7.2 50.4 %copy-start.11 = (f32[128]{0:T(128)S(1)}, f32[128]{0:T(128)}, u32[]{:S(2)}) copy-start(f32[128]{0:T(128)} %param.18) | copy-start | bytes 1540
  7.2 50.4 %copy-start.12 = (f32[128]{0:T(128)S(1)}, f32[128]{0:T(128)}, u32[]{:S(2)}) copy-start(f32[128]{0:T(128)} %param.19) | copy-start | bytes 1540
  9.6 12.3 %collective-permute-start.1 = (bf16[288,256]{1,0:T(8,128)(2,1)}, bf16[288,256]{1,0:T(8,128)(2,1)S(1)}, u32[]{:S(2)}, u32[]{:S(2)}) collective-permute-start(bf16[288,256]{1,0:T(8,128)(2,1)} %get-tuple-element.34), channel_id=1, source_target_pairs={{0,3},{1,0},{2,1},{3,2},{4,7},{5,4},{6,5},{7,6},{8,11},{9,8},{10,9... | collective-permute-start | bytes 442376 | tf_op jit(solution)/shard_map/ppermute | solution.py:356
  12.6 9.3 %collective-permute-start.2 = (bf16[288,256]{1,0:T(8,128)(2,1)}, bf16[288,256]{1,0:T(8,128)(2,1)S(1)}, u32[]{:S(2)}, u32[]{:S(2)}) collective-permute-start(bf16[288,256]{1,0:T(8,128)(2,1)} %get-tuple-element.35), channel_id=1, source_target_pairs={{0,2},{1,3},{2,0},{3,1},{4,6},{5,7},{6,4},{7,5},{8,10},{9,11},{10,... | collective-permute-start | bytes 442376 | tf_op jit(solution)/shard_map/ppermute | solution.py:356
  13.3 9.6 %collective-permute-start.3 = (bf16[288,256]{1,0:T(8,128)(2,1)}, bf16[288,256]{1,0:T(8,128)(2,1)S(1)}, u32[]{:S(2)}, u32[]{:S(2)}) collective-permute-start(bf16[288,256]{1,0:T(8,128)(2,1)} %get-tuple-element.36), channel_id=1, source_target_pairs={{0,1},{1,2},{2,3},{3,0},{4,5},{5,6},{6,7},{7,4},{8,9},{9,10},{10,1... | collective-permute-start | bytes 442376 | tf_op jit(solution)/shard_map/ppermute | solution.py:356
  16.0 12.7 %copy-start.13 = (bf16[192,512]{1,0:T(8,128)(2,1)S(1)}, bf16[192,512]{1,0:T(8,128)(2,1)}, u32[]{:S(2)}) copy-start(bf16[192,512]{1,0:T(8,128)(2,1)} %pack.1) | copy-start | bytes 589828
  16.0 7.5 %collective-permute-start = (bf16[192,512]{1,0:T(8,128)(2,1)}, bf16[192,512]{1,0:T(8,128)(2,1)S(1)}, u32[]{:S(2)}, u32[]{:S(2)}) collective-permute-start(bf16[192,512]{1,0:T(8,128)(2,1)} %pack.1), channel_id=1, source_target_pairs={{0,16},{16,0},{1,17},{17,1},{2,18},{18,2},{3,19},{19,3},{4,20},{20... | collective-permute-start | bytes 589832 | tf_op jit(solution)/shard_map/ppermute | solution.py:23
  25.5 140.8 %all-gather.7.cloned.1.call-start = ((), (), s32[]{:S(2)}) async-start(), calls=%async_computation.1 | async-start | bytes 3342336 | tf_op jit(solution)/shard_map/all_gather | solution.py:392
  26.5 11.2 %collective-permute-start.5 = (bf16[2,192,512]{2,1,0:T(8,128)(2,1)S(1)}, bf16[2,192,512]{2,1,0:T(8,128)(2,1)S(1)}, u32[]{:S(2)}, u32[]{:S(2)}) collective-permute-start(bf16[2,192,512]{2,1,0:T(8,128)(2,1)S(1)} %pad_maximum_fusion.3.refs_0_), channel_id=1, source_target_pairs={{0,96},{32,0},{64,32},{96,64},{1,97},{33,1},{65,33},{97,65},{2,98}... | collective-permute-start | bytes 1179656 | tf_op jit(solution)/shard_map/ppermute | solution.py:397
  26.7 15.1 %collective-permute-start.9 = (bf16[2,192,512]{2,1,0:T(8,128)(2,1)S(1)}, bf16[2,192,512]{2,1,0:T(8,128)(2,1)S(1)}, u32[]{:S(2)}, u32[]{:S(2)}) collective-permute-start(bf16[2,192,512]{2,1,0:T(8,128)(2,1)S(1)} %pad_maximum_fusion.3.refs_0_), channel_id=1, source_target_pairs={{0,32},{32,64},{64,96},{96,0},{1,33},{33,65},{65,97},{97,1},{2,34}... | collective-permute-start | bytes 1179656 | tf_op jit(solution)/shard_map/ppermute | solution.py:398
  28.6 25.1 %collective-permute-start.4 = (bf16[2,192,512]{2,1,0:T(8,128)(2,1)S(1)}, bf16[2,192,512]{2,1,0:T(8,128)(2,1)S(1)}, u32[]{:S(2)}, u32[]{:S(2)}) collective-permute-start(bf16[2,192,512]{2,1,0:T(8,128)(2,1)S(1)} %pad_maximum_fusion.3.refs_0_), channel_id=1, source_target_pairs={{0,8},{8,0},{1,9},{9,1},{2,10},{10,2},{3,11},{11,3},{4,12},{12,4},... | collective-permute-start | bytes 1179656 | tf_op jit(solution)/shard_map/ppermute | solution.py:23
  37.8 13.1 %collective-permute-start.7 = (bf16[1,192,512]{2,1,0:T(8,128)(2,1)S(1)}, bf16[1,192,512]{2,1,0:T(8,128)(2,1)S(1)}, u32[]{:S(2)}, u32[]{:S(2)}) collective-permute-start(bf16[1,192,512]{2,1,0:T(8,128)(2,1)S(1)} %slice.72), channel_id=1, source_target_pairs={{0,96},{32,0},{64,32},{96,64},{1,97},{33,1},{65,33},{97,65},{2,98}... | collective-permute-start | bytes 589832 | tf_op jit(solution)/shard_map/ppermute | solution.py:399
  41.9 9.1 %collective-permute-start.10 = (bf16[1,192,512]{2,1,0:T(8,128)(2,1)S(1)}, bf16[1,192,512]{2,1,0:T(8,128)(2,1)}, u32[]{:S(2)}, u32[]{:S(2)}) collective-permute-start(bf16[1,192,512]{2,1,0:T(8,128)(2,1)S(1)} %slice.73), channel_id=1, source_target_pairs={{0,32},{32,64},{64,96},{96,0},{1,33},{33,65},{65,97},{97,1},{2,34}... | collective-permute-start | bytes 589832 | tf_op jit(solution)/shard_map/ppermute | solution.py:399
  41.9 15.7 %collective-permute-start.12 = (bf16[2,192,512]{2,1,0:T(8,128)(2,1)S(1)}, bf16[2,192,512]{2,1,0:T(8,128)(2,1)S(1)}, u32[]{:S(2)}, u32[]{:S(2)}) collective-permute-start(bf16[2,192,512]{2,1,0:T(8,128)(2,1)S(1)} %collective-permute-done.9.refs_8_), channel_id=1, source_target_pairs={{0,8},{8,0},{1,9},{9,1},{2,10},{10,2},{3,11},{11,3},{4,12},{12,4},... | collective-permute-start | bytes 1179656 | tf_op jit(solution)/shard_map/ppermute | solution.py:23
  42.0 15.6 %collective-permute-start.6 = (bf16[2,192,512]{2,1,0:T(8,128)(2,1)S(1)}, bf16[2,192,512]{2,1,0:T(8,128)(2,1)S(1)}, u32[]{:S(2)}, u32[]{:S(2)}) collective-permute-start(bf16[2,192,512]{2,1,0:T(8,128)(2,1)S(1)} %collective-permute-done.5.refs_2_), channel_id=1, source_target_pairs={{0,8},{8,0},{1,9},{9,1},{2,10},{10,2},{3,11},{11,3},{4,12},{12,4},... | collective-permute-start | bytes 1179656 | tf_op jit(solution)/shard_map/ppermute | solution.py:23
  50.9 4.9 %collective-permute-start.11 = (bf16[1,192,512]{2,1,0:T(8,128)(2,1)}, bf16[1,192,512]{2,1,0:T(8,128)(2,1)}, u32[]{:S(2)}, u32[]{:S(2)}) collective-permute-start(bf16[1,192,512]{2,1,0:T(8,128)(2,1)} %collective-permute-done.10.refs_6_), channel_id=1, source_target_pairs={{0,8},{8,0},{1,9},{9,1},{2,10},{10,2},{3,11},{11,3},{4,12},{12,4},... | collective-permute-start | bytes 589832 | tf_op jit(solution)/shard_map/ppermute | solution.py:23
  50.9 2.8 %copy-start.4 = (bf16[1,192,512]{2,1,0:T(8,128)(2,1)}, bf16[1,192,512]{2,1,0:T(8,128)(2,1)S(1)}, u32[]{:S(2)}) copy-start(bf16[1,192,512]{2,1,0:T(8,128)(2,1)S(1)} %collective-permute-done.7.refs_4_) | copy-start | bytes 589828
  53.7 18.2 %collective-permute-start.17 = (bf16[8,64,512]{2,1,0:T(8,128)(2,1)}, bf16[8,64,512]{2,1,0:T(8,128)(2,1)S(1)}, u32[]{:S(2)}, u32[]{:S(2)}) collective-permute-start(bf16[8,64,512]{2,1,0:T(8,128)(2,1)} %slice_dynamic-update-slice_fusion), channel_id=1, source_target_pairs={{0,3},{1,0},{2,1},{3,2},{4,7},{5,4},{6,5},{7,6},{8,11},{9,8},{10,9... | collective-permute-start | bytes 1572872 | tf_op jit(solution)/shard_map/ppermute | solution.py:405
  53.7 20.4 %collective-permute-start.21 = (bf16[8,64,512]{2,1,0:T(8,128)(2,1)}, bf16[8,64,512]{2,1,0:T(8,128)(2,1)}, u32[]{:S(2)}, u32[]{:S(2)}) collective-permute-start(bf16[8,64,512]{2,1,0:T(8,128)(2,1)} %slice_dynamic-update-slice_fusion), channel_id=1, source_target_pairs={{0,1},{1,2},{2,3},{3,0},{4,5},{5,6},{6,7},{7,4},{8,9},{9,10},{10,1... | collective-permute-start | bytes 1572872 | tf_op jit(solution)/shard_map/ppermute | solution.py:406
  55.8 1.9 collective-permute-start.8
  57.7 2.2 copy-start.1
  68.0 11.4 %copy-start.8 = (bf16[1024,256]{1,0:T(8,128)(2,1)}, bf16[1024,256]{1,0:T(8,128)(2,1)S(1)}, u32[]{:S(2)}) copy-start(bf16[1024,256]{1,0:T(8,128)(2,1)S(1)} %get-tuple-element.39.q_ref) | copy-start | bytes 1572868
  69.8 17.0 %collective-permute-start.13 = (bf16[2,512,128]{2,1,0:T(8,128)(2,1)}, bf16[2,512,128]{2,1,0:T(8,128)(2,1)}, u32[]{:S(2)}, u32[]{:S(2)}) collective-permute-start(bf16[2,512,128]{2,1,0:T(8,128)(2,1)} %slice.56), channel_id=1, source_target_pairs={{0,8},{8,16},{16,24},{24,32},{32,40},{40,48},{48,56},{56,64},{64,7... | collective-permute-start | bytes 786440 | tf_op jit(solution)/shard_map/ppermute | solution.py:413
  72.7 29.8 %collective-permute-start.19 = (bf16[4,64,512]{2,1,0:T(8,128)(2,1)}, bf16[4,64,512]{2,1,0:T(8,128)(2,1)}, u32[]{:S(2)}, u32[]{:S(2)}) collective-permute-start(bf16[4,64,512]{2,1,0:T(8,128)(2,1)} %slice.80), channel_id=1, source_target_pairs={{0,3},{1,0},{2,1},{3,2},{4,7},{5,4},{6,5},{7,6},{8,11},{9,8},{10,9... | collective-permute-start | bytes 786440 | tf_op jit(solution)/shard_map/ppermute | solution.py:407
  75.8 26.7 %collective-permute-start.22 = (bf16[4,64,512]{2,1,0:T(8,128)(2,1)}, bf16[4,64,512]{2,1,0:T(8,128)(2,1)}, u32[]{:S(2)}, u32[]{:S(2)}) collective-permute-start(bf16[4,64,512]{2,1,0:T(8,128)(2,1)} %slice.81), channel_id=1, source_target_pairs={{0,1},{1,2},{2,3},{3,0},{4,5},{5,6},{6,7},{7,4},{8,9},{9,10},{10,1... | collective-permute-start | bytes 786440 | tf_op jit(solution)/shard_map/ppermute | solution.py:407
  76.4 38.6 %collective-permute-start.18 = (bf16[8,64,512]{2,1,0:T(8,128)(2,1)S(1)}, bf16[8,64,512]{2,1,0:T(8,128)(2,1)}, u32[]{:S(2)}, u32[]{:S(2)}) collective-permute-start(bf16[8,64,512]{2,1,0:T(8,128)(2,1)S(1)} %collective-permute-done.17.refs_10_), channel_id=1, source_target_pairs={{0,8},{8,0},{1,9},{9,1},{2,10},{10,2},{3,11},{11,3},{4,12},{12,4},... | collective-permute-start | bytes 1572872 | tf_op jit(solution)/shard_map/ppermute | solution.py:23
  79.3 35.6 %collective-permute-start.24 = (bf16[8,64,512]{2,1,0:T(8,128)(2,1)}, bf16[8,64,512]{2,1,0:T(8,128)(2,1)}, u32[]{:S(2)}, u32[]{:S(2)}) collective-permute-start(bf16[8,64,512]{2,1,0:T(8,128)(2,1)} %collective-permute-done.21.refs_16_), channel_id=1, source_target_pairs={{0,8},{8,0},{1,9},{9,1},{2,10},{10,2},{3,11},{11,3},{4,12},{12,4},... | collective-permute-start | bytes 1572872 | tf_op jit(solution)/shard_map/ppermute | solution.py:23
  95.6 5.0 %collective-permute-start.14 = (bf16[2,128,256]{2,1,0:T(8,128)(2,1)S(1)}, bf16[2,128,256]{2,1,0:T(8,128)(2,1)S(1)}, u32[]{:S(2)}, u32[]{:S(2)}) collective-permute-start(bf16[2,128,256]{2,1,0:T(8,128)(2,1)S(1)} %get-tuple-element.42), channel_id=1, source_target_pairs={{0,3},{1,0},{2,1},{3,2},{4,7},{5,4},{6,5},{7,6},{8,11},{9,8},{10,9... | collective-permute-start | bytes 393224 | tf_op jit(solution)/shard_map/ppermute | solution.py:356
  100.6 6.5 %collective-permute-start.15 = (bf16[2,128,256]{2,1,0:T(8,128)(2,1)S(1)}, bf16[2,128,256]{2,1,0:T(8,128)(2,1)S(1)}, u32[]{:S(2)}, u32[]{:S(2)}) collective-permute-start(bf16[2,128,256]{2,1,0:T(8,128)(2,1)S(1)} %get-tuple-element.43), channel_id=1, source_target_pairs={{0,2},{1,3},{2,0},{3,1},{4,6},{5,7},{6,4},{7,5},{8,10},{9,11},{10,... | collective-permute-start | bytes 393224 | tf_op jit(solution)/shard_map/ppermute | solution.py:356
  102.5 12.5 %collective-permute-start.20 = (bf16[4,64,512]{2,1,0:T(8,128)(2,1)}, bf16[4,64,512]{2,1,0:T(8,128)(2,1)S(1)}, u32[]{:S(2)}, u32[]{:S(2)}) collective-permute-start(bf16[4,64,512]{2,1,0:T(8,128)(2,1)} %collective-permute-done.19.refs_12_), channel_id=1, source_target_pairs={{0,8},{8,0},{1,9},{9,1},{2,10},{10,2},{3,11},{11,3},{4,12},{12,4},... | collective-permute-start | bytes 786440 | tf_op jit(solution)/shard_map/ppermute | solution.py:23
  102.5 12.5 %collective-permute-start.23 = (bf16[4,64,512]{2,1,0:T(8,128)(2,1)}, bf16[4,64,512]{2,1,0:T(8,128)(2,1)S(1)}, u32[]{:S(2)}, u32[]{:S(2)}) collective-permute-start(bf16[4,64,512]{2,1,0:T(8,128)(2,1)} %collective-permute-done.22.refs_14_), channel_id=1, source_target_pairs={{0,8},{8,0},{1,9},{9,1},{2,10},{10,2},{3,11},{11,3},{4,12},{12,4},... | collective-permute-start | bytes 786440 | tf_op jit(solution)/shard_map/ppermute | solution.py:23
  107.1 7.9 %collective-permute-start.16 = (bf16[2,128,256]{2,1,0:T(8,128)(2,1)S(1)}, bf16[2,128,256]{2,1,0:T(8,128)(2,1)S(1)}, u32[]{:S(2)}, u32[]{:S(2)}) collective-permute-start(bf16[2,128,256]{2,1,0:T(8,128)(2,1)S(1)} %get-tuple-element.44), channel_id=1, source_target_pairs={{0,1},{1,2},{2,3},{3,0},{4,5},{5,6},{6,7},{7,4},{8,9},{9,10},{10,1... | collective-permute-start | bytes 393224 | tf_op jit(solution)/shard_map/ppermute | solution.py:356
  115.9 31.1 %copy-start.17 = (f32[2048]{0:T(1024)S(1)}, f32[2048]{0:T(1024)}, u32[]{:S(2)}) copy-start(f32[2048]{0:T(1024)} %param.17) | copy-start | bytes 24580
  124.9 20.4 %collective-permute-start.25 = (bf16[128,2048]{1,0:T(8,128)(2,1)}, bf16[128,2048]{1,0:T(8,128)(2,1)S(1)}, u32[]{:S(2)}, u32[]{:S(2)}) collective-permute-start(bf16[128,2048]{1,0:T(8,128)(2,1)} %get-tuple-element.46), channel_id=1, source_target_pairs={{0,4},{4,0},{1,5},{5,1},{2,6},{6,2},{3,7},{7,3},{8,12},{12,8},{9,1... | collective-permute-start | bytes 1572872 | tf_op jit(solution)/shard_map/ppermute | solution.py:23
  147.2 24.8 %collective-permute-start.30 = (bf16[8,2,4,192,256]{4,3,2,1,0:T(8,128)(2,1)}, bf16[8,2,4,192,256]{4,3,2,1,0:T(8,128)(2,1)}, u32[]{:S(2)}, u32[]{:S(2)}) collective-permute-start(bf16[8,2,4,192,256]{4,3,2,1,0:T(8,128)(2,1)} %bitcast.13), channel_id=1, source_target_pairs={{0,8},{8,0},{1,9},{9,1},{2,10},{10,2},{3,11},{11,3},{4,12},{12,4},... | collective-permute-start | bytes 18874376 | tf_op jit(solution)/shard_map/ppermute | solution.py:23
  147.3 15.5 %collective-permute-start.26 = (bf16[128,2048]{1,0:T(8,128)(2,1)S(1)}, bf16[128,2048]{1,0:T(8,128)(2,1)S(1)}, u32[]{:S(2)}, u32[]{:S(2)}) collective-permute-start(bf16[128,2048]{1,0:T(8,128)(2,1)S(1)} %fusion.2.x0_ref), channel_id=1, source_target_pairs={{0,1},{1,2},{2,3},{3,0},{4,5},{5,6},{6,7},{7,4},{8,9},{9,10},{10,1... | collective-permute-start | bytes 1572872 | tf_op jit(solution)/shard_map/ppermute | solution.py:426
  148.2 14.8 %collective-permute-start.27 = (bf16[128,2048]{1,0:T(8,128)(2,1)S(1)}, bf16[128,2048]{1,0:T(8,128)(2,1)S(1)}, u32[]{:S(2)}, u32[]{:S(2)}) collective-permute-start(bf16[128,2048]{1,0:T(8,128)(2,1)S(1)} %fusion.2.x0_ref), channel_id=1, source_target_pairs={{0,3},{1,0},{2,1},{3,2},{4,7},{5,4},{6,5},{7,6},{8,11},{9,8},{10,9... | collective-permute-start | bytes 1572872 | tf_op jit(solution)/shard_map/ppermute | solution.py:427
  162.9 9.1 %collective-permute-start.28 = (bf16[64,2048]{1,0:T(8,128)(2,1)S(1)}, bf16[64,2048]{1,0:T(8,128)(2,1)S(1)}, u32[]{:S(2)}, u32[]{:S(2)}) collective-permute-start(bf16[64,2048]{1,0:T(8,128)(2,1)S(1)} %slice.82), channel_id=1, source_target_pairs={{0,1},{1,2},{2,3},{3,0},{4,5},{5,6},{6,7},{7,4},{8,9},{9,10},{10,1... | collective-permute-start | bytes 786440 | tf_op jit(solution)/shard_map/ppermute | solution.py:428
  163.0 9.0 %collective-permute-start.29 = (bf16[64,2048]{1,0:T(8,128)(2,1)S(1)}, bf16[64,2048]{1,0:T(8,128)(2,1)S(1)}, u32[]{:S(2)}, u32[]{:S(2)}) collective-permute-start(bf16[64,2048]{1,0:T(8,128)(2,1)S(1)} %slice.83), channel_id=1, source_target_pairs={{0,3},{1,0},{2,1},{3,2},{4,7},{5,4},{6,5},{7,6},{8,11},{9,8},{10,9... | collective-permute-start | bytes 786440 | tf_op jit(solution)/shard_map/ppermute | solution.py:429
  172.0 11.3 %collective-permute-start.31 = (bf16[8,2,4,96,256]{4,3,2,1,0:T(8,128)(2,1)}, bf16[8,2,4,96,256]{4,3,2,1,0:T(8,128)(2,1)S(1)}, u32[]{:S(2)}, u32[]{:S(2)}) collective-permute-start(bf16[8,2,4,96,256]{4,3,2,1,0:T(8,128)(2,1)} %bitcast.15), channel_id=1, source_target_pairs={{0,8},{8,0},{1,9},{9,1},{2,10},{10,2},{3,11},{11,3},{4,12},{12,4},... | collective-permute-start | bytes 9437192 | tf_op jit(solution)/shard_map/ppermute | solution.py:23
  172.0 2.8 %copy-start = (bf16[64,192,256]{2,1,0:T(8,128)(2,1)S(1)}, bf16[64,192,256]{2,1,0:T(8,128)(2,1)}, u32[]{:S(2)}) copy-start(bf16[64,192,256]{2,1,0:T(8,128)(2,1)} %all-gather.5.cloned.1.call-done) | copy-start | bytes 18874372
  174.8 8.6 %copy-start.2 = (bf16[64,96,256]{2,1,0:T(8,128)(2,1)S(1)}, bf16[64,96,256]{2,1,0:T(8,128)(2,1)}, u32[]{:S(2)}) copy-start(bf16[64,96,256]{2,1,0:T(8,128)(2,1)} %all-gather.7.cloned.1.call-done) | copy-start | bytes 9437188
  188.6 10.1 %collective-permute-start.32 = (bf16[64,2048]{1,0:T(8,128)(2,1)S(1)}, bf16[64,2048]{1,0:T(8,128)(2,1)S(1)}, u32[]{:S(2)}, u32[]{:S(2)}) collective-permute-start(bf16[64,2048]{1,0:T(8,128)(2,1)S(1)} %get-tuple-element.64), channel_id=1, source_target_pairs={{0,1},{1,2},{2,3},{3,0},{4,5},{5,6},{6,7},{7,4},{8,9},{9,10},{10,1... | collective-permute-start | bytes 786440 | tf_op jit(solution)/shard_map/ppermute | solution.py:434
  188.8 10.2 %collective-permute-start.34 = (bf16[64,2048]{1,0:T(8,128)(2,1)S(1)}, bf16[64,2048]{1,0:T(8,128)(2,1)S(1)}, u32[]{:S(2)}, u32[]{:S(2)}) collective-permute-start(bf16[64,2048]{1,0:T(8,128)(2,1)S(1)} %get-tuple-element.65), channel_id=1, source_target_pairs={{0,3},{1,0},{2,1},{3,2},{4,7},{5,4},{6,5},{7,6},{8,11},{9,8},{10,9... | collective-permute-start | bytes 786440 | tf_op jit(solution)/shard_map/ppermute | solution.py:435
  198.9 14.9 %collective-permute-start.33 = (bf16[128,2048]{1,0:T(8,128)(2,1)S(1)}, bf16[128,2048]{1,0:T(8,128)(2,1)S(1)}, u32[]{:S(2)}, u32[]{:S(2)}) collective-permute-start(bf16[128,2048]{1,0:T(8,128)(2,1)S(1)} %pad_maximum_fusion.1), channel_id=1, source_target_pairs={{0,1},{1,2},{2,3},{3,0},{4,5},{5,6},{6,7},{7,4},{8,9},{9,10},{10,1... | collective-permute-start | bytes 1572872 | tf_op jit(solution)/shard_map/ppermute | solution.py:438
  199.1 14.7 %collective-permute-start.35 = (bf16[128,2048]{1,0:T(8,128)(2,1)S(1)}, bf16[128,2048]{1,0:T(8,128)(2,1)S(1)}, u32[]{:S(2)}, u32[]{:S(2)}) collective-permute-start(bf16[128,2048]{1,0:T(8,128)(2,1)S(1)} %pad_maximum_fusion.2), channel_id=1, source_target_pairs={{0,3},{1,0},{2,1},{3,2},{4,7},{5,4},{6,5},{7,6},{8,11},{9,8},{10,9... | collective-permute-start | bytes 1572872 | tf_op jit(solution)/shard_map/ppermute | solution.py:439
  (8 other events, 8.8 us)
Sparse Core Ops, SparseCore 0:
  25.6 66.6 all-gather.4
  94.5 51.0 all-gather.6

commit v3 on v2

--- a/solution.py
+++ b/solution.py
@@ -23,24 +23,19 @@
     return lax.ppermute(block, axis, [(0, 1), (1, 0)])
 
 
-def shard(at_ref, e, side):
-    z, xh, core = at_ref[0], at_ref[1], at_ref[2]
-    return lax.rem(z + lax.div(jnp.int32(e), 2), 4) * 4 + lax.rem(xh + lax.rem(jnp.int32(e), 2), 2) * 2 + (core if side == 0 else 1 - core)
-
-
-PLACES = ((0, 0, 2), (1, 2, 2), (2, 4, 1), (3, 5, 1), (4, 6, 2))
-
-
-def qkv_kernel(at_ref, x_ref, *refs):
-    pieces, (gain_ref, qg_ref, kg_ref, cs_ref, q_ref, kv_ref, w_ref) = refs[:10], refs[10:]
+def qkv_kernel(core_ref, x_ref, own_ref, oth_ref, gain_ref, qg_ref, kg_ref, cs_ref, q_ref, kv_ref, tail_ref, w_ref):
+    core = core_ref[0]
 
     @pl.when(pl.program_id(0) == 0)
     def _():
-        for n, first, count in PLACES:
-            for side in range(2):
-                for i in range(count):
-                    at = pl.multiple_of(shard(at_ref, first + i, side) * 128, 128)
-                    w_ref[pl.ds(at, 128), :] = pieces[2 * n + side][i, :128]
+        def place(i, carry):
+            for src, side in ((own_ref, core), (oth_ref, 1 - core)):
+                at = pl.ds(pl.multiple_of((2 * i + side) * 128, 128), 128)
+                for k in range(4):
+                    w_ref[at, k * 128 : k * 128 + 128] = src[i, k * 128 : k * 128 + 128]
+            return carry
+
+        lax.fori_loop(0, 8, place, 0)
 
     x = x_ref[...].astype(F32)
     scale = lax.rsqrt(jnp.mean(x * x, axis=-1, keepdims=True) + 1e-06)
@@ -58,11 +53,18 @@
 
     q_ref[:, :128] = head(raw[:, :128], qg_ref[...])
     q_ref[:, 128:] = head(raw[:, 128:256], qg_ref[...])
-    kv_ref[0] = head(raw[:, 256:384], kg_ref[...])
-    kv_ref[1] = raw[:, 384:].astype(BF)
-
-
-def project(at, tokens, pieces, attn_gain, q_gain, key_gain, cs):
+    keys = head(raw[:, 256:384], kg_ref[...])
+    values = raw[:, 384:].astype(BF)
+    kv_ref[0] = keys
+    kv_ref[1] = values
+
+    @pl.when(pl.program_id(0) >= 2)
+    def _():
+        tail_ref[0] = keys
+        tail_ref[1] = values
+
+
+def project(core, tokens, own, oth, attn_gain, q_gain, key_gain, cs):
     rows = tokens.shape[0]
     tile = 256
     fixed = lambda *shape: pl.BlockSpec(shape, lambda i, c: (0,) * len(shape))
@@ -73,7 +75,8 @@
             grid=(rows // tile,),
             in_specs=[
                 pl.BlockSpec((tile, 2048), lambda i, c: (i, 0)),
-                *(fixed(count, 192, 512) for _, _, count in PLACES for _ in range(2)),
+                fixed(8, 512, 128),
+                fixed(8, 512, 128),
                 fixed(1, 2048),
                 fixed(1, 128),
                 fixed(1, 128),
@@ -82,20 +85,21 @@
             out_specs=[
                 pl.BlockSpec((tile, 256), lambda i, c: (i, 0)),
                 pl.BlockSpec((2, tile, 128), lambda i, c: (0, i, 0)),
+                pl.BlockSpec((2, tile, 128), lambda i, c: (0, jnp.maximum(i - 2, 0), 0)),
             ],
             scratch_shapes=[pltpu.VMEM((2048, 512), BF)],
         ),
         out_shape=(
             jax.ShapeDtypeStruct((rows, 256), BF),
             jax.ShapeDtypeStruct((2, rows, 128), BF),
+            jax.ShapeDtypeStruct((2, rows // 2, 128), BF),
         ),
         compiler_params=pltpu.CompilerParams(vmem_limit_bytes=40 << 20),
         name="qkv",
-    )(at, tokens, *pieces, attn_gain[None], q_gain[None], key_gain[None], cs)
-
-
-def attend_kernel(y_ref, q_ref, kv_ref, prior_ref, lo_ref, *refs):
-    out_ref = refs[4]
+    )(core, tokens, own, oth, attn_gain[None], q_gain[None], key_gain[None], cs)
+
+
+def attend_kernel(q_ref, kv_ref, prior_ref, lo_ref, out_ref):
     factor = HEAD ** (-0.5) * math.log2(math.e)
     nt = (((1,), (1,)), ((), ()))
     for i in range(4):
@@ -126,49 +130,37 @@
             for part in range(2):
                 block = 2 * i + part
                 out_ref[block % 4, block // 4, :, h * 128 : h * 128 + 128] = o[part * 128 : part * 128 + 128]
-    for k in range(4):
-        refs[k][...] = out_ref[lax.rem(y_ref[0] + k, 4)]
-
-
-def attend(y, q, kv, prior, lo):
-    vm = pl.BlockSpec(memory_space=pltpu.VMEM)
+
+
+def attend(q, kv, prior, lo):
     return pl.pallas_call(
         attend_kernel,
-        in_specs=[pl.BlockSpec(memory_space=pltpu.SMEM)] + [vm] * 4,
-        out_shape=[jax.ShapeDtypeStruct((2, 128, 256), BF)] * 4,
-        scratch_shapes=[pltpu.VMEM((4, 2, 128, 256), BF)],
+        out_shape=jax.ShapeDtypeStruct((4, 2, 128, 256), BF),
         compiler_params=pltpu.CompilerParams(vmem_limit_bytes=40 << 20),
         name="attend",
-    )(y, q, kv, prior, lo)
-
-
-def out_kernel(at_ref, c0_ref, c1_ref, c2_ref, c3_ref, *refs):
-    near, far, (keep_ref, send_ref, w_ref, x_ref, sems) = refs[:10], refs[10:18], refs[18:]
-    xl = at_ref[3]
+    )(q, kv, prior, lo)
+
+
+def out_kernel(at_ref, ctx_ref, own_ref, oth_ref, keep_ref, send_ref, w_ref, x_ref, sems):
+    core = at_ref[0]
+    xl = at_ref[1]
 
     def each(act):
-        sources = [(0, first, count, 128, near[2 * n : 2 * n + 2]) for n, first, count in PLACES]
-        for n, (s, first, count) in enumerate(((1, 0, 8), (2, 0, 4), (2, 4, 4), (3, 0, 8))):
-            sources.append((s, first, count, 0, far[2 * n : 2 * n + 2]))
-        for s, first, count, offset, pair in sources:
-            for side in range(2):
-
-                def step(i, carry, s=s, first=first, offset=offset, src=pair[side], side=side):
-                    at = pl.ds(pl.multiple_of(shard(at_ref, first + i, side) * 128, 128), 128)
-                    for k in range(4):
-                        act(pltpu.make_async_copy(
-                            src.at[i, offset : offset + 64, k * 128 : k * 128 + 128],
-                            w_ref.at[s * 256 + k * 64 : s * 256 + k * 64 + 64, at],
-                            sems.at[side, s, first + i, k],
-                        ))
-                    return carry
-
-                lax.fori_loop(0, count, step, 0)
+        def step(n, carry):
+            s, i = n // 8, lax.rem(n, 8)
+            for which, (src, side) in enumerate(((own_ref, core), (oth_ref, 1 - core))):
+                at = pl.ds(pl.multiple_of((2 * i + side) * 128, 128), 128)
+                act(pltpu.make_async_copy(
+                    src.at[s, i], w_ref.at[pl.ds(pl.multiple_of(s * 256, 256), 256), at], sems.at[which, s, i]
+                ))
+            return carry
+
+        lax.fori_loop(0, 32, step, 0)
 
     each(lambda c: c.start())
-    for s, c in enumerate((c0_ref, c1_ref, c2_ref, c3_ref)):
-        x_ref[:128, s * 256 : s * 256 + 256] = c[xl]
-        x_ref[128:, s * 256 : s * 256 + 256] = c[1 - xl]
+    for s in range(4):
+        x_ref[:128, s * 256 : s * 256 + 256] = ctx_ref[s, xl]
+        x_ref[128:, s * 256 : s * 256 + 256] = ctx_ref[s, 1 - xl]
     each(lambda c: c.wait())
     x = x_ref[...]
 
@@ -182,12 +174,12 @@
     lax.fori_loop(0, 4, column, 0)
 
 
-def out_project(at, ctx, near, far):
+def out_project(at, ctx, own, oth):
     vm = pl.BlockSpec(memory_space=pltpu.VMEM)
     anywhere = pl.BlockSpec(memory_space=pl.ANY)
     return pl.pallas_call(
         out_kernel,
-        in_specs=[pl.BlockSpec(memory_space=pltpu.SMEM)] + [vm] * 4 + [anywhere] * 18,
+        in_specs=[pl.BlockSpec(memory_space=pltpu.SMEM)] + [vm] + [anywhere] * 2,
         out_shape=(
             jax.ShapeDtypeStruct((128, 2048), F32),
             jax.ShapeDtypeStruct((128, 2048), BF),
@@ -195,11 +187,11 @@
         scratch_shapes=[
             pltpu.VMEM((1024, 2048), BF),
             pltpu.VMEM((256, 1024), BF),
-            pltpu.SemaphoreType.DMA((2, 4, 8, 4)),
+            pltpu.SemaphoreType.DMA((2, 4, 8)),
         ],
         compiler_params=pltpu.CompilerParams(vmem_limit_bytes=40 << 20),
         name="oproj",
-    )(at, *ctx, *near, *far)
+    )(at, ctx, own, oth)
 
 
 def fetcher(own_ref, oth_ref, w_ref, sems, y):
@@ -302,17 +294,16 @@
 
 
 def pack_kernel(q_ref, k_ref, v_ref, o_ref, out_ref):
-    out_ref[:128, :256] = q_ref[...].astype(BF)
-    out_ref[:128, 256:384] = k_ref[...].astype(BF)
-    out_ref[:128, 384:] = v_ref[...].astype(BF)
-    for k in range(4):
-        out_ref[128:, k * 128 : k * 128 + 128] = o_ref[k * 64 : k * 64 + 64].astype(BF)
+    parts = [q_ref[:, :128], q_ref[:, 128:], k_ref[...], v_ref[...], o_ref[...]]
+    whole = jnp.concatenate(parts, axis=0).astype(BF)
+    for i in range(8):
+        out_ref[i] = whole
 
 
 def pack(q, k, v, o):
     return pl.pallas_call(
         pack_kernel,
-        out_shape=jax.ShapeDtypeStruct((192, 512), BF),
+        out_shape=jax.ShapeDtypeStruct((8, 768, 128), BF),
         name="pack",
     )(q, k, v, o)
 
@@ -373,46 +364,38 @@
     down_weight,
 ):
     rows = tokens.shape[0]
-    at = jnp.stack([lax.axis_index(name).astype(jnp.int32) for name in ("z", "xh", "core", "xl")])
+    core = lax.axis_index("core").astype(jnp.int32)
     xl = lax.axis_index("xl").astype(jnp.int32)
     y = lax.axis_index("y").astype(jnp.int32)
     hold = lax.optimization_barrier
 
     packed = pack(q_weight, key_matrix, value_matrix, o_weight)
-    packed_xh = swap(packed, "xh")
+    at_own = lax.all_to_all(packed, ("z", "xh"), split_axis=0, concat_axis=0, tiled=True)
 
     parts = trade(prepare(y[None], gate_weight, up_weight, down_weight))
     half = HEAD // 2
     freq = jnp.exp(jnp.arange(half, dtype=F32) * (-2.0 * math.log(1000000.0) / HEAD))
     angle = positions.astype(F32)[:, None] * freq[None, :]
     cs = jnp.concatenate([jnp.cos(angle), jnp.sin(angle)], axis=1)
-    cs, packed_xh, *parts = hold((cs, packed_xh, *parts))
+    cs, at_own, *parts = hold((cs, at_own, *parts))
     gu_group, d_group = join(parts)
     gu_own = lax.all_gather(gu_group, ("z", "xh", "xl"), axis=0, tiled=False).reshape(8, 2, 4, 192, 256)
     d_own = lax.all_gather(d_group, ("z", "xh", "xl"), axis=0, tiled=False).reshape(8, 2, 4, 96, 256)
 
     lo = (jnp.arange(rows, dtype=jnp.int32) - positions)[:, None]
 
-    here = jnp.stack([packed, packed_xh])
-    up = lax.ppermute(here, "z", ring(3))
-    under = lax.ppermute(here, "z", ring(1))
-    across = [lax.ppermute(up[:1], "z", ring(3)), lax.ppermute(under[1:], "z", ring(1))]
-    near = []
-    for piece in (here, up, *across, under):
-        near += [piece, swap(piece, "core")]
-
-    o_here = jnp.concatenate([piece[:, 128:] for piece in near[::2]])
-    o_up = lax.ppermute(o_here, "y", ring(3))
-    o_down = lax.ppermute(o_here, "y", ring(1))
-    o_far = [lax.ppermute(o_up[:4], "y", ring(3)), lax.ppermute(o_down[4:], "y", ring(1))]
-    far = []
-    for piece in (o_up, *o_far, o_down):
-        far += [piece, swap(piece, "core")]
-
-    q, cache = project(at, tokens, near, attn_gain, q_gain, key_norm_gain, cs)
-    prior = lax.ppermute(cache[:, rows // 2 :], REQ, [(i - 1, i) for i in range(1, 16)])
-    ctx = trade(attend(y[None], q, cache, prior, lo))
-    keep, send = out_project(at, ctx, near, far)
+    at_oth = swap(at_own, "core")
+
+    o_wide = jnp.broadcast_to(at_own[None, :, 512:], (4, 8, 256, 128))
+    o_own = lax.all_to_all(o_wide, "y", split_axis=0, concat_axis=0, tiled=True)
+
+    q, cache, tail = project(core[None], tokens, at_own, at_oth, attn_gain, q_gain, key_norm_gain, cs)
+    prior = lax.ppermute(tail, REQ, [(i - 1, i) for i in range(1, 16)])
+    ctx = attend(q, cache, prior, lo)
+    ctx, o_own = hold((ctx, o_own))
+    o_oth = swap(o_own, "core")
+    ctx = lax.all_to_all(ctx, "y", split_axis=0, concat_axis=0, tiled=True)
+    keep, send = out_project(jnp.stack([core, xl]), ctx, o_own, o_oth)
     got = swap(send, "xl")
 
     own_rows = lax.dynamic_slice_in_dim(tokens, (xl * 4 + y) * 128, 128, 0).astype(F32)

time: 225 us -> 213 us (0.947)
  local copies, waits for them, and re-layouts: 18 us -> 9.86 us
  waiting for transfers between devices: 96 us -> 103 us
  starting transfers between devices: 43.8 us -> 38.7 us
  other arithmetic: 7.8 us -> 5.08 us
    all_gather x1, waiting for transfers between devices: 0.01 us -> 28 us  [per_device(): lax.all_gather(d_group, ('z', 'xh', 'xl'), axis=0, tiled=False)]
    all_to_all x0 -> x3, starting transfers between devices: none -> 17.2 us  [the longest x1 8.01 us: per_device(): lax.all_to_all(packed, ('z', 'xh'), split_axis=0, concat_axis=0, tiled=True)]
    ppermute x9 -> x1, waiting for transfers between devices: 23.9 us -> 8.06 us  [per_device(): prior = lax.ppermute(tail, REQ, [(i - 1, i) for i in range(1, 16)])]
    all_to_all x0 -> x3, waiting for transfers between devices: none -> 15.2 us  [the longest x1 10.1 us: per_device(): ctx = lax.all_to_all(ctx, 'y', split_axis=0, concat_axis=0, tiled=True)]
    ppermute x1, waiting for transfers between devices: 12.2 us -> 0.01 us  [per_device(): left = lax.ppermute(mlp_in, 'y', ring(1))]
    ppermute x1, waiting for transfers between devices: 0.01 us -> 11.8 us  [per_device(): right = lax.ppermute(mlp_in, 'y', ring(3))]
    ppermute x9 -> x1, starting transfers between devices: 11.9 us -> 2.43 us  [per_device(): prior = lax.ppermute(tail, REQ, [(i - 1, i) for i in range(1, 16)])]
    ppermute x6 -> x3, waiting for transfers between devices: 13.2 us -> 5.89 us  [trade(): lax.ppermute(parts[4 - k], 'y', ring(4 - k))]
  transfers between devices with their start and end apart: 38 -> 22, of which waited for: 15 -> 11; matrix products, arithmetic and copies ran while one was open for 7% -> 3% of each run, Pallas kernels for 14% -> 14%
where the time goes in v3:
time: 213 us; the launch traced here: 211 us
  waiting for transfers between devices  103 us (48%)
  Pallas kernels  39.3 us (18%)
  starting transfers between devices  38.7 us (18%)
  between operations  14.3 us (7%)
  local copies, waits for them, and re-layouts  9.86 us (5%)
  other arithmetic  5.08 us (2%)
    all_gather x1, waiting for transfers between devices, per_device(): lax.all_gather(d_group, ('z', 'xh', 'xl'), axis=0, tiled=False)  28 us
    ppermute x5, waiting for transfers between devices, swap(): return lax.ppermute(block, axis, [(0, 1), (1, 0)])  16.4 us
    ppermute x1, waiting for transfers between devices, per_device(): right = lax.ppermute(mlp_in, 'y', ring(3))  11.8 us
    ppermute x1, waiting for transfers between devices, per_device(): from_left = lax.ppermute(to_right, 'y', ring(1))  11.3 us
    all_to_all x1, waiting for transfers between devices, per_device(): ctx = lax.all_to_all(ctx, 'y', split_axis=0, concat_axis=0, tiled=True)  10.1 us
    pallas_call x1, Pallas kernels, gate_up(): pl.pallas_call(gate_kernel, in_specs=[pl.BlockSpec(memory_space=pltpu.SME...  8.55 us
    ppermute x1, waiting for transfers between devices, per_device(): prior = lax.ppermute(tail, REQ, [(i - 1, i) for i in range(1, 16)])  8.06 us
    all_to_all x1, starting transfers between devices, per_device(): lax.all_to_all(packed, ('z', 'xh'), split_axis=0, concat_axis=0, tiled=True)  8.01 us
  transfers between devices with their start and end apart: 22, of which 11 were waited for; matrix products, arithmetic and copies ran while one was open for 3% of the time, Pallas kernels for 14%

profile of v3, /device:TPU:32, one launch (start us, length us, event | category | flops | bytes accessed | tf_op | source)
XLA Modules:
  0.0 210.5 jit_solution(10595028398486049631)
XLA Ops:
  7.2 2.3 %pack.1 = bf16[8,768,128]{2,1,0:T(8,128)(2,1)} custom-call(f32[128,256]{1,0:T(8,128)} %q_ref.1, f32[128,128]{1,0:T(8,128)} %k_ref.1, f32[128,128]{1,0:T(8,128)} %v_ref.1, f32[256,128]{1,0:T(8,128)} %o_ref.1), custom_call_target="tpu_custom_call" | custom-call | tf_op jit(solution)/shard_map/pack/pallas_call | solution.py:304
  9.5 8.0 %all-to-all-start = ((bf16[8,768,128]{2,1,0:T(8,128)(2,1)}), bf16[8,768,128]{2,1,0:T(8,128)(2,1)S(1)}, u32[]{:S(2)}, u32[]{:S(2)}) async-start(bf16[8,768,128]{2,1,0:T(8,128)(2,1)} %pack.1), calls=%async_computation | async-start | bytes 3145728 | tf_op jit(solution)/shard_map/all_to_all | solution.py:373
  17.5 2.4 %prep.1 = (bf16[288,256]{1,0:T(8,128)(2,1)}, bf16[288,256]{1,0:T(8,128)(2,1)}, bf16[288,256]{1,0:T(8,128)(2,1)}, bf16[288,256]{1,0:T(8,128)(2,1)}) custom-call(s32[1]{0:T(128)} %bitcast.2.y_ref, f32[256,384]{1,0:T(8,128)} %gate_ref.1, f32[256,384]{1,0:T(8,128)} %up_ref.1, f32[384,256]{1,0:T(8,128)} %down_ref.1), custom_call_target="tpu_custom_call" | custom-call | tf_op jit(solution)/shard_map/prep/pallas_call | solution.py:323
  19.9 3.0 %collective-permute-start = (bf16[288,256]{1,0:T(8,128)(2,1)}, bf16[288,256]{1,0:T(8,128)(2,1)S(1)}, u32[]{:S(2)}, u32[]{:S(2)}) collective-permute-start(bf16[288,256]{1,0:T(8,128)(2,1)} %get-tuple-element.33), channel_id=1, source_target_pairs={{0,3},{1,0},{2,1},{3,2},{4,7},{5,4},{6,5},{7,6},{8,11},{9,8},{10,9... | collective-permute-start | bytes 442376 | tf_op jit(solution)/shard_map/ppermute | solution.py:347
  22.9 0.6 collective-permute-start.1
  23.5 1.0 collective-permute-start.2
  24.5 1.9 multiply_cosine_fusion
  26.4 0.2 pad_maximum_fusion.cs_ref
  26.6 2.3 %collective-permute-done.p1_ref = bf16[288,256]{1,0:T(8,128)(2,1)S(1)} collective-permute-done((bf16[288,256]{1,0:T(8,128)(2,1)}, bf16[288,256]{1,0:T(8,128)(2,1)S(1)}, u32[]{:S(2)}, u32[]{:S(2)}) %collective-permute-start) | collective-permute-done | bytes 147488 | tf_op jit(solution)/shard_map/ppermute | solution.py:347
  28.9 2.1 collective-permute-done.1.p2_ref
  31.0 1.5 collective-permute-done.2.p3_ref
  32.5 5.1 %all-to-all-done.own_ref = bf16[8,768,128]{2,1,0:T(8,128)(2,1)S(1)} async-done(((bf16[8,768,128]{2,1,0:T(8,128)(2,1)}), bf16[8,768,128]{2,1,0:T(8,128)(2,1)S(1)}, u32[]{:S(2)}, u32[]{:S(2)}) %all-to-all-start) | async-done | bytes 1572896 | tf_op jit(solution)/shard_map/all_to_all | solution.py:373
  37.7 2.0 join.1
  39.7 0.1 collective-permute-start.3
  39.8 1.8 broadcast_in_dim.33
  41.6 4.6 %all-to-all-start.1 = ((bf16[4,8,256,128]{3,2,1,0:T(8,128)(2,1)}), bf16[4,8,256,128]{3,2,1,0:T(8,128)(2,1)}, u32[]{:S(2)}, u32[]{:S(2)}) async-start(bf16[4,8,256,128]{3,2,1,0:T(8,128)(2,1)} %broadcast_in_dim.33), calls=%async_computation.1 | async-start | bytes 4194304 | tf_op jit(solution)/shard_map/all_to_all | solution.py:390
  46.3 2.2 %copy-done.1 = bf16[1024,2048]{1,0:T(8,128)(2,1)S(1)} copy-done((bf16[1024,2048]{1,0:T(8,128)(2,1)S(1)}, bf16[1024,2048]{1,0:T(8,128)(2,1)}, u32[]{:S(2)}) %copy-start.1) | copy-done | bytes 4194328
  48.5 7.1 %qkv.1 = (bf16[1024,256]{1,0:T(8,128)(2,1)S(1)}, bf16[2,1024,128]{2,1,0:T(8,128)(2,1)}, bf16[2,512,128]{2,1,0:T(8,128)(2,1)S(1)}) custom-call(s32[1]{0:T(128)} %bitcast.core_ref, bf16[1024,2048]{1,0:T(8,128)(2,1)S(1)} %copy-done.1, bf16[8,768,128]{2,1,0:T(8,128)(2,1)S(1)} %all-to-all-done.own_ref, bf16[8,768,128]{2,1,0:T(8,128)(2,1)} %collective-permute-done.3.oth_ref, ...), custom_call_target="tpu_custom_call" | custom-call | tf_op jit(solution)/shard_map/qkv/pallas_call | solution.py:71
  55.6 2.4 %collective-permute-start.4 = (bf16[2,512,128]{2,1,0:T(8,128)(2,1)S(1)}, bf16[2,512,128]{2,1,0:T(8,128)(2,1)S(1)}, u32[]{:S(2)}, u32[]{:S(2)}) collective-permute-start(bf16[2,512,128]{2,1,0:T(8,128)(2,1)S(1)} %get-tuple-element.40), channel_id=1, source_target_pairs={{0,8},{8,16},{16,24},{24,32},{32,40},{40,48},{48,56},{56,64},{64,7... | collective-permute-start | bytes 786440 | tf_op jit(solution)/shard_map/ppermute | solution.py:393
  58.0 0.2 copy.16.lo_ref
  58.3 8.1 %collective-permute-done.4.prior_ref = bf16[2,512,128]{2,1,0:T(8,128)(2,1)S(1)} collective-permute-done((bf16[2,512,128]{2,1,0:T(8,128)(2,1)S(1)}, bf16[2,512,128]{2,1,0:T(8,128)(2,1)S(1)}, u32[]{:S(2)}, u32[]{:S(2)}) %collective-permute-start.4) | collective-permute-done | bytes 262176 | tf_op jit(solution)/shard_map/ppermute | solution.py:393
  66.3 1.0 copy-done.3
  67.4 6.4 %attend.1 = bf16[4,2,128,256]{3,2,1,0:T(8,128)(2,1)} custom-call(bf16[1024,256]{1,0:T(8,128)(2,1)S(1)} %get-tuple-element.38.q_ref, bf16[2,1024,128]{2,1,0:T(8,128)(2,1)S(1)} %copy-done.3, bf16[2,512,128]{2,1,0:T(8,128)(2,1)S(1)} %collective-permute-done.4.prior_ref, s32[1024,1]{1,0:T(8,128)S(1)} %copy.16.lo_ref), custom_call_target="tpu_custom_call" | custom-call | tf_op jit(solution)/shard_map/attend/pallas_call | solution.py:136
  73.8 4.6 %all-to-all-start.2 = ((bf16[4,2,128,256]{3,2,1,0:T(8,128)(2,1)}), bf16[4,2,128,256]{3,2,1,0:T(8,128)(2,1)S(1)}, u32[]{:S(2)}, u32[]{:S(2)}) async-start(bf16[4,2,128,256]{3,2,1,0:T(8,128)(2,1)} %attend.1), calls=%async_computation.2 | async-start | bytes 1048576 | tf_op jit(solution)/shard_map/all_to_all | solution.py:397
  78.5 10.1 %all-to-all-done.2.ctx_ref = bf16[4,2,128,256]{3,2,1,0:T(8,128)(2,1)S(1)} async-done(((bf16[4,2,128,256]{3,2,1,0:T(8,128)(2,1)}), bf16[4,2,128,256]{3,2,1,0:T(8,128)(2,1)S(1)}, u32[]{:S(2)}, u32[]{:S(2)}) %all-to-all-start.2) | async-done | bytes 524320 | tf_op jit(solution)/shard_map/all_to_all | solution.py:397
  88.5 5.3 %oproj.1 = (f32[128,2048]{1,0:T(8,128)S(1)}, bf16[128,2048]{1,0:T(8,128)(2,1)S(1)}) custom-call(s32[2]{0:T(128)S(1)} %pad_add_fusion.at_ref, bf16[4,2,128,256]{3,2,1,0:T(8,128)(2,1)S(1)} %all-to-all-done.2.ctx_ref, bf16[4,8,256,128]{3,2,1,0:T(8,128)(2,1)} %all-to-all-done.1.own_ref, bf16[4,8,256,128]{3,2,1,0:T(8,128)(2,1)} %collective-permute-done.5.oth_ref), custom_call_target="tpu_custom_call" | custom-call | tf_op jit(solution)/shard_map/oproj/pallas_call | solution.py:180
  93.9 0.9 collective-permute-start.6
  94.8 16.4 %collective-permute-done.6 = bf16[128,2048]{1,0:T(8,128)(2,1)S(1)} collective-permute-done((bf16[128,2048]{1,0:T(8,128)(2,1)S(1)}, bf16[128,2048]{1,0:T(8,128)(2,1)S(1)}, u32[]{:S(2)}, u32[]{:S(2)}) %collective-permute-start.6) | collective-permute-done | bytes 524320 | tf_op jit(solution)/shard_map/ppermute | solution.py:23
  111.2 1.2 add_convert_fusion
  112.4 0.2 fusion
  112.6 0.2 fusion.2.x0_ref
  112.8 0.1 collective-permute-start.11
  112.9 2.8 %collective-permute-start.8 = (bf16[128,2048]{1,0:T(8,128)(2,1)S(1)}, bf16[128,2048]{1,0:T(8,128)(2,1)S(1)}, u32[]{:S(2)}, u32[]{:S(2)}) collective-permute-start(bf16[128,2048]{1,0:T(8,128)(2,1)S(1)} %fusion.2.x0_ref), channel_id=1, source_target_pairs={{0,3},{1,0},{2,1},{3,2},{4,7},{5,4},{6,5},{7,6},{8,11},{9,8},{10,9... | collective-permute-start | bytes 1572872 | tf_op jit(solution)/shard_map/ppermute | solution.py:410
  115.7 11.8 %collective-permute-done.8.x2_ref = bf16[128,2048]{1,0:T(8,128)(2,1)S(1)} collective-permute-done((bf16[128,2048]{1,0:T(8,128)(2,1)S(1)}, bf16[128,2048]{1,0:T(8,128)(2,1)S(1)}, u32[]{:S(2)}, u32[]{:S(2)}) %collective-permute-start.8) | collective-permute-done | bytes 524320 | tf_op jit(solution)/shard_map/ppermute | solution.py:410
  127.6 3.8 %collective-permute-start.10 = (bf16[64,2048]{1,0:T(8,128)(2,1)S(1)}, bf16[64,2048]{1,0:T(8,128)(2,1)S(1)}, u32[]{:S(2)}, u32[]{:S(2)}) collective-permute-start(bf16[64,2048]{1,0:T(8,128)(2,1)S(1)} %slice.37), channel_id=1, source_target_pairs={{0,3},{1,0},{2,1},{3,2},{4,7},{5,4},{6,5},{7,6},{8,11},{9,8},{10,9... | collective-permute-start | bytes 786440 | tf_op jit(solution)/shard_map/ppermute | solution.py:412
  131.4 28.0 %all-gather.7.cloned.1.call-done = bf16[64,96,256]{2,1,0:T(8,128)(2,1)} async-done(((bf16[4,96,256]{2,1,0:T(8,128)(2,1)}), bf16[64,96,256]{2,1,0:T(8,128)(2,1)}) %all-gather.7.cloned.1.call-update) | async-done | bytes 3145744 | tf_op jit(solution)/shard_map/all_gather | solution.py:383
  159.4 0.7 copy-done.4
  160.1 2.8 %copy-done = bf16[64,192,256]{2,1,0:T(8,128)(2,1)S(1)} copy-done((bf16[64,192,256]{2,1,0:T(8,128)(2,1)S(1)}, bf16[64,192,256]{2,1,0:T(8,128)(2,1)}, u32[]{:S(2)}) %copy-start) | copy-done | bytes 6291480
  162.9 0.9 copy-done.5
  163.9 8.5 %gate_up.1.hid_ref = bf16[512,1536]{1,0:T(8,128)(2,1)S(1)} custom-call(s32[1]{0:T(128)} %bitcast.2.y_ref, bf16[128,2048]{1,0:T(8,128)(2,1)S(1)} %fusion.2.x0_ref, bf16[128,2048]{1,0:T(8,128)(2,1)S(1)} %collective-permute-done.7.x1_ref, bf16[128,2048]{1,0:T(8,128)(2,1)S(1)} %collective-permute-done.8.x2_ref, bf16[64,2048]{1,0:T(8,128)(2,1)S(1)} %copy-done.5, ...), custom_call_target="tpu_custom_call" | custom-call | tf_op jit(solution)/shard_map/gate_up/pallas_call | solution.py:265
  172.4 5.2 %down.1 = (f32[128,2048]{1,0:T(8,128)S(1)}, bf16[128,2048]{1,0:T(8,128)(2,1)S(1)}, bf16[128,2048]{1,0:T(8,128)(2,1)S(1)}, bf16[128,2048]{1,0:T(8,128)(2,1)S(1)}) custom-call(s32[1]{0:T(128)} %bitcast.2.y_ref, bf16[512,1536]{1,0:T(8,128)(2,1)S(1)} %gate_up.1.hid_ref, bf16[8,2,4,96,256]{4,3,2,1,0:T(8,128)(2,1)S(1)} %bitcast.12, ...), custom_call_target="tpu_custom_call" | custom-call | tf_op jit(solution)/shard_map/down/pallas_call | solution.py:283
  177.7 1.5 collective-permute-start.13
  179.3 1.8 collective-permute-start.15
  181.1 6.6 %collective-permute-done.13 = bf16[64,2048]{1,0:T(8,128)(2,1)S(1)} collective-permute-done((bf16[64,2048]{1,0:T(8,128)(2,1)S(1)}, bf16[64,2048]{1,0:T(8,128)(2,1)S(1)}, u32[]{:S(2)}, u32[]{:S(2)}) %collective-permute-start.13) | collective-permute-done | bytes 262176 | tf_op jit(solution)/shard_map/ppermute | solution.py:417
  187.8 0.3 collective-permute-start.14
  188.3 3.0 %collective-permute-start.16 = (bf16[128,2048]{1,0:T(8,128)(2,1)S(1)}, bf16[128,2048]{1,0:T(8,128)(2,1)S(1)}, u32[]{:S(2)}, u32[]{:S(2)}) collective-permute-start(bf16[128,2048]{1,0:T(8,128)(2,1)S(1)} %pad_maximum_fusion.2), channel_id=1, source_target_pairs={{0,3},{1,0},{2,1},{3,2},{4,7},{5,4},{6,5},{7,6},{8,11},{9,8},{10,9... | collective-permute-start | bytes 1572872 | tf_op jit(solution)/shard_map/ppermute | solution.py:422
  191.3 11.3 %collective-permute-done.14 = bf16[128,2048]{1,0:T(8,128)(2,1)S(1)} collective-permute-done((bf16[128,2048]{1,0:T(8,128)(2,1)S(1)}, bf16[128,2048]{1,0:T(8,128)(2,1)S(1)}, u32[]{:S(2)}, u32[]{:S(2)}) %collective-permute-start.14) | collective-permute-done | bytes 524320 | tf_op jit(solution)/shard_map/ppermute | solution.py:421
  202.6 1.1 fusion.3
  (56 shorter events, 0.7 us)
Async XLA Ops:
  9.5 15.0 %copy-start.13 = (s32[1024]{0:T(1024)S(1)}, s32[1024]{0:T(1024)}, u32[]{:S(2)}) copy-start(s32[1024]{0:T(1024)} %param.15) | copy-start | bytes 12292
  9.5 28.2 %all-to-all-start = ((bf16[8,768,128]{2,1,0:T(8,128)(2,1)}), bf16[8,768,128]{2,1,0:T(8,128)(2,1)S(1)}, u32[]{:S(2)}, u32[]{:S(2)}) async-start(bf16[8,768,128]{2,1,0:T(8,128)(2,1)} %pack.1), calls=%async_computation | async-start | bytes 3145728 | tf_op jit(solution)/shard_map/all_to_all | solution.py:373
  17.5 95.3 %all-gather.5.cloned.1.call-start = ((), (), s32[]{:S(2)}) async-start(), calls=%async_computation.3 | async-start | bytes 6684672 | tf_op jit(solution)/shard_map/all_gather | solution.py:382
  19.9 9.0 %collective-permute-start = (bf16[288,256]{1,0:T(8,128)(2,1)}, bf16[288,256]{1,0:T(8,128)(2,1)S(1)}, u32[]{:S(2)}, u32[]{:S(2)}) collective-permute-start(bf16[288,256]{1,0:T(8,128)(2,1)} %get-tuple-element.33), channel_id=1, source_target_pairs={{0,3},{1,0},{2,1},{3,2},{4,7},{5,4},{6,5},{7,6},{8,11},{9,8},{10,9... | collective-permute-start | bytes 442376 | tf_op jit(solution)/shard_map/ppermute | solution.py:347
  22.9 8.1 %collective-permute-start.1 = (bf16[288,256]{1,0:T(8,128)(2,1)}, bf16[288,256]{1,0:T(8,128)(2,1)S(1)}, u32[]{:S(2)}, u32[]{:S(2)}) collective-permute-start(bf16[288,256]{1,0:T(8,128)(2,1)} %get-tuple-element.34), channel_id=1, source_target_pairs={{0,2},{1,3},{2,0},{3,1},{4,6},{5,7},{6,4},{7,5},{8,10},{9,11},{10,... | collective-permute-start | bytes 442376 | tf_op jit(solution)/shard_map/ppermute | solution.py:347
  23.5 9.0 %collective-permute-start.2 = (bf16[288,256]{1,0:T(8,128)(2,1)}, bf16[288,256]{1,0:T(8,128)(2,1)S(1)}, u32[]{:S(2)}, u32[]{:S(2)}) collective-permute-start(bf16[288,256]{1,0:T(8,128)(2,1)} %get-tuple-element.35), channel_id=1, source_target_pairs={{0,1},{1,2},{2,3},{3,0},{4,5},{5,6},{6,7},{7,4},{8,9},{9,10},{10,1... | collective-permute-start | bytes 442376 | tf_op jit(solution)/shard_map/ppermute | solution.py:347
  28.9 8.8 %copy-start.9 = (bf16[288,256]{1,0:T(8,128)(2,1)}, bf16[288,256]{1,0:T(8,128)(2,1)S(1)}, u32[]{:S(2)}) copy-start(bf16[288,256]{1,0:T(8,128)(2,1)S(1)} %collective-permute-done.p1_ref) | copy-start | bytes 442372
  31.0 6.7 %copy-start.10 = (bf16[288,256]{1,0:T(8,128)(2,1)}, bf16[288,256]{1,0:T(8,128)(2,1)S(1)}, u32[]{:S(2)}) copy-start(bf16[288,256]{1,0:T(8,128)(2,1)S(1)} %collective-permute-done.1.p2_ref) | copy-start | bytes 442372
  32.5 5.2 %copy-start.11 = (bf16[288,256]{1,0:T(8,128)(2,1)}, bf16[288,256]{1,0:T(8,128)(2,1)S(1)}, u32[]{:S(2)}) copy-start(bf16[288,256]{1,0:T(8,128)(2,1)S(1)} %collective-permute-done.2.p3_ref) | copy-start | bytes 442372
  39.7 6.6 %collective-permute-start.3 = (bf16[8,768,128]{2,1,0:T(8,128)(2,1)S(1)}, bf16[8,768,128]{2,1,0:T(8,128)(2,1)}, u32[]{:S(2)}, u32[]{:S(2)}) collective-permute-start(bf16[8,768,128]{2,1,0:T(8,128)(2,1)S(1)} %all-to-all-done.own_ref), channel_id=1, source_target_pairs={{0,8},{8,0},{1,9},{9,1},{2,10},{10,2},{3,11},{11,3},{4,12},{12,4},... | collective-permute-start | bytes 4718600 | tf_op jit(solution)/shard_map/ppermute | solution.py:23
  41.6 4.7 %copy-start.6 = (f32[2048]{0:T(1024)S(1)}, f32[2048]{0:T(1024)}, u32[]{:S(2)}) copy-start(f32[2048]{0:T(1024)} %param.16) | copy-start | bytes 24580
  41.6 4.7 %copy-start.7 = (f32[128]{0:T(128)S(1)}, f32[128]{0:T(128)}, u32[]{:S(2)}) copy-start(f32[128]{0:T(128)} %param.18) | copy-start | bytes 1540
  41.6 4.7 %copy-start.8 = (f32[128]{0:T(128)S(1)}, f32[128]{0:T(128)}, u32[]{:S(2)}) copy-start(f32[128]{0:T(128)} %param.19) | copy-start | bytes 1540
  41.6 32.2 %all-to-all-start.1 = ((bf16[4,8,256,128]{3,2,1,0:T(8,128)(2,1)}), bf16[4,8,256,128]{3,2,1,0:T(8,128)(2,1)}, u32[]{:S(2)}, u32[]{:S(2)}) async-start(bf16[4,8,256,128]{3,2,1,0:T(8,128)(2,1)} %broadcast_in_dim.33), calls=%async_computation.1 | async-start | bytes 4194304 | tf_op jit(solution)/shard_map/all_to_all | solution.py:390
  46.2 113.2 %all-gather.7.cloned.1.call-start = ((), (), s32[]{:S(2)}) async-start(), calls=%async_computation.4 | async-start | bytes 3342336 | tf_op jit(solution)/shard_map/all_gather | solution.py:383
  46.3 2.2 %copy-start.1 = (bf16[1024,2048]{1,0:T(8,128)(2,1)S(1)}, bf16[1024,2048]{1,0:T(8,128)(2,1)}, u32[]{:S(2)}) copy-start(bf16[1024,2048]{1,0:T(8,128)(2,1)} %x_ref.1) | copy-start | bytes 12582916
  55.6 10.7 %collective-permute-start.4 = (bf16[2,512,128]{2,1,0:T(8,128)(2,1)S(1)}, bf16[2,512,128]{2,1,0:T(8,128)(2,1)S(1)}, u32[]{:S(2)}, u32[]{:S(2)}) collective-permute-start(bf16[2,512,128]{2,1,0:T(8,128)(2,1)S(1)} %get-tuple-element.40), channel_id=1, source_target_pairs={{0,8},{8,16},{16,24},{24,32},{32,40},{40,48},{48,56},{56,64},{64,7... | collective-permute-start | bytes 786440 | tf_op jit(solution)/shard_map/ppermute | solution.py:393
  66.3 1.0 copy-start.3
  73.8 14.7 %collective-permute-start.5 = (bf16[4,8,256,128]{3,2,1,0:T(8,128)(2,1)}, bf16[4,8,256,128]{3,2,1,0:T(8,128)(2,1)}, u32[]{:S(2)}, u32[]{:S(2)}) collective-permute-start(bf16[4,8,256,128]{3,2,1,0:T(8,128)(2,1)} %all-to-all-done.1.own_ref), channel_id=1, source_target_pairs={{0,8},{8,0},{1,9},{9,1},{2,10},{10,2},{3,11},{11,3},{4,12},{12,4},... | collective-permute-start | bytes 6291464 | tf_op jit(solution)/shard_map/ppermute | solution.py:23
  73.8 14.7 %all-to-all-start.2 = ((bf16[4,2,128,256]{3,2,1,0:T(8,128)(2,1)}), bf16[4,2,128,256]{3,2,1,0:T(8,128)(2,1)S(1)}, u32[]{:S(2)}, u32[]{:S(2)}) async-start(bf16[4,2,128,256]{3,2,1,0:T(8,128)(2,1)} %attend.1), calls=%async_computation.2 | async-start | bytes 1048576 | tf_op jit(solution)/shard_map/all_to_all | solution.py:397
  93.9 18.7 %copy-start.12 = (f32[2048]{0:T(1024)S(1)}, f32[2048]{0:T(1024)}, u32[]{:S(2)}) copy-start(f32[2048]{0:T(1024)} %param.17) | copy-start | bytes 24580
  93.9 17.3 %collective-permute-start.6 = (bf16[128,2048]{1,0:T(8,128)(2,1)S(1)}, bf16[128,2048]{1,0:T(8,128)(2,1)S(1)}, u32[]{:S(2)}, u32[]{:S(2)}) collective-permute-start(bf16[128,2048]{1,0:T(8,128)(2,1)S(1)} %get-tuple-element.44), channel_id=1, source_target_pairs={{0,4},{4,0},{1,5},{5,1},{2,6},{6,2},{3,7},{7,3},{8,12},{12,8},{9,1... | collective-permute-start | bytes 1572872 | tf_op jit(solution)/shard_map/ppermute | solution.py:23
  112.8 47.3 %collective-permute-start.11 = (bf16[8,2,4,192,256]{4,3,2,1,0:T(8,128)(2,1)}, bf16[8,2,4,192,256]{4,3,2,1,0:T(8,128)(2,1)}, u32[]{:S(2)}, u32[]{:S(2)}) collective-permute-start(bf16[8,2,4,192,256]{4,3,2,1,0:T(8,128)(2,1)} %bitcast.9), channel_id=1, source_target_pairs={{0,8},{8,0},{1,9},{9,1},{2,10},{10,2},{3,11},{11,3},{4,12},{12,4},... | collective-permute-start | bytes 18874376 | tf_op jit(solution)/shard_map/ppermute | solution.py:23
  112.9 14.6 %collective-permute-start.8 = (bf16[128,2048]{1,0:T(8,128)(2,1)S(1)}, bf16[128,2048]{1,0:T(8,128)(2,1)S(1)}, u32[]{:S(2)}, u32[]{:S(2)}) collective-permute-start(bf16[128,2048]{1,0:T(8,128)(2,1)S(1)} %fusion.2.x0_ref), channel_id=1, source_target_pairs={{0,3},{1,0},{2,1},{3,2},{4,7},{5,4},{6,5},{7,6},{8,11},{9,8},{10,9... | collective-permute-start | bytes 1572872 | tf_op jit(solution)/shard_map/ppermute | solution.py:410
  115.7 15.6 %collective-permute-start.7 = (bf16[128,2048]{1,0:T(8,128)(2,1)S(1)}, bf16[128,2048]{1,0:T(8,128)(2,1)S(1)}, u32[]{:S(2)}, u32[]{:S(2)}) collective-permute-start(bf16[128,2048]{1,0:T(8,128)(2,1)S(1)} %fusion.2.x0_ref), channel_id=1, source_target_pairs={{0,1},{1,2},{2,3},{3,0},{4,5},{5,6},{6,7},{7,4},{8,9},{9,10},{10,1... | collective-permute-start | bytes 1572872 | tf_op jit(solution)/shard_map/ppermute | solution.py:409
  127.6 31.9 %collective-permute-start.10 = (bf16[64,2048]{1,0:T(8,128)(2,1)S(1)}, bf16[64,2048]{1,0:T(8,128)(2,1)S(1)}, u32[]{:S(2)}, u32[]{:S(2)}) collective-permute-start(bf16[64,2048]{1,0:T(8,128)(2,1)S(1)} %slice.37), channel_id=1, source_target_pairs={{0,3},{1,0},{2,1},{3,2},{4,7},{5,4},{6,5},{7,6},{8,11},{9,8},{10,9... | collective-permute-start | bytes 786440 | tf_op jit(solution)/shard_map/ppermute | solution.py:412
  131.3 28.1 %collective-permute-start.9 = (bf16[64,2048]{1,0:T(8,128)(2,1)S(1)}, bf16[64,2048]{1,0:T(8,128)(2,1)S(1)}, u32[]{:S(2)}, u32[]{:S(2)}) collective-permute-start(bf16[64,2048]{1,0:T(8,128)(2,1)S(1)} %slice.36), channel_id=1, source_target_pairs={{0,1},{1,2},{2,3},{3,0},{4,5},{5,6},{6,7},{7,4},{8,9},{9,10},{10,1... | collective-permute-start | bytes 786440 | tf_op jit(solution)/shard_map/ppermute | solution.py:411
  159.4 0.7 copy-start.4
  160.1 12.3 %collective-permute-start.12 = (bf16[8,2,4,96,256]{4,3,2,1,0:T(8,128)(2,1)}, bf16[8,2,4,96,256]{4,3,2,1,0:T(8,128)(2,1)S(1)}, u32[]{:S(2)}, u32[]{:S(2)}) collective-permute-start(bf16[8,2,4,96,256]{4,3,2,1,0:T(8,128)(2,1)} %bitcast.11), channel_id=1, source_target_pairs={{0,8},{8,0},{1,9},{9,1},{2,10},{10,2},{3,11},{11,3},{4,12},{12,4},... | collective-permute-start | bytes 9437192 | tf_op jit(solution)/shard_map/ppermute | solution.py:23
  160.1 2.8 %copy-start = (bf16[64,192,256]{2,1,0:T(8,128)(2,1)S(1)}, bf16[64,192,256]{2,1,0:T(8,128)(2,1)}, u32[]{:S(2)}) copy-start(bf16[64,192,256]{2,1,0:T(8,128)(2,1)} %all-gather.5.cloned.1.call-done) | copy-start | bytes 18874372
  162.9 0.9 copy-start.5
  163.9 8.6 %copy-start.2 = (bf16[64,96,256]{2,1,0:T(8,128)(2,1)S(1)}, bf16[64,96,256]{2,1,0:T(8,128)(2,1)}, u32[]{:S(2)}) copy-start(bf16[64,96,256]{2,1,0:T(8,128)(2,1)} %all-gather.7.cloned.1.call-done) | copy-start | bytes 9437188
  177.7 10.0 %collective-permute-start.13 = (bf16[64,2048]{1,0:T(8,128)(2,1)S(1)}, bf16[64,2048]{1,0:T(8,128)(2,1)S(1)}, u32[]{:S(2)}, u32[]{:S(2)}) collective-permute-start(bf16[64,2048]{1,0:T(8,128)(2,1)S(1)} %get-tuple-element.62), channel_id=1, source_target_pairs={{0,1},{1,2},{2,3},{3,0},{4,5},{5,6},{6,7},{7,4},{8,9},{9,10},{10,1... | collective-permute-start | bytes 786440 | tf_op jit(solution)/shard_map/ppermute | solution.py:417
  179.3 8.9 %collective-permute-start.15 = (bf16[64,2048]{1,0:T(8,128)(2,1)S(1)}, bf16[64,2048]{1,0:T(8,128)(2,1)S(1)}, u32[]{:S(2)}, u32[]{:S(2)}) collective-permute-start(bf16[64,2048]{1,0:T(8,128)(2,1)S(1)} %get-tuple-element.63), channel_id=1, source_target_pairs={{0,3},{1,0},{2,1},{3,2},{4,7},{5,4},{6,5},{7,6},{8,11},{9,8},{10,9... | collective-permute-start | bytes 786440 | tf_op jit(solution)/shard_map/ppermute | solution.py:418
  187.8 14.8 %collective-permute-start.14 = (bf16[128,2048]{1,0:T(8,128)(2,1)S(1)}, bf16[128,2048]{1,0:T(8,128)(2,1)S(1)}, u32[]{:S(2)}, u32[]{:S(2)}) collective-permute-start(bf16[128,2048]{1,0:T(8,128)(2,1)S(1)} %pad_maximum_fusion.1), channel_id=1, source_target_pairs={{0,1},{1,2},{2,3},{3,0},{4,5},{5,6},{6,7},{7,4},{8,9},{9,10},{10,1... | collective-permute-start | bytes 1572872 | tf_op jit(solution)/shard_map/ppermute | solution.py:421
  188.3 14.4 %collective-permute-start.16 = (bf16[128,2048]{1,0:T(8,128)(2,1)S(1)}, bf16[128,2048]{1,0:T(8,128)(2,1)S(1)}, u32[]{:S(2)}, u32[]{:S(2)}) collective-permute-start(bf16[128,2048]{1,0:T(8,128)(2,1)S(1)} %pad_maximum_fusion.2), channel_id=1, source_target_pairs={{0,3},{1,0},{2,1},{3,2},{4,7},{5,4},{6,5},{7,6},{8,11},{9,8},{10,9... | collective-permute-start | bytes 1572872 | tf_op jit(solution)/shard_map/ppermute | solution.py:422
Sparse Core Ops, SparseCore 0:
  39.8 64.2 all-gather.4
  106.3 53.0 all-gather.6

commit v4 on v3

--- a/solution.py
+++ b/solution.py
@@ -194,12 +194,12 @@
     )(at, ctx, own, oth)
 
 
-def fetcher(own_ref, oth_ref, w_ref, sems, y):
+def fetcher(own_ref, oth_ref, w_ref, sems, y, first):
     def copy(c, g, m):
         src = own_ref if c == 0 else oth_ref
         at = pl.multiple_of(((m // 4) * 4 + lax.rem(y + lax.rem(m, 4), 4)) * 256, 256)
         return pltpu.make_async_copy(
-            src.at[:, m // 4, lax.rem(m, 4), g * 96 : g * 96 + 96, :],
+            src.at[:, m // 4, lax.rem(m, 4), first + g * 96 : first + g * 96 + 96, :],
             w_ref.at[g, c * 8 : c * 8 + 8, :, pl.ds(at, 256)],
             sems.at[g, c, m],
         )
@@ -217,7 +217,7 @@
 
 def gate_kernel(y_ref, x0_ref, x1_ref, x2_ref, x3_ref, x4_ref, own_ref, oth_ref, hid_ref, w_ref, x_ref, sems):
     nt = (((1,), (1,)), ((), ()))
-    each = fetcher(own_ref, oth_ref, w_ref, sems, y_ref[0])
+    each = fetcher(own_ref, oth_ref, w_ref, sems, y_ref[0], 0)
     each(0, 2, lambda c: c.start())
     each(1, 2, lambda c: c.start())
     x_ref[0:128] = x0_ref[...]
@@ -239,21 +239,33 @@
             hid_ref[:, at : at + 256] = hidden.astype(BF)
 
 
-def down_kernel(y_ref, hid_ref, own_ref, oth_ref, keep_ref, left_ref, right_ref, far_ref, w_ref, sems):
-    each = fetcher(own_ref, oth_ref, w_ref, sems, y_ref[0])
+def far_kernel(y_ref, hid_ref, own_ref, oth_ref, top_ref, bottom_ref, w_ref, sems):
+    each = fetcher(own_ref, oth_ref, w_ref, sems, y_ref[0], 192)
     for c in range(2):
         each(c, 1, lambda copy: copy.start())
     for c in range(2):
         each(c, 1, lambda copy: copy.wait())
-    hid = hid_ref[...]
+    hid = hid_ref[384:]
+
+    def column(n, carry):
+        at = pl.ds(pl.multiple_of(n * 512, 512), 512)
+        out = jnp.dot(hid, w_ref[0, :, :, at].reshape(1536, 512), preferred_element_type=F32)
+        top_ref[:, at] = out[:64].astype(BF)
+        bottom_ref[:, at] = out[64:].astype(BF)
+        return carry
+
+    lax.fori_loop(0, 4, column, 0)
+
+
+def down_kernel(hid_ref, w_ref, keep_ref, left_ref, right_ref):
+    hid = hid_ref[:384]
 
     def column(n, carry):
         at = pl.ds(pl.multiple_of(n * 512, 512), 512)
         out = jnp.dot(hid, w_ref[0, :, :, at].reshape(1536, 512), preferred_element_type=F32)
         keep_ref[:, at] = out[:128]
         left_ref[:, at] = out[128:256].astype(BF)
-        right_ref[:, at] = out[256:384].astype(BF)
-        far_ref[:, at] = out[384:].astype(BF)
+        right_ref[:, at] = out[256:].astype(BF)
         return carry
 
     lax.fori_loop(0, 4, column, 0)
@@ -276,21 +288,28 @@
     )(y, *pieces, own, oth)
 
 
-def down(y, hidden, own, oth):
+def down_far(y, hidden, own, oth):
     vm = pl.BlockSpec(memory_space=pltpu.VMEM)
     hbm = pl.BlockSpec(memory_space=pltpu.HBM)
+    half = jax.ShapeDtypeStruct((64, 2048), BF)
+    return pl.pallas_call(
+        far_kernel,
+        in_specs=[pl.BlockSpec(memory_space=pltpu.SMEM), vm] + [hbm] * 2,
+        out_shape=(half, half, jax.ShapeDtypeStruct((1, 16, 96, 2048), BF)),
+        scratch_shapes=[pltpu.SemaphoreType.DMA((1, 2, 8))],
+        compiler_params=pltpu.CompilerParams(vmem_limit_bytes=40 << 20),
+        name="down_far",
+    )(y, hidden, own, oth)
+
+
+def down(hidden, weight):
     part = jax.ShapeDtypeStruct((128, 2048), BF)
     return pl.pallas_call(
         down_kernel,
-        in_specs=[pl.BlockSpec(memory_space=pltpu.SMEM), vm] + [hbm] * 2,
-        out_shape=(jax.ShapeDtypeStruct((128, 2048), F32), part, part, part),
-        scratch_shapes=[
-            pltpu.VMEM((1, 16, 96, 2048), BF),
-            pltpu.SemaphoreType.DMA((1, 2, 8)),
-        ],
+        out_shape=(jax.ShapeDtypeStruct((128, 2048), F32), part, part),
         compiler_params=pltpu.CompilerParams(vmem_limit_bytes=40 << 20),
         name="down",
-    )(y, hidden, own, oth)
+    )(hidden, weight)
 
 
 def pack_kernel(q_ref, k_ref, v_ref, o_ref, out_ref):
@@ -329,18 +348,13 @@
     )(y, gate, up, down)
 
 
-def join_kernel(p0_ref, p1_ref, p2_ref, p3_ref, gu_ref, d_ref):
+def join_kernel(p0_ref, p1_ref, p2_ref, p3_ref, out_ref):
     for k, ref in enumerate((p0_ref, p1_ref, p2_ref, p3_ref)):
-        gu_ref[k] = ref[:192]
-        d_ref[k] = ref[192:]
+        out_ref[k] = ref[...]
 
 
 def join(parts):
-    return pl.pallas_call(
-        join_kernel,
-        out_shape=(jax.ShapeDtypeStruct((4, 192, 256), BF), jax.ShapeDtypeStruct((4, 96, 256), BF)),
-        name="join",
-    )(*parts)
+    return pl.pallas_call(join_kernel, out_shape=jax.ShapeDtypeStruct((4, 288, 256), BF), name="join")(*parts)
 
 
 def trade(parts):
@@ -378,10 +392,7 @@
     angle = positions.astype(F32)[:, None] * freq[None, :]
     cs = jnp.concatenate([jnp.cos(angle), jnp.sin(angle)], axis=1)
     cs, at_own, *parts = hold((cs, at_own, *parts))
-    gu_group, d_group = join(parts)
-    gu_own = lax.all_gather(gu_group, ("z", "xh", "xl"), axis=0, tiled=False).reshape(8, 2, 4, 192, 256)
-    d_own = lax.all_gather(d_group, ("z", "xh", "xl"), axis=0, tiled=False).reshape(8, 2, 4, 96, 256)
-
+    mlp_own = lax.all_gather(join(parts), ("z", "xh", "xl"), axis=0, tiled=False).reshape(8, 2, 4, 288, 256)
     lo = (jnp.arange(rows, dtype=jnp.int32) - positions)[:, None]
 
     at_oth = swap(at_own, "core")
@@ -404,18 +415,17 @@
     scale = lax.rsqrt(jnp.mean(resid * resid, axis=-1, keepdims=True) + 1e-06)
     mlp_in = (resid * scale * mlp_gain).astype(BF)
 
-    gu_own, mlp_in = hold((gu_own, mlp_in))
-    gu_oth = swap(gu_own, "core")
     left = lax.ppermute(mlp_in, "y", ring(1))
     right = lax.ppermute(mlp_in, "y", ring(3))
+    mlp_own, left, right = hold((mlp_own, left, right))
+    mlp_oth = swap(mlp_own, "core")
     far_top = lax.ppermute(left[:64], "y", ring(1))
     far_bottom = lax.ppermute(right[64:], "y", ring(3))
-    d_own, left, right, far_top, far_bottom = hold((d_own, left, right, far_top, far_bottom))
-    d_oth = swap(d_own, "core")
-    hidden = gate_up(y[None], (mlp_in, left, right, far_top, far_bottom), gu_own, gu_oth)
-    keep, to_left, to_right, to_far = down(y[None], hidden, d_own, d_oth)
-    via_left = lax.ppermute(to_far[:64], "y", ring(1))
-    via_right = lax.ppermute(to_far[64:], "y", ring(3))
+    hidden = gate_up(y[None], (mlp_in, left, right, far_top, far_bottom), mlp_own, mlp_oth)
+    top, bottom, weight = down_far(y[None], hidden, mlp_own, mlp_oth)
+    via_left = lax.ppermute(top, "y", ring(1))
+    via_right = lax.ppermute(bottom, "y", ring(3))
+    keep, to_left, to_right = down(hidden, weight)
     to_right = jnp.concatenate([(to_right[:64].astype(F32) + via_left.astype(F32)).astype(BF), to_right[64:]])
     to_left = jnp.concatenate([to_left[:64], (to_left[64:].astype(F32) + via_right.astype(F32)).astype(BF)])
     from_left = lax.ppermute(to_right, "y", ring(1))

time: 213 us -> 206 us (0.967)
  starting transfers between devices: 38.7 us -> 33.3 us
  waiting for transfers between devices: 103 us -> 100 us
    all_gather x2 -> x1, waiting for transfers between devices: 28 us -> 0.01 us  [per_device(): lax.all_gather(join(parts), ('z', 'xh', 'xl'), axis=0, tiled=False)]
    ppermute x5 -> x4, waiting for transfers between devices: 16.4 us -> 29.8 us  [swap(): return lax.ppermute(block, axis, [(0, 1), (1, 0)])]
    ppermute x1, waiting for transfers between devices: 0.01 us -> 8.04 us  [per_device(): from_right = lax.ppermute(to_left, 'y', ring(3))]
    ppermute x1, waiting for transfers between devices: 0.01 us -> 6.69 us  [per_device(): far_bottom = lax.ppermute(right[64:], 'y', ring(3))]
    ppermute x1, waiting for transfers between devices: 11.3 us -> 5.47 us  [per_device(): from_left = lax.ppermute(to_right, 'y', ring(1))]
    ppermute x1, starting transfers between devices: 3.76 us -> 0.36 us  [per_device(): far_bottom = lax.ppermute(right[64:], 'y', ring(3))]
    pallas_call x2 -> x3, Pallas kernels: 7.19 us -> 9.82 us  [the longest x1 4.59 us: down_far(): pl.pallas_call(far_kernel, in_specs=[pl.BlockSpec(memory_space=pltpu.SMEM...]
    unnamed x28 -> x24, local copies, waits for them, and re-layouts: 7.7 us -> 7.91 us
  transfers between devices with their start and end apart: 22 -> 20, of which waited for: 11 -> 16; matrix products, arithmetic and copies ran while one was open for 3% -> 3% of each run, Pallas kernels for 14% -> 12%
where the time goes in v4:
time: 206 us; the launch traced here: 204 us
  waiting for transfers between devices  100 us (49%)
  Pallas kernels  41.4 us (20%)
  starting transfers between devices  33.3 us (16%)
  between operations  14.2 us (7%)
  local copies, waits for them, and re-layouts  10.1 us (5%)
  other arithmetic  5.4 us (3%)
    ppermute x4, waiting for transfers between devices, swap(): return lax.ppermute(block, axis, [(0, 1), (1, 0)])  29.8 us
    ppermute x1, waiting for transfers between devices, per_device(): right = lax.ppermute(mlp_in, 'y', ring(3))  10.5 us
    all_to_all x1, waiting for transfers between devices, per_device(): ctx = lax.all_to_all(ctx, 'y', split_axis=0, concat_axis=0, tiled=True)  10.1 us
    ppermute x1, waiting for transfers between devices, per_device(): prior = lax.ppermute(tail, REQ, [(i - 1, i) for i in range(1, 16)])  9.13 us
    pallas_call x1, Pallas kernels, gate_up(): pl.pallas_call(gate_kernel, in_specs=[pl.BlockSpec(memory_space=pltpu.SME...  8.55 us
    ppermute x1, waiting for transfers between devices, per_device(): from_right = lax.ppermute(to_left, 'y', ring(3))  8.04 us
    all_to_all x1, starting transfers between devices, per_device(): lax.all_to_all(packed, ('z', 'xh'), split_axis=0, concat_axis=0, tiled=True)  8.01 us
    unnamed x24, local copies, waits for them, and re-layouts  7.91 us
  transfers between devices with their start and end apart: 20, of which 16 were waited for; matrix products, arithmetic and copies ran while one was open for 3% of the time, Pallas kernels for 12%

profile of v4, /device:TPU:32, one launch (start us, length us, event | category | flops | bytes accessed | tf_op | source)
XLA Modules:
  0.0 204.5 jit_solution(18121058455171494481)
XLA Ops:
  7.2 2.3 %pack.1 = bf16[8,768,128]{2,1,0:T(8,128)(2,1)} custom-call(f32[128,256]{1,0:T(8,128)} %q_ref.1, f32[128,128]{1,0:T(8,128)} %k_ref.1, f32[128,128]{1,0:T(8,128)} %v_ref.1, f32[256,128]{1,0:T(8,128)} %o_ref.1), custom_call_target="tpu_custom_call" | custom-call | tf_op jit(solution)/shard_map/pack/pallas_call | solution.py:323
  9.5 8.0 %all-to-all-start = ((bf16[8,768,128]{2,1,0:T(8,128)(2,1)}), bf16[8,768,128]{2,1,0:T(8,128)(2,1)S(1)}, u32[]{:S(2)}, u32[]{:S(2)}) async-start(bf16[8,768,128]{2,1,0:T(8,128)(2,1)} %pack.1), calls=%async_computation | async-start | bytes 3145728 | tf_op jit(solution)/shard_map/all_to_all | solution.py:387
  17.5 2.3 %prep.1 = (bf16[288,256]{1,0:T(8,128)(2,1)}, bf16[288,256]{1,0:T(8,128)(2,1)}, bf16[288,256]{1,0:T(8,128)(2,1)}, bf16[288,256]{1,0:T(8,128)(2,1)}) custom-call(s32[1]{0:T(128)} %bitcast.2.y_ref, f32[256,384]{1,0:T(8,128)} %gate_ref.1, f32[256,384]{1,0:T(8,128)} %up_ref.1, f32[384,256]{1,0:T(8,128)} %down_ref.1), custom_call_target="tpu_custom_call" | custom-call | tf_op jit(solution)/shard_map/prep/pallas_call | solution.py:342
  19.9 3.0 %collective-permute-start = (bf16[288,256]{1,0:T(8,128)(2,1)}, bf16[288,256]{1,0:T(8,128)(2,1)S(1)}, u32[]{:S(2)}, u32[]{:S(2)}) collective-permute-start(bf16[288,256]{1,0:T(8,128)(2,1)} %get-tuple-element.29), channel_id=1, source_target_pairs={{0,3},{1,0},{2,1},{3,2},{4,7},{5,4},{6,5},{7,6},{8,11},{9,8},{10,9... | collective-permute-start | bytes 442376 | tf_op jit(solution)/shard_map/ppermute | solution.py:361
  22.9 0.6 collective-permute-start.1
  23.5 1.0 collective-permute-start.2
  24.5 1.9 multiply_cosine_fusion
  26.6 2.3 %collective-permute-done.p1_ref = bf16[288,256]{1,0:T(8,128)(2,1)S(1)} collective-permute-done((bf16[288,256]{1,0:T(8,128)(2,1)}, bf16[288,256]{1,0:T(8,128)(2,1)S(1)}, u32[]{:S(2)}, u32[]{:S(2)}) %collective-permute-start) | collective-permute-done | bytes 147488 | tf_op jit(solution)/shard_map/ppermute | solution.py:361
  28.9 2.1 %collective-permute-done.1.p2_ref = bf16[288,256]{1,0:T(8,128)(2,1)S(1)} collective-permute-done((bf16[288,256]{1,0:T(8,128)(2,1)}, bf16[288,256]{1,0:T(8,128)(2,1)S(1)}, u32[]{:S(2)}, u32[]{:S(2)}) %collective-permute-start.1) | collective-permute-done | bytes 147488 | tf_op jit(solution)/shard_map/ppermute | solution.py:361
  31.0 1.5 collective-permute-done.2.p3_ref
  32.5 5.2 %all-to-all-done.own_ref = bf16[8,768,128]{2,1,0:T(8,128)(2,1)S(1)} async-done(((bf16[8,768,128]{2,1,0:T(8,128)(2,1)}), bf16[8,768,128]{2,1,0:T(8,128)(2,1)S(1)}, u32[]{:S(2)}, u32[]{:S(2)}) %all-to-all-start) | async-done | bytes 1572896 | tf_op jit(solution)/shard_map/all_to_all | solution.py:387
  37.7 2.0 join.1
  39.8 1.8 broadcast_in_dim.33
  41.7 4.6 %all-to-all-start.1 = ((bf16[4,8,256,128]{3,2,1,0:T(8,128)(2,1)}), bf16[4,8,256,128]{3,2,1,0:T(8,128)(2,1)}, u32[]{:S(2)}, u32[]{:S(2)}) async-start(bf16[4,8,256,128]{3,2,1,0:T(8,128)(2,1)} %broadcast_in_dim.33), calls=%async_computation.1 | async-start | bytes 4194304 | tf_op jit(solution)/shard_map/all_to_all | solution.py:401
  46.3 2.2 %copy-done.1 = bf16[1024,2048]{1,0:T(8,128)(2,1)S(1)} copy-done((bf16[1024,2048]{1,0:T(8,128)(2,1)S(1)}, bf16[1024,2048]{1,0:T(8,128)(2,1)}, u32[]{:S(2)}) %copy-start.1) | copy-done | bytes 4194328
  48.5 7.2 %qkv.1 = (bf16[1024,256]{1,0:T(8,128)(2,1)S(1)}, bf16[2,1024,128]{2,1,0:T(8,128)(2,1)}, bf16[2,512,128]{2,1,0:T(8,128)(2,1)S(1)}) custom-call(s32[1]{0:T(128)} %bitcast.core_ref, bf16[1024,2048]{1,0:T(8,128)(2,1)S(1)} %copy-done.1, bf16[8,768,128]{2,1,0:T(8,128)(2,1)S(1)} %all-to-all-done.own_ref, bf16[8,768,128]{2,1,0:T(8,128)(2,1)} %collective-permute-done.3.oth_ref, ...), custom_call_target="tpu_custom_call" | custom-call | tf_op jit(solution)/shard_map/qkv/pallas_call | solution.py:71
  55.7 2.5 %collective-permute-start.4 = (bf16[2,512,128]{2,1,0:T(8,128)(2,1)S(1)}, bf16[2,512,128]{2,1,0:T(8,128)(2,1)S(1)}, u32[]{:S(2)}, u32[]{:S(2)}) collective-permute-start(bf16[2,512,128]{2,1,0:T(8,128)(2,1)S(1)} %get-tuple-element.36), channel_id=1, source_target_pairs={{0,8},{8,16},{16,24},{24,32},{32,40},{40,48},{48,56},{56,64},{64,7... | collective-permute-start | bytes 786440 | tf_op jit(solution)/shard_map/ppermute | solution.py:404
  58.4 9.1 %collective-permute-done.4.prior_ref = bf16[2,512,128]{2,1,0:T(8,128)(2,1)S(1)} collective-permute-done((bf16[2,512,128]{2,1,0:T(8,128)(2,1)S(1)}, bf16[2,512,128]{2,1,0:T(8,128)(2,1)S(1)}, u32[]{:S(2)}, u32[]{:S(2)}) %collective-permute-start.4) | collective-permute-done | bytes 262176 | tf_op jit(solution)/shard_map/ppermute | solution.py:404
  67.5 1.0 copy-done.3
  68.5 6.4 %attend.1 = bf16[4,2,128,256]{3,2,1,0:T(8,128)(2,1)} custom-call(bf16[1024,256]{1,0:T(8,128)(2,1)S(1)} %get-tuple-element.34.q_ref, bf16[2,1024,128]{2,1,0:T(8,128)(2,1)S(1)} %copy-done.3, bf16[2,512,128]{2,1,0:T(8,128)(2,1)S(1)} %collective-permute-done.4.prior_ref, s32[1024,1]{1,0:T(8,128)S(1)} %copy.16.lo_ref), custom_call_target="tpu_custom_call" | custom-call | tf_op jit(solution)/shard_map/attend/pallas_call | solution.py:136
  75.0 4.5 %all-to-all-start.2 = ((bf16[4,2,128,256]{3,2,1,0:T(8,128)(2,1)}), bf16[4,2,128,256]{3,2,1,0:T(8,128)(2,1)S(1)}, u32[]{:S(2)}, u32[]{:S(2)}) async-start(bf16[4,2,128,256]{3,2,1,0:T(8,128)(2,1)} %attend.1), calls=%async_computation.2 | async-start | bytes 1048576 | tf_op jit(solution)/shard_map/all_to_all | solution.py:408
  79.5 10.1 %all-to-all-done.2.ctx_ref = bf16[4,2,128,256]{3,2,1,0:T(8,128)(2,1)S(1)} async-done(((bf16[4,2,128,256]{3,2,1,0:T(8,128)(2,1)}), bf16[4,2,128,256]{3,2,1,0:T(8,128)(2,1)S(1)}, u32[]{:S(2)}, u32[]{:S(2)}) %all-to-all-start.2) | async-done | bytes 524320 | tf_op jit(solution)/shard_map/all_to_all | solution.py:408
  89.6 4.8 %oproj.1 = (f32[128,2048]{1,0:T(8,128)S(1)}, bf16[128,2048]{1,0:T(8,128)(2,1)S(1)}) custom-call(s32[2]{0:T(128)S(1)} %pad_add_fusion.at_ref, bf16[4,2,128,256]{3,2,1,0:T(8,128)(2,1)S(1)} %all-to-all-done.2.ctx_ref, bf16[4,8,256,128]{3,2,1,0:T(8,128)(2,1)} %all-to-all-done.1.own_ref, bf16[4,8,256,128]{3,2,1,0:T(8,128)(2,1)S(1)} %collective-permute-done.5.oth_ref), custom_call_target="tpu_custom_call" | custom-call | tf_op jit(solution)/shard_map/oproj/pallas_call | solution.py:180
  94.4 1.0 copy-done.2
  95.4 0.5 collective-permute-start.6
  96.0 24.9 %collective-permute-done.6 = bf16[128,2048]{1,0:T(8,128)(2,1)S(1)} collective-permute-done((bf16[128,2048]{1,0:T(8,128)(2,1)S(1)}, bf16[128,2048]{1,0:T(8,128)(2,1)S(1)}, u32[]{:S(2)}, u32[]{:S(2)}) %collective-permute-start.6) | collective-permute-done | bytes 524320 | tf_op jit(solution)/shard_map/ppermute | solution.py:23
  120.9 1.5 add_convert_fusion
  122.8 1.2 collective-permute-start.8
  124.1 0.9 collective-permute-start.7
  124.9 10.5 %collective-permute-done.8.x2_ref = bf16[128,2048]{1,0:T(8,128)(2,1)S(1)} collective-permute-done((bf16[128,2048]{1,0:T(8,128)(2,1)S(1)}, bf16[128,2048]{1,0:T(8,128)(2,1)S(1)}, u32[]{:S(2)}, u32[]{:S(2)}) %collective-permute-start.8) | collective-permute-done | bytes 524320 | tf_op jit(solution)/shard_map/ppermute | solution.py:419
  135.4 2.1 %collective-permute-done.7.x1_ref = bf16[128,2048]{1,0:T(8,128)(2,1)S(1)} collective-permute-done((bf16[128,2048]{1,0:T(8,128)(2,1)S(1)}, bf16[128,2048]{1,0:T(8,128)(2,1)S(1)}, u32[]{:S(2)}, u32[]{:S(2)}) %collective-permute-start.7) | collective-permute-done | bytes 524320 | tf_op jit(solution)/shard_map/ppermute | solution.py:418
  137.6 0.4 collective-permute-start.10
  137.9 1.7 collective-permute-start.9
  139.7 6.7 %collective-permute-done.10.x4_ref = bf16[64,2048]{1,0:T(8,128)(2,1)S(1)} collective-permute-done((bf16[64,2048]{1,0:T(8,128)(2,1)S(1)}, bf16[64,2048]{1,0:T(8,128)(2,1)S(1)}, u32[]{:S(2)}, u32[]{:S(2)}) %collective-permute-start.10) | collective-permute-done | bytes 262176 | tf_op jit(solution)/shard_map/ppermute | solution.py:423
  146.3 1.3 collective-permute-done.9.x3_ref
  147.6 4.9 %collective-permute-done.11.oth_ref = bf16[8,2,4,288,256]{4,3,2,1,0:T(8,128)(2,1)} collective-permute-done((bf16[8,2,4,288,256]{4,3,2,1,0:T(8,128)(2,1)}, bf16[8,2,4,288,256]{4,3,2,1,0:T(8,128)(2,1)}, u32[]{:S(2)}, u32[]{:S(2)}) %collective-permute-start.11) | collective-permute-done | bytes 9437216 | tf_op jit(solution)/shard_map/ppermute | solution.py:23
  152.5 3.7 %copy-done = bf16[64,288,256]{2,1,0:T(8,128)(2,1)S(1)} copy-done((bf16[64,288,256]{2,1,0:T(8,128)(2,1)S(1)}, bf16[64,288,256]{2,1,0:T(8,128)(2,1)}, u32[]{:S(2)}) %copy-start) | copy-done | bytes 9437208
  156.2 8.5 %gate_up.1.hid_ref = bf16[512,1536]{1,0:T(8,128)(2,1)S(1)} custom-call(s32[1]{0:T(128)} %bitcast.2.y_ref, bf16[128,2048]{1,0:T(8,128)(2,1)S(1)} %fusion.2.x0_ref, bf16[128,2048]{1,0:T(8,128)(2,1)S(1)} %collective-permute-done.7.x1_ref, bf16[128,2048]{1,0:T(8,128)(2,1)S(1)} %collective-permute-done.8.x2_ref, ...), custom_call_target="tpu_custom_call" | custom-call | tf_op jit(solution)/shard_map/gate_up/pallas_call | solution.py:277
  164.7 4.6 %down_far.1 = (bf16[64,2048]{1,0:T(8,128)(2,1)S(1)}, bf16[64,2048]{1,0:T(8,128)(2,1)S(1)}, bf16[1,16,96,2048]{3,2,1,0:T(8,128)(2,1)S(1)}) custom-call(s32[1]{0:T(128)} %bitcast.2.y_ref, bf16[512,1536]{1,0:T(8,128)(2,1)S(1)} %gate_up.1.hid_ref, bf16[8,2,4,288,256]{4,3,2,1,0:T(8,128)(2,1)} %bitcast.9, bf16[8,2,4,288,256]{4,3,2,1,0:T(8,128)(2,1)} %collective-permute-done.11.oth_ref), custom_call_target="tpu_custom_call" | custom-call | tf_op jit(solution)/shard_map/down_far/pallas_call | solution.py:295
  169.7 3.2 %down.1 = (f32[128,2048]{1,0:T(8,128)S(1)}, bf16[128,2048]{1,0:T(8,128)(2,1)S(1)}, bf16[128,2048]{1,0:T(8,128)(2,1)S(1)}) custom-call(bf16[512,1536]{1,0:T(8,128)(2,1)S(1)} %gate_up.1.hid_ref, bf16[1,16,96,2048]{3,2,1,0:T(8,128)(2,1)S(1)} %get-tuple-element.48.w_ref), custom_call_target="tpu_custom_call" | custom-call | tf_op jit(solution)/shard_map/down/pallas_call | solution.py:307
  173.0 1.8 collective-permute-start.12
  174.8 3.0 %collective-permute-done.14 = bf16[64,2048]{1,0:T(8,128)(2,1)S(1)} collective-permute-done((bf16[64,2048]{1,0:T(8,128)(2,1)S(1)}, bf16[64,2048]{1,0:T(8,128)(2,1)S(1)}, u32[]{:S(2)}, u32[]{:S(2)}) %collective-permute-start.14) | collective-permute-done | bytes 262176 | tf_op jit(solution)/shard_map/ppermute | solution.py:427
  177.9 1.6 collective-permute-start.15
  179.4 2.9 %collective-permute-done.12 = bf16[64,2048]{1,0:T(8,128)(2,1)S(1)} collective-permute-done((bf16[64,2048]{1,0:T(8,128)(2,1)S(1)}, bf16[64,2048]{1,0:T(8,128)(2,1)S(1)}, u32[]{:S(2)}, u32[]{:S(2)}) %collective-permute-start.12) | collective-permute-done | bytes 262176 | tf_op jit(solution)/shard_map/ppermute | solution.py:426
  182.4 0.6 collective-permute-start.13
  183.0 8.0 %collective-permute-done.15 = bf16[128,2048]{1,0:T(8,128)(2,1)S(1)} collective-permute-done((bf16[128,2048]{1,0:T(8,128)(2,1)S(1)}, bf16[128,2048]{1,0:T(8,128)(2,1)S(1)}, u32[]{:S(2)}, u32[]{:S(2)}) %collective-permute-start.15) | collective-permute-done | bytes 524320 | tf_op jit(solution)/shard_map/ppermute | solution.py:432
  191.1 5.5 %collective-permute-done.13 = bf16[128,2048]{1,0:T(8,128)(2,1)S(1)} collective-permute-done((bf16[128,2048]{1,0:T(8,128)(2,1)S(1)}, bf16[128,2048]{1,0:T(8,128)(2,1)S(1)}, u32[]{:S(2)}, u32[]{:S(2)}) %collective-permute-start.13) | collective-permute-done | bytes 524320 | tf_op jit(solution)/shard_map/ppermute | solution.py:431
  196.5 1.1 fusion.3
  (47 shorter events, 1.7 us)
Async XLA Ops:
  9.5 15.0 %copy-start.11 = (s32[1024]{0:T(1024)S(1)}, s32[1024]{0:T(1024)}, u32[]{:S(2)}) copy-start(s32[1024]{0:T(1024)} %param.15) | copy-start | bytes 12292
  9.5 28.2 %all-to-all-start = ((bf16[8,768,128]{2,1,0:T(8,128)(2,1)}), bf16[8,768,128]{2,1,0:T(8,128)(2,1)S(1)}, u32[]{:S(2)}, u32[]{:S(2)}) async-start(bf16[8,768,128]{2,1,0:T(8,128)(2,1)} %pack.1), calls=%async_computation | async-start | bytes 3145728 | tf_op jit(solution)/shard_map/all_to_all | solution.py:387
  17.5 120.0 %all-gather.3.cloned.1.call-start = ((), (), s32[]{:S(2)}) async-start(), calls=%async_computation.3 | async-start | bytes 10027008 | tf_op jit(solution)/shard_map/all_gather | solution.py:395
  19.9 9.0 %collective-permute-start = (bf16[288,256]{1,0:T(8,128)(2,1)}, bf16[288,256]{1,0:T(8,128)(2,1)S(1)}, u32[]{:S(2)}, u32[]{:S(2)}) collective-permute-start(bf16[288,256]{1,0:T(8,128)(2,1)} %get-tuple-element.29), channel_id=1, source_target_pairs={{0,3},{1,0},{2,1},{3,2},{4,7},{5,4},{6,5},{7,6},{8,11},{9,8},{10,9... | collective-permute-start | bytes 442376 | tf_op jit(solution)/shard_map/ppermute | solution.py:361
  22.9 8.1 %collective-permute-start.1 = (bf16[288,256]{1,0:T(8,128)(2,1)}, bf16[288,256]{1,0:T(8,128)(2,1)S(1)}, u32[]{:S(2)}, u32[]{:S(2)}) collective-permute-start(bf16[288,256]{1,0:T(8,128)(2,1)} %get-tuple-element.30), channel_id=1, source_target_pairs={{0,2},{1,3},{2,0},{3,1},{4,6},{5,7},{6,4},{7,5},{8,10},{9,11},{10,... | collective-permute-start | bytes 442376 | tf_op jit(solution)/shard_map/ppermute | solution.py:361
  23.5 9.0 %collective-permute-start.2 = (bf16[288,256]{1,0:T(8,128)(2,1)}, bf16[288,256]{1,0:T(8,128)(2,1)S(1)}, u32[]{:S(2)}, u32[]{:S(2)}) collective-permute-start(bf16[288,256]{1,0:T(8,128)(2,1)} %get-tuple-element.31), channel_id=1, source_target_pairs={{0,1},{1,2},{2,3},{3,0},{4,5},{5,6},{6,7},{7,4},{8,9},{9,10},{10,1... | collective-permute-start | bytes 442376 | tf_op jit(solution)/shard_map/ppermute | solution.py:361
  28.9 8.8 %copy-start.7 = (bf16[288,256]{1,0:T(8,128)(2,1)}, bf16[288,256]{1,0:T(8,128)(2,1)S(1)}, u32[]{:S(2)}) copy-start(bf16[288,256]{1,0:T(8,128)(2,1)S(1)} %collective-permute-done.p1_ref) | copy-start | bytes 442372
  31.0 6.7 %copy-start.8 = (bf16[288,256]{1,0:T(8,128)(2,1)}, bf16[288,256]{1,0:T(8,128)(2,1)S(1)}, u32[]{:S(2)}) copy-start(bf16[288,256]{1,0:T(8,128)(2,1)S(1)} %collective-permute-done.1.p2_ref) | copy-start | bytes 442372
  32.5 5.2 %copy-start.9 = (bf16[288,256]{1,0:T(8,128)(2,1)}, bf16[288,256]{1,0:T(8,128)(2,1)S(1)}, u32[]{:S(2)}) copy-start(bf16[288,256]{1,0:T(8,128)(2,1)S(1)} %collective-permute-done.2.p3_ref) | copy-start | bytes 442372
  39.7 6.6 %collective-permute-start.3 = (bf16[8,768,128]{2,1,0:T(8,128)(2,1)S(1)}, bf16[8,768,128]{2,1,0:T(8,128)(2,1)}, u32[]{:S(2)}, u32[]{:S(2)}) collective-permute-start(bf16[8,768,128]{2,1,0:T(8,128)(2,1)S(1)} %all-to-all-done.own_ref), channel_id=1, source_target_pairs={{0,8},{8,0},{1,9},{9,1},{2,10},{10,2},{3,11},{11,3},{4,12},{12,4},... | collective-permute-start | bytes 4718600 | tf_op jit(solution)/shard_map/ppermute | solution.py:23
  41.7 4.6 %copy-start.4 = (f32[2048]{0:T(1024)S(1)}, f32[2048]{0:T(1024)}, u32[]{:S(2)}) copy-start(f32[2048]{0:T(1024)} %param.16) | copy-start | bytes 24580
  41.7 4.6 %copy-start.5 = (f32[128]{0:T(128)S(1)}, f32[128]{0:T(128)}, u32[]{:S(2)}) copy-start(f32[128]{0:T(128)} %param.18) | copy-start | bytes 1540
  41.7 4.6 %copy-start.6 = (f32[128]{0:T(128)S(1)}, f32[128]{0:T(128)}, u32[]{:S(2)}) copy-start(f32[128]{0:T(128)} %param.19) | copy-start | bytes 1540
  41.7 33.3 %all-to-all-start.1 = ((bf16[4,8,256,128]{3,2,1,0:T(8,128)(2,1)}), bf16[4,8,256,128]{3,2,1,0:T(8,128)(2,1)}, u32[]{:S(2)}, u32[]{:S(2)}) async-start(bf16[4,8,256,128]{3,2,1,0:T(8,128)(2,1)} %broadcast_in_dim.33), calls=%async_computation.1 | async-start | bytes 4194304 | tf_op jit(solution)/shard_map/all_to_all | solution.py:401
  46.3 2.2 %copy-start.1 = (bf16[1024,2048]{1,0:T(8,128)(2,1)S(1)}, bf16[1024,2048]{1,0:T(8,128)(2,1)}, u32[]{:S(2)}) copy-start(bf16[1024,2048]{1,0:T(8,128)(2,1)} %x_ref.1) | copy-start | bytes 12582916
  55.7 11.8 %collective-permute-start.4 = (bf16[2,512,128]{2,1,0:T(8,128)(2,1)S(1)}, bf16[2,512,128]{2,1,0:T(8,128)(2,1)S(1)}, u32[]{:S(2)}, u32[]{:S(2)}) collective-permute-start(bf16[2,512,128]{2,1,0:T(8,128)(2,1)S(1)} %get-tuple-element.36), channel_id=1, source_target_pairs={{0,8},{8,16},{16,24},{24,32},{32,40},{40,48},{48,56},{56,64},{64,7... | collective-permute-start | bytes 786440 | tf_op jit(solution)/shard_map/ppermute | solution.py:404
  67.5 1.0 copy-start.3
  74.9 14.6 %collective-permute-start.5 = (bf16[4,8,256,128]{3,2,1,0:T(8,128)(2,1)}, bf16[4,8,256,128]{3,2,1,0:T(8,128)(2,1)S(1)}, u32[]{:S(2)}, u32[]{:S(2)}) collective-permute-start(bf16[4,8,256,128]{3,2,1,0:T(8,128)(2,1)} %all-to-all-done.1.own_ref), channel_id=1, source_target_pairs={{0,8},{8,0},{1,9},{9,1},{2,10},{10,2},{3,11},{11,3},{4,12},{12,4},... | collective-permute-start | bytes 6291464 | tf_op jit(solution)/shard_map/ppermute | solution.py:23
  75.0 14.6 %all-to-all-start.2 = ((bf16[4,2,128,256]{3,2,1,0:T(8,128)(2,1)}), bf16[4,2,128,256]{3,2,1,0:T(8,128)(2,1)S(1)}, u32[]{:S(2)}, u32[]{:S(2)}) async-start(bf16[4,2,128,256]{3,2,1,0:T(8,128)(2,1)} %attend.1), calls=%async_computation.2 | async-start | bytes 1048576 | tf_op jit(solution)/shard_map/all_to_all | solution.py:408
  94.4 1.0 copy-start.2
  95.4 27.2 %copy-start.10 = (f32[2048]{0:T(1024)S(1)}, f32[2048]{0:T(1024)}, u32[]{:S(2)}) copy-start(f32[2048]{0:T(1024)} %param.17) | copy-start | bytes 24580
  95.4 25.5 %collective-permute-start.6 = (bf16[128,2048]{1,0:T(8,128)(2,1)S(1)}, bf16[128,2048]{1,0:T(8,128)(2,1)S(1)}, u32[]{:S(2)}, u32[]{:S(2)}) collective-permute-start(bf16[128,2048]{1,0:T(8,128)(2,1)S(1)} %get-tuple-element.40), channel_id=1, source_target_pairs={{0,4},{4,0},{1,5},{5,1},{2,6},{6,2},{3,7},{7,3},{8,12},{12,8},{9,1... | collective-permute-start | bytes 1572872 | tf_op jit(solution)/shard_map/ppermute | solution.py:23
  122.8 12.6 %collective-permute-start.8 = (bf16[128,2048]{1,0:T(8,128)(2,1)S(1)}, bf16[128,2048]{1,0:T(8,128)(2,1)S(1)}, u32[]{:S(2)}, u32[]{:S(2)}) collective-permute-start(bf16[128,2048]{1,0:T(8,128)(2,1)S(1)} %fusion.2.x0_ref), channel_id=1, source_target_pairs={{0,3},{1,0},{2,1},{3,2},{4,7},{5,4},{6,5},{7,6},{8,11},{9,8},{10,9... | collective-permute-start | bytes 1572872 | tf_op jit(solution)/shard_map/ppermute | solution.py:419
  124.1 13.4 %collective-permute-start.7 = (bf16[128,2048]{1,0:T(8,128)(2,1)S(1)}, bf16[128,2048]{1,0:T(8,128)(2,1)S(1)}, u32[]{:S(2)}, u32[]{:S(2)}) collective-permute-start(bf16[128,2048]{1,0:T(8,128)(2,1)S(1)} %fusion.2.x0_ref), channel_id=1, source_target_pairs={{0,1},{1,2},{2,3},{3,0},{4,5},{5,6},{6,7},{7,4},{8,9},{9,10},{10,1... | collective-permute-start | bytes 1572872 | tf_op jit(solution)/shard_map/ppermute | solution.py:418
  137.5 15.0 %collective-permute-start.11 = (bf16[8,2,4,288,256]{4,3,2,1,0:T(8,128)(2,1)}, bf16[8,2,4,288,256]{4,3,2,1,0:T(8,128)(2,1)}, u32[]{:S(2)}, u32[]{:S(2)}) collective-permute-start(bf16[8,2,4,288,256]{4,3,2,1,0:T(8,128)(2,1)} %bitcast.8), channel_id=1, source_target_pairs={{0,8},{8,0},{1,9},{9,1},{2,10},{10,2},{3,11},{11,3},{4,12},{12,4},... | collective-permute-start | bytes 28311560 | tf_op jit(solution)/shard_map/ppermute | solution.py:23
  137.6 8.8 %collective-permute-start.10 = (bf16[64,2048]{1,0:T(8,128)(2,1)S(1)}, bf16[64,2048]{1,0:T(8,128)(2,1)S(1)}, u32[]{:S(2)}, u32[]{:S(2)}) collective-permute-start(bf16[64,2048]{1,0:T(8,128)(2,1)S(1)} %slice.23), channel_id=1, source_target_pairs={{0,3},{1,0},{2,1},{3,2},{4,7},{5,4},{6,5},{7,6},{8,11},{9,8},{10,9... | collective-permute-start | bytes 786440 | tf_op jit(solution)/shard_map/ppermute | solution.py:423
  137.9 9.7 %collective-permute-start.9 = (bf16[64,2048]{1,0:T(8,128)(2,1)S(1)}, bf16[64,2048]{1,0:T(8,128)(2,1)S(1)}, u32[]{:S(2)}, u32[]{:S(2)}) collective-permute-start(bf16[64,2048]{1,0:T(8,128)(2,1)S(1)} %slice.22), channel_id=1, source_target_pairs={{0,1},{1,2},{2,3},{3,0},{4,5},{5,6},{6,7},{7,4},{8,9},{9,10},{10,1... | collective-permute-start | bytes 786440 | tf_op jit(solution)/shard_map/ppermute | solution.py:422
  152.5 3.7 %copy-start = (bf16[64,288,256]{2,1,0:T(8,128)(2,1)S(1)}, bf16[64,288,256]{2,1,0:T(8,128)(2,1)}, u32[]{:S(2)}) copy-start(bf16[64,288,256]{2,1,0:T(8,128)(2,1)} %all-gather.3.cloned.1.call-done) | copy-start | bytes 28311556
  169.3 8.4 %collective-permute-start.14 = (bf16[64,2048]{1,0:T(8,128)(2,1)S(1)}, bf16[64,2048]{1,0:T(8,128)(2,1)S(1)}, u32[]{:S(2)}, u32[]{:S(2)}) collective-permute-start(bf16[64,2048]{1,0:T(8,128)(2,1)S(1)} %get-tuple-element.53), channel_id=1, source_target_pairs={{0,3},{1,0},{2,1},{3,2},{4,7},{5,4},{6,5},{7,6},{8,11},{9,8},{10,9... | collective-permute-start | bytes 786440 | tf_op jit(solution)/shard_map/ppermute | solution.py:427
  173.0 9.4 %collective-permute-start.12 = (bf16[64,2048]{1,0:T(8,128)(2,1)S(1)}, bf16[64,2048]{1,0:T(8,128)(2,1)S(1)}, u32[]{:S(2)}, u32[]{:S(2)}) collective-permute-start(bf16[64,2048]{1,0:T(8,128)(2,1)S(1)} %get-tuple-element.51), channel_id=1, source_target_pairs={{0,1},{1,2},{2,3},{3,0},{4,5},{5,6},{6,7},{7,4},{8,9},{9,10},{10,1... | collective-permute-start | bytes 786440 | tf_op jit(solution)/shard_map/ppermute | solution.py:426
  177.9 13.2 %collective-permute-start.15 = (bf16[128,2048]{1,0:T(8,128)(2,1)S(1)}, bf16[128,2048]{1,0:T(8,128)(2,1)S(1)}, u32[]{:S(2)}, u32[]{:S(2)}) collective-permute-start(bf16[128,2048]{1,0:T(8,128)(2,1)S(1)} %pad_maximum_fusion.2), channel_id=1, source_target_pairs={{0,3},{1,0},{2,1},{3,2},{4,7},{5,4},{6,5},{7,6},{8,11},{9,8},{10,9... | collective-permute-start | bytes 1572872 | tf_op jit(solution)/shard_map/ppermute | solution.py:432
  182.4 14.1 %collective-permute-start.13 = (bf16[128,2048]{1,0:T(8,128)(2,1)S(1)}, bf16[128,2048]{1,0:T(8,128)(2,1)S(1)}, u32[]{:S(2)}, u32[]{:S(2)}) collective-permute-start(bf16[128,2048]{1,0:T(8,128)(2,1)S(1)} %pad_maximum_fusion.1), channel_id=1, source_target_pairs={{0,1},{1,2},{2,3},{3,0},{4,5},{5,6},{6,7},{7,4},{8,9},{9,10},{10,1... | collective-permute-start | bytes 1572872 | tf_op jit(solution)/shard_map/ppermute | solution.py:431
Sparse Core Ops, SparseCore 0:
  39.8 85.8 all-gather.2

commit v5 on v4

--- a/solution.py
+++ b/solution.py
@@ -23,7 +23,26 @@
     return lax.ppermute(block, axis, [(0, 1), (1, 0)])
 
 
-def qkv_kernel(core_ref, x_ref, own_ref, oth_ref, gain_ref, qg_ref, kg_ref, cs_ref, q_ref, kv_ref, tail_ref, w_ref):
+def norm_kernel(x_ref, gain_ref, out_ref):
+    x = x_ref[...].astype(F32)
+    scale = lax.rsqrt(jnp.mean(x * x, axis=-1, keepdims=True) + 1e-06)
+    out_ref[...] = (x * scale * gain_ref[...]).astype(BF)
+
+
+def normalise(x, gain):
+    rows, tile = x.shape[0], min(256, x.shape[0])
+    block = pl.BlockSpec((tile, 2048), lambda i: (i, 0))
+    return pl.pallas_call(
+        norm_kernel,
+        grid=(rows // tile,),
+        in_specs=[block, pl.BlockSpec((1, 2048), lambda i: (0, 0))],
+        out_specs=block,
+        out_shape=jax.ShapeDtypeStruct(x.shape, BF),
+        name="norm",
+    )(x, gain[None])
+
+
+def qkv_kernel(core_ref, x_ref, own_ref, oth_ref, qg_ref, kg_ref, cs_ref, q_ref, kv_ref, tail_ref, w_ref):
     core = core_ref[0]
 
     @pl.when(pl.program_id(0) == 0)
@@ -37,10 +56,7 @@
 
         lax.fori_loop(0, 8, place, 0)
 
-    x = x_ref[...].astype(F32)
-    scale = lax.rsqrt(jnp.mean(x * x, axis=-1, keepdims=True) + 1e-06)
-    normed = (x * scale * gain_ref[...]).astype(BF)
-    raw = jnp.dot(normed, w_ref[...], preferred_element_type=F32)
+    raw = jnp.dot(x_ref[...], w_ref[...], preferred_element_type=F32)
     cs = cs_ref[...]
     turned = pltpu.roll(cs, 64, 1)
     low = lax.broadcasted_iota(jnp.int32, cs.shape, 1) < 64
@@ -64,8 +80,8 @@
         tail_ref[1] = values
 
 
-def project(core, tokens, own, oth, attn_gain, q_gain, key_gain, cs):
-    rows = tokens.shape[0]
+def project(core, normed, own, oth, q_gain, key_gain, cs):
+    rows = normed.shape[0]
     tile = 256
     fixed = lambda *shape: pl.BlockSpec(shape, lambda i, c: (0,) * len(shape))
     return pl.pallas_call(
@@ -77,7 +93,6 @@
                 pl.BlockSpec((tile, 2048), lambda i, c: (i, 0)),
                 fixed(8, 512, 128),
                 fixed(8, 512, 128),
-                fixed(1, 2048),
                 fixed(1, 128),
                 fixed(1, 128),
                 pl.BlockSpec((tile, 128), lambda i, c: (i, 0)),
@@ -96,7 +111,7 @@
         ),
         compiler_params=pltpu.CompilerParams(vmem_limit_bytes=40 << 20),
         name="qkv",
-    )(core, tokens, own, oth, attn_gain[None], q_gain[None], key_gain[None], cs)
+    )(core, normed, own, oth, q_gain[None], key_gain[None], cs)
 
 
 def attend_kernel(q_ref, kv_ref, prior_ref, lo_ref, out_ref):
@@ -215,37 +230,33 @@
     return each
 
 
-def gate_kernel(y_ref, x0_ref, x1_ref, x2_ref, x3_ref, x4_ref, own_ref, oth_ref, hid_ref, w_ref, x_ref, sems):
+def gate_kernel(y_ref, x0_ref, x1_ref, x2_ref, x3_ref, x4_ref, src_ref, hid_ref, w_ref, x_ref, sems):
     nt = (((1,), (1,)), ((), ()))
-    each = fetcher(own_ref, oth_ref, w_ref, sems, y_ref[0], 0)
+    each = fetcher(src_ref, src_ref, w_ref, sems, y_ref[0], 0)
     each(0, 2, lambda c: c.start())
-    each(1, 2, lambda c: c.start())
     x_ref[0:128] = x0_ref[...]
     x_ref[128:256] = x1_ref[...]
     x_ref[256:384] = x2_ref[...]
     x_ref[384:448] = x3_ref[...]
     x_ref[448:512] = x4_ref[...]
     x = x_ref[...]
-
-    for c in range(2):
-        each(c, 2, lambda copy: copy.wait())
-        gate_w = w_ref[0, c * 8 : c * 8 + 8].reshape(768, 2048)
-        up_w = w_ref[1, c * 8 : c * 8 + 8].reshape(768, 2048)
-        for t in range(3):
-            gate = lax.dot_general(x, gate_w[t * 256 : t * 256 + 256], nt, preferred_element_type=F32)
-            upper = lax.dot_general(x, up_w[t * 256 : t * 256 + 256], nt, preferred_element_type=F32)
-            hidden = gate / (1.0 + jnp.exp(-gate)) * upper
-            at = c * 768 + t * 256
-            hid_ref[:, at : at + 256] = hidden.astype(BF)
-
-
-def far_kernel(y_ref, hid_ref, own_ref, oth_ref, top_ref, bottom_ref, w_ref, sems):
+    each(0, 2, lambda copy: copy.wait())
+    gate_w = w_ref[0].reshape(768, 2048)
+    up_w = w_ref[1].reshape(768, 2048)
+    for t in range(3):
+        gate = lax.dot_general(x, gate_w[t * 256 : t * 256 + 256], nt, preferred_element_type=F32)
+        upper = lax.dot_general(x, up_w[t * 256 : t * 256 + 256], nt, preferred_element_type=F32)
+        hidden = gate / (1.0 + jnp.exp(-gate)) * upper
+        hid_ref[:, t * 256 : t * 256 + 256] = hidden.astype(BF)
+
+
+def far_kernel(y_ref, hid0_ref, hid1_ref, own_ref, oth_ref, top_ref, bottom_ref, w_ref, sems):
     each = fetcher(own_ref, oth_ref, w_ref, sems, y_ref[0], 192)
     for c in range(2):
         each(c, 1, lambda copy: copy.start())
     for c in range(2):
         each(c, 1, lambda copy: copy.wait())
-    hid = hid_ref[384:]
+    hid = jnp.concatenate([hid0_ref[384:], hid1_ref[384:]], axis=1)
 
     def column(n, carry):
         at = pl.ds(pl.multiple_of(n * 512, 512), 512)
@@ -257,8 +268,8 @@
     lax.fori_loop(0, 4, column, 0)
 
 
-def down_kernel(hid_ref, w_ref, keep_ref, left_ref, right_ref):
-    hid = hid_ref[:384]
+def down_kernel(hid0_ref, hid1_ref, w_ref, keep_ref, left_ref, right_ref):
+    hid = jnp.concatenate([hid0_ref[:384], hid1_ref[:384]], axis=1)
 
     def column(n, carry):
         at = pl.ds(pl.multiple_of(n * 512, 512), 512)
@@ -271,21 +282,21 @@
     lax.fori_loop(0, 4, column, 0)
 
 
-def gate_up(y, pieces, own, oth):
+def gate_up(y, pieces, src):
     vm = pl.BlockSpec(memory_space=pltpu.VMEM)
     hbm = pl.BlockSpec(memory_space=pltpu.HBM)
     return pl.pallas_call(
         gate_kernel,
-        in_specs=[pl.BlockSpec(memory_space=pltpu.SMEM)] + [vm] * 5 + [hbm] * 2,
-        out_shape=jax.ShapeDtypeStruct((512, 1536), BF),
+        in_specs=[pl.BlockSpec(memory_space=pltpu.SMEM)] + [vm] * 5 + [hbm],
+        out_shape=jax.ShapeDtypeStruct((512, 768), BF),
         scratch_shapes=[
-            pltpu.VMEM((2, 16, 96, 2048), BF),
+            pltpu.VMEM((2, 8, 96, 2048), BF),
             pltpu.VMEM((512, 2048), BF),
-            pltpu.SemaphoreType.DMA((2, 2, 8)),
+            pltpu.SemaphoreType.DMA((2, 1, 8)),
         ],
         compiler_params=pltpu.CompilerParams(vmem_limit_bytes=40 << 20),
         name="gate_up",
-    )(y, *pieces, own, oth)
+    )(y, *pieces, src)
 
 
 def down_far(y, hidden, own, oth):
@@ -294,12 +305,12 @@
     half = jax.ShapeDtypeStruct((64, 2048), BF)
     return pl.pallas_call(
         far_kernel,
-        in_specs=[pl.BlockSpec(memory_space=pltpu.SMEM), vm] + [hbm] * 2,
+        in_specs=[pl.BlockSpec(memory_space=pltpu.SMEM), vm, vm] + [hbm] * 2,
         out_shape=(half, half, jax.ShapeDtypeStruct((1, 16, 96, 2048), BF)),
         scratch_shapes=[pltpu.SemaphoreType.DMA((1, 2, 8))],
         compiler_params=pltpu.CompilerParams(vmem_limit_bytes=40 << 20),
         name="down_far",
-    )(y, hidden, own, oth)
+    )(y, *hidden, own, oth)
 
 
 def down(hidden, weight):
@@ -309,7 +320,7 @@
         out_shape=(jax.ShapeDtypeStruct((128, 2048), F32), part, part),
         compiler_params=pltpu.CompilerParams(vmem_limit_bytes=40 << 20),
         name="down",
-    )(hidden, weight)
+    )(*hidden, weight)
 
 
 def pack_kernel(q_ref, k_ref, v_ref, o_ref, out_ref):
@@ -391,7 +402,8 @@
     freq = jnp.exp(jnp.arange(half, dtype=F32) * (-2.0 * math.log(1000000.0) / HEAD))
     angle = positions.astype(F32)[:, None] * freq[None, :]
     cs = jnp.concatenate([jnp.cos(angle), jnp.sin(angle)], axis=1)
-    cs, at_own, *parts = hold((cs, at_own, *parts))
+    normed = normalise(tokens, attn_gain)
+    cs, normed, at_own, *parts = hold((cs, normed, at_own, *parts))
     mlp_own = lax.all_gather(join(parts), ("z", "xh", "xl"), axis=0, tiled=False).reshape(8, 2, 4, 288, 256)
     lo = (jnp.arange(rows, dtype=jnp.int32) - positions)[:, None]
 
@@ -400,10 +412,10 @@
     o_wide = jnp.broadcast_to(at_own[None, :, 512:], (4, 8, 256, 128))
     o_own = lax.all_to_all(o_wide, "y", split_axis=0, concat_axis=0, tiled=True)
 
-    q, cache, tail = project(core[None], tokens, at_own, at_oth, attn_gain, q_gain, key_norm_gain, cs)
+    q, cache, tail = project(core[None], normed, at_own, at_oth, q_gain, key_norm_gain, cs)
     prior = lax.ppermute(tail, REQ, [(i - 1, i) for i in range(1, 16)])
     ctx = attend(q, cache, prior, lo)
-    ctx, o_own = hold((ctx, o_own))
+    _, o_own = hold((ctx, o_own))
     o_oth = swap(o_own, "core")
     ctx = lax.all_to_all(ctx, "y", split_axis=0, concat_axis=0, tiled=True)
     keep, send = out_project(jnp.stack([core, xl]), ctx, o_own, o_oth)
@@ -415,13 +427,18 @@
     scale = lax.rsqrt(jnp.mean(resid * resid, axis=-1, keepdims=True) + 1e-06)
     mlp_in = (resid * scale * mlp_gain).astype(BF)
 
+    mlp_own, mlp_in = hold((mlp_own, mlp_in))
+    mlp_oth = swap(mlp_own, "core")
     left = lax.ppermute(mlp_in, "y", ring(1))
     right = lax.ppermute(mlp_in, "y", ring(3))
-    mlp_own, left, right = hold((mlp_own, left, right))
-    mlp_oth = swap(mlp_own, "core")
     far_top = lax.ppermute(left[:64], "y", ring(1))
     far_bottom = lax.ppermute(right[64:], "y", ring(3))
-    hidden = gate_up(y[None], (mlp_in, left, right, far_top, far_bottom), mlp_own, mlp_oth)
+    pieces = (mlp_in, left, right, far_top, far_bottom)
+    mlp_own = pltpu.with_memory_space_constraint(mlp_own, pltpu.HBM)
+    first = gate_up(y[None], pieces, mlp_own)
+    first, mlp_oth = hold((first, mlp_oth))
+    mlp_oth = pltpu.with_memory_space_constraint(mlp_oth, pltpu.HBM)
+    hidden = (first, gate_up(y[None], pieces, mlp_oth))
     top, bottom, weight = down_far(y[None], hidden, mlp_own, mlp_oth)
     via_left = lax.ppermute(top, "y", ring(1))
     via_right = lax.ppermute(bottom, "y", ring(3))

time: 206 us -> 208 us (level)
  Pallas kernels: 41.4 us -> 50.2 us
  waiting for transfers between devices: 100 us -> 91.8 us
    pallas_call x0 -> x1, Pallas kernels: none -> 5.42 us  [normalise(): pl.pallas_call(norm_kernel, grid=(rows // tile,), in_specs=[block, pl.Blo...]
    ppermute x3, waiting for transfers between devices: 5.89 us -> 0.55 us  [trade(): lax.ppermute(parts[4 - k], 'y', ring(4 - k))]
    ppermute x4, waiting for transfers between devices: 29.8 us -> 24.8 us  [swap(): return lax.ppermute(block, axis, [(0, 1), (1, 0)])]
    pallas_call x1 -> x2, Pallas kernels: 8.55 us -> 12.8 us  [gate_up(): pl.pallas_call(gate_kernel, in_specs=[pl.BlockSpec(memory_space=pltpu.SME...]
    all_gather x1, waiting for transfers between devices: 0.01 us -> 3.63 us  [per_device(): lax.all_gather(join(parts), ('z', 'xh', 'xl'), axis=0, tiled=False)]
    ppermute x1, starting transfers between devices: 0.36 us -> 3.76 us  [per_device(): far_bottom = lax.ppermute(right[64:], 'y', ring(3))]
    ppermute x1, waiting for transfers between devices: 1.29 us -> 3.51 us  [per_device(): far_top = lax.ppermute(left[:64], 'y', ring(1))]
    ppermute x1, waiting for transfers between devices: 2.1 us -> 0.01 us  [per_device(): left = lax.ppermute(mlp_in, 'y', ring(1))]
  transfers between devices with their start and end apart: 20 -> 20, of which waited for: 16 -> 13; matrix products, arithmetic and copies ran while one was open for 3% -> 3% of each run, Pallas kernels for 12% -> 17%
where the time goes in v5:
time: 208 us; the launch traced here: 207 us
  waiting for transfers between devices  91.8 us (44%)
  Pallas kernels  50.2 us (24%)
  starting transfers between devices  35.3 us (17%)
  between operations  14.3 us (7%)
  local copies, waits for them, and re-layouts  9.97 us (5%)
  other arithmetic  5.39 us (3%)
    ppermute x4, waiting for transfers between devices, swap(): return lax.ppermute(block, axis, [(0, 1), (1, 0)])  24.8 us
    pallas_call x2, Pallas kernels, gate_up(): pl.pallas_call(gate_kernel, in_specs=[pl.BlockSpec(memory_space=pltpu.SME...  12.8 us
    ppermute x1, waiting for transfers between devices, per_device(): right = lax.ppermute(mlp_in, 'y', ring(3))  11.9 us
    ppermute x1, waiting for transfers between devices, per_device(): prior = lax.ppermute(tail, REQ, [(i - 1, i) for i in range(1, 16)])  10.3 us
    all_to_all x1, waiting for transfers between devices, per_device(): ctx = lax.all_to_all(ctx, 'y', split_axis=0, concat_axis=0, tiled=True)  10.1 us
    all_to_all x1, starting transfers between devices, per_device(): lax.all_to_all(packed, ('z', 'xh'), split_axis=0, concat_axis=0, tiled=True)  7.88 us
    unnamed x20, local copies, waits for them, and re-layouts  7.85 us
    pallas_call x1, Pallas kernels, attend(): pl.pallas_call(attend_kernel, out_shape=jax.ShapeDtypeStruct((4, 2, 128,...  6.43 us
  transfers between devices with their start and end apart: 20, of which 13 were waited for; matrix products, arithmetic and copies ran while one was open for 3% of the time, Pallas kernels for 17%

profile of v5, /device:TPU:32, one launch (start us, length us, event | category | flops | bytes accessed | tf_op | source)
XLA Modules:
  0.0 207.0 jit_solution(2454315336528132453)
XLA Ops:
  7.2 2.3 %pack.1 = bf16[8,768,128]{2,1,0:T(8,128)(2,1)} custom-call(f32[128,256]{1,0:T(8,128)} %q_ref.1, f32[128,128]{1,0:T(8,128)} %k_ref.1, f32[128,128]{1,0:T(8,128)} %v_ref.1, f32[256,128]{1,0:T(8,128)} %o_ref.1), custom_call_target="tpu_custom_call" | custom-call | tf_op jit(solution)/shard_map/pack/pallas_call | solution.py:334
  9.5 7.9 %all-to-all-start = ((bf16[8,768,128]{2,1,0:T(8,128)(2,1)}), bf16[8,768,128]{2,1,0:T(8,128)(2,1)S(1)}, u32[]{:S(2)}, u32[]{:S(2)}) async-start(bf16[8,768,128]{2,1,0:T(8,128)(2,1)} %pack.1), calls=%async_computation | async-start | bytes 3145728 | tf_op jit(solution)/shard_map/all_to_all | solution.py:398
  17.4 2.3 %prep.1 = (bf16[288,256]{1,0:T(8,128)(2,1)}, bf16[288,256]{1,0:T(8,128)(2,1)}, bf16[288,256]{1,0:T(8,128)(2,1)}, bf16[288,256]{1,0:T(8,128)(2,1)}) custom-call(s32[1]{0:T(128)} %bitcast.3.y_ref, f32[256,384]{1,0:T(8,128)} %gate_ref.1, f32[256,384]{1,0:T(8,128)} %up_ref.1, f32[384,256]{1,0:T(8,128)} %down_ref.1), custom_call_target="tpu_custom_call" | custom-call | tf_op jit(solution)/shard_map/prep/pallas_call | solution.py:353
  19.7 3.0 %collective-permute-start = (bf16[288,256]{1,0:T(8,128)(2,1)}, bf16[288,256]{1,0:T(8,128)(2,1)S(1)}, u32[]{:S(2)}, u32[]{:S(2)}) collective-permute-start(bf16[288,256]{1,0:T(8,128)(2,1)} %get-tuple-element.30), channel_id=1, source_target_pairs={{0,3},{1,0},{2,1},{3,2},{4,7},{5,4},{6,5},{7,6},{8,11},{9,8},{10,9... | collective-permute-start | bytes 442376 | tf_op jit(solution)/shard_map/ppermute | solution.py:372
  22.8 0.6 collective-permute-start.1
  23.4 1.0 collective-permute-start.2
  24.4 1.9 multiply_cosine_fusion
  26.3 5.4 %norm.1.x_ref = bf16[1024,2048]{1,0:T(8,128)(2,1)} custom-call(bf16[1024,2048]{1,0:T(8,128)(2,1)} %x_ref.1, f32[1,2048]{1,0:T(1,128)} %bitcast.14), custom_call_target="tpu_custom_call" | custom-call | tf_op jit(solution)/shard_map/norm/pallas_call | solution.py:35
  31.7 0.2 pad_maximum_fusion.cs_ref
  31.9 0.5 collective-permute-done.2.p3_ref
  32.5 5.1 %all-to-all-done.own_ref = bf16[8,768,128]{2,1,0:T(8,128)(2,1)S(1)} async-done(((bf16[8,768,128]{2,1,0:T(8,128)(2,1)}), bf16[8,768,128]{2,1,0:T(8,128)(2,1)S(1)}, u32[]{:S(2)}, u32[]{:S(2)}) %all-to-all-start) | async-done | bytes 1572896 | tf_op jit(solution)/shard_map/all_to_all | solution.py:398
  37.5 2.0 join.1
  39.7 1.8 broadcast_in_dim.34
  41.5 4.5 %all-to-all-start.2 = ((bf16[4,8,256,128]{3,2,1,0:T(8,128)(2,1)}), bf16[4,8,256,128]{3,2,1,0:T(8,128)(2,1)}, u32[]{:S(2)}, u32[]{:S(2)}) async-start(bf16[4,8,256,128]{3,2,1,0:T(8,128)(2,1)} %broadcast_in_dim.34), calls=%async_computation.2 | async-start | bytes 4194304 | tf_op jit(solution)/shard_map/all_to_all | solution.py:413
  46.0 2.2 %copy-done = bf16[1024,2048]{1,0:T(8,128)(2,1)S(1)} copy-done((bf16[1024,2048]{1,0:T(8,128)(2,1)S(1)}, bf16[1024,2048]{1,0:T(8,128)(2,1)}, u32[]{:S(2)}) %copy-start) | copy-done | bytes 4194328
  48.2 6.3 %qkv.1 = (bf16[1024,256]{1,0:T(8,128)(2,1)S(1)}, bf16[2,1024,128]{2,1,0:T(8,128)(2,1)}, bf16[2,512,128]{2,1,0:T(8,128)(2,1)S(1)}) custom-call(s32[1]{0:T(128)} %bitcast.core_ref, bf16[1024,2048]{1,0:T(8,128)(2,1)S(1)} %copy-done, bf16[8,768,128]{2,1,0:T(8,128)(2,1)S(1)} %all-to-all-done.own_ref, bf16[8,768,128]{2,1,0:T(8,128)(2,1)} %collective-permute-done.3.oth_ref, ...), custom_call_target="tpu_custom_call" | custom-call | tf_op jit(solution)/shard_map/qkv/pallas_call | solution.py:87
  54.4 2.4 %collective-permute-start.4 = (bf16[2,512,128]{2,1,0:T(8,128)(2,1)S(1)}, bf16[2,512,128]{2,1,0:T(8,128)(2,1)S(1)}, u32[]{:S(2)}, u32[]{:S(2)}) collective-permute-start(bf16[2,512,128]{2,1,0:T(8,128)(2,1)S(1)} %get-tuple-element.38), channel_id=1, source_target_pairs={{0,8},{8,16},{16,24},{24,32},{32,40},{40,48},{48,56},{56,64},{64,7... | collective-permute-start | bytes 786440 | tf_op jit(solution)/shard_map/ppermute | solution.py:416
  56.8 0.2 copy.16.lo_ref
  57.1 10.3 %collective-permute-done.4.prior_ref = bf16[2,512,128]{2,1,0:T(8,128)(2,1)S(1)} collective-permute-done((bf16[2,512,128]{2,1,0:T(8,128)(2,1)S(1)}, bf16[2,512,128]{2,1,0:T(8,128)(2,1)S(1)}, u32[]{:S(2)}, u32[]{:S(2)}) %collective-permute-start.4) | collective-permute-done | bytes 262176 | tf_op jit(solution)/shard_map/ppermute | solution.py:416
  67.4 1.0 copy-done.2
  68.4 6.4 %attend.1 = bf16[4,2,128,256]{3,2,1,0:T(8,128)(2,1)} custom-call(bf16[1024,256]{1,0:T(8,128)(2,1)S(1)} %get-tuple-element.36.q_ref, bf16[2,1024,128]{2,1,0:T(8,128)(2,1)S(1)} %copy-done.2, bf16[2,512,128]{2,1,0:T(8,128)(2,1)S(1)} %collective-permute-done.4.prior_ref, s32[1024,1]{1,0:T(8,128)S(1)} %copy.16.lo_ref), custom_call_target="tpu_custom_call" | custom-call | tf_op jit(solution)/shard_map/attend/pallas_call | solution.py:151
  74.8 4.3 %all-to-all-start.1 = ((bf16[4,2,128,256]{3,2,1,0:T(8,128)(2,1)}), bf16[4,2,128,256]{3,2,1,0:T(8,128)(2,1)S(1)}, u32[]{:S(2)}, u32[]{:S(2)}) async-start(bf16[4,2,128,256]{3,2,1,0:T(8,128)(2,1)} %attend.1), calls=%async_computation.1 | async-start | bytes 1048576 | tf_op jit(solution)/shard_map/all_to_all | solution.py:420
  79.2 10.1 %all-to-all-done.1.ctx_ref = bf16[4,2,128,256]{3,2,1,0:T(8,128)(2,1)S(1)} async-done(((bf16[4,2,128,256]{3,2,1,0:T(8,128)(2,1)}), bf16[4,2,128,256]{3,2,1,0:T(8,128)(2,1)S(1)}, u32[]{:S(2)}, u32[]{:S(2)}) %all-to-all-start.1) | async-done | bytes 524320 | tf_op jit(solution)/shard_map/all_to_all | solution.py:420
  89.3 4.8 %oproj.1 = (f32[128,2048]{1,0:T(8,128)S(1)}, bf16[128,2048]{1,0:T(8,128)(2,1)S(1)}) custom-call(s32[2]{0:T(128)S(1)} %pad_add_fusion.at_ref, bf16[4,2,128,256]{3,2,1,0:T(8,128)(2,1)S(1)} %all-to-all-done.1.ctx_ref, bf16[4,8,256,128]{3,2,1,0:T(8,128)(2,1)} %all-to-all-done.2.own_ref, bf16[4,8,256,128]{3,2,1,0:T(8,128)(2,1)S(1)} %collective-permute-done.5.oth_ref), custom_call_target="tpu_custom_call" | custom-call | tf_op jit(solution)/shard_map/oproj/pallas_call | solution.py:195
  94.1 1.0 copy-done.1
  95.1 0.6 collective-permute-start.6
  95.8 24.8 %collective-permute-done.6 = bf16[128,2048]{1,0:T(8,128)(2,1)S(1)} collective-permute-done((bf16[128,2048]{1,0:T(8,128)(2,1)S(1)}, bf16[128,2048]{1,0:T(8,128)(2,1)S(1)}, u32[]{:S(2)}, u32[]{:S(2)}) %collective-permute-start.6) | collective-permute-done | bytes 524320 | tf_op jit(solution)/shard_map/ppermute | solution.py:23
  120.6 1.5 add_convert_fusion
  122.6 3.6 %all-gather.3.cloned.1.call-done = bf16[64,288,256]{2,1,0:T(8,128)(2,1)} async-done(((bf16[4,288,256]{2,1,0:T(8,128)(2,1)}), bf16[64,288,256]{2,1,0:T(8,128)(2,1)}) %all-gather.3.cloned.1.call-update) | async-done | bytes 9437200 | tf_op jit(solution)/shard_map/all_gather | solution.py:407
  126.2 2.7 %collective-permute-start.8 = (bf16[128,2048]{1,0:T(8,128)(2,1)S(1)}, bf16[128,2048]{1,0:T(8,128)(2,1)S(1)}, u32[]{:S(2)}, u32[]{:S(2)}) collective-permute-start(bf16[128,2048]{1,0:T(8,128)(2,1)S(1)} %fusion.2.x0_ref), channel_id=1, source_target_pairs={{0,3},{1,0},{2,1},{3,2},{4,7},{5,4},{6,5},{7,6},{8,11},{9,8},{10,9... | collective-permute-start | bytes 1572872 | tf_op jit(solution)/shard_map/ppermute | solution.py:433
  128.9 11.9 %collective-permute-done.8.x2_ref = bf16[128,2048]{1,0:T(8,128)(2,1)S(1)} collective-permute-done((bf16[128,2048]{1,0:T(8,128)(2,1)S(1)}, bf16[128,2048]{1,0:T(8,128)(2,1)S(1)}, u32[]{:S(2)}, u32[]{:S(2)}) %collective-permute-start.8) | collective-permute-done | bytes 524320 | tf_op jit(solution)/shard_map/ppermute | solution.py:433
  140.8 3.8 %collective-permute-start.10 = (bf16[64,2048]{1,0:T(8,128)(2,1)S(1)}, bf16[64,2048]{1,0:T(8,128)(2,1)S(1)}, u32[]{:S(2)}, u32[]{:S(2)}) collective-permute-start(bf16[64,2048]{1,0:T(8,128)(2,1)S(1)} %slice.29), channel_id=1, source_target_pairs={{0,3},{1,0},{2,1},{3,2},{4,7},{5,4},{6,5},{7,6},{8,11},{9,8},{10,9... | collective-permute-start | bytes 786440 | tf_op jit(solution)/shard_map/ppermute | solution.py:435
  144.7 5.3 %collective-permute-done.10.x4_ref = bf16[64,2048]{1,0:T(8,128)(2,1)S(1)} collective-permute-done((bf16[64,2048]{1,0:T(8,128)(2,1)S(1)}, bf16[64,2048]{1,0:T(8,128)(2,1)S(1)}, u32[]{:S(2)}, u32[]{:S(2)}) %collective-permute-start.10) | collective-permute-done | bytes 262176 | tf_op jit(solution)/shard_map/ppermute | solution.py:435
  150.0 3.5 %collective-permute-done.9.x3_ref = bf16[64,2048]{1,0:T(8,128)(2,1)S(1)} collective-permute-done((bf16[64,2048]{1,0:T(8,128)(2,1)S(1)}, bf16[64,2048]{1,0:T(8,128)(2,1)S(1)}, u32[]{:S(2)}, u32[]{:S(2)}) %collective-permute-start.9) | collective-permute-done | bytes 262176 | tf_op jit(solution)/shard_map/ppermute | solution.py:434
  153.5 6.4 %gate_up.2.hid0_ref = bf16[512,768]{1,0:T(8,128)(2,1)S(1)} custom-call(s32[1]{0:T(128)} %bitcast.3.y_ref, bf16[128,2048]{1,0:T(8,128)(2,1)S(1)} %fusion.2.x0_ref, bf16[128,2048]{1,0:T(8,128)(2,1)S(1)} %collective-permute-done.7.x1_ref, bf16[128,2048]{1,0:T(8,128)(2,1)S(1)} %collective-permute-done.8.x2_ref, ...), custom_call_target="tpu_custom_call" | custom-call | tf_op jit(solution)/shard_map/gate_up/pallas_call | solution.py:288
  159.9 3.6 %copy-done.5 = bf16[8,2,4,288,256]{4,3,2,1,0:T(8,128)(2,1)} copy-done((bf16[8,2,4,288,256]{4,3,2,1,0:T(8,128)(2,1)}, bf16[8,2,4,288,256]{4,3,2,1,0:T(8,128)(2,1)S(1)}, u32[]{:S(2)}) %copy-start.5) | copy-done | bytes 9437208
  163.6 6.4 %gate_up.3.hid1_ref = bf16[512,768]{1,0:T(8,128)(2,1)S(1)} custom-call(s32[1]{0:T(128)} %bitcast.3.y_ref, bf16[128,2048]{1,0:T(8,128)(2,1)S(1)} %fusion.2.x0_ref, bf16[128,2048]{1,0:T(8,128)(2,1)S(1)} %collective-permute-done.7.x1_ref, bf16[128,2048]{1,0:T(8,128)(2,1)S(1)} %collective-permute-done.8.x2_ref, ...), custom_call_target="tpu_custom_call" | custom-call | tf_op jit(solution)/shard_map/gate_up/pallas_call | solution.py:288
  170.0 4.6 %down_far.1 = (bf16[64,2048]{1,0:T(8,128)(2,1)S(1)}, bf16[64,2048]{1,0:T(8,128)(2,1)S(1)}, bf16[1,16,96,2048]{3,2,1,0:T(8,128)(2,1)S(1)}) custom-call(s32[1]{0:T(128)} %bitcast.3.y_ref, bf16[512,768]{1,0:T(8,128)(2,1)S(1)} %gate_up.2.hid0_ref, bf16[512,768]{1,0:T(8,128)(2,1)S(1)} %gate_up.3.hid1_ref, bf16[8,2,4,288,256]{4,3,2,1,0:T(8,128)(2,1)} %bitcast.12, ...), custom_call_target="tpu_custom_call" | custom-call | tf_op jit(solution)/shard_map/down_far/pallas_call | solution.py:306
  174.5 0.3 collective-permute-start.14
  174.8 3.2 %down.1 = (f32[128,2048]{1,0:T(8,128)S(1)}, bf16[128,2048]{1,0:T(8,128)(2,1)S(1)}, bf16[128,2048]{1,0:T(8,128)(2,1)S(1)}) custom-call(bf16[512,768]{1,0:T(8,128)(2,1)S(1)} %gate_up.2.hid0_ref, bf16[512,768]{1,0:T(8,128)(2,1)S(1)} %gate_up.3.hid1_ref, bf16[1,16,96,2048]{3,2,1,0:T(8,128)(2,1)S(1)} %get-tuple-element.50.w_ref), custom_call_target="tpu_custom_call" | custom-call | tf_op jit(solution)/shard_map/down/pallas_call | solution.py:318
  178.1 1.9 collective-permute-start.12
  180.0 1.4 collective-permute-done.14
  181.5 1.8 collective-permute-start.15
  183.3 2.9 %collective-permute-done.12 = bf16[64,2048]{1,0:T(8,128)(2,1)S(1)} collective-permute-done((bf16[64,2048]{1,0:T(8,128)(2,1)S(1)}, bf16[64,2048]{1,0:T(8,128)(2,1)S(1)}, u32[]{:S(2)}, u32[]{:S(2)}) %collective-permute-start.12) | collective-permute-done | bytes 262176 | tf_op jit(solution)/shard_map/ppermute | solution.py:443
  186.3 0.4 collective-permute-start.13
  186.6 6.4 %collective-permute-done.15 = bf16[128,2048]{1,0:T(8,128)(2,1)S(1)} collective-permute-done((bf16[128,2048]{1,0:T(8,128)(2,1)S(1)}, bf16[128,2048]{1,0:T(8,128)(2,1)S(1)}, u32[]{:S(2)}, u32[]{:S(2)}) %collective-permute-start.15) | collective-permute-done | bytes 524320 | tf_op jit(solution)/shard_map/ppermute | solution.py:449
  193.0 6.1 %collective-permute-done.13 = bf16[128,2048]{1,0:T(8,128)(2,1)S(1)} collective-permute-done((bf16[128,2048]{1,0:T(8,128)(2,1)S(1)}, bf16[128,2048]{1,0:T(8,128)(2,1)S(1)}, u32[]{:S(2)}, u32[]{:S(2)}) %collective-permute-start.13) | collective-permute-done | bytes 524320 | tf_op jit(solution)/shard_map/ppermute | solution.py:448
  199.0 1.1 fusion.3
  (45 shorter events, 1.0 us)
Async XLA Ops:
  7.2 17.2 %copy-start.9 = (s32[1024]{0:T(1024)S(1)}, s32[1024]{0:T(1024)}, u32[]{:S(2)}) copy-start(s32[1024]{0:T(1024)} %param.15) | copy-start | bytes 12292
  9.5 28.0 %all-to-all-start = ((bf16[8,768,128]{2,1,0:T(8,128)(2,1)}), bf16[8,768,128]{2,1,0:T(8,128)(2,1)S(1)}, u32[]{:S(2)}, u32[]{:S(2)}) async-start(bf16[8,768,128]{2,1,0:T(8,128)(2,1)} %pack.1), calls=%async_computation | async-start | bytes 3145728 | tf_op jit(solution)/shard_map/all_to_all | solution.py:398
  17.4 108.8 %all-gather.3.cloned.1.call-start = ((), (), s32[]{:S(2)}) async-start(), calls=%async_computation.3 | async-start | bytes 10027008 | tf_op jit(solution)/shard_map/all_gather | solution.py:407
  19.7 12.2 %collective-permute-start = (bf16[288,256]{1,0:T(8,128)(2,1)}, bf16[288,256]{1,0:T(8,128)(2,1)S(1)}, u32[]{:S(2)}, u32[]{:S(2)}) collective-permute-start(bf16[288,256]{1,0:T(8,128)(2,1)} %get-tuple-element.30), channel_id=1, source_target_pairs={{0,3},{1,0},{2,1},{3,2},{4,7},{5,4},{6,5},{7,6},{8,11},{9,8},{10,9... | collective-permute-start | bytes 442376 | tf_op jit(solution)/shard_map/ppermute | solution.py:372
  22.8 9.2 %collective-permute-start.1 = (bf16[288,256]{1,0:T(8,128)(2,1)}, bf16[288,256]{1,0:T(8,128)(2,1)S(1)}, u32[]{:S(2)}, u32[]{:S(2)}) collective-permute-start(bf16[288,256]{1,0:T(8,128)(2,1)} %get-tuple-element.31), channel_id=1, source_target_pairs={{0,2},{1,3},{2,0},{3,1},{4,6},{5,7},{6,4},{7,5},{8,10},{9,11},{10,... | collective-permute-start | bytes 442376 | tf_op jit(solution)/shard_map/ppermute | solution.py:372
  23.4 9.1 %collective-permute-start.2 = (bf16[288,256]{1,0:T(8,128)(2,1)}, bf16[288,256]{1,0:T(8,128)(2,1)}, u32[]{:S(2)}, u32[]{:S(2)}) collective-permute-start(bf16[288,256]{1,0:T(8,128)(2,1)} %get-tuple-element.32), channel_id=1, source_target_pairs={{0,1},{1,2},{2,3},{3,0},{4,5},{5,6},{6,7},{7,4},{8,9},{9,10},{10,1... | collective-permute-start | bytes 442376 | tf_op jit(solution)/shard_map/ppermute | solution.py:372
  31.9 5.6 %copy-start.6 = (bf16[288,256]{1,0:T(8,128)(2,1)}, bf16[288,256]{1,0:T(8,128)(2,1)S(1)}, u32[]{:S(2)}) copy-start(bf16[288,256]{1,0:T(8,128)(2,1)S(1)} %collective-permute-done.p1_ref) | copy-start | bytes 442372
  31.9 5.6 %copy-start.7 = (bf16[288,256]{1,0:T(8,128)(2,1)}, bf16[288,256]{1,0:T(8,128)(2,1)S(1)}, u32[]{:S(2)}) copy-start(bf16[288,256]{1,0:T(8,128)(2,1)S(1)} %collective-permute-done.1.p2_ref) | copy-start | bytes 442372
  39.5 6.4 %copy-start.3 = (f32[128]{0:T(128)S(1)}, f32[128]{0:T(128)}, u32[]{:S(2)}) copy-start(f32[128]{0:T(128)} %param.18) | copy-start | bytes 1540
  39.6 6.4 %copy-start.4 = (f32[128]{0:T(128)S(1)}, f32[128]{0:T(128)}, u32[]{:S(2)}) copy-start(f32[128]{0:T(128)} %param.19) | copy-start | bytes 1540
  39.6 6.4 %collective-permute-start.3 = (bf16[8,768,128]{2,1,0:T(8,128)(2,1)S(1)}, bf16[8,768,128]{2,1,0:T(8,128)(2,1)}, u32[]{:S(2)}, u32[]{:S(2)}) collective-permute-start(bf16[8,768,128]{2,1,0:T(8,128)(2,1)S(1)} %all-to-all-done.own_ref), channel_id=1, source_target_pairs={{0,8},{8,0},{1,9},{9,1},{2,10},{10,2},{3,11},{11,3},{4,12},{12,4},... | collective-permute-start | bytes 4718600 | tf_op jit(solution)/shard_map/ppermute | solution.py:23
  41.5 33.3 %all-to-all-start.2 = ((bf16[4,8,256,128]{3,2,1,0:T(8,128)(2,1)}), bf16[4,8,256,128]{3,2,1,0:T(8,128)(2,1)}, u32[]{:S(2)}, u32[]{:S(2)}) async-start(bf16[4,8,256,128]{3,2,1,0:T(8,128)(2,1)} %broadcast_in_dim.34), calls=%async_computation.2 | async-start | bytes 4194304 | tf_op jit(solution)/shard_map/all_to_all | solution.py:413
  46.0 2.2 %copy-start = (bf16[1024,2048]{1,0:T(8,128)(2,1)S(1)}, bf16[1024,2048]{1,0:T(8,128)(2,1)}, u32[]{:S(2)}) copy-start(bf16[1024,2048]{1,0:T(8,128)(2,1)} %norm.1.x_ref) | copy-start | bytes 12582916
  54.4 12.9 %collective-permute-start.4 = (bf16[2,512,128]{2,1,0:T(8,128)(2,1)S(1)}, bf16[2,512,128]{2,1,0:T(8,128)(2,1)S(1)}, u32[]{:S(2)}, u32[]{:S(2)}) collective-permute-start(bf16[2,512,128]{2,1,0:T(8,128)(2,1)S(1)} %get-tuple-element.38), channel_id=1, source_target_pairs={{0,8},{8,16},{16,24},{24,32},{32,40},{40,48},{48,56},{56,64},{64,7... | collective-permute-start | bytes 786440 | tf_op jit(solution)/shard_map/ppermute | solution.py:416
  67.4 1.0 copy-start.2
  74.8 14.4 %collective-permute-start.5 = (bf16[4,8,256,128]{3,2,1,0:T(8,128)(2,1)}, bf16[4,8,256,128]{3,2,1,0:T(8,128)(2,1)S(1)}, u32[]{:S(2)}, u32[]{:S(2)}) collective-permute-start(bf16[4,8,256,128]{3,2,1,0:T(8,128)(2,1)} %all-to-all-done.2.own_ref), channel_id=1, source_target_pairs={{0,8},{8,0},{1,9},{9,1},{2,10},{10,2},{3,11},{11,3},{4,12},{12,4},... | collective-permute-start | bytes 6291464 | tf_op jit(solution)/shard_map/ppermute | solution.py:23
  74.8 14.4 %all-to-all-start.1 = ((bf16[4,2,128,256]{3,2,1,0:T(8,128)(2,1)}), bf16[4,2,128,256]{3,2,1,0:T(8,128)(2,1)S(1)}, u32[]{:S(2)}, u32[]{:S(2)}) async-start(bf16[4,2,128,256]{3,2,1,0:T(8,128)(2,1)} %attend.1), calls=%async_computation.1 | async-start | bytes 1048576 | tf_op jit(solution)/shard_map/all_to_all | solution.py:420
  79.1 43.2 %copy-start.8 = (f32[2048]{0:T(1024)S(1)}, f32[2048]{0:T(1024)}, u32[]{:S(2)}) copy-start(f32[2048]{0:T(1024)} %param.17) | copy-start | bytes 24580
  94.1 1.0 copy-start.1
  95.1 25.5 %collective-permute-start.6 = (bf16[128,2048]{1,0:T(8,128)(2,1)S(1)}, bf16[128,2048]{1,0:T(8,128)(2,1)S(1)}, u32[]{:S(2)}, u32[]{:S(2)}) collective-permute-start(bf16[128,2048]{1,0:T(8,128)(2,1)S(1)} %get-tuple-element.41), channel_id=1, source_target_pairs={{0,4},{4,0},{1,5},{5,1},{2,6},{6,2},{3,7},{7,3},{8,12},{12,8},{9,1... | collective-permute-start | bytes 1572872 | tf_op jit(solution)/shard_map/ppermute | solution.py:23
  126.2 33.7 %collective-permute-start.11 = (bf16[8,2,4,288,256]{4,3,2,1,0:T(8,128)(2,1)}, bf16[8,2,4,288,256]{4,3,2,1,0:T(8,128)(2,1)S(1)}, u32[]{:S(2)}, u32[]{:S(2)}) collective-permute-start(bf16[8,2,4,288,256]{4,3,2,1,0:T(8,128)(2,1)} %bitcast.10), channel_id=1, source_target_pairs={{0,8},{8,0},{1,9},{9,1},{2,10},{10,2},{3,11},{11,3},{4,12},{12,4},... | collective-permute-start | bytes 28311560 | tf_op jit(solution)/shard_map/ppermute | solution.py:23
  126.2 14.6 %collective-permute-start.8 = (bf16[128,2048]{1,0:T(8,128)(2,1)S(1)}, bf16[128,2048]{1,0:T(8,128)(2,1)S(1)}, u32[]{:S(2)}, u32[]{:S(2)}) collective-permute-start(bf16[128,2048]{1,0:T(8,128)(2,1)S(1)} %fusion.2.x0_ref), channel_id=1, source_target_pairs={{0,3},{1,0},{2,1},{3,2},{4,7},{5,4},{6,5},{7,6},{8,11},{9,8},{10,9... | collective-permute-start | bytes 1572872 | tf_op jit(solution)/shard_map/ppermute | solution.py:433
  128.9 15.6 %collective-permute-start.7 = (bf16[128,2048]{1,0:T(8,128)(2,1)S(1)}, bf16[128,2048]{1,0:T(8,128)(2,1)S(1)}, u32[]{:S(2)}, u32[]{:S(2)}) collective-permute-start(bf16[128,2048]{1,0:T(8,128)(2,1)S(1)} %fusion.2.x0_ref), channel_id=1, source_target_pairs={{0,1},{1,2},{2,3},{3,0},{4,5},{5,6},{6,7},{7,4},{8,9},{9,10},{10,1... | collective-permute-start | bytes 1572872 | tf_op jit(solution)/shard_map/ppermute | solution.py:432
  140.8 9.2 %collective-permute-start.10 = (bf16[64,2048]{1,0:T(8,128)(2,1)S(1)}, bf16[64,2048]{1,0:T(8,128)(2,1)S(1)}, u32[]{:S(2)}, u32[]{:S(2)}) collective-permute-start(bf16[64,2048]{1,0:T(8,128)(2,1)S(1)} %slice.29), channel_id=1, source_target_pairs={{0,3},{1,0},{2,1},{3,2},{4,7},{5,4},{6,5},{7,6},{8,11},{9,8},{10,9... | collective-permute-start | bytes 786440 | tf_op jit(solution)/shard_map/ppermute | solution.py:435
  144.6 8.9 %collective-permute-start.9 = (bf16[64,2048]{1,0:T(8,128)(2,1)S(1)}, bf16[64,2048]{1,0:T(8,128)(2,1)S(1)}, u32[]{:S(2)}, u32[]{:S(2)}) collective-permute-start(bf16[64,2048]{1,0:T(8,128)(2,1)S(1)} %slice.28), channel_id=1, source_target_pairs={{0,1},{1,2},{2,3},{3,0},{4,5},{5,6},{6,7},{7,4},{8,9},{9,10},{10,1... | collective-permute-start | bytes 786440 | tf_op jit(solution)/shard_map/ppermute | solution.py:434
  159.9 3.6 %copy-start.5 = (bf16[8,2,4,288,256]{4,3,2,1,0:T(8,128)(2,1)}, bf16[8,2,4,288,256]{4,3,2,1,0:T(8,128)(2,1)S(1)}, u32[]{:S(2)}) copy-start(bf16[8,2,4,288,256]{4,3,2,1,0:T(8,128)(2,1)S(1)} %collective-permute-done.11.src_ref.oth_ref) | copy-start | bytes 28311556
  174.5 6.8 %collective-permute-start.14 = (bf16[64,2048]{1,0:T(8,128)(2,1)S(1)}, bf16[64,2048]{1,0:T(8,128)(2,1)S(1)}, u32[]{:S(2)}, u32[]{:S(2)}) collective-permute-start(bf16[64,2048]{1,0:T(8,128)(2,1)S(1)} %get-tuple-element.55), channel_id=1, source_target_pairs={{0,3},{1,0},{2,1},{3,2},{4,7},{5,4},{6,5},{7,6},{8,11},{9,8},{10,9... | collective-permute-start | bytes 786440 | tf_op jit(solution)/shard_map/ppermute | solution.py:444
  178.1 8.1 %collective-permute-start.12 = (bf16[64,2048]{1,0:T(8,128)(2,1)S(1)}, bf16[64,2048]{1,0:T(8,128)(2,1)S(1)}, u32[]{:S(2)}, u32[]{:S(2)}) collective-permute-start(bf16[64,2048]{1,0:T(8,128)(2,1)S(1)} %get-tuple-element.53), channel_id=1, source_target_pairs={{0,1},{1,2},{2,3},{3,0},{4,5},{5,6},{6,7},{7,4},{8,9},{9,10},{10,1... | collective-permute-start | bytes 786440 | tf_op jit(solution)/shard_map/ppermute | solution.py:443
  181.5 11.5 %collective-permute-start.15 = (bf16[128,2048]{1,0:T(8,128)(2,1)S(1)}, bf16[128,2048]{1,0:T(8,128)(2,1)S(1)}, u32[]{:S(2)}, u32[]{:S(2)}) collective-permute-start(bf16[128,2048]{1,0:T(8,128)(2,1)S(1)} %pad_maximum_fusion.2), channel_id=1, source_target_pairs={{0,3},{1,0},{2,1},{3,2},{4,7},{5,4},{6,5},{7,6},{8,11},{9,8},{10,9... | collective-permute-start | bytes 1572872 | tf_op jit(solution)/shard_map/ppermute | solution.py:449
  186.3 12.8 %collective-permute-start.13 = (bf16[128,2048]{1,0:T(8,128)(2,1)S(1)}, bf16[128,2048]{1,0:T(8,128)(2,1)S(1)}, u32[]{:S(2)}, u32[]{:S(2)}) collective-permute-start(bf16[128,2048]{1,0:T(8,128)(2,1)S(1)} %pad_maximum_fusion.1), channel_id=1, source_target_pairs={{0,1},{1,2},{2,3},{3,0},{4,5},{5,6},{6,7},{7,4},{8,9},{9,10},{10,1... | collective-permute-start | bytes 1572872 | tf_op jit(solution)/shard_map/ppermute | solution.py:448
Sparse Core Ops, SparseCore 0:
  39.7 86.4 all-gather.2

commit v6 on v4

--- a/solution.py
+++ b/solution.py
@@ -23,7 +23,26 @@
     return lax.ppermute(block, axis, [(0, 1), (1, 0)])
 
 
-def qkv_kernel(core_ref, x_ref, own_ref, oth_ref, gain_ref, qg_ref, kg_ref, cs_ref, q_ref, kv_ref, tail_ref, w_ref):
+def norm_kernel(x_ref, gain_ref, out_ref):
+    x = x_ref[...].astype(F32)
+    scale = lax.rsqrt(jnp.mean(x * x, axis=-1, keepdims=True) + 1e-06)
+    out_ref[...] = (x * scale * gain_ref[...]).astype(BF)
+
+
+def normalise(x, gain):
+    rows, tile = x.shape[0], min(256, x.shape[0])
+    block = pl.BlockSpec((tile, 2048), lambda i: (i, 0))
+    return pl.pallas_call(
+        norm_kernel,
+        grid=(rows // tile,),
+        in_specs=[block, pl.BlockSpec((1, 2048), lambda i: (0, 0))],
+        out_specs=block,
+        out_shape=jax.ShapeDtypeStruct(x.shape, BF),
+        name="norm",
+    )(x, gain[None])
+
+
+def qkv_kernel(core_ref, x_ref, own_ref, oth_ref, qg_ref, kg_ref, cs_ref, q_ref, kv_ref, tail_ref, w_ref):
     core = core_ref[0]
 
     @pl.when(pl.program_id(0) == 0)
@@ -37,10 +56,7 @@
 
         lax.fori_loop(0, 8, place, 0)
 
-    x = x_ref[...].astype(F32)
-    scale = lax.rsqrt(jnp.mean(x * x, axis=-1, keepdims=True) + 1e-06)
-    normed = (x * scale * gain_ref[...]).astype(BF)
-    raw = jnp.dot(normed, w_ref[...], preferred_element_type=F32)
+    raw = jnp.dot(x_ref[...], w_ref[...], preferred_element_type=F32)
     cs = cs_ref[...]
     turned = pltpu.roll(cs, 64, 1)
     low = lax.broadcasted_iota(jnp.int32, cs.shape, 1) < 64
@@ -64,8 +80,8 @@
         tail_ref[1] = values
 
 
-def project(core, tokens, own, oth, attn_gain, q_gain, key_gain, cs):
-    rows = tokens.shape[0]
+def project(core, normed, own, oth, q_gain, key_gain, cs):
+    rows = normed.shape[0]
     tile = 256
     fixed = lambda *shape: pl.BlockSpec(shape, lambda i, c: (0,) * len(shape))
     return pl.pallas_call(
@@ -77,7 +93,6 @@
                 pl.BlockSpec((tile, 2048), lambda i, c: (i, 0)),
                 fixed(8, 512, 128),
                 fixed(8, 512, 128),
-                fixed(1, 2048),
                 fixed(1, 128),
                 fixed(1, 128),
                 pl.BlockSpec((tile, 128), lambda i, c: (i, 0)),
@@ -96,13 +111,14 @@
         ),
         compiler_params=pltpu.CompilerParams(vmem_limit_bytes=40 << 20),
         name="qkv",
-    )(core, tokens, own, oth, attn_gain[None], q_gain[None], key_gain[None], cs)
-
-
-def attend_kernel(q_ref, kv_ref, prior_ref, lo_ref, out_ref):
+    )(core, normed, own, oth, q_gain[None], key_gain[None], cs)
+
+
+def attend_kernel(half_ref, q_ref, kv_ref, prior_ref, lo_ref, out_ref):
     factor = HEAD ** (-0.5) * math.log2(math.e)
     nt = (((1,), (1,)), ((), ()))
-    for i in range(4):
+
+    def block(i):
         first = i * 256
         skip = 256 if i == 3 else 0
         count = first + 256
@@ -112,8 +128,10 @@
         near = (col >= lo) & (col <= row)
         prior_col = lax.broadcasted_iota(jnp.int32, (256, 512 - skip), 1) + (skip - 512)
         far = prior_col >= lo
-        for h in range(2):
-            q = q_ref[first : first + 256, h * 128 : h * 128 + 128]
+
+        def head(h, carry):
+            lanes = pl.ds(pl.multiple_of(h * 128, 128), 128)
+            q = q_ref[first : first + 256, lanes]
             s1 = lax.dot_general(q, kv_ref[0, :count], nt, preferred_element_type=F32)
             s0 = lax.dot_general(q, prior_ref[0, skip:], nt, preferred_element_type=F32)
             s1 = jnp.where(near, s1, -1e30)
@@ -128,70 +146,97 @@
             o = o + jnp.dot(p0, prior_ref[1, skip:], preferred_element_type=F32)
             o = o.astype(BF)
             for part in range(2):
-                block = 2 * i + part
-                out_ref[block % 4, block // 4, :, h * 128 : h * 128 + 128] = o[part * 128 : part * 128 + 128]
-
-
-def attend(q, kv, prior, lo):
+                out_ref[(2 * i + part) % 4, :, lanes] = o[part * 128 : part * 128 + 128]
+            return carry
+
+        lax.fori_loop(0, 2, head, 0)
+
+    @pl.when(half_ref[0] == 0)
+    def _():
+        block(0)
+        block(1)
+
+    @pl.when(half_ref[0] == 1)
+    def _():
+        block(2)
+        block(3)
+
+
+def attend(half, q, kv, prior, lo):
+    vm = pl.BlockSpec(memory_space=pltpu.VMEM)
     return pl.pallas_call(
         attend_kernel,
-        out_shape=jax.ShapeDtypeStruct((4, 2, 128, 256), BF),
+        in_specs=[pl.BlockSpec(memory_space=pltpu.SMEM)] + [vm] * 4,
+        out_shape=jax.ShapeDtypeStruct((4, 128, 256), BF),
         compiler_params=pltpu.CompilerParams(vmem_limit_bytes=40 << 20),
         name="attend",
-    )(q, kv, prior, lo)
-
-
-def out_kernel(at_ref, ctx_ref, own_ref, oth_ref, keep_ref, send_ref, w_ref, x_ref, sems):
-    core = at_ref[0]
-    xl = at_ref[1]
-
-    def each(act):
-        def step(n, carry):
-            s, i = n // 8, lax.rem(n, 8)
-            for which, (src, side) in enumerate(((own_ref, core), (oth_ref, 1 - core))):
-                at = pl.ds(pl.multiple_of((2 * i + side) * 128, 128), 128)
-                act(pltpu.make_async_copy(
-                    src.at[s, i], w_ref.at[pl.ds(pl.multiple_of(s * 256, 256), 256), at], sems.at[which, s, i]
-                ))
-            return carry
-
-        lax.fori_loop(0, 32, step, 0)
-
-    each(lambda c: c.start())
-    for s in range(4):
-        x_ref[:128, s * 256 : s * 256 + 256] = ctx_ref[s, xl]
-        x_ref[128:, s * 256 : s * 256 + 256] = ctx_ref[s, 1 - xl]
-    each(lambda c: c.wait())
-    x = x_ref[...]
+    )(half, q, kv, prior, lo)
+
+
+def out_columns(y, ctx_ref, w_ref, out_ref):
+    x = jnp.concatenate([ctx_ref[lax.rem(y + k, 4)] for k in range(4)], axis=1)
 
     def column(n, carry):
         at = pl.ds(pl.multiple_of(n * 512, 512), 512)
-        total = jnp.dot(x, w_ref[:, at], preferred_element_type=F32)
-        keep_ref[:, at] = total[:128]
-        send_ref[:, at] = total[128:].astype(BF)
+        out_ref[:, at] = jnp.dot(x, w_ref[:, at], preferred_element_type=F32).astype(out_ref.dtype)
         return carry
 
     lax.fori_loop(0, 4, column, 0)
 
 
-def out_project(at, ctx, own, oth):
+def out_first_kernel(at_ref, ctx_ref, *refs):
+    pieces, (send_ref, w_ref, sems) = refs[:10], refs[10:]
+    core = at_ref[0]
+
+    def each(act):
+        for n, (s, first, count, offset) in enumerate(
+            ((0, 0, 8, 512), (1, 0, 8, 0), (2, 0, 4, 0), (2, 4, 4, 0), (3, 0, 8, 0))
+        ):
+            def step(i, carry, n=n, s=s, first=first, offset=offset):
+                for side in range(2):
+                    column = 2 * (first + i) + (core if side == 0 else 1 - core)
+                    act(pltpu.make_async_copy(
+                        pieces[2 * n + side].at[i, offset : offset + 256],
+                        w_ref.at[s * 256 : s * 256 + 256, pl.ds(pl.multiple_of(column * 128, 128), 128)],
+                        sems.at[side, s, first + i],
+                    ))
+                return carry
+
+            lax.fori_loop(0, count, step, 0)
+
+    each(lambda c: c.start())
+    each(lambda c: c.wait())
+    out_columns(at_ref[1], ctx_ref, w_ref, send_ref)
+
+
+def out_second_kernel(at_ref, ctx_ref, w_ref, keep_ref):
+    out_columns(at_ref[1], ctx_ref, w_ref, keep_ref)
+
+
+def out_first(at, ctx, pieces):
+    return pl.pallas_call(
+        out_first_kernel,
+        in_specs=[
+            pl.BlockSpec(memory_space=pltpu.SMEM),
+            pl.BlockSpec(memory_space=pltpu.VMEM),
+            *[pl.BlockSpec(memory_space=pl.ANY)] * 10,
+        ],
+        out_shape=(jax.ShapeDtypeStruct((128, 2048), BF), jax.ShapeDtypeStruct((1024, 2048), BF)),
+        scratch_shapes=[pltpu.SemaphoreType.DMA((2, 4, 8))],
+        compiler_params=pltpu.CompilerParams(vmem_limit_bytes=40 << 20),
+        name="out_first",
+    )(at, ctx, *pieces)
+
+
+def out_second(at, ctx, weight):
     vm = pl.BlockSpec(memory_space=pltpu.VMEM)
-    anywhere = pl.BlockSpec(memory_space=pl.ANY)
-    return pl.pallas_call(
-        out_kernel,
-        in_specs=[pl.BlockSpec(memory_space=pltpu.SMEM)] + [vm] + [anywhere] * 2,
-        out_shape=(
-            jax.ShapeDtypeStruct((128, 2048), F32),
-            jax.ShapeDtypeStruct((128, 2048), BF),
-        ),
-        scratch_shapes=[
-            pltpu.VMEM((1024, 2048), BF),
-            pltpu.VMEM((256, 1024), BF),
-            pltpu.SemaphoreType.DMA((2, 4, 8)),
-        ],
-        compiler_params=pltpu.CompilerParams(vmem_limit_bytes=40 << 20),
-        name="oproj",
-    )(at, ctx, own, oth)
+    return pl.pallas_call(
+        out_second_kernel,
+        in_specs=[pl.BlockSpec(memory_space=pltpu.SMEM), vm, vm],
+        out_shape=jax.ShapeDtypeStruct((128, 2048), F32),
+        compiler_params=pltpu.CompilerParams(vmem_limit_bytes=40 << 20),
+        name="out_second",
+    )(at, ctx, weight)
 
 
 def fetcher(own_ref, oth_ref, w_ref, sems, y, first):
@@ -391,23 +436,31 @@
     freq = jnp.exp(jnp.arange(half, dtype=F32) * (-2.0 * math.log(1000000.0) / HEAD))
     angle = positions.astype(F32)[:, None] * freq[None, :]
     cs = jnp.concatenate([jnp.cos(angle), jnp.sin(angle)], axis=1)
-    cs, at_own, *parts = hold((cs, at_own, *parts))
+    normed = normalise(tokens, attn_gain)
+    cs, normed, at_own, *parts = hold((cs, normed, at_own, *parts))
     mlp_own = lax.all_gather(join(parts), ("z", "xh", "xl"), axis=0, tiled=False).reshape(8, 2, 4, 288, 256)
     lo = (jnp.arange(rows, dtype=jnp.int32) - positions)[:, None]
 
     at_oth = swap(at_own, "core")
 
-    o_wide = jnp.broadcast_to(at_own[None, :, 512:], (4, 8, 256, 128))
-    o_own = lax.all_to_all(o_wide, "y", split_axis=0, concat_axis=0, tiled=True)
-
-    q, cache, tail = project(core[None], tokens, at_own, at_oth, attn_gain, q_gain, key_norm_gain, cs)
+    o_here = at_own[:, 512:]
+    o_up = lax.ppermute(o_here, "y", ring(3))
+    o_down = lax.ppermute(o_here, "y", ring(1))
+    q, cache, tail = project(core[None], normed, at_own, at_oth, q_gain, key_norm_gain, cs)
     prior = lax.ppermute(tail, REQ, [(i - 1, i) for i in range(1, 16)])
-    ctx = attend(q, cache, prior, lo)
-    ctx, o_own = hold((ctx, o_own))
-    o_oth = swap(o_own, "core")
-    ctx = lax.all_to_all(ctx, "y", split_axis=0, concat_axis=0, tiled=True)
-    keep, send = out_project(jnp.stack([core, xl]), ctx, o_own, o_oth)
+    _, o_up, o_down = hold((prior, o_up, o_down))
+    o_far = [lax.ppermute(o_up[:4], "y", ring(3)), lax.ppermute(o_down[4:], "y", ring(1))]
+    turn = lambda part: lax.all_to_all(part, "y", split_axis=0, concat_axis=0, tiled=True)
+    at = jnp.stack([core, y])
+    theirs = attend(1 - xl[None], q, cache, prior, lo)
+    _, q, *rest = hold((theirs, q, o_up, *o_far, o_down))
+    pieces = [at_own, at_oth]
+    for piece in rest:
+        pieces += [piece, swap(piece, "core")]
+    mine = attend(xl[None], q, cache, prior, lo)
+    send, o_whole = out_first(at, turn(theirs), pieces)
     got = swap(send, "xl")
+    keep = out_second(at, turn(mine), o_whole)
 
     own_rows = lax.dynamic_slice_in_dim(tokens, (xl * 4 + y) * 128, 128, 0).astype(F32)
     resid = (own_rows + (keep + got.astype(F32))).astype(BF)
@@ -421,6 +474,7 @@
     mlp_oth = swap(mlp_own, "core")
     far_top = lax.ppermute(left[:64], "y", ring(1))
     far_bottom = lax.ppermute(right[64:], "y", ring(3))
+    mlp_own = pltpu.with_memory_space_constraint(mlp_own, pltpu.HBM)
     hidden = gate_up(y[None], (mlp_in, left, right, far_top, far_bottom), mlp_own, mlp_oth)
     top, bottom, weight = down_far(y[None], hidden, mlp_own, mlp_oth)
     via_left = lax.ppermute(top, "y", ring(1))

time: 206 us -> 219 us (1.063)
  waiting for transfers between devices: 100 us -> 81.5 us
  local copies, waits for them, and re-layouts: 10.1 us -> 23 us
  Pallas kernels: 41.4 us -> 54.2 us
  starting transfers between devices: 33.3 us -> 38.8 us
    ppermute x4 -> x7, waiting for transfers between devices: 29.8 us -> 8.64 us  [swap(): return lax.ppermute(block, axis, [(0, 1), (1, 0)])]
    pallas_call x2 -> x5, Pallas kernels: 11.3 us -> 21.3 us  [the longest x2 8.01 us: attend(): pl.pallas_call(attend_kernel, in_specs=[pl.BlockSpec(memory_space=pltpu.S...]
    unnamed x24 -> x44, local copies, waits for them, and re-layouts: 7.91 us -> 17.7 us
    ppermute x0 -> x4, starting transfers between devices: none -> 6.47 us  [the longest x1 1.75 us: per_device(): lax.ppermute(o_up[:4], 'y', ring(3))]
    ppermute x3, waiting for transfers between devices: 5.89 us -> 0.01 us  [trade(): lax.ppermute(parts[4 - k], 'y', ring(4 - k))]
    pallas_call x1, Pallas kernels: 8.55 us -> 13.4 us  [gate_up(): pl.pallas_call(gate_kernel, in_specs=[pl.BlockSpec(memory_space=pltpu.SME...]
    slice x1 -> x3, local copies, waits for them, and re-layouts: 0.04 us -> 4.18 us  [the longest x1 1.67 us: per_device(): o_down[4:]]
    all_to_all x2, waiting for transfers between devices: 10.1 us -> 13.6 us  [per_device(): lax.all_to_all(part, 'y', split_axis=0, concat_axis=0, tiled=True)]
  transfers between devices with their start and end apart: 20 -> 27, of which waited for: 16 -> 15; matrix products, arithmetic and copies ran while one was open for 3% -> 5% of each run, Pallas kernels for 12% -> 15%
where the time goes in v6:
time: 219 us; the launch traced here: 218 us
  waiting for transfers between devices  81.5 us (37%)
  Pallas kernels  54.2 us (25%)
  starting transfers between devices  38.8 us (18%)
  local copies, waits for them, and re-layouts  23 us (11%)
  between operations  14.4 us (7%)
  other arithmetic  5.9 us (3%)
    unnamed x44, local copies, waits for them, and re-layouts  17.7 us
    all_to_all x2, waiting for transfers between devices, per_device(): lax.all_to_all(part, 'y', split_axis=0, concat_axis=0, tiled=True)  13.6 us
    pallas_call x1, Pallas kernels, gate_up(): pl.pallas_call(gate_kernel, in_specs=[pl.BlockSpec(memory_space=pltpu.SME...  13.4 us
    ppermute x1, waiting for transfers between devices, per_device(): prior = lax.ppermute(tail, REQ, [(i - 1, i) for i in range(1, 16)])  10.9 us
    ppermute x1, waiting for transfers between devices, per_device(): right = lax.ppermute(mlp_in, 'y', ring(3))  10.8 us
    ppermute x7, waiting for transfers between devices, swap(): return lax.ppermute(block, axis, [(0, 1), (1, 0)])  8.64 us
    ppermute x1, waiting for transfers between devices, per_device(): from_left = lax.ppermute(to_right, 'y', ring(1))  8.16 us
    pallas_call x2, Pallas kernels, attend(): pl.pallas_call(attend_kernel, in_specs=[pl.BlockSpec(memory_space=pltpu.S...  8.01 us
  transfers between devices with their start and end apart: 27, of which 15 were waited for; matrix products, arithmetic and copies ran while one was open for 5% of the time, Pallas kernels for 15%

profile of v6, /device:TPU:32, one launch (start us, length us, event | category | flops | bytes accessed | tf_op | source)
XLA Modules:
  0.0 217.8 jit_solution(16218470373651713037)
XLA Ops:
  7.2 2.3 %pack.1 = bf16[8,768,128]{2,1,0:T(8,128)(2,1)} custom-call(f32[128,256]{1,0:T(8,128)} %q_ref.1, f32[128,128]{1,0:T(8,128)} %k_ref.1, f32[128,128]{1,0:T(8,128)} %v_ref.1, f32[256,128]{1,0:T(8,128)} %o_ref.1), custom_call_target="tpu_custom_call" | custom-call | tf_op jit(solution)/shard_map/pack/pallas_call | solution.py:368
  9.5 7.9 %all-to-all-start = ((bf16[8,768,128]{2,1,0:T(8,128)(2,1)}), bf16[8,768,128]{2,1,0:T(8,128)(2,1)S(1)}, u32[]{:S(2)}, u32[]{:S(2)}) async-start(bf16[8,768,128]{2,1,0:T(8,128)(2,1)} %pack.1), calls=%async_computation | async-start | bytes 3145728 | tf_op jit(solution)/shard_map/all_to_all | solution.py:432
  17.4 2.3 %prep.1 = (bf16[288,256]{1,0:T(8,128)(2,1)}, bf16[288,256]{1,0:T(8,128)(2,1)}, bf16[288,256]{1,0:T(8,128)(2,1)}, bf16[288,256]{1,0:T(8,128)(2,1)}) custom-call(s32[1]{0:T(128)} %bitcast.1.y_ref, f32[256,384]{1,0:T(8,128)} %gate_ref.1, f32[256,384]{1,0:T(8,128)} %up_ref.1, f32[384,256]{1,0:T(8,128)} %down_ref.1), custom_call_target="tpu_custom_call" | custom-call | tf_op jit(solution)/shard_map/prep/pallas_call | solution.py:387
  19.7 3.0 %collective-permute-start = (bf16[288,256]{1,0:T(8,128)(2,1)}, bf16[288,256]{1,0:T(8,128)(2,1)S(1)}, u32[]{:S(2)}, u32[]{:S(2)}) collective-permute-start(bf16[288,256]{1,0:T(8,128)(2,1)} %get-tuple-element.35), channel_id=1, source_target_pairs={{0,3},{1,0},{2,1},{3,2},{4,7},{5,4},{6,5},{7,6},{8,11},{9,8},{10,9... | collective-permute-start | bytes 442376 | tf_op jit(solution)/shard_map/ppermute | solution.py:406
  24.4 1.9 multiply_cosine_fusion
  26.3 5.4 %norm.1.x_ref = bf16[1024,2048]{1,0:T(8,128)(2,1)} custom-call(bf16[1024,2048]{1,0:T(8,128)(2,1)} %x_ref.1, f32[1,2048]{1,0:T(1,128)} %bitcast.14), custom_call_target="tpu_custom_call" | custom-call | tf_op jit(solution)/shard_map/norm/pallas_call | solution.py:35
  32.7 4.8 %all-to-all-done.own_ref.refs_0_ = bf16[8,768,128]{2,1,0:T(8,128)(2,1)S(1)} async-done(((bf16[8,768,128]{2,1,0:T(8,128)(2,1)}), bf16[8,768,128]{2,1,0:T(8,128)(2,1)S(1)}, u32[]{:S(2)}, u32[]{:S(2)}) %all-to-all-start) | async-done | bytes 1572896 | tf_op jit(solution)/shard_map/all_to_all | solution.py:432
  37.5 2.0 join.1
  40.5 1.6 collective-permute-start.6
  42.1 1.7 collective-permute-start.5
  43.8 2.2 %copy-done.1 = bf16[1024,2048]{1,0:T(8,128)(2,1)S(1)} copy-done((bf16[1024,2048]{1,0:T(8,128)(2,1)S(1)}, bf16[1024,2048]{1,0:T(8,128)(2,1)}, u32[]{:S(2)}) %copy-start.1) | copy-done | bytes 4194328
  47.0 5.0 %qkv.1 = (bf16[1024,256]{1,0:T(8,128)(2,1)S(1)}, bf16[2,1024,128]{2,1,0:T(8,128)(2,1)}, bf16[2,512,128]{2,1,0:T(8,128)(2,1)S(1)}) custom-call(s32[1]{0:T(128)} %bitcast.core_ref, bf16[1024,2048]{1,0:T(8,128)(2,1)S(1)} %copy-done.1, bf16[8,768,128]{2,1,0:T(8,128)(2,1)S(1)} %all-to-all-done.own_ref.refs_0_, ...), custom_call_target="tpu_custom_call" | custom-call | tf_op jit(solution)/shard_map/qkv/pallas_call | solution.py:87
  52.8 1.9 collective-permute-start.4
  54.7 1.7 collective-permute-done.6.refs_8_
  56.5 10.9 %collective-permute-done.4.prior_ref = bf16[2,512,128]{2,1,0:T(8,128)(2,1)S(1)} collective-permute-done((bf16[2,512,128]{2,1,0:T(8,128)(2,1)S(1)}, bf16[2,512,128]{2,1,0:T(8,128)(2,1)S(1)}, u32[]{:S(2)}, u32[]{:S(2)}) %collective-permute-start.4) | collective-permute-done | bytes 262176 | tf_op jit(solution)/shard_map/ppermute | solution.py:450
  67.4 1.7 slice.28
  69.0 1.7 slice.29
  70.7 1.5 collective-permute-start.8
  72.2 1.7 collective-permute-start.7
  78.2 4.2 %attend.2 = bf16[4,128,256]{2,1,0:T(8,128)(2,1)S(1)} custom-call(s32[1]{0:T(128)S(6)} %sub.6.half_ref, bf16[1024,256]{1,0:T(8,128)(2,1)S(1)} %copy-done.11, bf16[2,1024,128]{2,1,0:T(8,128)(2,1)S(1)} %copy-done.8, bf16[2,512,128]{2,1,0:T(8,128)(2,1)S(1)} %collective-permute-done.4.prior_ref, s32[1024,1]{1,0:T(8,128)S(1)} %copy-done.4), custom_call_target="tpu_custom_call" | custom-call | tf_op jit(solution)/shard_map/attend/pallas_call | solution.py:167
  84.1 4.2 %all-to-all-start.2 = ((bf16[4,128,256]{2,1,0:T(8,128)(2,1)}), bf16[4,128,256]{2,1,0:T(8,128)(2,1)}, u32[]{:S(2)}, u32[]{:S(2)}) async-start(bf16[4,128,256]{2,1,0:T(8,128)(2,1)} %copy-done.14), calls=%async_computation.2 | async-start | bytes 524288 | tf_op jit(solution)/shard_map/all_to_all | solution.py:453
  88.4 7.0 %all-to-all-done.2.ctx_ref = bf16[4,128,256]{2,1,0:T(8,128)(2,1)} async-done(((bf16[4,128,256]{2,1,0:T(8,128)(2,1)}), bf16[4,128,256]{2,1,0:T(8,128)(2,1)}, u32[]{:S(2)}, u32[]{:S(2)}) %all-to-all-start.2) | async-done | bytes 262176 | tf_op jit(solution)/shard_map/all_to_all | solution.py:453
  95.5 6.0 %out_first.1 = (bf16[128,2048]{1,0:T(8,128)(2,1)}, bf16[1024,2048]{1,0:T(8,128)(2,1)S(1)}) custom-call(s32[2]{0:T(128)S(1)} %pad_add_fusion.at_ref, bf16[4,128,256]{2,1,0:T(8,128)(2,1)} %all-to-all-done.2.ctx_ref, bf16[8,768,128]{2,1,0:T(8,128)(2,1)S(1)} %all-to-all-done.own_ref.refs_0_, bf16[8,768,128]{2,1,0:T(8,128)(2,1)S(1)} %collective-permute-done.3.oth_ref.refs_1_, ...), custom_call_target="tpu_custom_call" | custom-call | tf_op jit(solution)/shard_map/out_first/pallas_call | solution.py:217
  101.5 2.0 copy-done.6
  103.6 3.9 %attend.3 = bf16[4,128,256]{2,1,0:T(8,128)(2,1)} custom-call(s32[1]{0:T(128)} %bitcast.2.half_ref, bf16[1024,256]{1,0:T(8,128)(2,1)S(1)} %copy-done.12, bf16[2,1024,128]{2,1,0:T(8,128)(2,1)S(1)} %copy-done.9, bf16[2,512,128]{2,1,0:T(8,128)(2,1)S(1)} %collective-permute-done.4.prior_ref, s32[1024,1]{1,0:T(8,128)S(1)} %copy-done.5), custom_call_target="tpu_custom_call" | custom-call | tf_op jit(solution)/shard_map/attend/pallas_call | solution.py:167
  107.5 3.4 %all-to-all-start.1 = ((bf16[4,128,256]{2,1,0:T(8,128)(2,1)}), bf16[4,128,256]{2,1,0:T(8,128)(2,1)S(1)}, u32[]{:S(2)}, u32[]{:S(2)}) async-start(bf16[4,128,256]{2,1,0:T(8,128)(2,1)} %attend.3), calls=%async_computation.1 | async-start | bytes 524288 | tf_op jit(solution)/shard_map/all_to_all | solution.py:453
  110.9 6.6 %all-to-all-done.1.ctx_ref = bf16[4,128,256]{2,1,0:T(8,128)(2,1)S(1)} async-done(((bf16[4,128,256]{2,1,0:T(8,128)(2,1)}), bf16[4,128,256]{2,1,0:T(8,128)(2,1)S(1)}, u32[]{:S(2)}, u32[]{:S(2)}) %all-to-all-start.1) | async-done | bytes 262176 | tf_op jit(solution)/shard_map/all_to_all | solution.py:453
  117.5 2.2 %copy-done.7 = bf16[1024,2048]{1,0:T(8,128)(2,1)S(1)} copy-done((bf16[1024,2048]{1,0:T(8,128)(2,1)S(1)}, bf16[1024,2048]{1,0:T(8,128)(2,1)}, u32[]{:S(2)}) %copy-start.7) | copy-done | bytes 4194328
  119.7 1.8 out_second.1
  121.5 4.1 %collective-permute-done.13 = bf16[128,2048]{1,0:T(8,128)(2,1)S(1)} collective-permute-done((bf16[128,2048]{1,0:T(8,128)(2,1)}, bf16[128,2048]{1,0:T(8,128)(2,1)S(1)}, u32[]{:S(2)}, u32[]{:S(2)}) %collective-permute-start.13) | collective-permute-done | bytes 524320 | tf_op jit(solution)/shard_map/ppermute | solution.py:23
  125.6 1.2 add_convert_fusion
  127.3 2.8 %collective-permute-start.15 = (bf16[128,2048]{1,0:T(8,128)(2,1)S(1)}, bf16[128,2048]{1,0:T(8,128)(2,1)S(1)}, u32[]{:S(2)}, u32[]{:S(2)}) collective-permute-start(bf16[128,2048]{1,0:T(8,128)(2,1)S(1)} %fusion.2.x0_ref), channel_id=1, source_target_pairs={{0,3},{1,0},{2,1},{3,2},{4,7},{5,4},{6,5},{7,6},{8,11},{9,8},{10,9... | collective-permute-start | bytes 1572872 | tf_op jit(solution)/shard_map/ppermute | solution.py:472
  130.1 10.8 %collective-permute-done.15.x2_ref = bf16[128,2048]{1,0:T(8,128)(2,1)S(1)} collective-permute-done((bf16[128,2048]{1,0:T(8,128)(2,1)S(1)}, bf16[128,2048]{1,0:T(8,128)(2,1)S(1)}, u32[]{:S(2)}, u32[]{:S(2)}) %collective-permute-start.15) | collective-permute-done | bytes 524320 | tf_op jit(solution)/shard_map/ppermute | solution.py:472
  140.9 3.4 %collective-permute-done.14.x1_ref = bf16[128,2048]{1,0:T(8,128)(2,1)S(1)} collective-permute-done((bf16[128,2048]{1,0:T(8,128)(2,1)S(1)}, bf16[128,2048]{1,0:T(8,128)(2,1)S(1)}, u32[]{:S(2)}, u32[]{:S(2)}) %collective-permute-start.14) | collective-permute-done | bytes 524320 | tf_op jit(solution)/shard_map/ppermute | solution.py:471
  144.7 1.7 collective-permute-start.16
  146.4 6.7 %collective-permute-done.17.x4_ref = bf16[64,2048]{1,0:T(8,128)(2,1)S(1)} collective-permute-done((bf16[64,2048]{1,0:T(8,128)(2,1)S(1)}, bf16[64,2048]{1,0:T(8,128)(2,1)S(1)}, u32[]{:S(2)}, u32[]{:S(2)}) %collective-permute-start.17) | collective-permute-done | bytes 262176 | tf_op jit(solution)/shard_map/ppermute | solution.py:476
  153.1 1.5 collective-permute-done.16.x3_ref
  154.7 4.5 %collective-permute-done.18.oth_ref = bf16[8,2,4,288,256]{4,3,2,1,0:T(8,128)(2,1)S(1)} collective-permute-done((bf16[8,2,4,288,256]{4,3,2,1,0:T(8,128)(2,1)}, bf16[8,2,4,288,256]{4,3,2,1,0:T(8,128)(2,1)S(1)}, u32[]{:S(2)}, u32[]{:S(2)}) %collective-permute-start.18) | collective-permute-done | bytes 9437216 | tf_op jit(solution)/shard_map/ppermute | solution.py:23
  159.2 13.4 %gate_up.1.hid_ref = bf16[512,1536]{1,0:T(8,128)(2,1)S(1)} custom-call(s32[1]{0:T(128)} %bitcast.1.y_ref, bf16[128,2048]{1,0:T(8,128)(2,1)S(1)} %fusion.2.x0_ref, bf16[128,2048]{1,0:T(8,128)(2,1)S(1)} %collective-permute-done.14.x1_ref, bf16[128,2048]{1,0:T(8,128)(2,1)S(1)} %collective-permute-done.15.x2_ref, ...), custom_call_target="tpu_custom_call" | custom-call | tf_op jit(solution)/shard_map/gate_up/pallas_call | solution.py:322
  172.6 4.6 %down_far.1 = (bf16[64,2048]{1,0:T(8,128)(2,1)S(1)}, bf16[64,2048]{1,0:T(8,128)(2,1)S(1)}, bf16[1,16,96,2048]{3,2,1,0:T(8,128)(2,1)S(1)}) custom-call(s32[1]{0:T(128)} %bitcast.1.y_ref, bf16[512,1536]{1,0:T(8,128)(2,1)S(1)} %gate_up.1.hid_ref, bf16[8,2,4,288,256]{4,3,2,1,0:T(8,128)(2,1)} %bitcast.12, bf16[8,2,4,288,256]{4,3,2,1,0:T(8,128)(2,1)} %copy-done), custom_call_target="tpu_custom_call" | custom-call | tf_op jit(solution)/shard_map/down_far/pallas_call | solution.py:340
  177.2 2.7 %copy-done.2 = bf16[1,16,96,2048]{3,2,1,0:T(8,128)(2,1)} copy-done((bf16[1,16,96,2048]{3,2,1,0:T(8,128)(2,1)}, bf16[1,16,96,2048]{3,2,1,0:T(8,128)(2,1)S(1)}, u32[]{:S(2)}) %copy-start.2) | copy-done | bytes 6291480
  180.2 2.8 %copy-done.3 = bf16[1,16,96,2048]{3,2,1,0:T(8,128)(2,1)S(1)} copy-done((bf16[1,16,96,2048]{3,2,1,0:T(8,128)(2,1)S(1)}, bf16[1,16,96,2048]{3,2,1,0:T(8,128)(2,1)}, u32[]{:S(2)}) %copy-start.3) | copy-done | bytes 6291480
  183.0 3.2 %down.1 = (f32[128,2048]{1,0:T(8,128)S(1)}, bf16[128,2048]{1,0:T(8,128)(2,1)S(1)}, bf16[128,2048]{1,0:T(8,128)(2,1)S(1)}) custom-call(bf16[512,1536]{1,0:T(8,128)(2,1)S(1)} %gate_up.1.hid_ref, bf16[1,16,96,2048]{3,2,1,0:T(8,128)(2,1)S(1)} %copy-done.3), custom_call_target="tpu_custom_call" | custom-call | tf_op jit(solution)/shard_map/down/pallas_call | solution.py:352
  186.3 1.8 collective-permute-start.19
  188.4 1.6 collective-permute-start.22
  189.9 5.7 %collective-permute-done.19 = bf16[64,2048]{1,0:T(8,128)(2,1)S(1)} collective-permute-done((bf16[64,2048]{1,0:T(8,128)(2,1)S(1)}, bf16[64,2048]{1,0:T(8,128)(2,1)S(1)}, u32[]{:S(2)}, u32[]{:S(2)}) %collective-permute-start.19) | collective-permute-done | bytes 262176 | tf_op jit(solution)/shard_map/ppermute | solution.py:480
  196.3 5.3 %collective-permute-done.22 = bf16[128,2048]{1,0:T(8,128)(2,1)S(1)} collective-permute-done((bf16[128,2048]{1,0:T(8,128)(2,1)S(1)}, bf16[128,2048]{1,0:T(8,128)(2,1)S(1)}, u32[]{:S(2)}, u32[]{:S(2)}) %collective-permute-start.22) | collective-permute-done | bytes 524320 | tf_op jit(solution)/shard_map/ppermute | solution.py:486
  201.7 8.2 %collective-permute-done.20 = bf16[128,2048]{1,0:T(8,128)(2,1)S(1)} collective-permute-done((bf16[128,2048]{1,0:T(8,128)(2,1)S(1)}, bf16[128,2048]{1,0:T(8,128)(2,1)S(1)}, u32[]{:S(2)}, u32[]{:S(2)}) %collective-permute-start.20) | collective-permute-done | bytes 524320 | tf_op jit(solution)/shard_map/ppermute | solution.py:485
  (85 shorter events, 14.8 us)
Async XLA Ops:
  7.2 17.2 %copy-start.21 = (s32[1024]{0:T(1024)S(1)}, s32[1024]{0:T(1024)}, u32[]{:S(2)}) copy-start(s32[1024]{0:T(1024)} %param.15) | copy-start | bytes 12292
  9.5 28.0 %all-to-all-start = ((bf16[8,768,128]{2,1,0:T(8,128)(2,1)}), bf16[8,768,128]{2,1,0:T(8,128)(2,1)S(1)}, u32[]{:S(2)}, u32[]{:S(2)}) async-start(bf16[8,768,128]{2,1,0:T(8,128)(2,1)} %pack.1), calls=%async_computation | async-start | bytes 3145728 | tf_op jit(solution)/shard_map/all_to_all | solution.py:432
  17.4 126.9 %all-gather.3.cloned.1.call-start = ((), (), s32[]{:S(2)}) async-start(), calls=%async_computation.3 | async-start | bytes 10027008 | tf_op jit(solution)/shard_map/all_gather | solution.py:441
  19.7 13.0 %collective-permute-start = (bf16[288,256]{1,0:T(8,128)(2,1)}, bf16[288,256]{1,0:T(8,128)(2,1)S(1)}, u32[]{:S(2)}, u32[]{:S(2)}) collective-permute-start(bf16[288,256]{1,0:T(8,128)(2,1)} %get-tuple-element.35), channel_id=1, source_target_pairs={{0,3},{1,0},{2,1},{3,2},{4,7},{5,4},{6,5},{7,6},{8,11},{9,8},{10,9... | collective-permute-start | bytes 442376 | tf_op jit(solution)/shard_map/ppermute | solution.py:406
  22.7 10.0 %collective-permute-start.1 = (bf16[288,256]{1,0:T(8,128)(2,1)}, bf16[288,256]{1,0:T(8,128)(2,1)S(1)}, u32[]{:S(2)}, u32[]{:S(2)}) collective-permute-start(bf16[288,256]{1,0:T(8,128)(2,1)} %get-tuple-element.36), channel_id=1, source_target_pairs={{0,2},{1,3},{2,0},{3,1},{4,6},{5,7},{6,4},{7,5},{8,10},{9,11},{10,... | collective-permute-start | bytes 442376 | tf_op jit(solution)/shard_map/ppermute | solution.py:406
  23.4 9.3 %collective-permute-start.2 = (bf16[288,256]{1,0:T(8,128)(2,1)}, bf16[288,256]{1,0:T(8,128)(2,1)S(1)}, u32[]{:S(2)}, u32[]{:S(2)}) collective-permute-start(bf16[288,256]{1,0:T(8,128)(2,1)} %get-tuple-element.37), channel_id=1, source_target_pairs={{0,1},{1,2},{2,3},{3,0},{4,5},{5,6},{6,7},{7,4},{8,9},{9,10},{10,1... | collective-permute-start | bytes 442376 | tf_op jit(solution)/shard_map/ppermute | solution.py:406
  31.7 12.1 %copy-start.15 = (f32[128]{0:T(128)S(1)}, f32[128]{0:T(128)}, u32[]{:S(2)}) copy-start(f32[128]{0:T(128)} %param.18) | copy-start | bytes 1540
  31.7 12.1 %copy-start.16 = (f32[128]{0:T(128)S(1)}, f32[128]{0:T(128)}, u32[]{:S(2)}) copy-start(f32[128]{0:T(128)} %param.19) | copy-start | bytes 1540
  32.7 4.8 %copy-start.17 = (bf16[288,256]{1,0:T(8,128)(2,1)}, bf16[288,256]{1,0:T(8,128)(2,1)S(1)}, u32[]{:S(2)}) copy-start(bf16[288,256]{1,0:T(8,128)(2,1)S(1)} %collective-permute-done.p1_ref) | copy-start | bytes 442372
  32.7 4.8 %copy-start.18 = (bf16[288,256]{1,0:T(8,128)(2,1)}, bf16[288,256]{1,0:T(8,128)(2,1)S(1)}, u32[]{:S(2)}) copy-start(bf16[288,256]{1,0:T(8,128)(2,1)S(1)} %collective-permute-done.1.p2_ref) | copy-start | bytes 442372
  32.7 4.8 %copy-start.19 = (bf16[288,256]{1,0:T(8,128)(2,1)}, bf16[288,256]{1,0:T(8,128)(2,1)S(1)}, u32[]{:S(2)}) copy-start(bf16[288,256]{1,0:T(8,128)(2,1)S(1)} %collective-permute-done.2.p3_ref) | copy-start | bytes 442372
  39.6 4.2 %collective-permute-start.3 = (bf16[8,768,128]{2,1,0:T(8,128)(2,1)S(1)}, bf16[8,768,128]{2,1,0:T(8,128)(2,1)S(1)}, u32[]{:S(2)}, u32[]{:S(2)}) collective-permute-start(bf16[8,768,128]{2,1,0:T(8,128)(2,1)S(1)} %all-to-all-done.own_ref.refs_0_), channel_id=1, source_target_pairs={{0,8},{8,0},{1,9},{9,1},{2,10},{10,2},{3,11},{11,3},{4,12},{12,4},... | collective-permute-start | bytes 4718600 | tf_op jit(solution)/shard_map/ppermute | solution.py:23
  40.5 15.9 %collective-permute-start.6 = (bf16[8,256,128]{2,1,0:T(8,128)(2,1)}, bf16[8,256,128]{2,1,0:T(8,128)(2,1)}, u32[]{:S(2)}, u32[]{:S(2)}) collective-permute-start(bf16[8,256,128]{2,1,0:T(8,128)(2,1)} %slice.27), channel_id=1, source_target_pairs={{0,1},{1,2},{2,3},{3,0},{4,5},{5,6},{6,7},{7,4},{8,9},{9,10},{10,1... | collective-permute-start | bytes 1572872 | tf_op jit(solution)/shard_map/ppermute | solution.py:448
  42.1 14.4 %collective-permute-start.5 = (bf16[8,256,128]{2,1,0:T(8,128)(2,1)}, bf16[8,256,128]{2,1,0:T(8,128)(2,1)}, u32[]{:S(2)}, u32[]{:S(2)}) collective-permute-start(bf16[8,256,128]{2,1,0:T(8,128)(2,1)} %slice.27), channel_id=1, source_target_pairs={{0,3},{1,0},{2,1},{3,2},{4,7},{5,4},{6,5},{7,6},{8,11},{9,8},{10,9... | collective-permute-start | bytes 1572872 | tf_op jit(solution)/shard_map/ppermute | solution.py:447
  43.8 2.2 %copy-start.1 = (bf16[1024,2048]{1,0:T(8,128)(2,1)S(1)}, bf16[1024,2048]{1,0:T(8,128)(2,1)}, u32[]{:S(2)}) copy-start(bf16[1024,2048]{1,0:T(8,128)(2,1)} %norm.1.x_ref) | copy-start | bytes 12582916
  46.0 1.0 copy-start.13
  52.0 0.8 copy-start.10
  52.8 14.5 %collective-permute-start.4 = (bf16[2,512,128]{2,1,0:T(8,128)(2,1)S(1)}, bf16[2,512,128]{2,1,0:T(8,128)(2,1)S(1)}, u32[]{:S(2)}, u32[]{:S(2)}) collective-permute-start(bf16[2,512,128]{2,1,0:T(8,128)(2,1)S(1)} %get-tuple-element.43), channel_id=1, source_target_pairs={{0,8},{8,16},{16,24},{24,32},{32,40},{40,48},{48,56},{56,64},{64,7... | collective-permute-start | bytes 786440 | tf_op jit(solution)/shard_map/ppermute | solution.py:450
  70.7 12.4 %collective-permute-start.8 = (bf16[4,256,128]{2,1,0:T(8,128)(2,1)}, bf16[4,256,128]{2,1,0:T(8,128)(2,1)}, u32[]{:S(2)}, u32[]{:S(2)}) collective-permute-start(bf16[4,256,128]{2,1,0:T(8,128)(2,1)} %slice.29), channel_id=1, source_target_pairs={{0,1},{1,2},{2,3},{3,0},{4,5},{5,6},{6,7},{7,4},{8,9},{9,10},{10,1... | collective-permute-start | bytes 786440 | tf_op jit(solution)/shard_map/ppermute | solution.py:452
  72.2 10.9 %collective-permute-start.7 = (bf16[4,256,128]{2,1,0:T(8,128)(2,1)}, bf16[4,256,128]{2,1,0:T(8,128)(2,1)}, u32[]{:S(2)}, u32[]{:S(2)}) collective-permute-start(bf16[4,256,128]{2,1,0:T(8,128)(2,1)} %slice.28), channel_id=1, source_target_pairs={{0,3},{1,0},{2,1},{3,2},{4,7},{5,4},{6,5},{7,6},{8,11},{9,8},{10,9... | collective-permute-start | bytes 786440 | tf_op jit(solution)/shard_map/ppermute | solution.py:452
  75.0 1.2 copy-start.4
  76.2 1.0 copy-start.8
  77.2 1.0 copy-start.11
  83.1 12.4 %collective-permute-start.9 = (bf16[8,256,128]{2,1,0:T(8,128)(2,1)}, bf16[8,256,128]{2,1,0:T(8,128)(2,1)}, u32[]{:S(2)}, u32[]{:S(2)}) collective-permute-start(bf16[8,256,128]{2,1,0:T(8,128)(2,1)} %collective-permute-done.5.refs_2_), channel_id=1, source_target_pairs={{0,8},{8,0},{1,9},{9,1},{2,10},{10,2},{3,11},{11,3},{4,12},{12,4},... | collective-permute-start | bytes 1572872 | tf_op jit(solution)/shard_map/ppermute | solution.py:23
  83.1 12.4 %collective-permute-start.12 = (bf16[8,256,128]{2,1,0:T(8,128)(2,1)}, bf16[8,256,128]{2,1,0:T(8,128)(2,1)}, u32[]{:S(2)}, u32[]{:S(2)}) collective-permute-start(bf16[8,256,128]{2,1,0:T(8,128)(2,1)} %collective-permute-done.6.refs_8_), channel_id=1, source_target_pairs={{0,8},{8,0},{1,9},{9,1},{2,10},{10,2},{3,11},{11,3},{4,12},{12,4},... | collective-permute-start | bytes 1572872 | tf_op jit(solution)/shard_map/ppermute | solution.py:23
  83.6 11.8 %collective-permute-start.10 = (bf16[4,256,128]{2,1,0:T(8,128)(2,1)}, bf16[4,256,128]{2,1,0:T(8,128)(2,1)}, u32[]{:S(2)}, u32[]{:S(2)}) collective-permute-start(bf16[4,256,128]{2,1,0:T(8,128)(2,1)} %collective-permute-done.7.refs_4_), channel_id=1, source_target_pairs={{0,8},{8,0},{1,9},{9,1},{2,10},{10,2},{3,11},{11,3},{4,12},{12,4},... | collective-permute-start | bytes 786440 | tf_op jit(solution)/shard_map/ppermute | solution.py:23
  83.7 11.7 %collective-permute-start.11 = (bf16[4,256,128]{2,1,0:T(8,128)(2,1)}, bf16[4,256,128]{2,1,0:T(8,128)(2,1)}, u32[]{:S(2)}, u32[]{:S(2)}) collective-permute-start(bf16[4,256,128]{2,1,0:T(8,128)(2,1)} %collective-permute-done.8.refs_6_), channel_id=1, source_target_pairs={{0,8},{8,0},{1,9},{9,1},{2,10},{10,2},{3,11},{11,3},{4,12},{12,4},... | collective-permute-start | bytes 786440 | tf_op jit(solution)/shard_map/ppermute | solution.py:23
  84.1 11.3 %all-to-all-start.2 = ((bf16[4,128,256]{2,1,0:T(8,128)(2,1)}), bf16[4,128,256]{2,1,0:T(8,128)(2,1)}, u32[]{:S(2)}, u32[]{:S(2)}) async-start(bf16[4,128,256]{2,1,0:T(8,128)(2,1)} %copy-done.14), calls=%async_computation.2 | async-start | bytes 524288 | tf_op jit(solution)/shard_map/all_to_all | solution.py:453
  95.4 8.1 %copy-start.5 = (s32[1024,1]{1,0:T(8,128)S(1)}, s32[1024,1]{1,0:T(8,128)}, u32[]{:S(2)}) copy-start(s32[1024,1]{1,0:T(8,128)} %copy.17.lo_ref) | copy-start | bytes 12292
  95.4 8.1 %copy-start.9 = (bf16[2,1024,128]{2,1,0:T(8,128)(2,1)S(1)}, bf16[2,1024,128]{2,1,0:T(8,128)(2,1)}, u32[]{:S(2)}) copy-start(bf16[2,1024,128]{2,1,0:T(8,128)(2,1)} %get-tuple-element.33.kv_ref) | copy-start | bytes 1572868
  95.4 8.1 %copy-start.12 = (bf16[1024,256]{1,0:T(8,128)(2,1)S(1)}, bf16[1024,256]{1,0:T(8,128)(2,1)}, u32[]{:S(2)}) copy-start(bf16[1024,256]{1,0:T(8,128)(2,1)} %copy-done.10) | copy-start | bytes 1572868
  101.5 2.0 copy-start.6
  103.6 22.1 %collective-permute-start.13 = (bf16[128,2048]{1,0:T(8,128)(2,1)}, bf16[128,2048]{1,0:T(8,128)(2,1)S(1)}, u32[]{:S(2)}, u32[]{:S(2)}) collective-permute-start(bf16[128,2048]{1,0:T(8,128)(2,1)} %get-tuple-element.52), channel_id=1, source_target_pairs={{0,4},{4,0},{1,5},{5,1},{2,6},{6,2},{3,7},{7,3},{8,12},{12,8},{9,1... | collective-permute-start | bytes 1572872 | tf_op jit(solution)/shard_map/ppermute | solution.py:23
  107.5 10.1 %all-to-all-start.1 = ((bf16[4,128,256]{2,1,0:T(8,128)(2,1)}), bf16[4,128,256]{2,1,0:T(8,128)(2,1)S(1)}, u32[]{:S(2)}, u32[]{:S(2)}) async-start(bf16[4,128,256]{2,1,0:T(8,128)(2,1)} %attend.3), calls=%async_computation.1 | async-start | bytes 524288 | tf_op jit(solution)/shard_map/all_to_all | solution.py:453
  117.5 2.2 %copy-start.7 = (bf16[1024,2048]{1,0:T(8,128)(2,1)S(1)}, bf16[1024,2048]{1,0:T(8,128)(2,1)}, u32[]{:S(2)}) copy-start(bf16[1024,2048]{1,0:T(8,128)(2,1)} %copy-done.6) | copy-start | bytes 12582916
  119.7 7.4 %copy-start.20 = (f32[2048]{0:T(1024)S(1)}, f32[2048]{0:T(1024)}, u32[]{:S(2)}) copy-start(f32[2048]{0:T(1024)} %param.17) | copy-start | bytes 24580
  127.3 13.6 %collective-permute-start.15 = (bf16[128,2048]{1,0:T(8,128)(2,1)S(1)}, bf16[128,2048]{1,0:T(8,128)(2,1)S(1)}, u32[]{:S(2)}, u32[]{:S(2)}) collective-permute-start(bf16[128,2048]{1,0:T(8,128)(2,1)S(1)} %fusion.2.x0_ref), channel_id=1, source_target_pairs={{0,3},{1,0},{2,1},{3,2},{4,7},{5,4},{6,5},{7,6},{8,11},{9,8},{10,9... | collective-permute-start | bytes 1572872 | tf_op jit(solution)/shard_map/ppermute | solution.py:472
  130.1 14.2 %collective-permute-start.14 = (bf16[128,2048]{1,0:T(8,128)(2,1)S(1)}, bf16[128,2048]{1,0:T(8,128)(2,1)S(1)}, u32[]{:S(2)}, u32[]{:S(2)}) collective-permute-start(bf16[128,2048]{1,0:T(8,128)(2,1)S(1)} %fusion.2.x0_ref), channel_id=1, source_target_pairs={{0,1},{1,2},{2,3},{3,0},{4,5},{5,6},{6,7},{7,4},{8,9},{9,10},{10,1... | collective-permute-start | bytes 1572872 | tf_op jit(solution)/shard_map/ppermute | solution.py:471
  144.3 14.9 %collective-permute-start.18 = (bf16[8,2,4,288,256]{4,3,2,1,0:T(8,128)(2,1)}, bf16[8,2,4,288,256]{4,3,2,1,0:T(8,128)(2,1)S(1)}, u32[]{:S(2)}, u32[]{:S(2)}) collective-permute-start(bf16[8,2,4,288,256]{4,3,2,1,0:T(8,128)(2,1)} %bitcast.10), channel_id=1, source_target_pairs={{0,8},{8,0},{1,9},{9,1},{2,10},{10,2},{3,11},{11,3},{4,12},{12,4},... | collective-permute-start | bytes 28311560 | tf_op jit(solution)/shard_map/ppermute | solution.py:23
  144.3 8.8 %collective-permute-start.17 = (bf16[64,2048]{1,0:T(8,128)(2,1)S(1)}, bf16[64,2048]{1,0:T(8,128)(2,1)S(1)}, u32[]{:S(2)}, u32[]{:S(2)}) collective-permute-start(bf16[64,2048]{1,0:T(8,128)(2,1)S(1)} %slice.31), channel_id=1, source_target_pairs={{0,3},{1,0},{2,1},{3,2},{4,7},{5,4},{6,5},{7,6},{8,11},{9,8},{10,9... | collective-permute-start | bytes 786440 | tf_op jit(solution)/shard_map/ppermute | solution.py:476
  144.7 9.9 %collective-permute-start.16 = (bf16[64,2048]{1,0:T(8,128)(2,1)S(1)}, bf16[64,2048]{1,0:T(8,128)(2,1)S(1)}, u32[]{:S(2)}, u32[]{:S(2)}) collective-permute-start(bf16[64,2048]{1,0:T(8,128)(2,1)S(1)} %slice.30), channel_id=1, source_target_pairs={{0,1},{1,2},{2,3},{3,0},{4,5},{5,6},{6,7},{7,4},{8,9},{9,10},{10,1... | collective-permute-start | bytes 786440 | tf_op jit(solution)/shard_map/ppermute | solution.py:475
  159.2 13.5 %copy-start = (bf16[8,2,4,288,256]{4,3,2,1,0:T(8,128)(2,1)}, bf16[8,2,4,288,256]{4,3,2,1,0:T(8,128)(2,1)S(1)}, u32[]{:S(2)}) copy-start(bf16[8,2,4,288,256]{4,3,2,1,0:T(8,128)(2,1)S(1)} %collective-permute-done.18.oth_ref) | copy-start | bytes 28311556
  177.2 2.7 %copy-start.2 = (bf16[1,16,96,2048]{3,2,1,0:T(8,128)(2,1)}, bf16[1,16,96,2048]{3,2,1,0:T(8,128)(2,1)S(1)}, u32[]{:S(2)}) copy-start(bf16[1,16,96,2048]{3,2,1,0:T(8,128)(2,1)S(1)} %get-tuple-element.60.w_ref) | copy-start | bytes 18874372
  179.9 8.3 %collective-permute-start.21 = (bf16[64,2048]{1,0:T(8,128)(2,1)S(1)}, bf16[64,2048]{1,0:T(8,128)(2,1)S(1)}, u32[]{:S(2)}, u32[]{:S(2)}) collective-permute-start(bf16[64,2048]{1,0:T(8,128)(2,1)S(1)} %get-tuple-element.65), channel_id=1, source_target_pairs={{0,3},{1,0},{2,1},{3,2},{4,7},{5,4},{6,5},{7,6},{8,11},{9,8},{10,9... | collective-permute-start | bytes 786440 | tf_op jit(solution)/shard_map/ppermute | solution.py:481
  180.2 2.8 %copy-start.3 = (bf16[1,16,96,2048]{3,2,1,0:T(8,128)(2,1)S(1)}, bf16[1,16,96,2048]{3,2,1,0:T(8,128)(2,1)}, u32[]{:S(2)}) copy-start(bf16[1,16,96,2048]{3,2,1,0:T(8,128)(2,1)} %copy-done.2) | copy-start | bytes 18874372
  186.3 9.3 %collective-permute-start.19 = (bf16[64,2048]{1,0:T(8,128)(2,1)S(1)}, bf16[64,2048]{1,0:T(8,128)(2,1)S(1)}, u32[]{:S(2)}, u32[]{:S(2)}) collective-permute-start(bf16[64,2048]{1,0:T(8,128)(2,1)S(1)} %get-tuple-element.63), channel_id=1, source_target_pairs={{0,1},{1,2},{2,3},{3,0},{4,5},{5,6},{6,7},{7,4},{8,9},{9,10},{10,1... | collective-permute-start | bytes 786440 | tf_op jit(solution)/shard_map/ppermute | solution.py:480
  188.4 13.3 %collective-permute-start.22 = (bf16[128,2048]{1,0:T(8,128)(2,1)S(1)}, bf16[128,2048]{1,0:T(8,128)(2,1)S(1)}, u32[]{:S(2)}, u32[]{:S(2)}) collective-permute-start(bf16[128,2048]{1,0:T(8,128)(2,1)S(1)} %pad_maximum_fusion.2), channel_id=1, source_target_pairs={{0,3},{1,0},{2,1},{3,2},{4,7},{5,4},{6,5},{7,6},{8,11},{9,8},{10,9... | collective-permute-start | bytes 1572872 | tf_op jit(solution)/shard_map/ppermute | solution.py:486
  195.7 14.1 %collective-permute-start.20 = (bf16[128,2048]{1,0:T(8,128)(2,1)S(1)}, bf16[128,2048]{1,0:T(8,128)(2,1)S(1)}, u32[]{:S(2)}, u32[]{:S(2)}) collective-permute-start(bf16[128,2048]{1,0:T(8,128)(2,1)S(1)} %pad_maximum_fusion.1), channel_id=1, source_target_pairs={{0,1},{1,2},{2,3},{3,0},{4,5},{5,6},{6,7},{7,4},{8,9},{9,10},{10,1... | collective-permute-start | bytes 1572872 | tf_op jit(solution)/shard_map/ppermute | solution.py:485
  (1 other events, 0.7 us)
Sparse Core Ops, SparseCore 0:
  39.7 83.8 all-gather.2

commit v7 on v4

--- a/solution.py
+++ b/solution.py
@@ -194,20 +194,60 @@
     )(at, ctx, own, oth)
 
 
-def fetcher(own_ref, oth_ref, w_ref, sems, y, first):
-    def copy(c, g, m):
-        src = own_ref if c == 0 else oth_ref
+def mid_kernel(m_ref, x_ref, keep_ref, got_ref, gain_ref, resid_ref, top_ref, bottom_ref):
+    resid = (x_ref[...].astype(F32) + (keep_ref[...] + got_ref[...].astype(F32))).astype(BF)
+    resid_ref[...] = resid
+    wide = resid.astype(F32)
+    scale = lax.rsqrt(jnp.mean(wide * wide, axis=-1, keepdims=True) + 1e-06)
+    normed = (wide * scale * gain_ref[...]).astype(BF)
+    top_ref[...] = normed[:64]
+    bottom_ref[...] = normed[64:]
+
+
+def middle(m, tokens, keep, got, gain):
+    whole = lambda *shape: pl.BlockSpec(shape, lambda i, m: (0,) * len(shape))
+    return pl.pallas_call(
+        mid_kernel,
+        grid_spec=pltpu.PrefetchScalarGridSpec(
+            num_scalar_prefetch=1,
+            grid=(1,),
+            in_specs=[
+                pl.BlockSpec((128, 2048), lambda i, m: (m[0], 0)),
+                whole(128, 2048),
+                whole(128, 2048),
+                whole(1, 2048),
+            ],
+            out_specs=[whole(128, 2048), whole(64, 2048), whole(64, 2048)],
+        ),
+        out_shape=(
+            jax.ShapeDtypeStruct((128, 2048), BF),
+            jax.ShapeDtypeStruct((64, 2048), BF),
+            jax.ShapeDtypeStruct((64, 2048), BF),
+        ),
+        name="mid",
+    )(m, tokens, keep, got, gain[None])
+
+
+def last_kernel(resid_ref, keep_ref, lt_ref, lb_ref, rt_ref, rb_ref, out_ref):
+    for at, left, right in ((slice(0, 64), lt_ref, rt_ref), (slice(64, 128), lb_ref, rb_ref)):
+        total = keep_ref[at] + left[...].astype(F32) + right[...].astype(F32)
+        out_ref[at] = (resid_ref[at].astype(F32) + total).astype(BF)
+
+
+def fetcher(src_ref, w_ref, sems, y, first):
+    def copy(g, m):
         at = pl.multiple_of(((m // 4) * 4 + lax.rem(y + lax.rem(m, 4), 4)) * 256, 256)
+        row = (first + g) * 96
         return pltpu.make_async_copy(
-            src.at[:, m // 4, lax.rem(m, 4), first + g * 96 : first + g * 96 + 96, :],
-            w_ref.at[g, c * 8 : c * 8 + 8, :, pl.ds(at, 256)],
-            sems.at[g, c, m],
+            src_ref.at[:, m // 4, lax.rem(m, 4), row : row + 96, :],
+            w_ref.at[g, :, :, pl.ds(at, 256)],
+            sems.at[g, m],
         )
 
-    def each(c, groups, act):
+    def each(groups, act):
         def step(m, carry):
-            for g in range(groups):
-                act(copy(c, g, m))
+            for g in groups:
+                act(copy(g, m))
             return carry
 
         lax.fori_loop(0, 8, step, 0)
@@ -215,22 +255,36 @@
     return each
 
 
-def gate_kernel(y_ref, x0_ref, x1_ref, x2_ref, x3_ref, x4_ref, own_ref, oth_ref, hid_ref, w_ref, x_ref, sems):
+def load_kernel(y_ref, src_ref, w_ref, sems):
+    each = fetcher(src_ref, w_ref, sems, y_ref[0], 0)
+    each(range(3), lambda copy: copy.start())
+    each(range(3), lambda copy: copy.wait())
+
+
+def load(y, src):
+    return pl.pallas_call(
+        load_kernel,
+        in_specs=[pl.BlockSpec(memory_space=pltpu.SMEM), pl.BlockSpec(memory_space=pltpu.HBM)],
+        out_shape=jax.ShapeDtypeStruct((3, 8, 96, 2048), BF),
+        scratch_shapes=[pltpu.SemaphoreType.DMA((3, 8))],
+        compiler_params=pltpu.CompilerParams(vmem_limit_bytes=40 << 20),
+        name="load",
+    )(y, src)
+
+
+def gate_kernel(y_ref, *refs):
+    pieces, (own_ref, src_ref, hid_ref, oth_ref, x_ref, sems) = refs[:8], refs[8:]
     nt = (((1,), (1,)), ((), ()))
-    each = fetcher(own_ref, oth_ref, w_ref, sems, y_ref[0], 0)
-    each(0, 2, lambda c: c.start())
-    each(1, 2, lambda c: c.start())
-    x_ref[0:128] = x0_ref[...]
-    x_ref[128:256] = x1_ref[...]
-    x_ref[256:384] = x2_ref[...]
-    x_ref[384:448] = x3_ref[...]
-    x_ref[448:512] = x4_ref[...]
+    each = fetcher(src_ref, oth_ref, sems, y_ref[0], 0)
+    each(range(3), lambda copy: copy.start())
+    for k, piece in enumerate(pieces):
+        x_ref[k * 64 : k * 64 + 64] = piece[...]
     x = x_ref[...]
-
-    for c in range(2):
-        each(c, 2, lambda copy: copy.wait())
-        gate_w = w_ref[0, c * 8 : c * 8 + 8].reshape(768, 2048)
-        up_w = w_ref[1, c * 8 : c * 8 + 8].reshape(768, 2048)
+    for c, w_ref in enumerate((own_ref, oth_ref)):
+        if c == 1:
+            each(range(3), lambda copy: copy.wait())
+        gate_w = w_ref[0].reshape(768, 2048)
+        up_w = w_ref[1].reshape(768, 2048)
         for t in range(3):
             gate = lax.dot_general(x, gate_w[t * 256 : t * 256 + 256], nt, preferred_element_type=F32)
             upper = lax.dot_general(x, up_w[t * 256 : t * 256 + 256], nt, preferred_element_type=F32)
@@ -239,77 +293,53 @@
             hid_ref[:, at : at + 256] = hidden.astype(BF)
 
 
-def far_kernel(y_ref, hid_ref, own_ref, oth_ref, top_ref, bottom_ref, w_ref, sems):
-    each = fetcher(own_ref, oth_ref, w_ref, sems, y_ref[0], 192)
-    for c in range(2):
-        each(c, 1, lambda copy: copy.start())
-    for c in range(2):
-        each(c, 1, lambda copy: copy.wait())
-    hid = hid_ref[384:]
-
+def gate_up(y, pieces, own, src):
+    vm = pl.BlockSpec(memory_space=pltpu.VMEM)
+    return pl.pallas_call(
+        gate_kernel,
+        in_specs=[pl.BlockSpec(memory_space=pltpu.SMEM)] + [vm] * 9 + [pl.BlockSpec(memory_space=pltpu.HBM)],
+        out_shape=(jax.ShapeDtypeStruct((512, 1536), BF), jax.ShapeDtypeStruct((3, 8, 96, 2048), BF)),
+        scratch_shapes=[pltpu.VMEM((512, 2048), BF), pltpu.SemaphoreType.DMA((3, 8))],
+        compiler_params=pltpu.CompilerParams(vmem_limit_bytes=40 << 20),
+        name="gate_up",
+    )(y, *pieces, own, src)
+
+
+def down_columns(hid, own_ref, oth_ref, store):
     def column(n, carry):
         at = pl.ds(pl.multiple_of(n * 512, 512), 512)
-        out = jnp.dot(hid, w_ref[0, :, :, at].reshape(1536, 512), preferred_element_type=F32)
+        out = jnp.dot(hid[:, :768], own_ref[2, :, :, at].reshape(768, 512), preferred_element_type=F32)
+        out = out + jnp.dot(hid[:, 768:], oth_ref[2, :, :, at].reshape(768, 512), preferred_element_type=F32)
+        store(at, out)
+        return carry
+
+    lax.fori_loop(0, 4, column, 0)
+
+
+def far_kernel(hid_ref, own_ref, oth_ref, top_ref, bottom_ref):
+    def store(at, out):
         top_ref[:, at] = out[:64].astype(BF)
         bottom_ref[:, at] = out[64:].astype(BF)
-        return carry
-
-    lax.fori_loop(0, 4, column, 0)
-
-
-def down_kernel(hid_ref, w_ref, keep_ref, left_ref, right_ref):
-    hid = hid_ref[:384]
-
-    def column(n, carry):
-        at = pl.ds(pl.multiple_of(n * 512, 512), 512)
-        out = jnp.dot(hid, w_ref[0, :, :, at].reshape(1536, 512), preferred_element_type=F32)
+
+    down_columns(hid_ref[384:], own_ref, oth_ref, store)
+
+
+def near_kernel(hid_ref, own_ref, oth_ref, keep_ref, lt_ref, lb_ref, rt_ref, rb_ref):
+    def store(at, out):
         keep_ref[:, at] = out[:128]
-        left_ref[:, at] = out[128:256].astype(BF)
-        right_ref[:, at] = out[256:].astype(BF)
-        return carry
-
-    lax.fori_loop(0, 4, column, 0)
-
-
-def gate_up(y, pieces, own, oth):
-    vm = pl.BlockSpec(memory_space=pltpu.VMEM)
-    hbm = pl.BlockSpec(memory_space=pltpu.HBM)
-    return pl.pallas_call(
-        gate_kernel,
-        in_specs=[pl.BlockSpec(memory_space=pltpu.SMEM)] + [vm] * 5 + [hbm] * 2,
-        out_shape=jax.ShapeDtypeStruct((512, 1536), BF),
-        scratch_shapes=[
-            pltpu.VMEM((2, 16, 96, 2048), BF),
-            pltpu.VMEM((512, 2048), BF),
-            pltpu.SemaphoreType.DMA((2, 2, 8)),
-        ],
-        compiler_params=pltpu.CompilerParams(vmem_limit_bytes=40 << 20),
-        name="gate_up",
-    )(y, *pieces, own, oth)
-
-
-def down_far(y, hidden, own, oth):
-    vm = pl.BlockSpec(memory_space=pltpu.VMEM)
-    hbm = pl.BlockSpec(memory_space=pltpu.HBM)
-    half = jax.ShapeDtypeStruct((64, 2048), BF)
-    return pl.pallas_call(
-        far_kernel,
-        in_specs=[pl.BlockSpec(memory_space=pltpu.SMEM), vm] + [hbm] * 2,
-        out_shape=(half, half, jax.ShapeDtypeStruct((1, 16, 96, 2048), BF)),
-        scratch_shapes=[pltpu.SemaphoreType.DMA((1, 2, 8))],
-        compiler_params=pltpu.CompilerParams(vmem_limit_bytes=40 << 20),
-        name="down_far",
-    )(y, hidden, own, oth)
-
-
-def down(hidden, weight):
-    part = jax.ShapeDtypeStruct((128, 2048), BF)
-    return pl.pallas_call(
-        down_kernel,
-        out_shape=(jax.ShapeDtypeStruct((128, 2048), F32), part, part),
-        compiler_params=pltpu.CompilerParams(vmem_limit_bytes=40 << 20),
-        name="down",
-    )(hidden, weight)
+        for k, ref in enumerate((lt_ref, lb_ref, rt_ref, rb_ref)):
+            ref[:, at] = out[128 + 64 * k : 192 + 64 * k].astype(BF)
+
+    down_columns(hid_ref[:384], own_ref, oth_ref, store)
+
+
+def down(kernel, name, outs, hidden, own, oth):
+    return pl.pallas_call(
+        kernel,
+        out_shape=outs,
+        compiler_params=pltpu.CompilerParams(vmem_limit_bytes=40 << 20),
+        name=name,
+    )(hidden, own, oth)
 
 
 def pack_kernel(q_ref, k_ref, v_ref, o_ref, out_ref):
@@ -409,29 +439,38 @@
     keep, send = out_project(jnp.stack([core, xl]), ctx, o_own, o_oth)
     got = swap(send, "xl")
 
-    own_rows = lax.dynamic_slice_in_dim(tokens, (xl * 4 + y) * 128, 128, 0).astype(F32)
-    resid = (own_rows + (keep + got.astype(F32))).astype(BF)
-    resid = hold(resid).astype(F32)
-    scale = lax.rsqrt(jnp.mean(resid * resid, axis=-1, keepdims=True) + 1e-06)
-    mlp_in = (resid * scale * mlp_gain).astype(BF)
-
-    left = lax.ppermute(mlp_in, "y", ring(1))
-    right = lax.ppermute(mlp_in, "y", ring(3))
-    mlp_own, left, right = hold((mlp_own, left, right))
+    resid, top, bottom = middle((xl * 4 + y)[None], tokens, keep, got, mlp_gain)
+    to_right, to_left = ring(1), ring(3)
+    left_top = lax.ppermute(top, "y", to_right)
+    right_bottom = lax.ppermute(bottom, "y", to_left)
+    left_bottom = lax.ppermute(bottom, "y", to_right)
+    right_top = lax.ppermute(top, "y", to_left)
+    far_top = lax.ppermute(left_top, "y", to_right)
+    far_bottom = lax.ppermute(right_bottom, "y", to_left)
+    mlp_own, _, _ = hold((mlp_own, left_top, right_bottom))
     mlp_oth = swap(mlp_own, "core")
-    far_top = lax.ppermute(left[:64], "y", ring(1))
-    far_bottom = lax.ppermute(right[64:], "y", ring(3))
-    hidden = gate_up(y[None], (mlp_in, left, right, far_top, far_bottom), mlp_own, mlp_oth)
-    top, bottom, weight = down_far(y[None], hidden, mlp_own, mlp_oth)
-    via_left = lax.ppermute(top, "y", ring(1))
-    via_right = lax.ppermute(bottom, "y", ring(3))
-    keep, to_left, to_right = down(hidden, weight)
-    to_right = jnp.concatenate([(to_right[:64].astype(F32) + via_left.astype(F32)).astype(BF), to_right[64:]])
-    to_left = jnp.concatenate([to_left[:64], (to_left[64:].astype(F32) + via_right.astype(F32)).astype(BF)])
-    from_left = lax.ppermute(to_right, "y", ring(1))
-    from_right = lax.ppermute(to_left, "y", ring(3))
-    total = keep + from_left.astype(F32) + from_right.astype(F32)
-    return ((resid + total).astype(BF), cache)
+    own = load(y[None], pltpu.with_memory_space_constraint(mlp_own, pltpu.HBM))
+    pieces = (top, bottom, left_top, left_bottom, right_top, right_bottom, far_top, far_bottom)
+    hidden, oth = gate_up(y[None], pieces, own, mlp_oth)
+
+    half = jax.ShapeDtypeStruct((64, 2048), BF)
+    far_top, far_bottom = down(far_kernel, "down_far", (half, half), hidden, own, oth)
+    via_left = lax.ppermute(far_top, "y", to_right)
+    via_right = lax.ppermute(far_bottom, "y", to_left)
+    whole = jax.ShapeDtypeStruct((128, 2048), F32)
+    keep, left_top, left_bottom, right_top, right_bottom = down(
+        near_kernel, "down", (whole, half, half, half, half), hidden, own, oth
+    )
+    got_left_bottom = lax.ppermute(right_bottom, "y", to_right)
+    got_right_top = lax.ppermute(left_top, "y", to_left)
+    right_top = (right_top.astype(F32) + via_left.astype(F32)).astype(BF)
+    left_bottom = (left_bottom.astype(F32) + via_right.astype(F32)).astype(BF)
+    got_left_top = lax.ppermute(right_top, "y", to_right)
+    got_right_bottom = lax.ppermute(left_bottom, "y", to_left)
+    out = pl.pallas_call(last_kernel, out_shape=jax.ShapeDtypeStruct((128, 2048), BF), name="last")(
+        resid, keep, got_left_top, got_left_bottom, got_right_top, got_right_bottom
+    )
+    return (out, cache)
 
 
 def solution(mesh):

time: 206 us -> 212 us (1.029)
  waiting for transfers between devices: 100 us -> 73.5 us
  Pallas kernels: 41.4 us -> 58.1 us
  starting transfers between devices: 33.3 us -> 44.7 us
  local copies, waits for them, and re-layouts: 10.1 us -> 16.1 us
  other arithmetic: 5.4 us -> 2.3 us
    ppermute x8 -> x12, waiting for transfers between devices: 39.9 us -> 18.5 us  [the longest x1 5.06 us: per_device(): left_top = lax.ppermute(top, 'y', to_right)]
    pallas_call x2 -> x5, Pallas kernels: 7.79 us -> 21.5 us  [the longest x2 12.1 us: down(): pl.pallas_call(kernel, out_shape=outs, compiler_params=pltpu.CompilerPara...]
    ppermute x8 -> x12, starting transfers between devices: 8.51 us -> 19.8 us  [the longest x1 3.76 us: per_device(): got_right_bottom = lax.ppermute(left_bottom, 'y', to_left)]
    unnamed x24 -> x42, local copies, waits for them, and re-layouts: 7.91 us -> 14 us
    ppermute x4, waiting for transfers between devices: 29.8 us -> 24.9 us  [swap(): return lax.ppermute(block, axis, [(0, 1), (1, 0)])]
    pallas_call x1, Pallas kernels: 8.55 us -> 11.5 us  [gate_up(): pl.pallas_call(gate_kernel, in_specs=[pl.BlockSpec(memory_space=pltpu.SME...]
    convert_element_type x5 -> x2, other arithmetic: 2.94 us -> 0.13 us  [the longest x1 0.06 us: per_device(): right_top = (right_top.astype(F32) + via_left.astype(F32)).astype(BF)]
  transfers between devices with their start and end apart: 20 -> 24, of which waited for: 16 -> 13; matrix products, arithmetic and copies ran while one was open for 3% -> 2% of each run, Pallas kernels for 12% -> 16%
where the time goes in v7:
time: 212 us; the launch traced here: 209 us
  waiting for transfers between devices  73.5 us (35%)
  Pallas kernels  58.1 us (27%)
  starting transfers between devices  44.7 us (21%)
  local copies, waits for them, and re-layouts  16.1 us (8%)
  between operations  14.3 us (7%)
  other arithmetic  2.3 us (1%)
    ppermute x4, waiting for transfers between devices, swap(): return lax.ppermute(block, axis, [(0, 1), (1, 0)])  24.9 us
    unnamed x42, local copies, waits for them, and re-layouts  14 us
    pallas_call x2, Pallas kernels, down(): pl.pallas_call(kernel, out_shape=outs, compiler_params=pltpu.CompilerPara...  12.1 us
    pallas_call x1, Pallas kernels, gate_up(): pl.pallas_call(gate_kernel, in_specs=[pl.BlockSpec(memory_space=pltpu.SME...  11.5 us
    all_to_all x1, waiting for transfers between devices, per_device(): ctx = lax.all_to_all(ctx, 'y', split_axis=0, concat_axis=0, tiled=True)  10.1 us
    ppermute x1, waiting for transfers between devices, per_device(): prior = lax.ppermute(tail, REQ, [(i - 1, i) for i in range(1, 16)])  9.05 us
    all_to_all x1, starting transfers between devices, per_device(): lax.all_to_all(packed, ('z', 'xh'), split_axis=0, concat_axis=0, tiled=True)  8.01 us
    pallas_call x1, Pallas kernels, project(): pl.pallas_call(qkv_kernel, grid_spec=pltpu.PrefetchScalarGridSpec(num_sca...  7.21 us
  transfers between devices with their start and end apart: 24, of which 13 were waited for; matrix products, arithmetic and copies ran while one was open for 2% of the time, Pallas kernels for 16%

profile of v7, /device:TPU:32, one launch (start us, length us, event | category | flops | bytes accessed | tf_op | source)
XLA Modules:
  0.0 209.0 jit_solution(15786587849376599768)
XLA Ops:
  7.2 2.3 %pack.1 = bf16[8,768,128]{2,1,0:T(8,128)(2,1)} custom-call(f32[128,256]{1,0:T(8,128)} %q_ref.1, f32[128,128]{1,0:T(8,128)} %k_ref.1, f32[128,128]{1,0:T(8,128)} %v_ref.1, f32[256,128]{1,0:T(8,128)} %o_ref.1), custom_call_target="tpu_custom_call" | custom-call | tf_op jit(solution)/shard_map/pack/pallas_call | solution.py:353
  9.5 8.0 %all-to-all-start = ((bf16[8,768,128]{2,1,0:T(8,128)(2,1)}), bf16[8,768,128]{2,1,0:T(8,128)(2,1)S(1)}, u32[]{:S(2)}, u32[]{:S(2)}) async-start(bf16[8,768,128]{2,1,0:T(8,128)(2,1)} %pack.1), calls=%async_computation | async-start | bytes 3145728 | tf_op jit(solution)/shard_map/all_to_all | solution.py:417
  17.5 2.3 %prep.1 = (bf16[288,256]{1,0:T(8,128)(2,1)}, bf16[288,256]{1,0:T(8,128)(2,1)}, bf16[288,256]{1,0:T(8,128)(2,1)}, bf16[288,256]{1,0:T(8,128)(2,1)}) custom-call(s32[1]{0:T(128)} %bitcast.3.y_ref, f32[256,384]{1,0:T(8,128)} %gate_ref.1, f32[256,384]{1,0:T(8,128)} %up_ref.1, f32[384,256]{1,0:T(8,128)} %down_ref.1), custom_call_target="tpu_custom_call" | custom-call | tf_op jit(solution)/shard_map/prep/pallas_call | solution.py:372
  19.8 3.0 %collective-permute-start = (bf16[288,256]{1,0:T(8,128)(2,1)}, bf16[288,256]{1,0:T(8,128)(2,1)S(1)}, u32[]{:S(2)}, u32[]{:S(2)}) collective-permute-start(bf16[288,256]{1,0:T(8,128)(2,1)} %get-tuple-element.33), channel_id=1, source_target_pairs={{0,3},{1,0},{2,1},{3,2},{4,7},{5,4},{6,5},{7,6},{8,11},{9,8},{10,9... | collective-permute-start | bytes 442376 | tf_op jit(solution)/shard_map/ppermute | solution.py:391
  22.9 0.6 collective-permute-start.1
  23.5 1.0 collective-permute-start.2
  24.5 1.9 multiply_cosine_fusion
  26.6 2.3 %collective-permute-done.p1_ref = bf16[288,256]{1,0:T(8,128)(2,1)S(1)} collective-permute-done((bf16[288,256]{1,0:T(8,128)(2,1)}, bf16[288,256]{1,0:T(8,128)(2,1)S(1)}, u32[]{:S(2)}, u32[]{:S(2)}) %collective-permute-start) | collective-permute-done | bytes 147488 | tf_op jit(solution)/shard_map/ppermute | solution.py:391
  28.9 2.1 collective-permute-done.1.p2_ref
  31.0 1.5 collective-permute-done.2.p3_ref
  32.5 5.2 %all-to-all-done.own_ref = bf16[8,768,128]{2,1,0:T(8,128)(2,1)S(1)} async-done(((bf16[8,768,128]{2,1,0:T(8,128)(2,1)}), bf16[8,768,128]{2,1,0:T(8,128)(2,1)S(1)}, u32[]{:S(2)}, u32[]{:S(2)}) %all-to-all-start) | async-done | bytes 1572896 | tf_op jit(solution)/shard_map/all_to_all | solution.py:417
  37.7 2.0 join.1
  39.8 1.8 broadcast_in_dim.38
  41.7 4.6 %all-to-all-start.1 = ((bf16[4,8,256,128]{3,2,1,0:T(8,128)(2,1)}), bf16[4,8,256,128]{3,2,1,0:T(8,128)(2,1)}, u32[]{:S(2)}, u32[]{:S(2)}) async-start(bf16[4,8,256,128]{3,2,1,0:T(8,128)(2,1)} %broadcast_in_dim.38), calls=%async_computation.1 | async-start | bytes 4194304 | tf_op jit(solution)/shard_map/all_to_all | solution.py:431
  46.3 2.2 %copy-done.3 = bf16[1024,2048]{1,0:T(8,128)(2,1)S(1)} copy-done((bf16[1024,2048]{1,0:T(8,128)(2,1)S(1)}, bf16[1024,2048]{1,0:T(8,128)(2,1)}, u32[]{:S(2)}) %copy-start.3) | copy-done | bytes 4194328
  48.5 7.2 %qkv.1 = (bf16[1024,256]{1,0:T(8,128)(2,1)S(1)}, bf16[2,1024,128]{2,1,0:T(8,128)(2,1)}, bf16[2,512,128]{2,1,0:T(8,128)(2,1)S(1)}) custom-call(s32[1]{0:T(128)} %bitcast.1.core_ref, bf16[1024,2048]{1,0:T(8,128)(2,1)S(1)} %copy-done.3, bf16[8,768,128]{2,1,0:T(8,128)(2,1)S(1)} %all-to-all-done.own_ref, bf16[8,768,128]{2,1,0:T(8,128)(2,1)} %collective-permute-done.3.oth_ref, ...), custom_call_target="tpu_custom_call" | custom-call | tf_op jit(solution)/shard_map/qkv/pallas_call | solution.py:71
  55.7 2.4 %collective-permute-start.4 = (bf16[2,512,128]{2,1,0:T(8,128)(2,1)S(1)}, bf16[2,512,128]{2,1,0:T(8,128)(2,1)S(1)}, u32[]{:S(2)}, u32[]{:S(2)}) collective-permute-start(bf16[2,512,128]{2,1,0:T(8,128)(2,1)S(1)} %get-tuple-element.40), channel_id=1, source_target_pairs={{0,8},{8,16},{16,24},{24,32},{32,40},{40,48},{48,56},{56,64},{64,7... | collective-permute-start | bytes 786440 | tf_op jit(solution)/shard_map/ppermute | solution.py:434
  58.4 9.0 %collective-permute-done.4.prior_ref = bf16[2,512,128]{2,1,0:T(8,128)(2,1)S(1)} collective-permute-done((bf16[2,512,128]{2,1,0:T(8,128)(2,1)S(1)}, bf16[2,512,128]{2,1,0:T(8,128)(2,1)S(1)}, u32[]{:S(2)}, u32[]{:S(2)}) %collective-permute-start.4) | collective-permute-done | bytes 262176 | tf_op jit(solution)/shard_map/ppermute | solution.py:434
  67.5 1.0 copy-done.6
  68.5 6.4 %attend.1 = bf16[4,2,128,256]{3,2,1,0:T(8,128)(2,1)} custom-call(bf16[1024,256]{1,0:T(8,128)(2,1)S(1)} %get-tuple-element.38.q_ref, bf16[2,1024,128]{2,1,0:T(8,128)(2,1)S(1)} %copy-done.6, bf16[2,512,128]{2,1,0:T(8,128)(2,1)S(1)} %collective-permute-done.4.prior_ref, s32[1024,1]{1,0:T(8,128)S(1)} %copy.16.lo_ref), custom_call_target="tpu_custom_call" | custom-call | tf_op jit(solution)/shard_map/attend/pallas_call | solution.py:136
  74.9 4.4 %all-to-all-start.2 = ((bf16[4,2,128,256]{3,2,1,0:T(8,128)(2,1)}), bf16[4,2,128,256]{3,2,1,0:T(8,128)(2,1)S(1)}, u32[]{:S(2)}, u32[]{:S(2)}) async-start(bf16[4,2,128,256]{3,2,1,0:T(8,128)(2,1)} %attend.1), calls=%async_computation.2 | async-start | bytes 1048576 | tf_op jit(solution)/shard_map/all_to_all | solution.py:438
  79.4 10.1 %all-to-all-done.2.ctx_ref = bf16[4,2,128,256]{3,2,1,0:T(8,128)(2,1)S(1)} async-done(((bf16[4,2,128,256]{3,2,1,0:T(8,128)(2,1)}), bf16[4,2,128,256]{3,2,1,0:T(8,128)(2,1)S(1)}, u32[]{:S(2)}, u32[]{:S(2)}) %all-to-all-start.2) | async-done | bytes 524320 | tf_op jit(solution)/shard_map/all_to_all | solution.py:438
  89.5 4.8 %oproj.1 = (f32[128,2048]{1,0:T(8,128)S(1)}, bf16[128,2048]{1,0:T(8,128)(2,1)S(1)}) custom-call(s32[2]{0:T(128)S(1)} %pad_add_fusion.at_ref, bf16[4,2,128,256]{3,2,1,0:T(8,128)(2,1)S(1)} %all-to-all-done.2.ctx_ref, bf16[4,8,256,128]{3,2,1,0:T(8,128)(2,1)} %all-to-all-done.1.own_ref, bf16[4,8,256,128]{3,2,1,0:T(8,128)(2,1)S(1)} %collective-permute-done.5.oth_ref), custom_call_target="tpu_custom_call" | custom-call | tf_op jit(solution)/shard_map/oproj/pallas_call | solution.py:180
  94.4 1.0 copy-done.5
  95.9 24.9 %collective-permute-done.6.got_ref = bf16[128,2048]{1,0:T(8,128)(2,1)S(1)} collective-permute-done((bf16[128,2048]{1,0:T(8,128)(2,1)S(1)}, bf16[128,2048]{1,0:T(8,128)(2,1)S(1)}, u32[]{:S(2)}, u32[]{:S(2)}) %collective-permute-start.6) | collective-permute-done | bytes 524320 | tf_op jit(solution)/shard_map/ppermute | solution.py:23
  120.8 0.8 copy-done.12
  121.6 2.8 %mid.1 = (bf16[128,2048]{1,0:T(8,128)(2,1)}, bf16[64,2048]{1,0:T(8,128)(2,1)}, bf16[64,2048]{1,0:T(8,128)(2,1)}) custom-call(s32[1]{0:T(128)} %bitcast.m_ref, bf16[1024,2048]{1,0:T(8,128)(2,1)} %x_ref.3, f32[128,2048]{1,0:T(8,128)} %copy-done.5, bf16[128,2048]{1,0:T(8,128)(2,1)} %copy-done.12, f32[1,2048]{1,0:T(1,128)} %bitcast.16), custom_call_target="tpu_custom_call" | custom-call | tf_op jit(solution)/shard_map/mid/pallas_call | solution.py:209
  125.0 2.6 %collective-permute-start.10 = (bf16[64,2048]{1,0:T(8,128)(2,1)}, bf16[64,2048]{1,0:T(8,128)(2,1)S(1)}, u32[]{:S(2)}, u32[]{:S(2)}) collective-permute-start(bf16[64,2048]{1,0:T(8,128)(2,1)} %get-tuple-element.47.refs_1_), channel_id=1, source_target_pairs={{0,3},{1,0},{2,1},{3,2},{4,7},{5,4},{6,5},{7,6},{8,11},{9,8},{10,9... | collective-permute-start | bytes 786440 | tf_op jit(solution)/shard_map/ppermute | solution.py:445
  127.6 5.1 %collective-permute-done.7.refs_2_ = bf16[64,2048]{1,0:T(8,128)(2,1)S(1)} collective-permute-done((bf16[64,2048]{1,0:T(8,128)(2,1)}, bf16[64,2048]{1,0:T(8,128)(2,1)S(1)}, u32[]{:S(2)}, u32[]{:S(2)}) %collective-permute-start.7) | collective-permute-done | bytes 262176 | tf_op jit(solution)/shard_map/ppermute | solution.py:444
  132.8 2.9 %collective-permute-start.9 = (bf16[64,2048]{1,0:T(8,128)(2,1)}, bf16[64,2048]{1,0:T(8,128)(2,1)S(1)}, u32[]{:S(2)}, u32[]{:S(2)}) collective-permute-start(bf16[64,2048]{1,0:T(8,128)(2,1)} %get-tuple-element.46.refs_0_), channel_id=1, source_target_pairs={{0,3},{1,0},{2,1},{3,2},{4,7},{5,4},{6,5},{7,6},{8,11},{9,8},{10,9... | collective-permute-start | bytes 786440 | tf_op jit(solution)/shard_map/ppermute | solution.py:447
  135.7 3.3 %collective-permute-start.12 = (bf16[64,2048]{1,0:T(8,128)(2,1)S(1)}, bf16[64,2048]{1,0:T(8,128)(2,1)S(1)}, u32[]{:S(2)}, u32[]{:S(2)}) collective-permute-start(bf16[64,2048]{1,0:T(8,128)(2,1)S(1)} %collective-permute-done.10.refs_5_), channel_id=1, source_target_pairs={{0,3},{1,0},{2,1},{3,2},{4,7},{5,4},{6,5},{7,6},{8,11},{9,8},{10,9... | collective-permute-start | bytes 786440 | tf_op jit(solution)/shard_map/ppermute | solution.py:449
  139.0 3.9 %load.1.refs_8_.own_ref = bf16[3,8,96,2048]{3,2,1,0:T(8,128)(2,1)S(1)} custom-call(s32[1]{0:T(128)} %bitcast.3.y_ref, bf16[8,2,4,288,256]{4,3,2,1,0:T(8,128)(2,1)} %bitcast.14), custom_call_target="tpu_custom_call" | custom-call | tf_op jit(solution)/shard_map/load/pallas_call | solution.py:265
  142.9 3.6 %copy-done = bf16[3,8,96,2048]{3,2,1,0:T(8,128)(2,1)} copy-done((bf16[3,8,96,2048]{3,2,1,0:T(8,128)(2,1)}, bf16[3,8,96,2048]{3,2,1,0:T(8,128)(2,1)S(1)}, u32[]{:S(2)}) %copy-start) | copy-done | bytes 9437208
  146.5 4.6 %collective-permute-done.11.refs_6_ = bf16[64,2048]{1,0:T(8,128)(2,1)S(1)} collective-permute-done((bf16[64,2048]{1,0:T(8,128)(2,1)S(1)}, bf16[64,2048]{1,0:T(8,128)(2,1)S(1)}, u32[]{:S(2)}, u32[]{:S(2)}) %collective-permute-start.11) | collective-permute-done | bytes 262176 | tf_op jit(solution)/shard_map/ppermute | solution.py:448
  151.1 11.5 %gate_up.1 = (bf16[512,1536]{1,0:T(8,128)(2,1)S(1)}, bf16[3,8,96,2048]{3,2,1,0:T(8,128)(2,1)S(1)}) custom-call(s32[1]{0:T(128)} %bitcast.3.y_ref, bf16[64,2048]{1,0:T(8,128)(2,1)S(1)} %copy-done.7, bf16[64,2048]{1,0:T(8,128)(2,1)S(1)} %copy-done.8, bf16[64,2048]{1,0:T(8,128)(2,1)S(1)} %collective-permute-done.7.refs_2_, ...), custom_call_target="tpu_custom_call" | custom-call | tf_op jit(solution)/shard_map/gate_up/pallas_call | solution.py:298
  162.6 3.6 %copy-done.2 = bf16[3,8,96,2048]{3,2,1,0:T(8,128)(2,1)} copy-done((bf16[3,8,96,2048]{3,2,1,0:T(8,128)(2,1)}, bf16[3,8,96,2048]{3,2,1,0:T(8,128)(2,1)S(1)}, u32[]{:S(2)}) %copy-start.2) | copy-done | bytes 9437208
  166.3 5.2 %down_far.1 = (bf16[64,2048]{1,0:T(8,128)(2,1)S(1)}, bf16[64,2048]{1,0:T(8,128)(2,1)S(1)}) custom-call(bf16[512,1536]{1,0:T(8,128)(2,1)S(1)} %get-tuple-element.53.hid_ref, bf16[3,8,96,2048]{3,2,1,0:T(8,128)(2,1)S(1)} %copy-done.1, bf16[3,8,96,2048]{3,2,1,0:T(8,128)(2,1)} %copy-done.2), custom_call_target="tpu_custom_call" | custom-call | tf_op jit(solution)/shard_map/down_far/pallas_call | solution.py:337
  171.6 6.9 %down.1 = (f32[128,2048]{1,0:T(8,128)S(1)}, bf16[64,2048]{1,0:T(8,128)(2,1)S(1)}, bf16[64,2048]{1,0:T(8,128)(2,1)S(1)}, bf16[64,2048]{1,0:T(8,128)(2,1)S(1)}, bf16[64,2048]{1,0:T(8,128)(2,1)S(1)}) custom-call(bf16[512,1536]{1,0:T(8,128)(2,1)S(1)} %get-tuple-element.53.hid_ref, bf16[3,8,96,2048]{3,2,1,0:T(8,128)(2,1)S(1)} %copy-done.1, ...), custom_call_target="tpu_custom_call" | custom-call | tf_op jit(solution)/shard_map/down/pallas_call | solution.py:337
  178.5 1.0 copy-done.4
  179.5 3.2 %collective-permute-start.18 = (bf16[64,2048]{1,0:T(8,128)(2,1)S(1)}, bf16[64,2048]{1,0:T(8,128)(2,1)S(1)}, u32[]{:S(2)}, u32[]{:S(2)}) collective-permute-start(bf16[64,2048]{1,0:T(8,128)(2,1)S(1)} %get-tuple-element.61), channel_id=1, source_target_pairs={{0,3},{1,0},{2,1},{3,2},{4,7},{5,4},{6,5},{7,6},{8,11},{9,8},{10,9... | collective-permute-start | bytes 786440 | tf_op jit(solution)/shard_map/ppermute | solution.py:459
  182.8 3.2 %collective-permute-start.17 = (bf16[64,2048]{1,0:T(8,128)(2,1)S(1)}, bf16[64,2048]{1,0:T(8,128)(2,1)S(1)}, u32[]{:S(2)}, u32[]{:S(2)}) collective-permute-start(bf16[64,2048]{1,0:T(8,128)(2,1)S(1)} %get-tuple-element.59), channel_id=1, source_target_pairs={{0,3},{1,0},{2,1},{3,2},{4,7},{5,4},{6,5},{7,6},{8,11},{9,8},{10,9... | collective-permute-start | bytes 786440 | tf_op jit(solution)/shard_map/ppermute | solution.py:465
  186.1 3.4 %collective-permute-done.18 = bf16[64,2048]{1,0:T(8,128)(2,1)S(1)} collective-permute-done((bf16[64,2048]{1,0:T(8,128)(2,1)S(1)}, bf16[64,2048]{1,0:T(8,128)(2,1)S(1)}, u32[]{:S(2)}, u32[]{:S(2)}) %collective-permute-start.18) | collective-permute-done | bytes 262176 | tf_op jit(solution)/shard_map/ppermute | solution.py:459
  189.6 3.8 %collective-permute-start.19 = (bf16[64,2048]{1,0:T(8,128)(2,1)S(1)}, bf16[64,2048]{1,0:T(8,128)(2,1)S(1)}, u32[]{:S(2)}, u32[]{:S(2)}) collective-permute-start(bf16[64,2048]{1,0:T(8,128)(2,1)S(1)} %add_convert_fusion), channel_id=1, source_target_pairs={{0,3},{1,0},{2,1},{3,2},{4,7},{5,4},{6,5},{7,6},{8,11},{9,8},{10,9... | collective-permute-start | bytes 786440 | tf_op jit(solution)/shard_map/ppermute | solution.py:469
  193.3 1.8 collective-permute-done.17.rt_ref
  195.1 1.4 collective-permute-done.15.lt_ref
  196.6 2.2 %collective-permute-done.19.rb_ref = bf16[64,2048]{1,0:T(8,128)(2,1)S(1)} collective-permute-done((bf16[64,2048]{1,0:T(8,128)(2,1)S(1)}, bf16[64,2048]{1,0:T(8,128)(2,1)S(1)}, u32[]{:S(2)}, u32[]{:S(2)}) %collective-permute-start.19) | collective-permute-done | bytes 262176 | tf_op jit(solution)/shard_map/ppermute | solution.py:469
  198.8 0.7 copy-done.16
  199.5 2.7 %last.1 = bf16[128,2048]{1,0:T(8,128)(2,1)} custom-call(bf16[128,2048]{1,0:T(8,128)(2,1)} %get-tuple-element.45.resid_ref, f32[128,2048]{1,0:T(8,128)} %copy-done.4, bf16[64,2048]{1,0:T(8,128)(2,1)} %copy-done.15, bf16[64,2048]{1,0:T(8,128)(2,1)} %copy-done.13, bf16[64,2048]{1,0:T(8,128)(2,1)} %copy-done.14, bf16[64,2048]{1,0:T(8,128)(2,1)} %copy-done.16), custom_call_target="tpu_custom_call" | custom-call | tf_op jit(solution)/shard_map/last/pallas_call | solution.py:470
  (65 shorter events, 2.3 us)
Async XLA Ops:
  9.5 15.0 %copy-start.20 = (s32[1024]{0:T(1024)S(1)}, s32[1024]{0:T(1024)}, u32[]{:S(2)}) copy-start(s32[1024]{0:T(1024)} %param.15) | copy-start | bytes 12292
  9.5 28.2 %all-to-all-start = ((bf16[8,768,128]{2,1,0:T(8,128)(2,1)}), bf16[8,768,128]{2,1,0:T(8,128)(2,1)S(1)}, u32[]{:S(2)}, u32[]{:S(2)}) async-start(bf16[8,768,128]{2,1,0:T(8,128)(2,1)} %pack.1), calls=%async_computation | async-start | bytes 3145728 | tf_op jit(solution)/shard_map/all_to_all | solution.py:417
  17.5 115.2 %all-gather.3.cloned.1.call-start = ((), (), s32[]{:S(2)}) async-start(), calls=%async_computation.3 | async-start | bytes 10027008 | tf_op jit(solution)/shard_map/all_gather | solution.py:425
  19.8 9.0 %collective-permute-start = (bf16[288,256]{1,0:T(8,128)(2,1)}, bf16[288,256]{1,0:T(8,128)(2,1)S(1)}, u32[]{:S(2)}, u32[]{:S(2)}) collective-permute-start(bf16[288,256]{1,0:T(8,128)(2,1)} %get-tuple-element.33), channel_id=1, source_target_pairs={{0,3},{1,0},{2,1},{3,2},{4,7},{5,4},{6,5},{7,6},{8,11},{9,8},{10,9... | collective-permute-start | bytes 442376 | tf_op jit(solution)/shard_map/ppermute | solution.py:391
  22.9 8.1 %collective-permute-start.1 = (bf16[288,256]{1,0:T(8,128)(2,1)}, bf16[288,256]{1,0:T(8,128)(2,1)S(1)}, u32[]{:S(2)}, u32[]{:S(2)}) collective-permute-start(bf16[288,256]{1,0:T(8,128)(2,1)} %get-tuple-element.34), channel_id=1, source_target_pairs={{0,2},{1,3},{2,0},{3,1},{4,6},{5,7},{6,4},{7,5},{8,10},{9,11},{10,... | collective-permute-start | bytes 442376 | tf_op jit(solution)/shard_map/ppermute | solution.py:391
  23.5 9.0 %collective-permute-start.2 = (bf16[288,256]{1,0:T(8,128)(2,1)}, bf16[288,256]{1,0:T(8,128)(2,1)S(1)}, u32[]{:S(2)}, u32[]{:S(2)}) collective-permute-start(bf16[288,256]{1,0:T(8,128)(2,1)} %get-tuple-element.35), channel_id=1, source_target_pairs={{0,1},{1,2},{2,3},{3,0},{4,5},{5,6},{6,7},{7,4},{8,9},{9,10},{10,1... | collective-permute-start | bytes 442376 | tf_op jit(solution)/shard_map/ppermute | solution.py:391
  28.9 8.8 %copy-start.17 = (bf16[288,256]{1,0:T(8,128)(2,1)}, bf16[288,256]{1,0:T(8,128)(2,1)S(1)}, u32[]{:S(2)}) copy-start(bf16[288,256]{1,0:T(8,128)(2,1)S(1)} %collective-permute-done.p1_ref) | copy-start | bytes 442372
  31.0 6.7 %copy-start.18 = (bf16[288,256]{1,0:T(8,128)(2,1)}, bf16[288,256]{1,0:T(8,128)(2,1)S(1)}, u32[]{:S(2)}) copy-start(bf16[288,256]{1,0:T(8,128)(2,1)S(1)} %collective-permute-done.1.p2_ref) | copy-start | bytes 442372
  32.5 5.2 %copy-start.19 = (bf16[288,256]{1,0:T(8,128)(2,1)}, bf16[288,256]{1,0:T(8,128)(2,1)S(1)}, u32[]{:S(2)}) copy-start(bf16[288,256]{1,0:T(8,128)(2,1)S(1)} %collective-permute-done.2.p3_ref) | copy-start | bytes 442372
  39.7 6.6 %collective-permute-start.3 = (bf16[8,768,128]{2,1,0:T(8,128)(2,1)S(1)}, bf16[8,768,128]{2,1,0:T(8,128)(2,1)}, u32[]{:S(2)}, u32[]{:S(2)}) collective-permute-start(bf16[8,768,128]{2,1,0:T(8,128)(2,1)S(1)} %all-to-all-done.own_ref), channel_id=1, source_target_pairs={{0,8},{8,0},{1,9},{9,1},{2,10},{10,2},{3,11},{11,3},{4,12},{12,4},... | collective-permute-start | bytes 4718600 | tf_op jit(solution)/shard_map/ppermute | solution.py:23
  41.7 4.6 %copy-start.9 = (f32[2048]{0:T(1024)S(1)}, f32[2048]{0:T(1024)}, u32[]{:S(2)}) copy-start(f32[2048]{0:T(1024)} %param.16) | copy-start | bytes 24580
  41.7 4.7 %copy-start.10 = (f32[128]{0:T(128)S(1)}, f32[128]{0:T(128)}, u32[]{:S(2)}) copy-start(f32[128]{0:T(128)} %param.18) | copy-start | bytes 1540
  41.7 4.7 %copy-start.11 = (f32[128]{0:T(128)S(1)}, f32[128]{0:T(128)}, u32[]{:S(2)}) copy-start(f32[128]{0:T(128)} %param.19) | copy-start | bytes 1540
  41.7 33.3 %all-to-all-start.1 = ((bf16[4,8,256,128]{3,2,1,0:T(8,128)(2,1)}), bf16[4,8,256,128]{3,2,1,0:T(8,128)(2,1)}, u32[]{:S(2)}, u32[]{:S(2)}) async-start(bf16[4,8,256,128]{3,2,1,0:T(8,128)(2,1)} %broadcast_in_dim.38), calls=%async_computation.1 | async-start | bytes 4194304 | tf_op jit(solution)/shard_map/all_to_all | solution.py:431
  46.3 2.2 %copy-start.3 = (bf16[1024,2048]{1,0:T(8,128)(2,1)S(1)}, bf16[1024,2048]{1,0:T(8,128)(2,1)}, u32[]{:S(2)}) copy-start(bf16[1024,2048]{1,0:T(8,128)(2,1)} %x_ref.3) | copy-start | bytes 12582916
  55.7 11.7 %collective-permute-start.4 = (bf16[2,512,128]{2,1,0:T(8,128)(2,1)S(1)}, bf16[2,512,128]{2,1,0:T(8,128)(2,1)S(1)}, u32[]{:S(2)}, u32[]{:S(2)}) collective-permute-start(bf16[2,512,128]{2,1,0:T(8,128)(2,1)S(1)} %get-tuple-element.40), channel_id=1, source_target_pairs={{0,8},{8,16},{16,24},{24,32},{32,40},{40,48},{48,56},{56,64},{64,7... | collective-permute-start | bytes 786440 | tf_op jit(solution)/shard_map/ppermute | solution.py:434
  67.5 1.0 copy-start.6
  74.9 14.6 %collective-permute-start.5 = (bf16[4,8,256,128]{3,2,1,0:T(8,128)(2,1)}, bf16[4,8,256,128]{3,2,1,0:T(8,128)(2,1)S(1)}, u32[]{:S(2)}, u32[]{:S(2)}) collective-permute-start(bf16[4,8,256,128]{3,2,1,0:T(8,128)(2,1)} %all-to-all-done.1.own_ref), channel_id=1, source_target_pairs={{0,8},{8,0},{1,9},{9,1},{2,10},{10,2},{3,11},{11,3},{4,12},{12,4},... | collective-permute-start | bytes 6291464 | tf_op jit(solution)/shard_map/ppermute | solution.py:23
  74.9 14.6 %all-to-all-start.2 = ((bf16[4,2,128,256]{3,2,1,0:T(8,128)(2,1)}), bf16[4,2,128,256]{3,2,1,0:T(8,128)(2,1)S(1)}, u32[]{:S(2)}, u32[]{:S(2)}) async-start(bf16[4,2,128,256]{3,2,1,0:T(8,128)(2,1)} %attend.1), calls=%async_computation.2 | async-start | bytes 1048576 | tf_op jit(solution)/shard_map/all_to_all | solution.py:438
  94.4 1.0 copy-start.5
  95.3 25.5 %collective-permute-start.6 = (bf16[128,2048]{1,0:T(8,128)(2,1)S(1)}, bf16[128,2048]{1,0:T(8,128)(2,1)S(1)}, u32[]{:S(2)}, u32[]{:S(2)}) collective-permute-start(bf16[128,2048]{1,0:T(8,128)(2,1)S(1)} %get-tuple-element.44), channel_id=1, source_target_pairs={{0,4},{4,0},{1,5},{5,1},{2,6},{6,2},{3,7},{7,3},{8,12},{12,8},{9,1... | collective-permute-start | bytes 1572872 | tf_op jit(solution)/shard_map/ppermute | solution.py:23
  120.8 0.8 copy-start.12
  124.3 8.3 %collective-permute-start.7 = (bf16[64,2048]{1,0:T(8,128)(2,1)}, bf16[64,2048]{1,0:T(8,128)(2,1)S(1)}, u32[]{:S(2)}, u32[]{:S(2)}) collective-permute-start(bf16[64,2048]{1,0:T(8,128)(2,1)} %get-tuple-element.46.refs_0_), channel_id=1, source_target_pairs={{0,1},{1,2},{2,3},{3,0},{4,5},{5,6},{6,7},{7,4},{8,9},{9,10},{10,1... | collective-permute-start | bytes 786440 | tf_op jit(solution)/shard_map/ppermute | solution.py:444
  125.0 7.7 %collective-permute-start.10 = (bf16[64,2048]{1,0:T(8,128)(2,1)}, bf16[64,2048]{1,0:T(8,128)(2,1)S(1)}, u32[]{:S(2)}, u32[]{:S(2)}) collective-permute-start(bf16[64,2048]{1,0:T(8,128)(2,1)} %get-tuple-element.47.refs_1_), channel_id=1, source_target_pairs={{0,3},{1,0},{2,1},{3,2},{4,7},{5,4},{6,5},{7,6},{8,11},{9,8},{10,9... | collective-permute-start | bytes 786440 | tf_op jit(solution)/shard_map/ppermute | solution.py:445
  132.7 18.5 %copy-start.7 = (bf16[64,2048]{1,0:T(8,128)(2,1)S(1)}, bf16[64,2048]{1,0:T(8,128)(2,1)}, u32[]{:S(2)}) copy-start(bf16[64,2048]{1,0:T(8,128)(2,1)} %get-tuple-element.46.refs_0_) | copy-start | bytes 786436
  132.7 18.5 %copy-start.8 = (bf16[64,2048]{1,0:T(8,128)(2,1)S(1)}, bf16[64,2048]{1,0:T(8,128)(2,1)}, u32[]{:S(2)}) copy-start(bf16[64,2048]{1,0:T(8,128)(2,1)} %get-tuple-element.47.refs_1_) | copy-start | bytes 786436
  132.7 18.5 %collective-permute-start.13 = (bf16[8,2,4,288,256]{4,3,2,1,0:T(8,128)(2,1)}, bf16[8,2,4,288,256]{4,3,2,1,0:T(8,128)(2,1)}, u32[]{:S(2)}, u32[]{:S(2)}) collective-permute-start(bf16[8,2,4,288,256]{4,3,2,1,0:T(8,128)(2,1)} %bitcast.13), channel_id=1, source_target_pairs={{0,8},{8,0},{1,9},{9,1},{2,10},{10,2},{3,11},{11,3},{4,12},{12,4},... | collective-permute-start | bytes 28311560 | tf_op jit(solution)/shard_map/ppermute | solution.py:23
  132.8 13.8 %collective-permute-start.9 = (bf16[64,2048]{1,0:T(8,128)(2,1)}, bf16[64,2048]{1,0:T(8,128)(2,1)S(1)}, u32[]{:S(2)}, u32[]{:S(2)}) collective-permute-start(bf16[64,2048]{1,0:T(8,128)(2,1)} %get-tuple-element.46.refs_0_), channel_id=1, source_target_pairs={{0,3},{1,0},{2,1},{3,2},{4,7},{5,4},{6,5},{7,6},{8,11},{9,8},{10,9... | collective-permute-start | bytes 786440 | tf_op jit(solution)/shard_map/ppermute | solution.py:447
  135.7 10.8 %collective-permute-start.8 = (bf16[64,2048]{1,0:T(8,128)(2,1)}, bf16[64,2048]{1,0:T(8,128)(2,1)S(1)}, u32[]{:S(2)}, u32[]{:S(2)}) collective-permute-start(bf16[64,2048]{1,0:T(8,128)(2,1)} %get-tuple-element.47.refs_1_), channel_id=1, source_target_pairs={{0,1},{1,2},{2,3},{3,0},{4,5},{5,6},{6,7},{7,4},{8,9},{9,10},{10,1... | collective-permute-start | bytes 786440 | tf_op jit(solution)/shard_map/ppermute | solution.py:446
  135.7 15.4 %collective-permute-start.11 = (bf16[64,2048]{1,0:T(8,128)(2,1)S(1)}, bf16[64,2048]{1,0:T(8,128)(2,1)S(1)}, u32[]{:S(2)}, u32[]{:S(2)}) collective-permute-start(bf16[64,2048]{1,0:T(8,128)(2,1)S(1)} %collective-permute-done.7.refs_2_), channel_id=1, source_target_pairs={{0,1},{1,2},{2,3},{3,0},{4,5},{5,6},{6,7},{7,4},{8,9},{9,10},{10,1... | collective-permute-start | bytes 786440 | tf_op jit(solution)/shard_map/ppermute | solution.py:448
  135.7 15.4 %collective-permute-start.12 = (bf16[64,2048]{1,0:T(8,128)(2,1)S(1)}, bf16[64,2048]{1,0:T(8,128)(2,1)S(1)}, u32[]{:S(2)}, u32[]{:S(2)}) collective-permute-start(bf16[64,2048]{1,0:T(8,128)(2,1)S(1)} %collective-permute-done.10.refs_5_), channel_id=1, source_target_pairs={{0,3},{1,0},{2,1},{3,2},{4,7},{5,4},{6,5},{7,6},{8,11},{9,8},{10,9... | collective-permute-start | bytes 786440 | tf_op jit(solution)/shard_map/ppermute | solution.py:449
  142.9 3.7 %copy-start = (bf16[3,8,96,2048]{3,2,1,0:T(8,128)(2,1)}, bf16[3,8,96,2048]{3,2,1,0:T(8,128)(2,1)S(1)}, u32[]{:S(2)}) copy-start(bf16[3,8,96,2048]{3,2,1,0:T(8,128)(2,1)S(1)} %load.1.refs_8_.own_ref) | copy-start | bytes 28311556
  151.1 15.1 %copy-start.1 = (bf16[3,8,96,2048]{3,2,1,0:T(8,128)(2,1)S(1)}, bf16[3,8,96,2048]{3,2,1,0:T(8,128)(2,1)}, u32[]{:S(2)}) copy-start(bf16[3,8,96,2048]{3,2,1,0:T(8,128)(2,1)} %copy-done) | copy-start | bytes 28311556
  162.6 3.6 %copy-start.2 = (bf16[3,8,96,2048]{3,2,1,0:T(8,128)(2,1)}, bf16[3,8,96,2048]{3,2,1,0:T(8,128)(2,1)S(1)}, u32[]{:S(2)}) copy-start(bf16[3,8,96,2048]{3,2,1,0:T(8,128)(2,1)S(1)} %get-tuple-element.54.oth_ref) | copy-start | bytes 28311556
  171.5 14.5 %collective-permute-start.14 = (bf16[64,2048]{1,0:T(8,128)(2,1)S(1)}, bf16[64,2048]{1,0:T(8,128)(2,1)S(1)}, u32[]{:S(2)}, u32[]{:S(2)}) collective-permute-start(bf16[64,2048]{1,0:T(8,128)(2,1)S(1)} %get-tuple-element.57), channel_id=1, source_target_pairs={{0,1},{1,2},{2,3},{3,0},{4,5},{5,6},{6,7},{7,4},{8,9},{9,10},{10,1... | collective-permute-start | bytes 786440 | tf_op jit(solution)/shard_map/ppermute | solution.py:458
  178.5 1.0 copy-start.4
  179.5 10.0 %collective-permute-start.18 = (bf16[64,2048]{1,0:T(8,128)(2,1)S(1)}, bf16[64,2048]{1,0:T(8,128)(2,1)S(1)}, u32[]{:S(2)}, u32[]{:S(2)}) collective-permute-start(bf16[64,2048]{1,0:T(8,128)(2,1)S(1)} %get-tuple-element.61), channel_id=1, source_target_pairs={{0,3},{1,0},{2,1},{3,2},{4,7},{5,4},{6,5},{7,6},{8,11},{9,8},{10,9... | collective-permute-start | bytes 786440 | tf_op jit(solution)/shard_map/ppermute | solution.py:459
  182.7 10.6 %collective-permute-start.16 = (bf16[64,2048]{1,0:T(8,128)(2,1)S(1)}, bf16[64,2048]{1,0:T(8,128)(2,1)S(1)}, u32[]{:S(2)}, u32[]{:S(2)}) collective-permute-start(bf16[64,2048]{1,0:T(8,128)(2,1)S(1)} %get-tuple-element.58), channel_id=1, source_target_pairs={{0,1},{1,2},{2,3},{3,0},{4,5},{5,6},{6,7},{7,4},{8,9},{9,10},{10,1... | collective-permute-start | bytes 786440 | tf_op jit(solution)/shard_map/ppermute | solution.py:464
  182.8 12.4 %collective-permute-start.17 = (bf16[64,2048]{1,0:T(8,128)(2,1)S(1)}, bf16[64,2048]{1,0:T(8,128)(2,1)S(1)}, u32[]{:S(2)}, u32[]{:S(2)}) collective-permute-start(bf16[64,2048]{1,0:T(8,128)(2,1)S(1)} %get-tuple-element.59), channel_id=1, source_target_pairs={{0,3},{1,0},{2,1},{3,2},{4,7},{5,4},{6,5},{7,6},{8,11},{9,8},{10,9... | collective-permute-start | bytes 786440 | tf_op jit(solution)/shard_map/ppermute | solution.py:465
  186.1 10.5 %collective-permute-start.15 = (bf16[64,2048]{1,0:T(8,128)(2,1)S(1)}, bf16[64,2048]{1,0:T(8,128)(2,1)S(1)}, u32[]{:S(2)}, u32[]{:S(2)}) collective-permute-start(bf16[64,2048]{1,0:T(8,128)(2,1)S(1)} %add_convert_fusion.1), channel_id=1, source_target_pairs={{0,1},{1,2},{2,3},{3,0},{4,5},{5,6},{6,7},{7,4},{8,9},{9,10},{10,1... | collective-permute-start | bytes 786440 | tf_op jit(solution)/shard_map/ppermute | solution.py:468
  189.6 9.2 %collective-permute-start.19 = (bf16[64,2048]{1,0:T(8,128)(2,1)S(1)}, bf16[64,2048]{1,0:T(8,128)(2,1)S(1)}, u32[]{:S(2)}, u32[]{:S(2)}) collective-permute-start(bf16[64,2048]{1,0:T(8,128)(2,1)S(1)} %add_convert_fusion), channel_id=1, source_target_pairs={{0,3},{1,0},{2,1},{3,2},{4,7},{5,4},{6,5},{7,6},{8,11},{9,8},{10,9... | collective-permute-start | bytes 786440 | tf_op jit(solution)/shard_map/ppermute | solution.py:469
  193.3 5.4 %copy-start.13 = (bf16[64,2048]{1,0:T(8,128)(2,1)}, bf16[64,2048]{1,0:T(8,128)(2,1)S(1)}, u32[]{:S(2)}) copy-start(bf16[64,2048]{1,0:T(8,128)(2,1)S(1)} %collective-permute-done.16.lb_ref) | copy-start | bytes 786436
  195.1 3.6 %copy-start.14 = (bf16[64,2048]{1,0:T(8,128)(2,1)}, bf16[64,2048]{1,0:T(8,128)(2,1)S(1)}, u32[]{:S(2)}) copy-start(bf16[64,2048]{1,0:T(8,128)(2,1)S(1)} %collective-permute-done.17.rt_ref) | copy-start | bytes 786436
  196.6 2.2 %copy-start.15 = (bf16[64,2048]{1,0:T(8,128)(2,1)}, bf16[64,2048]{1,0:T(8,128)(2,1)S(1)}, u32[]{:S(2)}) copy-start(bf16[64,2048]{1,0:T(8,128)(2,1)S(1)} %collective-permute-done.15.lt_ref) | copy-start | bytes 786436
  198.8 0.7 copy-start.16
Sparse Core Ops, SparseCore 0:
  39.8 85.8 all-gather.2

commit v8 on v4

--- a/solution.py
+++ b/solution.py
@@ -99,10 +99,11 @@
     )(core, tokens, own, oth, attn_gain[None], q_gain[None], key_gain[None], cs)
 
 
-def attend_kernel(q_ref, kv_ref, prior_ref, lo_ref, out_ref):
+def attend_kernel(half_ref, q_ref, kv_ref, prior_ref, lo_ref, out_ref):
     factor = HEAD ** (-0.5) * math.log2(math.e)
     nt = (((1,), (1,)), ((), ()))
-    for i in range(4):
+
+    def block(i):
         first = i * 256
         skip = 256 if i == 3 else 0
         count = first + 256
@@ -112,8 +113,10 @@
         near = (col >= lo) & (col <= row)
         prior_col = lax.broadcasted_iota(jnp.int32, (256, 512 - skip), 1) + (skip - 512)
         far = prior_col >= lo
-        for h in range(2):
-            q = q_ref[first : first + 256, h * 128 : h * 128 + 128]
+
+        def head(h, carry):
+            lanes = pl.ds(pl.multiple_of(h * 128, 128), 128)
+            q = q_ref[first : first + 256, lanes]
             s1 = lax.dot_general(q, kv_ref[0, :count], nt, preferred_element_type=F32)
             s0 = lax.dot_general(q, prior_ref[0, skip:], nt, preferred_element_type=F32)
             s1 = jnp.where(near, s1, -1e30)
@@ -128,22 +131,35 @@
             o = o + jnp.dot(p0, prior_ref[1, skip:], preferred_element_type=F32)
             o = o.astype(BF)
             for part in range(2):
-                block = 2 * i + part
-                out_ref[block % 4, block // 4, :, h * 128 : h * 128 + 128] = o[part * 128 : part * 128 + 128]
-
-
-def attend(q, kv, prior, lo):
+                out_ref[(2 * i + part) % 4, :, lanes] = o[part * 128 : part * 128 + 128]
+            return carry
+
+        lax.fori_loop(0, 2, head, 0)
+
+    @pl.when(half_ref[0] == 0)
+    def _():
+        block(0)
+        block(1)
+
+    @pl.when(half_ref[0] == 1)
+    def _():
+        block(2)
+        block(3)
+
+
+def attend(half, q, kv, prior, lo):
+    vm = pl.BlockSpec(memory_space=pltpu.VMEM)
     return pl.pallas_call(
         attend_kernel,
-        out_shape=jax.ShapeDtypeStruct((4, 2, 128, 256), BF),
+        in_specs=[pl.BlockSpec(memory_space=pltpu.SMEM)] + [vm] * 4,
+        out_shape=jax.ShapeDtypeStruct((4, 128, 256), BF),
         compiler_params=pltpu.CompilerParams(vmem_limit_bytes=40 << 20),
         name="attend",
-    )(q, kv, prior, lo)
-
-
-def out_kernel(at_ref, ctx_ref, own_ref, oth_ref, keep_ref, send_ref, w_ref, x_ref, sems):
-    core = at_ref[0]
-    xl = at_ref[1]
+    )(half, q, kv, prior, lo)
+
+
+def out_kernel(core_ref, ctx_ref, own_ref, oth_ref, out_ref, w_ref, sems):
+    core = core_ref[0]
 
     def each(act):
         def step(n, carry):
@@ -158,40 +174,28 @@
         lax.fori_loop(0, 32, step, 0)
 
     each(lambda c: c.start())
-    for s in range(4):
-        x_ref[:128, s * 256 : s * 256 + 256] = ctx_ref[s, xl]
-        x_ref[128:, s * 256 : s * 256 + 256] = ctx_ref[s, 1 - xl]
+    x = jnp.concatenate([ctx_ref[s] for s in range(4)], axis=1)
     each(lambda c: c.wait())
-    x = x_ref[...]
 
     def column(n, carry):
         at = pl.ds(pl.multiple_of(n * 512, 512), 512)
-        total = jnp.dot(x, w_ref[:, at], preferred_element_type=F32)
-        keep_ref[:, at] = total[:128]
-        send_ref[:, at] = total[128:].astype(BF)
+        out_ref[:, at] = jnp.dot(x, w_ref[:, at], preferred_element_type=F32).astype(out_ref.dtype)
         return carry
 
     lax.fori_loop(0, 4, column, 0)
 
 
-def out_project(at, ctx, own, oth):
+def out_project(core, ctx, own, oth, dtype):
     vm = pl.BlockSpec(memory_space=pltpu.VMEM)
     anywhere = pl.BlockSpec(memory_space=pl.ANY)
     return pl.pallas_call(
         out_kernel,
-        in_specs=[pl.BlockSpec(memory_space=pltpu.SMEM)] + [vm] + [anywhere] * 2,
-        out_shape=(
-            jax.ShapeDtypeStruct((128, 2048), F32),
-            jax.ShapeDtypeStruct((128, 2048), BF),
-        ),
-        scratch_shapes=[
-            pltpu.VMEM((1024, 2048), BF),
-            pltpu.VMEM((256, 1024), BF),
-            pltpu.SemaphoreType.DMA((2, 4, 8)),
-        ],
+        in_specs=[pl.BlockSpec(memory_space=pltpu.SMEM), vm, anywhere, anywhere],
+        out_shape=jax.ShapeDtypeStruct((128, 2048), dtype),
+        scratch_shapes=[pltpu.VMEM((1024, 2048), BF), pltpu.SemaphoreType.DMA((2, 4, 8))],
         compiler_params=pltpu.CompilerParams(vmem_limit_bytes=40 << 20),
         name="oproj",
-    )(at, ctx, own, oth)
+    )(core, ctx, own, oth)
 
 
 def fetcher(own_ref, oth_ref, w_ref, sems, y, first):
@@ -391,8 +395,9 @@
     freq = jnp.exp(jnp.arange(half, dtype=F32) * (-2.0 * math.log(1000000.0) / HEAD))
     angle = positions.astype(F32)[:, None] * freq[None, :]
     cs = jnp.concatenate([jnp.cos(angle), jnp.sin(angle)], axis=1)
-    cs, at_own, *parts = hold((cs, at_own, *parts))
-    mlp_own = lax.all_gather(join(parts), ("z", "xh", "xl"), axis=0, tiled=False).reshape(8, 2, 4, 288, 256)
+    group = join(parts)
+    cs, at_own, group = hold((cs, at_own, group))
+    mlp_own = lax.all_gather(group, ("z", "xh", "xl"), axis=0, tiled=False).reshape(8, 2, 4, 288, 256)
     lo = (jnp.arange(rows, dtype=jnp.int32) - positions)[:, None]
 
     at_oth = swap(at_own, "core")
@@ -400,14 +405,19 @@
     o_wide = jnp.broadcast_to(at_own[None, :, 512:], (4, 8, 256, 128))
     o_own = lax.all_to_all(o_wide, "y", split_axis=0, concat_axis=0, tiled=True)
 
-    q, cache, tail = project(core[None], tokens, at_own, at_oth, attn_gain, q_gain, key_norm_gain, cs)
+    rows_in = pltpu.with_memory_space_constraint(tokens, pltpu.HBM)
+    q, cache, tail = project(core[None], rows_in, at_own, at_oth, attn_gain, q_gain, key_norm_gain, cs)
     prior = lax.ppermute(tail, REQ, [(i - 1, i) for i in range(1, 16)])
-    ctx = attend(q, cache, prior, lo)
-    ctx, o_own = hold((ctx, o_own))
+    turn = lambda part: lax.all_to_all(part, "y", split_axis=0, concat_axis=0, tiled=True)
+    theirs = attend(1 - xl[None], q, cache, prior, lo)
+    _, q = hold((theirs, q))
+    mine = attend(xl[None], q, cache, prior, lo)
+    _, o_own = hold((mine, o_own))
     o_oth = swap(o_own, "core")
-    ctx = lax.all_to_all(ctx, "y", split_axis=0, concat_axis=0, tiled=True)
-    keep, send = out_project(jnp.stack([core, xl]), ctx, o_own, o_oth)
+    send = out_project(core[None], turn(theirs), o_own, o_oth, BF)
     got = swap(send, "xl")
+    _, mine = hold((send, mine))
+    keep = out_project(core[None], turn(mine), o_own, o_oth, F32)
 
     own_rows = lax.dynamic_slice_in_dim(tokens, (xl * 4 + y) * 128, 128, 0).astype(F32)
     resid = (own_rows + (keep + got.astype(F32))).astype(BF)
@@ -426,6 +436,7 @@
     via_left = lax.ppermute(top, "y", ring(1))
     via_right = lax.ppermute(bottom, "y", ring(3))
     keep, to_left, to_right = down(hidden, weight)
+    via_left, via_right = hold((via_left, via_right))
     to_right = jnp.concatenate([(to_right[:64].astype(F32) + via_left.astype(F32)).astype(BF), to_right[64:]])
     to_left = jnp.concatenate([to_left[:64], (to_left[64:].astype(F32) + via_right.astype(F32)).astype(BF)])
     from_left = lax.ppermute(to_right, "y", ring(1))

time: 206 us -> 200 us (0.971)
  waiting for transfers between devices: 100 us -> 77 us
  blocking collectives: 0 us -> 11.7 us
  Pallas kernels: 41.4 us -> 46.4 us
    ppermute x4, waiting for transfers between devices: 29.8 us -> 14.5 us  [swap(): return lax.ppermute(block, axis, [(0, 1), (1, 0)])]
    all_to_all x0 -> x1, blocking collectives: none -> 11.7 us  [per_device(): lax.all_to_all(part, 'y', split_axis=0, concat_axis=0, tiled=True)]
    all_to_all x1, waiting for transfers between devices: 10.1 us -> 6.64 us  [per_device(): lax.all_to_all(part, 'y', split_axis=0, concat_axis=0, tiled=True)]
    ppermute x1, waiting for transfers between devices: 2.98 us -> 0.01 us  [per_device(): via_right = lax.ppermute(bottom, 'y', ring(3))]
    ppermute x1, starting transfers between devices: 0.35 us -> 3.22 us  [per_device(): via_right = lax.ppermute(bottom, 'y', ring(3))]
    all_to_all x1, waiting for transfers between devices: 5.16 us -> 2.61 us  [per_device(): lax.all_to_all(packed, ('z', 'xh'), split_axis=0, concat_axis=0, tiled=True)]
    pallas_call x1 -> x2, Pallas kernels: 4.85 us -> 7.28 us  [out_project(): pl.pallas_call(out_kernel, in_specs=[pl.BlockSpec(memory_space=pltpu.SMEM...]
    ppermute x1, waiting for transfers between devices: 8.04 us -> 10.2 us  [per_device(): from_right = lax.ppermute(to_left, 'y', ring(3))]
  transfers between devices with their start and end apart: 20 -> 20, of which waited for: 16 -> 15; matrix products, arithmetic and copies ran while one was open for 3% -> 3% of each run, Pallas kernels for 12% -> 16%
where the time goes in v8:
time: 200 us; the launch traced here: 199 us
  waiting for transfers between devices  77 us (38%)
  Pallas kernels  46.4 us (23%)
  starting transfers between devices  34 us (17%)
  between operations  14.3 us (7%)
  blocking collectives  11.7 us (6%)
  local copies, waits for them, and re-layouts  10.9 us (5%)
  other arithmetic  5.02 us (3%)
    ppermute x4, waiting for transfers between devices, swap(): return lax.ppermute(block, axis, [(0, 1), (1, 0)])  14.5 us
    all_to_all x1, blocking collectives, per_device(): lax.all_to_all(part, 'y', split_axis=0, concat_axis=0, tiled=True)  11.7 us
    ppermute x1, waiting for transfers between devices, per_device(): right = lax.ppermute(mlp_in, 'y', ring(3))  10.5 us
    ppermute x1, waiting for transfers between devices, per_device(): from_right = lax.ppermute(to_left, 'y', ring(3))  10.2 us
    ppermute x1, waiting for transfers between devices, per_device(): prior = lax.ppermute(tail, REQ, [(i - 1, i) for i in range(1, 16)])  9.93 us
    pallas_call x1, Pallas kernels, gate_up(): pl.pallas_call(gate_kernel, in_specs=[pl.BlockSpec(memory_space=pltpu.SME...  8.54 us
    pallas_call x2, Pallas kernels, attend(): pl.pallas_call(attend_kernel, in_specs=[pl.BlockSpec(memory_space=pltpu.S...  8.18 us
    all_to_all x1, starting transfers between devices, per_device(): lax.all_to_all(packed, ('z', 'xh'), split_axis=0, concat_axis=0, tiled=True)  8.01 us
  transfers between devices with their start and end apart: 20, of which 15 were waited for; matrix products, arithmetic and copies ran while one was open for 3% of the time, Pallas kernels for 16%

profile of v8, /device:TPU:32, one launch (start us, length us, event | category | flops | bytes accessed | tf_op | source)
XLA Modules:
  0.0 199.3 jit_solution(5976640042209979883)
XLA Ops:
  7.2 2.3 %pack.1 = bf16[8,768,128]{2,1,0:T(8,128)(2,1)} custom-call(f32[128,256]{1,0:T(8,128)} %q_ref.1, f32[128,128]{1,0:T(8,128)} %k_ref.1, f32[128,128]{1,0:T(8,128)} %v_ref.1, f32[256,128]{1,0:T(8,128)} %o_ref.1), custom_call_target="tpu_custom_call" | custom-call | tf_op jit(solution)/shard_map/pack/pallas_call | solution.py:327
  9.5 8.0 %all-to-all-start = ((bf16[8,768,128]{2,1,0:T(8,128)(2,1)}), bf16[8,768,128]{2,1,0:T(8,128)(2,1)}, u32[]{:S(2)}, u32[]{:S(2)}) async-start(bf16[8,768,128]{2,1,0:T(8,128)(2,1)} %pack.1), calls=%async_computation | async-start | bytes 3145728 | tf_op jit(solution)/shard_map/all_to_all | solution.py:391
  17.5 2.3 %prep.1 = (bf16[288,256]{1,0:T(8,128)(2,1)}, bf16[288,256]{1,0:T(8,128)(2,1)}, bf16[288,256]{1,0:T(8,128)(2,1)}, bf16[288,256]{1,0:T(8,128)(2,1)}) custom-call(s32[1]{0:T(128)} %bitcast.2.y_ref, f32[256,384]{1,0:T(8,128)} %gate_ref.1, f32[256,384]{1,0:T(8,128)} %up_ref.1, f32[384,256]{1,0:T(8,128)} %down_ref.1), custom_call_target="tpu_custom_call" | custom-call | tf_op jit(solution)/shard_map/prep/pallas_call | solution.py:346
  19.9 3.0 %collective-permute-start = (bf16[288,256]{1,0:T(8,128)(2,1)}, bf16[288,256]{1,0:T(8,128)(2,1)S(1)}, u32[]{:S(2)}, u32[]{:S(2)}) collective-permute-start(bf16[288,256]{1,0:T(8,128)(2,1)} %get-tuple-element.27), channel_id=1, source_target_pairs={{0,3},{1,0},{2,1},{3,2},{4,7},{5,4},{6,5},{7,6},{8,11},{9,8},{10,9... | collective-permute-start | bytes 442376 | tf_op jit(solution)/shard_map/ppermute | solution.py:365
  23.5 1.0 collective-permute-start.2
  24.5 1.9 multiply_cosine_fusion
  26.6 2.3 %collective-permute-done.p1_ref = bf16[288,256]{1,0:T(8,128)(2,1)S(1)} collective-permute-done((bf16[288,256]{1,0:T(8,128)(2,1)}, bf16[288,256]{1,0:T(8,128)(2,1)S(1)}, u32[]{:S(2)}, u32[]{:S(2)}) %collective-permute-start) | collective-permute-done | bytes 147488 | tf_op jit(solution)/shard_map/ppermute | solution.py:365
  28.9 2.1 %collective-permute-done.1.p2_ref = bf16[288,256]{1,0:T(8,128)(2,1)S(1)} collective-permute-done((bf16[288,256]{1,0:T(8,128)(2,1)}, bf16[288,256]{1,0:T(8,128)(2,1)S(1)}, u32[]{:S(2)}, u32[]{:S(2)}) %collective-permute-start.1) | collective-permute-done | bytes 147488 | tf_op jit(solution)/shard_map/ppermute | solution.py:365
  31.0 1.5 collective-permute-done.2.p3_ref
  32.5 0.7 copy-done.10
  33.2 2.0 %join.1 = bf16[4,288,256]{2,1,0:T(8,128)(2,1)} custom-call(bf16[288,256]{1,0:T(8,128)(2,1)} %get-tuple-element.26.p0_ref, bf16[288,256]{1,0:T(8,128)(2,1)} %copy-done.8, bf16[288,256]{1,0:T(8,128)(2,1)} %copy-done.9, bf16[288,256]{1,0:T(8,128)(2,1)} %copy-done.10), custom_call_target="tpu_custom_call" | custom-call | tf_op jit(solution)/shard_map/join/pallas_call | solution.py:361
  35.1 2.6 %all-to-all-done.own_ref = bf16[8,768,128]{2,1,0:T(8,128)(2,1)} async-done(((bf16[8,768,128]{2,1,0:T(8,128)(2,1)}), bf16[8,768,128]{2,1,0:T(8,128)(2,1)}, u32[]{:S(2)}, u32[]{:S(2)}) %all-to-all-start) | async-done | bytes 1572896 | tf_op jit(solution)/shard_map/all_to_all | solution.py:391
  37.9 1.1 slice.21
  39.0 1.8 broadcast_in_dim.43
  40.8 4.6 %all-to-all-start.2 = ((bf16[4,8,256,128]{3,2,1,0:T(8,128)(2,1)}), bf16[4,8,256,128]{3,2,1,0:T(8,128)(2,1)S(1)}, u32[]{:S(2)}, u32[]{:S(2)}) async-start(bf16[4,8,256,128]{3,2,1,0:T(8,128)(2,1)} %broadcast_in_dim.43), calls=%async_computation.2 | async-start | bytes 4194304 | tf_op jit(solution)/shard_map/all_to_all | solution.py:406
  45.4 7.9 %qkv.1 = (bf16[1024,256]{1,0:T(8,128)(2,1)S(1)}, bf16[2,1024,128]{2,1,0:T(8,128)(2,1)}, bf16[2,512,128]{2,1,0:T(8,128)(2,1)}) custom-call(s32[1]{0:T(128)} %bitcast.core_ref, bf16[1024,2048]{1,0:T(8,128)(2,1)} %x_ref.1, bf16[8,768,128]{2,1,0:T(8,128)(2,1)} %all-to-all-done.own_ref, bf16[8,768,128]{2,1,0:T(8,128)(2,1)} %collective-permute-done.3.oth_ref, ...), custom_call_target="tpu_custom_call" | custom-call | tf_op jit(solution)/shard_map/qkv/pallas_call | solution.py:71
  53.3 2.1 %collective-permute-start.4 = (bf16[2,512,128]{2,1,0:T(8,128)(2,1)}, bf16[2,512,128]{2,1,0:T(8,128)(2,1)S(1)}, u32[]{:S(2)}, u32[]{:S(2)}) collective-permute-start(bf16[2,512,128]{2,1,0:T(8,128)(2,1)} %get-tuple-element.34), channel_id=1, source_target_pairs={{0,8},{8,16},{16,24},{24,32},{32,40},{40,48},{48,56},{56,64},{64,7... | collective-permute-start | bytes 786440 | tf_op jit(solution)/shard_map/ppermute | solution.py:410
  55.7 9.9 %collective-permute-done.4.prior_ref = bf16[2,512,128]{2,1,0:T(8,128)(2,1)S(1)} collective-permute-done((bf16[2,512,128]{2,1,0:T(8,128)(2,1)}, bf16[2,512,128]{2,1,0:T(8,128)(2,1)S(1)}, u32[]{:S(2)}, u32[]{:S(2)}) %collective-permute-start.4) | collective-permute-done | bytes 262176 | tf_op jit(solution)/shard_map/ppermute | solution.py:410
  65.6 1.0 copy-done.3
  66.7 4.2 %attend.2 = bf16[4,128,256]{2,1,0:T(8,128)(2,1)S(1)} custom-call(s32[1]{0:T(128)S(6)} %sub.6.half_ref, bf16[1024,256]{1,0:T(8,128)(2,1)S(1)} %get-tuple-element.35.q_ref, bf16[2,1024,128]{2,1,0:T(8,128)(2,1)S(1)} %copy-done.3, bf16[2,512,128]{2,1,0:T(8,128)(2,1)S(1)} %collective-permute-done.4.prior_ref, s32[1024,1]{1,0:T(8,128)S(1)} %copy.17.lo_ref), custom_call_target="tpu_custom_call" | custom-call | tf_op jit(solution)/shard_map/attend/pallas_call | solution.py:152
  70.9 0.7 copy-done.4
  71.5 4.0 %attend.3 = bf16[4,128,256]{2,1,0:T(8,128)(2,1)} custom-call(s32[1]{0:T(128)} %bitcast.1.half_ref, bf16[1024,256]{1,0:T(8,128)(2,1)S(1)} %get-tuple-element.35.q_ref, bf16[2,1024,128]{2,1,0:T(8,128)(2,1)S(1)} %copy-done.3, bf16[2,512,128]{2,1,0:T(8,128)(2,1)S(1)} %collective-permute-done.4.prior_ref, s32[1024,1]{1,0:T(8,128)S(1)} %copy.17.lo_ref), custom_call_target="tpu_custom_call" | custom-call | tf_op jit(solution)/shard_map/attend/pallas_call | solution.py:152
  75.6 11.7 %all_to_all.20.ctx_ref = bf16[4,128,256]{2,1,0:T(8,128)(2,1)S(1)} all-to-all(bf16[4,128,256]{2,1,0:T(8,128)(2,1)} %copy-done.4), channel_id=1, replica_groups=mesh['z'=4,'xh'=2,'core'=2,'xl'=2,'y'=4] {'y'}, dimensions={0} | all-to-all | bytes 524288 | tf_op jit(solution)/shard_map/all_to_all | solution.py:411
  87.3 3.6 %oproj.2 = bf16[128,2048]{1,0:T(8,128)(2,1)S(1)} custom-call(s32[1]{0:T(128)} %bitcast.core_ref, bf16[4,128,256]{2,1,0:T(8,128)(2,1)S(1)} %all_to_all.20.ctx_ref, bf16[4,8,256,128]{3,2,1,0:T(8,128)(2,1)S(1)} %all-to-all-done.2.own_ref, bf16[4,8,256,128]{3,2,1,0:T(8,128)(2,1)S(1)} %collective-permute-done.5.oth_ref), custom_call_target="tpu_custom_call" | custom-call | tf_op jit(solution)/shard_map/oproj/pallas_call | solution.py:191
  91.5 3.4 %all-to-all-start.3 = ((bf16[4,128,256]{2,1,0:T(8,128)(2,1)}), bf16[4,128,256]{2,1,0:T(8,128)(2,1)S(1)}, u32[]{:S(2)}, u32[]{:S(2)}) async-start(bf16[4,128,256]{2,1,0:T(8,128)(2,1)} %attend.3), calls=%async_computation.3 | async-start | bytes 524288 | tf_op jit(solution)/shard_map/all_to_all | solution.py:411
  94.9 6.6 %all-to-all-done.3.ctx_ref = bf16[4,128,256]{2,1,0:T(8,128)(2,1)S(1)} async-done(((bf16[4,128,256]{2,1,0:T(8,128)(2,1)}), bf16[4,128,256]{2,1,0:T(8,128)(2,1)S(1)}, u32[]{:S(2)}, u32[]{:S(2)}) %all-to-all-start.3) | async-done | bytes 262176 | tf_op jit(solution)/shard_map/all_to_all | solution.py:411
  101.5 1.6 copy-done.2
  103.1 3.6 %oproj.3 = f32[128,2048]{1,0:T(8,128)S(1)} custom-call(s32[1]{0:T(128)} %bitcast.core_ref, bf16[4,128,256]{2,1,0:T(8,128)(2,1)S(1)} %all-to-all-done.3.ctx_ref, bf16[4,8,256,128]{3,2,1,0:T(8,128)(2,1)S(1)} %all-to-all-done.2.own_ref, bf16[4,8,256,128]{3,2,1,0:T(8,128)(2,1)S(1)} %copy-done.2), custom_call_target="tpu_custom_call" | custom-call | tf_op jit(solution)/shard_map/oproj/pallas_call | solution.py:191
  106.8 9.7 %collective-permute-done.6 = bf16[128,2048]{1,0:T(8,128)(2,1)S(1)} collective-permute-done((bf16[128,2048]{1,0:T(8,128)(2,1)S(1)}, bf16[128,2048]{1,0:T(8,128)(2,1)S(1)}, u32[]{:S(2)}, u32[]{:S(2)}) %collective-permute-start.6) | collective-permute-done | bytes 524320 | tf_op jit(solution)/shard_map/ppermute | solution.py:23
  116.5 1.2 add_convert_fusion
  118.1 1.2 collective-permute-start.8
  119.3 0.9 collective-permute-start.7
  120.2 10.5 %collective-permute-done.8.x2_ref = bf16[128,2048]{1,0:T(8,128)(2,1)S(1)} collective-permute-done((bf16[128,2048]{1,0:T(8,128)(2,1)S(1)}, bf16[128,2048]{1,0:T(8,128)(2,1)S(1)}, u32[]{:S(2)}, u32[]{:S(2)}) %collective-permute-start.8) | collective-permute-done | bytes 524320 | tf_op jit(solution)/shard_map/ppermute | solution.py:429
  130.7 2.1 %collective-permute-done.7.x1_ref = bf16[128,2048]{1,0:T(8,128)(2,1)S(1)} collective-permute-done((bf16[128,2048]{1,0:T(8,128)(2,1)S(1)}, bf16[128,2048]{1,0:T(8,128)(2,1)S(1)}, u32[]{:S(2)}, u32[]{:S(2)}) %collective-permute-start.7) | collective-permute-done | bytes 524320 | tf_op jit(solution)/shard_map/ppermute | solution.py:428
  133.2 1.7 collective-permute-start.9
  134.9 6.7 %collective-permute-done.10.x4_ref = bf16[64,2048]{1,0:T(8,128)(2,1)S(1)} collective-permute-done((bf16[64,2048]{1,0:T(8,128)(2,1)S(1)}, bf16[64,2048]{1,0:T(8,128)(2,1)S(1)}, u32[]{:S(2)}, u32[]{:S(2)}) %collective-permute-start.10) | collective-permute-done | bytes 262176 | tf_op jit(solution)/shard_map/ppermute | solution.py:433
  141.6 1.3 collective-permute-done.9.x3_ref
  142.9 4.9 %collective-permute-done.11.oth_ref = bf16[8,2,4,288,256]{4,3,2,1,0:T(8,128)(2,1)} collective-permute-done((bf16[8,2,4,288,256]{4,3,2,1,0:T(8,128)(2,1)}, bf16[8,2,4,288,256]{4,3,2,1,0:T(8,128)(2,1)}, u32[]{:S(2)}, u32[]{:S(2)}) %collective-permute-start.11) | collective-permute-done | bytes 9437216 | tf_op jit(solution)/shard_map/ppermute | solution.py:23
  147.8 3.7 %copy-done = bf16[64,288,256]{2,1,0:T(8,128)(2,1)S(1)} copy-done((bf16[64,288,256]{2,1,0:T(8,128)(2,1)S(1)}, bf16[64,288,256]{2,1,0:T(8,128)(2,1)}, u32[]{:S(2)}) %copy-start) | copy-done | bytes 9437208
  151.4 8.5 %gate_up.1.hid_ref = bf16[512,1536]{1,0:T(8,128)(2,1)S(1)} custom-call(s32[1]{0:T(128)} %bitcast.2.y_ref, bf16[128,2048]{1,0:T(8,128)(2,1)S(1)} %fusion.2.x0_ref, bf16[128,2048]{1,0:T(8,128)(2,1)S(1)} %collective-permute-done.7.x1_ref, bf16[128,2048]{1,0:T(8,128)(2,1)S(1)} %collective-permute-done.8.x2_ref, ...), custom_call_target="tpu_custom_call" | custom-call | tf_op jit(solution)/shard_map/gate_up/pallas_call | solution.py:281
  160.0 4.6 %down_far.1 = (bf16[64,2048]{1,0:T(8,128)(2,1)S(1)}, bf16[64,2048]{1,0:T(8,128)(2,1)S(1)}, bf16[1,16,96,2048]{3,2,1,0:T(8,128)(2,1)S(1)}) custom-call(s32[1]{0:T(128)} %bitcast.2.y_ref, bf16[512,1536]{1,0:T(8,128)(2,1)S(1)} %gate_up.1.hid_ref, bf16[8,2,4,288,256]{4,3,2,1,0:T(8,128)(2,1)} %bitcast.9, bf16[8,2,4,288,256]{4,3,2,1,0:T(8,128)(2,1)} %collective-permute-done.11.oth_ref), custom_call_target="tpu_custom_call" | custom-call | tf_op jit(solution)/shard_map/down_far/pallas_call | solution.py:299
  164.7 3.2 %collective-permute-start.13 = (bf16[64,2048]{1,0:T(8,128)(2,1)S(1)}, bf16[64,2048]{1,0:T(8,128)(2,1)S(1)}, u32[]{:S(2)}, u32[]{:S(2)}) collective-permute-start(bf16[64,2048]{1,0:T(8,128)(2,1)S(1)} %get-tuple-element.46), channel_id=1, source_target_pairs={{0,3},{1,0},{2,1},{3,2},{4,7},{5,4},{6,5},{7,6},{8,11},{9,8},{10,9... | collective-permute-start | bytes 786440 | tf_op jit(solution)/shard_map/ppermute | solution.py:437
  167.9 3.2 %down.1 = (f32[128,2048]{1,0:T(8,128)S(1)}, bf16[128,2048]{1,0:T(8,128)(2,1)S(1)}, bf16[128,2048]{1,0:T(8,128)(2,1)S(1)}) custom-call(bf16[512,1536]{1,0:T(8,128)(2,1)S(1)} %gate_up.1.hid_ref, bf16[1,16,96,2048]{3,2,1,0:T(8,128)(2,1)S(1)} %get-tuple-element.42.w_ref), custom_call_target="tpu_custom_call" | custom-call | tf_op jit(solution)/shard_map/down/pallas_call | solution.py:311
  171.2 3.1 %collective-permute-done.12 = bf16[64,2048]{1,0:T(8,128)(2,1)S(1)} collective-permute-done((bf16[64,2048]{1,0:T(8,128)(2,1)S(1)}, bf16[64,2048]{1,0:T(8,128)(2,1)S(1)}, u32[]{:S(2)}, u32[]{:S(2)}) %collective-permute-start.12) | collective-permute-done | bytes 262176 | tf_op jit(solution)/shard_map/ppermute | solution.py:436
  174.4 3.0 %collective-permute-start.15 = (bf16[128,2048]{1,0:T(8,128)(2,1)S(1)}, bf16[128,2048]{1,0:T(8,128)(2,1)S(1)}, u32[]{:S(2)}, u32[]{:S(2)}) collective-permute-start(bf16[128,2048]{1,0:T(8,128)(2,1)S(1)} %pad_maximum_fusion.2), channel_id=1, source_target_pairs={{0,3},{1,0},{2,1},{3,2},{4,7},{5,4},{6,5},{7,6},{8,11},{9,8},{10,9... | collective-permute-start | bytes 1572872 | tf_op jit(solution)/shard_map/ppermute | solution.py:443
  177.6 10.2 %collective-permute-done.15 = bf16[128,2048]{1,0:T(8,128)(2,1)S(1)} collective-permute-done((bf16[128,2048]{1,0:T(8,128)(2,1)S(1)}, bf16[128,2048]{1,0:T(8,128)(2,1)S(1)}, u32[]{:S(2)}, u32[]{:S(2)}) %collective-permute-start.15) | collective-permute-done | bytes 524320 | tf_op jit(solution)/shard_map/ppermute | solution.py:443
  187.8 3.5 %collective-permute-done.14 = bf16[128,2048]{1,0:T(8,128)(2,1)S(1)} collective-permute-done((bf16[128,2048]{1,0:T(8,128)(2,1)S(1)}, bf16[128,2048]{1,0:T(8,128)(2,1)S(1)}, u32[]{:S(2)}, u32[]{:S(2)}) %collective-permute-start.14) | collective-permute-done | bytes 524320 | tf_op jit(solution)/shard_map/ppermute | solution.py:442
  191.3 1.1 fusion.3
  (51 shorter events, 3.0 us)
Async XLA Ops:
  9.5 15.0 %copy-start.12 = (s32[1024]{0:T(1024)S(1)}, s32[1024]{0:T(1024)}, u32[]{:S(2)}) copy-start(s32[1024]{0:T(1024)} %param.15) | copy-start | bytes 12292
  9.5 28.3 %all-to-all-start = ((bf16[8,768,128]{2,1,0:T(8,128)(2,1)}), bf16[8,768,128]{2,1,0:T(8,128)(2,1)}, u32[]{:S(2)}, u32[]{:S(2)}) async-start(bf16[8,768,128]{2,1,0:T(8,128)(2,1)} %pack.1), calls=%async_computation | async-start | bytes 3145728 | tf_op jit(solution)/shard_map/all_to_all | solution.py:391
  17.5 115.3 %all-gather.3.cloned.1.call-start = ((), (), s32[]{:S(2)}) async-start(), calls=%async_computation.4 | async-start | bytes 10027008 | tf_op jit(solution)/shard_map/all_gather | solution.py:400
  19.9 9.0 %collective-permute-start = (bf16[288,256]{1,0:T(8,128)(2,1)}, bf16[288,256]{1,0:T(8,128)(2,1)S(1)}, u32[]{:S(2)}, u32[]{:S(2)}) collective-permute-start(bf16[288,256]{1,0:T(8,128)(2,1)} %get-tuple-element.27), channel_id=1, source_target_pairs={{0,3},{1,0},{2,1},{3,2},{4,7},{5,4},{6,5},{7,6},{8,11},{9,8},{10,9... | collective-permute-start | bytes 442376 | tf_op jit(solution)/shard_map/ppermute | solution.py:365
  22.9 8.1 %collective-permute-start.1 = (bf16[288,256]{1,0:T(8,128)(2,1)}, bf16[288,256]{1,0:T(8,128)(2,1)S(1)}, u32[]{:S(2)}, u32[]{:S(2)}) collective-permute-start(bf16[288,256]{1,0:T(8,128)(2,1)} %get-tuple-element.28), channel_id=1, source_target_pairs={{0,2},{1,3},{2,0},{3,1},{4,6},{5,7},{6,4},{7,5},{8,10},{9,11},{10,... | collective-permute-start | bytes 442376 | tf_op jit(solution)/shard_map/ppermute | solution.py:365
  23.5 9.0 %collective-permute-start.2 = (bf16[288,256]{1,0:T(8,128)(2,1)}, bf16[288,256]{1,0:T(8,128)(2,1)S(1)}, u32[]{:S(2)}, u32[]{:S(2)}) collective-permute-start(bf16[288,256]{1,0:T(8,128)(2,1)} %get-tuple-element.29), channel_id=1, source_target_pairs={{0,1},{1,2},{2,3},{3,0},{4,5},{5,6},{6,7},{7,4},{8,9},{9,10},{10,1... | collective-permute-start | bytes 442376 | tf_op jit(solution)/shard_map/ppermute | solution.py:365
  28.9 3.6 %copy-start.8 = (bf16[288,256]{1,0:T(8,128)(2,1)}, bf16[288,256]{1,0:T(8,128)(2,1)S(1)}, u32[]{:S(2)}) copy-start(bf16[288,256]{1,0:T(8,128)(2,1)S(1)} %collective-permute-done.p1_ref) | copy-start | bytes 442372
  31.0 1.5 copy-start.9
  32.5 0.7 copy-start.10
  37.8 7.6 %collective-permute-start.3 = (bf16[8,768,128]{2,1,0:T(8,128)(2,1)}, bf16[8,768,128]{2,1,0:T(8,128)(2,1)}, u32[]{:S(2)}, u32[]{:S(2)}) collective-permute-start(bf16[8,768,128]{2,1,0:T(8,128)(2,1)} %all-to-all-done.own_ref), channel_id=1, source_target_pairs={{0,8},{8,0},{1,9},{9,1},{2,10},{10,2},{3,11},{11,3},{4,12},{12,4},... | collective-permute-start | bytes 4718600 | tf_op jit(solution)/shard_map/ppermute | solution.py:23
  40.8 4.6 %copy-start.5 = (f32[2048]{0:T(1024)S(1)}, f32[2048]{0:T(1024)}, u32[]{:S(2)}) copy-start(f32[2048]{0:T(1024)} %param.16) | copy-start | bytes 24580
  40.8 4.6 %copy-start.6 = (f32[128]{0:T(128)S(1)}, f32[128]{0:T(128)}, u32[]{:S(2)}) copy-start(f32[128]{0:T(128)} %param.18) | copy-start | bytes 1540
  40.8 4.6 %copy-start.7 = (f32[128]{0:T(128)S(1)}, f32[128]{0:T(128)}, u32[]{:S(2)}) copy-start(f32[128]{0:T(128)} %param.19) | copy-start | bytes 1540
  40.8 34.8 %all-to-all-start.2 = ((bf16[4,8,256,128]{3,2,1,0:T(8,128)(2,1)}), bf16[4,8,256,128]{3,2,1,0:T(8,128)(2,1)S(1)}, u32[]{:S(2)}, u32[]{:S(2)}) async-start(bf16[4,8,256,128]{3,2,1,0:T(8,128)(2,1)} %broadcast_in_dim.43), calls=%async_computation.2 | async-start | bytes 4194304 | tf_op jit(solution)/shard_map/all_to_all | solution.py:406
  53.3 12.3 %collective-permute-start.4 = (bf16[2,512,128]{2,1,0:T(8,128)(2,1)}, bf16[2,512,128]{2,1,0:T(8,128)(2,1)S(1)}, u32[]{:S(2)}, u32[]{:S(2)}) collective-permute-start(bf16[2,512,128]{2,1,0:T(8,128)(2,1)} %get-tuple-element.34), channel_id=1, source_target_pairs={{0,8},{8,16},{16,24},{24,32},{32,40},{40,48},{48,56},{56,64},{64,7... | collective-permute-start | bytes 786440 | tf_op jit(solution)/shard_map/ppermute | solution.py:410
  65.6 1.0 copy-start.3
  70.8 0.7 copy-start.4
  75.6 11.7 %collective-permute-start.5 = (bf16[4,8,256,128]{3,2,1,0:T(8,128)(2,1)S(1)}, bf16[4,8,256,128]{3,2,1,0:T(8,128)(2,1)S(1)}, u32[]{:S(2)}, u32[]{:S(2)}) collective-permute-start(bf16[4,8,256,128]{3,2,1,0:T(8,128)(2,1)S(1)} %all-to-all-done.2.own_ref), channel_id=1, source_target_pairs={{0,8},{8,0},{1,9},{9,1},{2,10},{10,2},{3,11},{11,3},{4,12},{12,4},... | collective-permute-start | bytes 6291464 | tf_op jit(solution)/shard_map/ppermute | solution.py:23
  87.3 3.6 %copy-start.1 = (bf16[4,8,256,128]{3,2,1,0:T(8,128)(2,1)}, bf16[4,8,256,128]{3,2,1,0:T(8,128)(2,1)S(1)}, u32[]{:S(2)}) copy-start(bf16[4,8,256,128]{3,2,1,0:T(8,128)(2,1)S(1)} %collective-permute-done.5.oth_ref) | copy-start | bytes 6291460
  90.9 25.5 %collective-permute-start.6 = (bf16[128,2048]{1,0:T(8,128)(2,1)S(1)}, bf16[128,2048]{1,0:T(8,128)(2,1)S(1)}, u32[]{:S(2)}, u32[]{:S(2)}) collective-permute-start(bf16[128,2048]{1,0:T(8,128)(2,1)S(1)} %oproj.2), channel_id=1, source_target_pairs={{0,4},{4,0},{1,5},{5,1},{2,6},{6,2},{3,7},{7,3},{8,12},{12,8},{9,1... | collective-permute-start | bytes 1572872 | tf_op jit(solution)/shard_map/ppermute | solution.py:23
  91.5 10.1 %all-to-all-start.3 = ((bf16[4,128,256]{2,1,0:T(8,128)(2,1)}), bf16[4,128,256]{2,1,0:T(8,128)(2,1)S(1)}, u32[]{:S(2)}, u32[]{:S(2)}) async-start(bf16[4,128,256]{2,1,0:T(8,128)(2,1)} %attend.3), calls=%async_computation.3 | async-start | bytes 524288 | tf_op jit(solution)/shard_map/all_to_all | solution.py:411
  101.5 1.6 copy-start.2
  106.8 11.1 %copy-start.11 = (f32[2048]{0:T(1024)S(1)}, f32[2048]{0:T(1024)}, u32[]{:S(2)}) copy-start(f32[2048]{0:T(1024)} %param.17) | copy-start | bytes 24580
  118.1 12.6 %collective-permute-start.8 = (bf16[128,2048]{1,0:T(8,128)(2,1)S(1)}, bf16[128,2048]{1,0:T(8,128)(2,1)S(1)}, u32[]{:S(2)}, u32[]{:S(2)}) collective-permute-start(bf16[128,2048]{1,0:T(8,128)(2,1)S(1)} %fusion.2.x0_ref), channel_id=1, source_target_pairs={{0,3},{1,0},{2,1},{3,2},{4,7},{5,4},{6,5},{7,6},{8,11},{9,8},{10,9... | collective-permute-start | bytes 1572872 | tf_op jit(solution)/shard_map/ppermute | solution.py:429
  119.3 13.4 %collective-permute-start.7 = (bf16[128,2048]{1,0:T(8,128)(2,1)S(1)}, bf16[128,2048]{1,0:T(8,128)(2,1)S(1)}, u32[]{:S(2)}, u32[]{:S(2)}) collective-permute-start(bf16[128,2048]{1,0:T(8,128)(2,1)S(1)} %fusion.2.x0_ref), channel_id=1, source_target_pairs={{0,1},{1,2},{2,3},{3,0},{4,5},{5,6},{6,7},{7,4},{8,9},{9,10},{10,1... | collective-permute-start | bytes 1572872 | tf_op jit(solution)/shard_map/ppermute | solution.py:428
  132.8 15.0 %collective-permute-start.11 = (bf16[8,2,4,288,256]{4,3,2,1,0:T(8,128)(2,1)}, bf16[8,2,4,288,256]{4,3,2,1,0:T(8,128)(2,1)}, u32[]{:S(2)}, u32[]{:S(2)}) collective-permute-start(bf16[8,2,4,288,256]{4,3,2,1,0:T(8,128)(2,1)} %bitcast.8), channel_id=1, source_target_pairs={{0,8},{8,0},{1,9},{9,1},{2,10},{10,2},{3,11},{11,3},{4,12},{12,4},... | collective-permute-start | bytes 28311560 | tf_op jit(solution)/shard_map/ppermute | solution.py:23
  132.8 8.8 %collective-permute-start.10 = (bf16[64,2048]{1,0:T(8,128)(2,1)S(1)}, bf16[64,2048]{1,0:T(8,128)(2,1)S(1)}, u32[]{:S(2)}, u32[]{:S(2)}) collective-permute-start(bf16[64,2048]{1,0:T(8,128)(2,1)S(1)} %slice.23), channel_id=1, source_target_pairs={{0,3},{1,0},{2,1},{3,2},{4,7},{5,4},{6,5},{7,6},{8,11},{9,8},{10,9... | collective-permute-start | bytes 786440 | tf_op jit(solution)/shard_map/ppermute | solution.py:433
  133.2 9.7 %collective-permute-start.9 = (bf16[64,2048]{1,0:T(8,128)(2,1)S(1)}, bf16[64,2048]{1,0:T(8,128)(2,1)S(1)}, u32[]{:S(2)}, u32[]{:S(2)}) collective-permute-start(bf16[64,2048]{1,0:T(8,128)(2,1)S(1)} %slice.22), channel_id=1, source_target_pairs={{0,1},{1,2},{2,3},{3,0},{4,5},{5,6},{6,7},{7,4},{8,9},{9,10},{10,1... | collective-permute-start | bytes 786440 | tf_op jit(solution)/shard_map/ppermute | solution.py:432
  147.8 3.7 %copy-start = (bf16[64,288,256]{2,1,0:T(8,128)(2,1)S(1)}, bf16[64,288,256]{2,1,0:T(8,128)(2,1)}, u32[]{:S(2)}) copy-start(bf16[64,288,256]{2,1,0:T(8,128)(2,1)} %all-gather.3.cloned.1.call-done) | copy-start | bytes 28311556
  164.6 9.6 %collective-permute-start.12 = (bf16[64,2048]{1,0:T(8,128)(2,1)S(1)}, bf16[64,2048]{1,0:T(8,128)(2,1)S(1)}, u32[]{:S(2)}, u32[]{:S(2)}) collective-permute-start(bf16[64,2048]{1,0:T(8,128)(2,1)S(1)} %get-tuple-element.45), channel_id=1, source_target_pairs={{0,1},{1,2},{2,3},{3,0},{4,5},{5,6},{6,7},{7,4},{8,9},{9,10},{10,1... | collective-permute-start | bytes 786440 | tf_op jit(solution)/shard_map/ppermute | solution.py:436
  164.7 9.6 %collective-permute-start.13 = (bf16[64,2048]{1,0:T(8,128)(2,1)S(1)}, bf16[64,2048]{1,0:T(8,128)(2,1)S(1)}, u32[]{:S(2)}, u32[]{:S(2)}) collective-permute-start(bf16[64,2048]{1,0:T(8,128)(2,1)S(1)} %get-tuple-element.46), channel_id=1, source_target_pairs={{0,3},{1,0},{2,1},{3,2},{4,7},{5,4},{6,5},{7,6},{8,11},{9,8},{10,9... | collective-permute-start | bytes 786440 | tf_op jit(solution)/shard_map/ppermute | solution.py:437
  174.4 13.4 %collective-permute-start.15 = (bf16[128,2048]{1,0:T(8,128)(2,1)S(1)}, bf16[128,2048]{1,0:T(8,128)(2,1)S(1)}, u32[]{:S(2)}, u32[]{:S(2)}) collective-permute-start(bf16[128,2048]{1,0:T(8,128)(2,1)S(1)} %pad_maximum_fusion.2), channel_id=1, source_target_pairs={{0,3},{1,0},{2,1},{3,2},{4,7},{5,4},{6,5},{7,6},{8,11},{9,8},{10,9... | collective-permute-start | bytes 1572872 | tf_op jit(solution)/shard_map/ppermute | solution.py:443
  177.5 13.8 %collective-permute-start.14 = (bf16[128,2048]{1,0:T(8,128)(2,1)S(1)}, bf16[128,2048]{1,0:T(8,128)(2,1)S(1)}, u32[]{:S(2)}, u32[]{:S(2)}) collective-permute-start(bf16[128,2048]{1,0:T(8,128)(2,1)S(1)} %pad_maximum_fusion.1), channel_id=1, source_target_pairs={{0,1},{1,2},{2,3},{3,0},{4,5},{5,6},{6,7},{7,4},{8,9},{9,10},{10,1... | collective-permute-start | bytes 1572872 | tf_op jit(solution)/shard_map/ppermute | solution.py:442
Sparse Core Ops, SparseCore 0:
  37.9 85.7 all-gather.2

commit v9 on v8

--- a/solution.py
+++ b/solution.py
@@ -94,9 +94,28 @@
             jax.ShapeDtypeStruct((2, rows, 128), BF),
             jax.ShapeDtypeStruct((2, rows // 2, 128), BF),
         ),
-        compiler_params=pltpu.CompilerParams(vmem_limit_bytes=40 << 20),
+        compiler_params=pltpu.CompilerParams(vmem_limit_bytes=24 << 20),
         name="qkv",
     )(core, tokens, own, oth, attn_gain[None], q_gain[None], key_gain[None], cs)
+
+
+def widen_kernel(src_ref, out_ref, sems):
+    copies = [pltpu.make_async_copy(src_ref.at[:, 512:], out_ref.at[k], sems.at[k]) for k in range(4)]
+    for copy in copies:
+        copy.start()
+    for copy in copies:
+        copy.wait()
+
+
+def widen(gathered):
+    return pl.pallas_call(
+        widen_kernel,
+        in_specs=[pl.BlockSpec(memory_space=pl.ANY)],
+        out_specs=pl.BlockSpec(memory_space=pl.ANY),
+        out_shape=jax.ShapeDtypeStruct((4, 8, 256, 128), BF),
+        scratch_shapes=[pltpu.SemaphoreType.DMA((4,))],
+        name="widen",
+    )(gathered)
 
 
 def attend_kernel(half_ref, q_ref, kv_ref, prior_ref, lo_ref, out_ref):
@@ -153,7 +172,7 @@
         attend_kernel,
         in_specs=[pl.BlockSpec(memory_space=pltpu.SMEM)] + [vm] * 4,
         out_shape=jax.ShapeDtypeStruct((4, 128, 256), BF),
-        compiler_params=pltpu.CompilerParams(vmem_limit_bytes=40 << 20),
+        compiler_params=pltpu.CompilerParams(vmem_limit_bytes=20 << 20),
         name="attend",
     )(half, q, kv, prior, lo)
 
@@ -193,7 +212,7 @@
         in_specs=[pl.BlockSpec(memory_space=pltpu.SMEM), vm, anywhere, anywhere],
         out_shape=jax.ShapeDtypeStruct((128, 2048), dtype),
         scratch_shapes=[pltpu.VMEM((1024, 2048), BF), pltpu.SemaphoreType.DMA((2, 4, 8))],
-        compiler_params=pltpu.CompilerParams(vmem_limit_bytes=40 << 20),
+        compiler_params=pltpu.CompilerParams(vmem_limit_bytes=14 << 20),
         name="oproj",
     )(core, ctx, own, oth)
 
@@ -219,37 +238,33 @@
     return each
 
 
-def gate_kernel(y_ref, x0_ref, x1_ref, x2_ref, x3_ref, x4_ref, own_ref, oth_ref, hid_ref, w_ref, x_ref, sems):
+def gate_kernel(y_ref, x0_ref, x1_ref, x2_ref, x3_ref, x4_ref, src_ref, hid_ref, w_ref, x_ref, sems):
     nt = (((1,), (1,)), ((), ()))
-    each = fetcher(own_ref, oth_ref, w_ref, sems, y_ref[0], 0)
+    each = fetcher(src_ref, src_ref, w_ref, sems, y_ref[0], 0)
     each(0, 2, lambda c: c.start())
-    each(1, 2, lambda c: c.start())
     x_ref[0:128] = x0_ref[...]
     x_ref[128:256] = x1_ref[...]
     x_ref[256:384] = x2_ref[...]
     x_ref[384:448] = x3_ref[...]
     x_ref[448:512] = x4_ref[...]
     x = x_ref[...]
-
-    for c in range(2):
-        each(c, 2, lambda copy: copy.wait())
-        gate_w = w_ref[0, c * 8 : c * 8 + 8].reshape(768, 2048)
-        up_w = w_ref[1, c * 8 : c * 8 + 8].reshape(768, 2048)
-        for t in range(3):
-            gate = lax.dot_general(x, gate_w[t * 256 : t * 256 + 256], nt, preferred_element_type=F32)
-            upper = lax.dot_general(x, up_w[t * 256 : t * 256 + 256], nt, preferred_element_type=F32)
-            hidden = gate / (1.0 + jnp.exp(-gate)) * upper
-            at = c * 768 + t * 256
-            hid_ref[:, at : at + 256] = hidden.astype(BF)
-
-
-def far_kernel(y_ref, hid_ref, own_ref, oth_ref, top_ref, bottom_ref, w_ref, sems):
+    each(0, 2, lambda copy: copy.wait())
+    gate_w = w_ref[0].reshape(768, 2048)
+    up_w = w_ref[1].reshape(768, 2048)
+    for t in range(3):
+        gate = lax.dot_general(x, gate_w[t * 256 : t * 256 + 256], nt, preferred_element_type=F32)
+        upper = lax.dot_general(x, up_w[t * 256 : t * 256 + 256], nt, preferred_element_type=F32)
+        hidden = gate / (1.0 + jnp.exp(-gate)) * upper
+        hid_ref[:, t * 256 : t * 256 + 256] = hidden.astype(BF)
+
+
+def far_kernel(y_ref, hid0_ref, hid1_ref, own_ref, oth_ref, top_ref, bottom_ref, w_ref, sems):
     each = fetcher(own_ref, oth_ref, w_ref, sems, y_ref[0], 192)
     for c in range(2):
         each(c, 1, lambda copy: copy.start())
     for c in range(2):
         each(c, 1, lambda copy: copy.wait())
-    hid = hid_ref[384:]
+    hid = jnp.concatenate([hid0_ref[384:], hid1_ref[384:]], axis=1)
 
     def column(n, carry):
         at = pl.ds(pl.multiple_of(n * 512, 512), 512)
@@ -261,8 +276,8 @@
     lax.fori_loop(0, 4, column, 0)
 
 
-def down_kernel(hid_ref, w_ref, keep_ref, left_ref, right_ref):
-    hid = hid_ref[:384]
+def down_kernel(hid0_ref, hid1_ref, w_ref, keep_ref, left_ref, right_ref):
+    hid = jnp.concatenate([hid0_ref[:384], hid1_ref[:384]], axis=1)
 
     def column(n, carry):
         at = pl.ds(pl.multiple_of(n * 512, 512), 512)
@@ -275,21 +290,21 @@
     lax.fori_loop(0, 4, column, 0)
 
 
-def gate_up(y, pieces, own, oth):
+def gate_up(y, pieces, src):
     vm = pl.BlockSpec(memory_space=pltpu.VMEM)
     hbm = pl.BlockSpec(memory_space=pltpu.HBM)
     return pl.pallas_call(
         gate_kernel,
-        in_specs=[pl.BlockSpec(memory_space=pltpu.SMEM)] + [vm] * 5 + [hbm] * 2,
-        out_shape=jax.ShapeDtypeStruct((512, 1536), BF),
+        in_specs=[pl.BlockSpec(memory_space=pltpu.SMEM)] + [vm] * 5 + [hbm],
+        out_shape=jax.ShapeDtypeStruct((512, 768), BF),
         scratch_shapes=[
-            pltpu.VMEM((2, 16, 96, 2048), BF),
+            pltpu.VMEM((2, 8, 96, 2048), BF),
             pltpu.VMEM((512, 2048), BF),
-            pltpu.SemaphoreType.DMA((2, 2, 8)),
+            pltpu.SemaphoreType.DMA((2, 1, 8)),
         ],
-        compiler_params=pltpu.CompilerParams(vmem_limit_bytes=40 << 20),
+        compiler_params=pltpu.CompilerParams(vmem_limit_bytes=18 << 20),
         name="gate_up",
-    )(y, *pieces, own, oth)
+    )(y, *pieces, src)
 
 
 def down_far(y, hidden, own, oth):
@@ -298,12 +313,12 @@
     half = jax.ShapeDtypeStruct((64, 2048), BF)
     return pl.pallas_call(
         far_kernel,
-        in_specs=[pl.BlockSpec(memory_space=pltpu.SMEM), vm] + [hbm] * 2,
+        in_specs=[pl.BlockSpec(memory_space=pltpu.SMEM), vm, vm] + [hbm] * 2,
         out_shape=(half, half, jax.ShapeDtypeStruct((1, 16, 96, 2048), BF)),
         scratch_shapes=[pltpu.SemaphoreType.DMA((1, 2, 8))],
-        compiler_params=pltpu.CompilerParams(vmem_limit_bytes=40 << 20),
+        compiler_params=pltpu.CompilerParams(vmem_limit_bytes=14 << 20),
         name="down_far",
-    )(y, hidden, own, oth)
+    )(y, *hidden, own, oth)
 
 
 def down(hidden, weight):
@@ -311,9 +326,9 @@
     return pl.pallas_call(
         down_kernel,
         out_shape=(jax.ShapeDtypeStruct((128, 2048), F32), part, part),
-        compiler_params=pltpu.CompilerParams(vmem_limit_bytes=40 << 20),
+        compiler_params=pltpu.CompilerParams(vmem_limit_bytes=14 << 20),
         name="down",
-    )(hidden, weight)
+    )(*hidden, weight)
 
 
 def pack_kernel(q_ref, k_ref, v_ref, o_ref, out_ref):
@@ -402,8 +417,7 @@
 
     at_oth = swap(at_own, "core")
 
-    o_wide = jnp.broadcast_to(at_own[None, :, 512:], (4, 8, 256, 128))
-    o_own = lax.all_to_all(o_wide, "y", split_axis=0, concat_axis=0, tiled=True)
+    o_own = lax.all_to_all(widen(at_own), "y", split_axis=0, concat_axis=0, tiled=True)
 
     rows_in = pltpu.with_memory_space_constraint(tokens, pltpu.HBM)
     q, cache, tail = project(core[None], rows_in, at_own, at_oth, attn_gain, q_gain, key_norm_gain, cs)
@@ -431,7 +445,11 @@
     mlp_oth = swap(mlp_own, "core")
     far_top = lax.ppermute(left[:64], "y", ring(1))
     far_bottom = lax.ppermute(right[64:], "y", ring(3))
-    hidden = gate_up(y[None], (mlp_in, left, right, far_top, far_bottom), mlp_own, mlp_oth)
+    pieces = (mlp_in, left, right, far_top, far_bottom)
+    mlp_own = pltpu.with_memory_space_constraint(mlp_own, pltpu.HBM)
+    first = gate_up(y[None], pieces, mlp_own)
+    first, mlp_oth = hold((first, mlp_oth))
+    hidden = (first, gate_up(y[None], pieces, mlp_oth))
     top, bottom, weight = down_far(y[None], hidden, mlp_own, mlp_oth)
     via_left = lax.ppermute(top, "y", ring(1))
     via_right = lax.ppermute(bottom, "y", ring(3))

time: 200 us -> 242 us (1.21)
  Pallas kernels: 46.4 us -> 113 us
  waiting for transfers between devices: 77 us -> 58.5 us
  local copies, waits for them, and re-layouts: 10.9 us -> 4.31 us
    pallas_call x0 -> x1, Pallas kernels: none -> 64.7 us  [widen(): pl.pallas_call(widen_kernel, in_specs=[pl.BlockSpec(memory_space=pl.ANY)]...]
    ppermute x4, waiting for transfers between devices: 14.5 us -> 0.01 us  [swap(): return lax.ppermute(block, axis, [(0, 1), (1, 0)])]
    unnamed x26 -> x24, local copies, waits for them, and re-layouts: 7.71 us -> 4.01 us
    pallas_call x1 -> x2, Pallas kernels: 8.54 us -> 11.1 us  [gate_up(): pl.pallas_call(gate_kernel, in_specs=[pl.BlockSpec(memory_space=pltpu.SME...]
  transfers between devices with their start and end apart: 20 -> 20, of which waited for: 15 -> 13; matrix products, arithmetic and copies ran while one was open for 3% -> 2% of each run, Pallas kernels for 16% -> 42%
where the time goes in v9:
time: 242 us; the launch traced here: 241 us
  Pallas kernels  113 us (47%)
  waiting for transfers between devices  58.5 us (24%)
  starting transfers between devices  34.6 us (14%)
  between operations  14.3 us (6%)
  blocking collectives  12.1 us (5%)
  other arithmetic  5.07 us (2%)
  local copies, waits for them, and re-layouts  4.31 us (2%)
    pallas_call x1, Pallas kernels, widen(): pl.pallas_call(widen_kernel, in_specs=[pl.BlockSpec(memory_space=pl.ANY)]...  64.7 us
    all_to_all x1, blocking collectives, per_device(): lax.all_to_all(part, 'y', split_axis=0, concat_axis=0, tiled=True)  12.1 us
    pallas_call x2, Pallas kernels, gate_up(): pl.pallas_call(gate_kernel, in_specs=[pl.BlockSpec(memory_space=pltpu.SME...  11.1 us
    ppermute x1, waiting for transfers between devices, per_device(): right = lax.ppermute(mlp_in, 'y', ring(3))  9.78 us
    ppermute x1, waiting for transfers between devices, per_device(): from_right = lax.ppermute(to_left, 'y', ring(3))  9.51 us
    pallas_call x2, Pallas kernels, attend(): pl.pallas_call(attend_kernel, in_specs=[pl.BlockSpec(memory_space=pltpu.S...  8.18 us
    all_to_all x1, starting transfers between devices, per_device(): lax.all_to_all(packed, ('z', 'xh'), split_axis=0, concat_axis=0, tiled=True)  8.01 us
    ppermute x1, waiting for transfers between devices, per_device(): prior = lax.ppermute(tail, REQ, [(i - 1, i) for i in range(1, 16)])  7.94 us
  transfers between devices with their start and end apart: 20, of which 13 were waited for; matrix products, arithmetic and copies ran while one was open for 2% of the time, Pallas kernels for 42%

profile of v9, /device:TPU:32, one launch (start us, length us, event | category | flops | bytes accessed | tf_op | source)
XLA Modules:
  0.0 241.5 jit_solution(1062885667142219941)
XLA Ops:
  7.2 2.3 pack.1
  9.5 8.0 %all-to-all-start = ((bf16[8,768,128]{2,1,0:T(8,128)(2,1)}), bf16[8,768,128]{2,1,0:T(8,128)(2,1)}, u32[]{:S(2)}, u32[]{:S(2)}) async-start(bf16[8,768,128]{2,1,0:T(8,128)(2,1)} %pack.1), calls=%async_computation | async-start | bytes 3145728 | tf_op jit(solution)/shard_map/all_to_all | solution.py:406
  17.5 2.3 prep.1
  19.9 3.0 %collective-permute-start = (bf16[288,256]{1,0:T(8,128)(2,1)}, bf16[288,256]{1,0:T(8,128)(2,1)S(1)}, u32[]{:S(2)}, u32[]{:S(2)}) collective-permute-start(bf16[288,256]{1,0:T(8,128)(2,1)} %get-tuple-element.29), channel_id=1, source_target_pairs={{0,3},{1,0},{2,1},{3,2},{4,7},{5,4},{6,5},{7,6},{8,11},{9,8},{10,9... | collective-permute-start | bytes 442376 | tf_op jit(solution)/shard_map/ppermute | solution.py:380
  22.9 0.6 collective-permute-start.1
  23.5 1.0 collective-permute-start.2
  24.5 1.9 multiply_cosine_fusion
  26.6 2.3 collective-permute-done.p1_ref
  28.9 2.1 collective-permute-done.1.p2_ref
  31.0 1.5 collective-permute-done.2.p3_ref
  32.5 0.7 copy-done.9
  33.2 2.0 join.1
  35.2 2.6 %all-to-all-done.own_ref.src_ref = bf16[8,768,128]{2,1,0:T(8,128)(2,1)} async-done(((bf16[8,768,128]{2,1,0:T(8,128)(2,1)}), bf16[8,768,128]{2,1,0:T(8,128)(2,1)}, u32[]{:S(2)}, u32[]{:S(2)}) %all-to-all-start) | async-done | bytes 1572896 | tf_op jit(solution)/shard_map/all_to_all | solution.py:406
  37.9 64.7 %widen.1 = bf16[4,8,256,128]{3,2,1,0:T(8,128)(2,1)} custom-call(bf16[8,768,128]{2,1,0:T(8,128)(2,1)} %all-to-all-done.own_ref.src_ref), custom_call_target="tpu_custom_call" | custom-call | tf_op jit(solution)/shard_map/widen/pallas_call | solution.py:111
  102.6 4.6 %all-to-all-start.2 = ((bf16[4,8,256,128]{3,2,1,0:T(8,128)(2,1)}), bf16[4,8,256,128]{3,2,1,0:T(8,128)(2,1)S(1)}, u32[]{:S(2)}, u32[]{:S(2)}) async-start(bf16[4,8,256,128]{3,2,1,0:T(8,128)(2,1)} %widen.1), calls=%async_computation.2 | async-start | bytes 4194304 | tf_op jit(solution)/shard_map/all_to_all | solution.py:420
  107.2 7.8 %qkv.1 = (bf16[1024,256]{1,0:T(8,128)(2,1)S(1)}, bf16[2,1024,128]{2,1,0:T(8,128)(2,1)}, bf16[2,512,128]{2,1,0:T(8,128)(2,1)}) custom-call(s32[1]{0:T(128)} %bitcast.core_ref, bf16[1024,2048]{1,0:T(8,128)(2,1)} %x_ref.1, bf16[8,768,128]{2,1,0:T(8,128)(2,1)} %all-to-all-done.own_ref.src_ref, bf16[8,768,128]{2,1,0:T(8,128)(2,1)} %collective-permute-done.3.oth_ref, ...), custom_call_target="tpu_custom_call" | custom-call | tf_op jit(solution)/shard_map/qkv/pallas_call | solution.py:71
  115.0 2.1 collective-permute-start.4
  117.4 7.9 %collective-permute-done.4.prior_ref = bf16[2,512,128]{2,1,0:T(8,128)(2,1)S(1)} collective-permute-done((bf16[2,512,128]{2,1,0:T(8,128)(2,1)}, bf16[2,512,128]{2,1,0:T(8,128)(2,1)S(1)}, u32[]{:S(2)}, u32[]{:S(2)}) %collective-permute-start.4) | collective-permute-done | bytes 262176 | tf_op jit(solution)/shard_map/ppermute | solution.py:424
  125.3 1.0 copy-done.2
  126.4 4.2 %attend.2 = bf16[4,128,256]{2,1,0:T(8,128)(2,1)S(1)} custom-call(s32[1]{0:T(128)S(6)} %sub.6.half_ref, bf16[1024,256]{1,0:T(8,128)(2,1)S(1)} %get-tuple-element.37.q_ref, bf16[2,1024,128]{2,1,0:T(8,128)(2,1)S(1)} %copy-done.2, bf16[2,512,128]{2,1,0:T(8,128)(2,1)S(1)} %collective-permute-done.4.prior_ref, s32[1024,1]{1,0:T(8,128)S(1)} %copy.17.lo_ref), custom_call_target="tpu_custom_call" | custom-call | tf_op jit(solution)/shard_map/attend/pallas_call | solution.py:171
  130.5 0.7 copy-done.3
  131.2 4.0 %attend.3 = bf16[4,128,256]{2,1,0:T(8,128)(2,1)} custom-call(s32[1]{0:T(128)} %bitcast.1.half_ref, bf16[1024,256]{1,0:T(8,128)(2,1)S(1)} %get-tuple-element.37.q_ref, bf16[2,1024,128]{2,1,0:T(8,128)(2,1)S(1)} %copy-done.2, bf16[2,512,128]{2,1,0:T(8,128)(2,1)S(1)} %collective-permute-done.4.prior_ref, s32[1024,1]{1,0:T(8,128)S(1)} %copy.17.lo_ref), custom_call_target="tpu_custom_call" | custom-call | tf_op jit(solution)/shard_map/attend/pallas_call | solution.py:171
  135.2 12.1 %all_to_all.20.ctx_ref = bf16[4,128,256]{2,1,0:T(8,128)(2,1)S(1)} all-to-all(bf16[4,128,256]{2,1,0:T(8,128)(2,1)} %copy-done.3), channel_id=1, replica_groups=mesh['z'=4,'xh'=2,'core'=2,'xl'=2,'y'=4] {'y'}, dimensions={0} | all-to-all | bytes 524288 | tf_op jit(solution)/shard_map/all_to_all | solution.py:425
  147.4 3.6 %oproj.2 = bf16[128,2048]{1,0:T(8,128)(2,1)S(1)} custom-call(s32[1]{0:T(128)} %bitcast.core_ref, bf16[4,128,256]{2,1,0:T(8,128)(2,1)S(1)} %all_to_all.20.ctx_ref, bf16[4,8,256,128]{3,2,1,0:T(8,128)(2,1)S(1)} %all-to-all-done.2.own_ref, bf16[4,8,256,128]{3,2,1,0:T(8,128)(2,1)S(1)} %collective-permute-done.5.oth_ref), custom_call_target="tpu_custom_call" | custom-call | tf_op jit(solution)/shard_map/oproj/pallas_call | solution.py:210
  151.1 1.1 collective-permute-start.6
  152.2 3.4 %all-to-all-start.3 = ((bf16[4,128,256]{2,1,0:T(8,128)(2,1)}), bf16[4,128,256]{2,1,0:T(8,128)(2,1)S(1)}, u32[]{:S(2)}, u32[]{:S(2)}) async-start(bf16[4,128,256]{2,1,0:T(8,128)(2,1)} %attend.3), calls=%async_computation.3 | async-start | bytes 524288 | tf_op jit(solution)/shard_map/all_to_all | solution.py:425
  155.6 6.6 %all-to-all-done.3.ctx_ref = bf16[4,128,256]{2,1,0:T(8,128)(2,1)S(1)} async-done(((bf16[4,128,256]{2,1,0:T(8,128)(2,1)}), bf16[4,128,256]{2,1,0:T(8,128)(2,1)S(1)}, u32[]{:S(2)}, u32[]{:S(2)}) %all-to-all-start.3) | async-done | bytes 262176 | tf_op jit(solution)/shard_map/all_to_all | solution.py:425
  162.2 1.6 copy-done.1
  163.8 3.6 %oproj.3 = f32[128,2048]{1,0:T(8,128)S(1)} custom-call(s32[1]{0:T(128)} %bitcast.core_ref, bf16[4,128,256]{2,1,0:T(8,128)(2,1)S(1)} %all-to-all-done.3.ctx_ref, bf16[4,8,256,128]{3,2,1,0:T(8,128)(2,1)S(1)} %all-to-all-done.2.own_ref, bf16[4,8,256,128]{3,2,1,0:T(8,128)(2,1)S(1)} %copy-done.1), custom_call_target="tpu_custom_call" | custom-call | tf_op jit(solution)/shard_map/oproj/pallas_call | solution.py:210
  167.5 1.3 add_convert_fusion
  169.2 1.2 collective-permute-start.8
  170.4 0.9 collective-permute-start.7
  171.3 9.8 %collective-permute-done.8.x2_ref = bf16[128,2048]{1,0:T(8,128)(2,1)S(1)} collective-permute-done((bf16[128,2048]{1,0:T(8,128)(2,1)S(1)}, bf16[128,2048]{1,0:T(8,128)(2,1)S(1)}, u32[]{:S(2)}, u32[]{:S(2)}) %collective-permute-start.8) | collective-permute-done | bytes 524320 | tf_op jit(solution)/shard_map/ppermute | solution.py:443
  181.0 2.2 collective-permute-done.7.x1_ref
  183.7 1.7 collective-permute-start.9
  185.4 6.7 %collective-permute-done.10.x4_ref = bf16[64,2048]{1,0:T(8,128)(2,1)S(1)} collective-permute-done((bf16[64,2048]{1,0:T(8,128)(2,1)S(1)}, bf16[64,2048]{1,0:T(8,128)(2,1)S(1)}, u32[]{:S(2)}, u32[]{:S(2)}) %collective-permute-start.10) | collective-permute-done | bytes 262176 | tf_op jit(solution)/shard_map/ppermute | solution.py:447
  192.1 1.3 collective-permute-done.9.x3_ref
  193.4 6.4 %gate_up.2.hid0_ref = bf16[512,768]{1,0:T(8,128)(2,1)S(1)} custom-call(s32[1]{0:T(128)} %bitcast.2.y_ref, bf16[128,2048]{1,0:T(8,128)(2,1)S(1)} %fusion.2.x0_ref, bf16[128,2048]{1,0:T(8,128)(2,1)S(1)} %collective-permute-done.7.x1_ref, bf16[128,2048]{1,0:T(8,128)(2,1)S(1)} %collective-permute-done.8.x2_ref, ...), custom_call_target="tpu_custom_call" | custom-call | tf_op jit(solution)/shard_map/gate_up/pallas_call | solution.py:296
  199.8 4.7 %gate_up.3.hid1_ref = bf16[512,768]{1,0:T(8,128)(2,1)S(1)} custom-call(s32[1]{0:T(128)} %bitcast.2.y_ref, bf16[128,2048]{1,0:T(8,128)(2,1)S(1)} %fusion.2.x0_ref, bf16[128,2048]{1,0:T(8,128)(2,1)S(1)} %collective-permute-done.7.x1_ref, bf16[128,2048]{1,0:T(8,128)(2,1)S(1)} %collective-permute-done.8.x2_ref, ...), custom_call_target="tpu_custom_call" | custom-call | tf_op jit(solution)/shard_map/gate_up/pallas_call | solution.py:296
  204.5 3.6 %down_far.1 = (bf16[64,2048]{1,0:T(8,128)(2,1)S(1)}, bf16[64,2048]{1,0:T(8,128)(2,1)S(1)}, bf16[1,16,96,2048]{3,2,1,0:T(8,128)(2,1)S(1)}) custom-call(s32[1]{0:T(128)} %bitcast.2.y_ref, bf16[512,768]{1,0:T(8,128)(2,1)S(1)} %gate_up.2.hid0_ref, bf16[512,768]{1,0:T(8,128)(2,1)S(1)} %gate_up.3.hid1_ref, bf16[8,2,4,288,256]{4,3,2,1,0:T(8,128)(2,1)} %bitcast.13, ...), custom_call_target="tpu_custom_call" | custom-call | tf_op jit(solution)/shard_map/down_far/pallas_call | solution.py:314
  208.1 0.5 collective-permute-start.12
  208.7 2.8 %collective-permute-start.13 = (bf16[64,2048]{1,0:T(8,128)(2,1)S(1)}, bf16[64,2048]{1,0:T(8,128)(2,1)S(1)}, u32[]{:S(2)}, u32[]{:S(2)}) collective-permute-start(bf16[64,2048]{1,0:T(8,128)(2,1)S(1)} %get-tuple-element.50), channel_id=1, source_target_pairs={{0,3},{1,0},{2,1},{3,2},{4,7},{5,4},{6,5},{7,6},{8,11},{9,8},{10,9... | collective-permute-start | bytes 786440 | tf_op jit(solution)/shard_map/ppermute | solution.py:455
  211.4 3.2 %down.1 = (f32[128,2048]{1,0:T(8,128)S(1)}, bf16[128,2048]{1,0:T(8,128)(2,1)S(1)}, bf16[128,2048]{1,0:T(8,128)(2,1)S(1)}) custom-call(bf16[512,768]{1,0:T(8,128)(2,1)S(1)} %gate_up.2.hid0_ref, bf16[512,768]{1,0:T(8,128)(2,1)S(1)} %gate_up.3.hid1_ref, bf16[1,16,96,2048]{3,2,1,0:T(8,128)(2,1)S(1)} %get-tuple-element.46.w_ref), custom_call_target="tpu_custom_call" | custom-call | tf_op jit(solution)/shard_map/down/pallas_call | solution.py:326
  214.7 2.4 collective-permute-done.12
  217.3 3.0 %collective-permute-start.15 = (bf16[128,2048]{1,0:T(8,128)(2,1)S(1)}, bf16[128,2048]{1,0:T(8,128)(2,1)S(1)}, u32[]{:S(2)}, u32[]{:S(2)}) collective-permute-start(bf16[128,2048]{1,0:T(8,128)(2,1)S(1)} %pad_maximum_fusion.2), channel_id=1, source_target_pairs={{0,3},{1,0},{2,1},{3,2},{4,7},{5,4},{6,5},{7,6},{8,11},{9,8},{10,9... | collective-permute-start | bytes 1572872 | tf_op jit(solution)/shard_map/ppermute | solution.py:461
  220.5 9.5 %collective-permute-done.15 = bf16[128,2048]{1,0:T(8,128)(2,1)S(1)} collective-permute-done((bf16[128,2048]{1,0:T(8,128)(2,1)S(1)}, bf16[128,2048]{1,0:T(8,128)(2,1)S(1)}, u32[]{:S(2)}, u32[]{:S(2)}) %collective-permute-start.15) | collective-permute-done | bytes 524320 | tf_op jit(solution)/shard_map/ppermute | solution.py:461
  230.0 3.5 %collective-permute-done.14 = bf16[128,2048]{1,0:T(8,128)(2,1)S(1)} collective-permute-done((bf16[128,2048]{1,0:T(8,128)(2,1)S(1)}, bf16[128,2048]{1,0:T(8,128)(2,1)S(1)}, u32[]{:S(2)}, u32[]{:S(2)}) %collective-permute-start.14) | collective-permute-done | bytes 524320 | tf_op jit(solution)/shard_map/ppermute | solution.py:460
  233.5 1.1 fusion.3
  (49 shorter events, 1.7 us)
Async XLA Ops:
  9.5 15.0 %copy-start.11 = (s32[1024]{0:T(1024)S(1)}, s32[1024]{0:T(1024)}, u32[]{:S(2)}) copy-start(s32[1024]{0:T(1024)} %param.15) | copy-start | bytes 12292
  9.5 28.3 %all-to-all-start = ((bf16[8,768,128]{2,1,0:T(8,128)(2,1)}), bf16[8,768,128]{2,1,0:T(8,128)(2,1)}, u32[]{:S(2)}, u32[]{:S(2)}) async-start(bf16[8,768,128]{2,1,0:T(8,128)(2,1)} %pack.1), calls=%async_computation | async-start | bytes 3145728 | tf_op jit(solution)/shard_map/all_to_all | solution.py:406
  17.5 165.8 %all-gather.3.cloned.1.call-start = ((), (), s32[]{:S(2)}) async-start(), calls=%async_computation.4 | async-start | bytes 10027008 | tf_op jit(solution)/shard_map/all_gather | solution.py:415
  19.9 9.0 %collective-permute-start = (bf16[288,256]{1,0:T(8,128)(2,1)}, bf16[288,256]{1,0:T(8,128)(2,1)S(1)}, u32[]{:S(2)}, u32[]{:S(2)}) collective-permute-start(bf16[288,256]{1,0:T(8,128)(2,1)} %get-tuple-element.29), channel_id=1, source_target_pairs={{0,3},{1,0},{2,1},{3,2},{4,7},{5,4},{6,5},{7,6},{8,11},{9,8},{10,9... | collective-permute-start | bytes 442376 | tf_op jit(solution)/shard_map/ppermute | solution.py:380
  22.9 8.1 %collective-permute-start.1 = (bf16[288,256]{1,0:T(8,128)(2,1)}, bf16[288,256]{1,0:T(8,128)(2,1)S(1)}, u32[]{:S(2)}, u32[]{:S(2)}) collective-permute-start(bf16[288,256]{1,0:T(8,128)(2,1)} %get-tuple-element.30), channel_id=1, source_target_pairs={{0,2},{1,3},{2,0},{3,1},{4,6},{5,7},{6,4},{7,5},{8,10},{9,11},{10,... | collective-permute-start | bytes 442376 | tf_op jit(solution)/shard_map/ppermute | solution.py:380
  23.5 9.0 %collective-permute-start.2 = (bf16[288,256]{1,0:T(8,128)(2,1)}, bf16[288,256]{1,0:T(8,128)(2,1)S(1)}, u32[]{:S(2)}, u32[]{:S(2)}) collective-permute-start(bf16[288,256]{1,0:T(8,128)(2,1)} %get-tuple-element.31), channel_id=1, source_target_pairs={{0,1},{1,2},{2,3},{3,0},{4,5},{5,6},{6,7},{7,4},{8,9},{9,10},{10,1... | collective-permute-start | bytes 442376 | tf_op jit(solution)/shard_map/ppermute | solution.py:380
  28.9 3.6 %copy-start.7 = (bf16[288,256]{1,0:T(8,128)(2,1)}, bf16[288,256]{1,0:T(8,128)(2,1)S(1)}, u32[]{:S(2)}) copy-start(bf16[288,256]{1,0:T(8,128)(2,1)S(1)} %collective-permute-done.p1_ref) | copy-start | bytes 442372
  31.0 1.5 copy-start.8
  32.5 0.7 copy-start.9
  37.8 69.4 %collective-permute-start.3 = (bf16[8,768,128]{2,1,0:T(8,128)(2,1)}, bf16[8,768,128]{2,1,0:T(8,128)(2,1)}, u32[]{:S(2)}, u32[]{:S(2)}) collective-permute-start(bf16[8,768,128]{2,1,0:T(8,128)(2,1)} %all-to-all-done.own_ref.src_ref), channel_id=1, source_target_pairs={{0,8},{8,0},{1,9},{9,1},{2,10},{10,2},{3,11},{11,3},{4,12},{12,4},... | collective-permute-start | bytes 4718600 | tf_op jit(solution)/shard_map/ppermute | solution.py:23
  102.6 4.6 %copy-start.4 = (f32[2048]{0:T(1024)S(1)}, f32[2048]{0:T(1024)}, u32[]{:S(2)}) copy-start(f32[2048]{0:T(1024)} %param.16) | copy-start | bytes 24580
  102.6 4.6 %copy-start.5 = (f32[128]{0:T(128)S(1)}, f32[128]{0:T(128)}, u32[]{:S(2)}) copy-start(f32[128]{0:T(128)} %param.18) | copy-start | bytes 1540
  102.6 4.6 %copy-start.6 = (f32[128]{0:T(128)S(1)}, f32[128]{0:T(128)}, u32[]{:S(2)}) copy-start(f32[128]{0:T(128)} %param.19) | copy-start | bytes 1540
  102.6 32.7 %all-to-all-start.2 = ((bf16[4,8,256,128]{3,2,1,0:T(8,128)(2,1)}), bf16[4,8,256,128]{3,2,1,0:T(8,128)(2,1)S(1)}, u32[]{:S(2)}, u32[]{:S(2)}) async-start(bf16[4,8,256,128]{3,2,1,0:T(8,128)(2,1)} %widen.1), calls=%async_computation.2 | async-start | bytes 4194304 | tf_op jit(solution)/shard_map/all_to_all | solution.py:420
  115.0 10.3 %collective-permute-start.4 = (bf16[2,512,128]{2,1,0:T(8,128)(2,1)}, bf16[2,512,128]{2,1,0:T(8,128)(2,1)S(1)}, u32[]{:S(2)}, u32[]{:S(2)}) collective-permute-start(bf16[2,512,128]{2,1,0:T(8,128)(2,1)} %get-tuple-element.36), channel_id=1, source_target_pairs={{0,8},{8,16},{16,24},{24,32},{32,40},{40,48},{48,56},{56,64},{64,7... | collective-permute-start | bytes 786440 | tf_op jit(solution)/shard_map/ppermute | solution.py:424
  125.3 1.0 copy-start.2
  130.5 0.7 copy-start.3
  135.2 12.1 %collective-permute-start.5 = (bf16[4,8,256,128]{3,2,1,0:T(8,128)(2,1)S(1)}, bf16[4,8,256,128]{3,2,1,0:T(8,128)(2,1)S(1)}, u32[]{:S(2)}, u32[]{:S(2)}) collective-permute-start(bf16[4,8,256,128]{3,2,1,0:T(8,128)(2,1)S(1)} %all-to-all-done.2.own_ref), channel_id=1, source_target_pairs={{0,8},{8,0},{1,9},{9,1},{2,10},{10,2},{3,11},{11,3},{4,12},{12,4},... | collective-permute-start | bytes 6291464 | tf_op jit(solution)/shard_map/ppermute | solution.py:23
  147.4 3.6 %copy-start = (bf16[4,8,256,128]{3,2,1,0:T(8,128)(2,1)}, bf16[4,8,256,128]{3,2,1,0:T(8,128)(2,1)S(1)}, u32[]{:S(2)}) copy-start(bf16[4,8,256,128]{3,2,1,0:T(8,128)(2,1)S(1)} %collective-permute-done.5.oth_ref) | copy-start | bytes 6291460
  151.1 16.4 %collective-permute-start.6 = (bf16[128,2048]{1,0:T(8,128)(2,1)S(1)}, bf16[128,2048]{1,0:T(8,128)(2,1)S(1)}, u32[]{:S(2)}, u32[]{:S(2)}) collective-permute-start(bf16[128,2048]{1,0:T(8,128)(2,1)S(1)} %oproj.2), channel_id=1, source_target_pairs={{0,4},{4,0},{1,5},{5,1},{2,6},{6,2},{3,7},{7,3},{8,12},{12,8},{9,1... | collective-permute-start | bytes 1572872 | tf_op jit(solution)/shard_map/ppermute | solution.py:23
  152.2 10.1 %all-to-all-start.3 = ((bf16[4,128,256]{2,1,0:T(8,128)(2,1)}), bf16[4,128,256]{2,1,0:T(8,128)(2,1)S(1)}, u32[]{:S(2)}, u32[]{:S(2)}) async-start(bf16[4,128,256]{2,1,0:T(8,128)(2,1)} %attend.3), calls=%async_computation.3 | async-start | bytes 524288 | tf_op jit(solution)/shard_map/all_to_all | solution.py:425
  162.2 1.6 copy-start.1
  167.5 1.5 copy-start.10
  169.2 11.9 %collective-permute-start.8 = (bf16[128,2048]{1,0:T(8,128)(2,1)S(1)}, bf16[128,2048]{1,0:T(8,128)(2,1)S(1)}, u32[]{:S(2)}, u32[]{:S(2)}) collective-permute-start(bf16[128,2048]{1,0:T(8,128)(2,1)S(1)} %fusion.2.x0_ref), channel_id=1, source_target_pairs={{0,3},{1,0},{2,1},{3,2},{4,7},{5,4},{6,5},{7,6},{8,11},{9,8},{10,9... | collective-permute-start | bytes 1572872 | tf_op jit(solution)/shard_map/ppermute | solution.py:443
  170.4 12.9 %collective-permute-start.7 = (bf16[128,2048]{1,0:T(8,128)(2,1)S(1)}, bf16[128,2048]{1,0:T(8,128)(2,1)S(1)}, u32[]{:S(2)}, u32[]{:S(2)}) collective-permute-start(bf16[128,2048]{1,0:T(8,128)(2,1)S(1)} %fusion.2.x0_ref), channel_id=1, source_target_pairs={{0,1},{1,2},{2,3},{3,0},{4,5},{5,6},{6,7},{7,4},{8,9},{9,10},{10,1... | collective-permute-start | bytes 1572872 | tf_op jit(solution)/shard_map/ppermute | solution.py:442
  183.3 16.5 %collective-permute-start.11 = (bf16[8,2,4,288,256]{4,3,2,1,0:T(8,128)(2,1)}, bf16[8,2,4,288,256]{4,3,2,1,0:T(8,128)(2,1)S(1)}, u32[]{:S(2)}, u32[]{:S(2)}) collective-permute-start(bf16[8,2,4,288,256]{4,3,2,1,0:T(8,128)(2,1)} %bitcast.11), channel_id=1, source_target_pairs={{0,8},{8,0},{1,9},{9,1},{2,10},{10,2},{3,11},{11,3},{4,12},{12,4},... | collective-permute-start | bytes 28311560 | tf_op jit(solution)/shard_map/ppermute | solution.py:23
  183.3 8.8 %collective-permute-start.10 = (bf16[64,2048]{1,0:T(8,128)(2,1)S(1)}, bf16[64,2048]{1,0:T(8,128)(2,1)S(1)}, u32[]{:S(2)}, u32[]{:S(2)}) collective-permute-start(bf16[64,2048]{1,0:T(8,128)(2,1)S(1)} %slice.19), channel_id=1, source_target_pairs={{0,3},{1,0},{2,1},{3,2},{4,7},{5,4},{6,5},{7,6},{8,11},{9,8},{10,9... | collective-permute-start | bytes 786440 | tf_op jit(solution)/shard_map/ppermute | solution.py:447
  183.7 9.7 %collective-permute-start.9 = (bf16[64,2048]{1,0:T(8,128)(2,1)S(1)}, bf16[64,2048]{1,0:T(8,128)(2,1)S(1)}, u32[]{:S(2)}, u32[]{:S(2)}) collective-permute-start(bf16[64,2048]{1,0:T(8,128)(2,1)S(1)} %slice.18), channel_id=1, source_target_pairs={{0,1},{1,2},{2,3},{3,0},{4,5},{5,6},{6,7},{7,4},{8,9},{9,10},{10,1... | collective-permute-start | bytes 786440 | tf_op jit(solution)/shard_map/ppermute | solution.py:446
  208.1 9.0 %collective-permute-start.12 = (bf16[64,2048]{1,0:T(8,128)(2,1)S(1)}, bf16[64,2048]{1,0:T(8,128)(2,1)S(1)}, u32[]{:S(2)}, u32[]{:S(2)}) collective-permute-start(bf16[64,2048]{1,0:T(8,128)(2,1)S(1)} %get-tuple-element.49), channel_id=1, source_target_pairs={{0,1},{1,2},{2,3},{3,0},{4,5},{5,6},{6,7},{7,4},{8,9},{9,10},{10,1... | collective-permute-start | bytes 786440 | tf_op jit(solution)/shard_map/ppermute | solution.py:454
  208.7 8.5 %collective-permute-start.13 = (bf16[64,2048]{1,0:T(8,128)(2,1)S(1)}, bf16[64,2048]{1,0:T(8,128)(2,1)S(1)}, u32[]{:S(2)}, u32[]{:S(2)}) collective-permute-start(bf16[64,2048]{1,0:T(8,128)(2,1)S(1)} %get-tuple-element.50), channel_id=1, source_target_pairs={{0,3},{1,0},{2,1},{3,2},{4,7},{5,4},{6,5},{7,6},{8,11},{9,8},{10,9... | collective-permute-start | bytes 786440 | tf_op jit(solution)/shard_map/ppermute | solution.py:455
  217.3 12.7 %collective-permute-start.15 = (bf16[128,2048]{1,0:T(8,128)(2,1)S(1)}, bf16[128,2048]{1,0:T(8,128)(2,1)S(1)}, u32[]{:S(2)}, u32[]{:S(2)}) collective-permute-start(bf16[128,2048]{1,0:T(8,128)(2,1)S(1)} %pad_maximum_fusion.2), channel_id=1, source_target_pairs={{0,3},{1,0},{2,1},{3,2},{4,7},{5,4},{6,5},{7,6},{8,11},{9,8},{10,9... | collective-permute-start | bytes 1572872 | tf_op jit(solution)/shard_map/ppermute | solution.py:461
  220.4 13.1 %collective-permute-start.14 = (bf16[128,2048]{1,0:T(8,128)(2,1)S(1)}, bf16[128,2048]{1,0:T(8,128)(2,1)S(1)}, u32[]{:S(2)}, u32[]{:S(2)}) collective-permute-start(bf16[128,2048]{1,0:T(8,128)(2,1)S(1)} %pad_maximum_fusion.1), channel_id=1, source_target_pairs={{0,1},{1,2},{2,3},{3,0},{4,5},{5,6},{6,7},{7,4},{8,9},{9,10},{10,1... | collective-permute-start | bytes 1572872 | tf_op jit(solution)/shard_map/ppermute | solution.py:460
Sparse Core Ops, SparseCore 0:
  37.9 75.1 all-gather.2

commit v10 on v9

--- a/solution.py
+++ b/solution.py
@@ -99,21 +99,18 @@
     )(core, tokens, own, oth, attn_gain[None], q_gain[None], key_gain[None], cs)
 
 
-def widen_kernel(src_ref, out_ref, sems):
-    copies = [pltpu.make_async_copy(src_ref.at[:, 512:], out_ref.at[k], sems.at[k]) for k in range(4)]
-    for copy in copies:
-        copy.start()
-    for copy in copies:
-        copy.wait()
+def widen_kernel(src_ref, out_ref):
+    for k in range(4):
+        out_ref[k] = src_ref[...]
 
 
 def widen(gathered):
     return pl.pallas_call(
         widen_kernel,
-        in_specs=[pl.BlockSpec(memory_space=pl.ANY)],
-        out_specs=pl.BlockSpec(memory_space=pl.ANY),
+        grid=(1,),
+        in_specs=[pl.BlockSpec((8, 256, 128), lambda i: (0, 2, 0))],
+        out_specs=pl.BlockSpec((4, 8, 256, 128), lambda i: (0, 0, 0, 0)),
         out_shape=jax.ShapeDtypeStruct((4, 8, 256, 128), BF),
-        scratch_shapes=[pltpu.SemaphoreType.DMA((4,))],
         name="widen",
     )(gathered)
 

time: 242 us -> 192 us (0.79)
  Pallas kernels: 113 us -> 50.6 us
  waiting for transfers between devices: 58.5 us -> 70.9 us
    pallas_call x1, Pallas kernels: 64.7 us -> 2.64 us  [widen(): pl.pallas_call(widen_kernel, grid=(1,), in_specs=[pl.BlockSpec((8, 256, 1...]
    ppermute x4, waiting for transfers between devices: 0.01 us -> 9.59 us  [swap(): return lax.ppermute(block, axis, [(0, 1), (1, 0)])]
  transfers between devices with their start and end apart: 20 -> 20, of which waited for: 13 -> 14; matrix products, arithmetic and copies ran while one was open for 2% -> 2% of each run, Pallas kernels for 42% -> 21%
where the time goes in v10:
time: 192 us; the launch traced here: 191 us
  waiting for transfers between devices  70.9 us (37%)
  Pallas kernels  50.6 us (26%)
  starting transfers between devices  34 us (18%)
  between operations  14.3 us (7%)
  blocking collectives  11.7 us (6%)
  other arithmetic  5.06 us (3%)
  local copies, waits for them, and re-layouts  4.38 us (2%)
    all_to_all x1, blocking collectives, per_device(): lax.all_to_all(part, 'y', split_axis=0, concat_axis=0, tiled=True)  11.7 us
    pallas_call x2, Pallas kernels, gate_up(): pl.pallas_call(gate_kernel, in_specs=[pl.BlockSpec(memory_space=pltpu.SME...  11.1 us
    ppermute x1, waiting for transfers between devices, per_device(): right = lax.ppermute(mlp_in, 'y', ring(3))  10.5 us
    ppermute x1, waiting for transfers between devices, per_device(): prior = lax.ppermute(tail, REQ, [(i - 1, i) for i in range(1, 16)])  10.2 us
    ppermute x4, waiting for transfers between devices, swap(): return lax.ppermute(block, axis, [(0, 1), (1, 0)])  9.59 us
    ppermute x1, waiting for transfers between devices, per_device(): from_right = lax.ppermute(to_left, 'y', ring(3))  9.51 us
    pallas_call x2, Pallas kernels, attend(): pl.pallas_call(attend_kernel, in_specs=[pl.BlockSpec(memory_space=pltpu.S...  8.18 us
    all_to_all x1, starting transfers between devices, per_device(): lax.all_to_all(packed, ('z', 'xh'), split_axis=0, concat_axis=0, tiled=True)  8.01 us
  transfers between devices with their start and end apart: 20, of which 14 were waited for; matrix products, arithmetic and copies ran while one was open for 2% of the time, Pallas kernels for 21%

profile of v10, /device:TPU:32, one launch (start us, length us, event | category | flops | bytes accessed | tf_op | source)
XLA Modules:
  0.0 190.9 jit_solution(5129386077407845288)
XLA Ops:
  7.2 2.3 %pack.1 = bf16[8,768,128]{2,1,0:T(8,128)(2,1)} custom-call(f32[128,256]{1,0:T(8,128)} %q_ref.1, f32[128,128]{1,0:T(8,128)} %k_ref.1, f32[128,128]{1,0:T(8,128)} %v_ref.1, f32[256,128]{1,0:T(8,128)} %o_ref.1), custom_call_target="tpu_custom_call" | custom-call | tf_op jit(solution)/shard_map/pack/pallas_call | solution.py:339
  9.5 8.0 %all-to-all-start = ((bf16[8,768,128]{2,1,0:T(8,128)(2,1)}), bf16[8,768,128]{2,1,0:T(8,128)(2,1)}, u32[]{:S(2)}, u32[]{:S(2)}) async-start(bf16[8,768,128]{2,1,0:T(8,128)(2,1)} %pack.1), calls=%async_computation | async-start | bytes 3145728 | tf_op jit(solution)/shard_map/all_to_all | solution.py:403
  17.5 2.3 %prep.1 = (bf16[288,256]{1,0:T(8,128)(2,1)}, bf16[288,256]{1,0:T(8,128)(2,1)}, bf16[288,256]{1,0:T(8,128)(2,1)}, bf16[288,256]{1,0:T(8,128)(2,1)}) custom-call(s32[1]{0:T(128)} %bitcast.2.y_ref, f32[256,384]{1,0:T(8,128)} %gate_ref.1, f32[256,384]{1,0:T(8,128)} %up_ref.1, f32[384,256]{1,0:T(8,128)} %down_ref.1), custom_call_target="tpu_custom_call" | custom-call | tf_op jit(solution)/shard_map/prep/pallas_call | solution.py:358
  19.9 3.0 %collective-permute-start = (bf16[288,256]{1,0:T(8,128)(2,1)}, bf16[288,256]{1,0:T(8,128)(2,1)S(1)}, u32[]{:S(2)}, u32[]{:S(2)}) collective-permute-start(bf16[288,256]{1,0:T(8,128)(2,1)} %get-tuple-element.29), channel_id=1, source_target_pairs={{0,3},{1,0},{2,1},{3,2},{4,7},{5,4},{6,5},{7,6},{8,11},{9,8},{10,9... | collective-permute-start | bytes 442376 | tf_op jit(solution)/shard_map/ppermute | solution.py:377
  22.9 0.6 collective-permute-start.1
  23.5 1.0 collective-permute-start.2
  24.5 1.9 multiply_cosine_fusion
  26.6 2.3 %collective-permute-done.p1_ref = bf16[288,256]{1,0:T(8,128)(2,1)S(1)} collective-permute-done((bf16[288,256]{1,0:T(8,128)(2,1)}, bf16[288,256]{1,0:T(8,128)(2,1)S(1)}, u32[]{:S(2)}, u32[]{:S(2)}) %collective-permute-start) | collective-permute-done | bytes 147488 | tf_op jit(solution)/shard_map/ppermute | solution.py:377
  28.9 2.1 %collective-permute-done.1.p2_ref = bf16[288,256]{1,0:T(8,128)(2,1)S(1)} collective-permute-done((bf16[288,256]{1,0:T(8,128)(2,1)}, bf16[288,256]{1,0:T(8,128)(2,1)S(1)}, u32[]{:S(2)}, u32[]{:S(2)}) %collective-permute-start.1) | collective-permute-done | bytes 147488 | tf_op jit(solution)/shard_map/ppermute | solution.py:377
  31.0 1.5 collective-permute-done.2.p3_ref
  32.5 0.7 copy-done.9
  33.2 2.0 %join.1 = bf16[4,288,256]{2,1,0:T(8,128)(2,1)} custom-call(bf16[288,256]{1,0:T(8,128)(2,1)} %get-tuple-element.28.p0_ref, bf16[288,256]{1,0:T(8,128)(2,1)} %copy-done.7, bf16[288,256]{1,0:T(8,128)(2,1)} %copy-done.8, bf16[288,256]{1,0:T(8,128)(2,1)} %copy-done.9), custom_call_target="tpu_custom_call" | custom-call | tf_op jit(solution)/shard_map/join/pallas_call | solution.py:373
  35.2 2.6 %all-to-all-done.own_ref.src_ref = bf16[8,768,128]{2,1,0:T(8,128)(2,1)} async-done(((bf16[8,768,128]{2,1,0:T(8,128)(2,1)}), bf16[8,768,128]{2,1,0:T(8,128)(2,1)}, u32[]{:S(2)}, u32[]{:S(2)}) %all-to-all-start) | async-done | bytes 1572896 | tf_op jit(solution)/shard_map/all_to_all | solution.py:403
  37.9 2.6 %widen.1 = bf16[4,8,256,128]{3,2,1,0:T(8,128)(2,1)} custom-call(bf16[8,768,128]{2,1,0:T(8,128)(2,1)} %all-to-all-done.own_ref.src_ref), custom_call_target="tpu_custom_call" | custom-call | tf_op jit(solution)/shard_map/widen/pallas_call | solution.py:108
  40.5 4.6 %all-to-all-start.2 = ((bf16[4,8,256,128]{3,2,1,0:T(8,128)(2,1)}), bf16[4,8,256,128]{3,2,1,0:T(8,128)(2,1)S(1)}, u32[]{:S(2)}, u32[]{:S(2)}) async-start(bf16[4,8,256,128]{3,2,1,0:T(8,128)(2,1)} %widen.1), calls=%async_computation.2 | async-start | bytes 4194304 | tf_op jit(solution)/shard_map/all_to_all | solution.py:417
  45.1 7.9 %qkv.1 = (bf16[1024,256]{1,0:T(8,128)(2,1)S(1)}, bf16[2,1024,128]{2,1,0:T(8,128)(2,1)}, bf16[2,512,128]{2,1,0:T(8,128)(2,1)}) custom-call(s32[1]{0:T(128)} %bitcast.core_ref, bf16[1024,2048]{1,0:T(8,128)(2,1)} %x_ref.1, bf16[8,768,128]{2,1,0:T(8,128)(2,1)} %all-to-all-done.own_ref.src_ref, bf16[8,768,128]{2,1,0:T(8,128)(2,1)} %collective-permute-done.3.oth_ref, ...), custom_call_target="tpu_custom_call" | custom-call | tf_op jit(solution)/shard_map/qkv/pallas_call | solution.py:71
  53.1 2.1 %collective-permute-start.4 = (bf16[2,512,128]{2,1,0:T(8,128)(2,1)}, bf16[2,512,128]{2,1,0:T(8,128)(2,1)S(1)}, u32[]{:S(2)}, u32[]{:S(2)}) collective-permute-start(bf16[2,512,128]{2,1,0:T(8,128)(2,1)} %get-tuple-element.36), channel_id=1, source_target_pairs={{0,8},{8,16},{16,24},{24,32},{32,40},{40,48},{48,56},{56,64},{64,7... | collective-permute-start | bytes 786440 | tf_op jit(solution)/shard_map/ppermute | solution.py:421
  55.4 10.2 %collective-permute-done.4.prior_ref = bf16[2,512,128]{2,1,0:T(8,128)(2,1)S(1)} collective-permute-done((bf16[2,512,128]{2,1,0:T(8,128)(2,1)}, bf16[2,512,128]{2,1,0:T(8,128)(2,1)S(1)}, u32[]{:S(2)}, u32[]{:S(2)}) %collective-permute-start.4) | collective-permute-done | bytes 262176 | tf_op jit(solution)/shard_map/ppermute | solution.py:421
  65.6 1.0 copy-done.2
  66.6 4.2 %attend.2 = bf16[4,128,256]{2,1,0:T(8,128)(2,1)S(1)} custom-call(s32[1]{0:T(128)S(6)} %sub.6.half_ref, bf16[1024,256]{1,0:T(8,128)(2,1)S(1)} %get-tuple-element.37.q_ref, bf16[2,1024,128]{2,1,0:T(8,128)(2,1)S(1)} %copy-done.2, bf16[2,512,128]{2,1,0:T(8,128)(2,1)S(1)} %collective-permute-done.4.prior_ref, s32[1024,1]{1,0:T(8,128)S(1)} %copy.17.lo_ref), custom_call_target="tpu_custom_call" | custom-call | tf_op jit(solution)/shard_map/attend/pallas_call | solution.py:168
  70.8 0.7 copy-done.3
  71.5 4.0 %attend.3 = bf16[4,128,256]{2,1,0:T(8,128)(2,1)} custom-call(s32[1]{0:T(128)} %bitcast.1.half_ref, bf16[1024,256]{1,0:T(8,128)(2,1)S(1)} %get-tuple-element.37.q_ref, bf16[2,1024,128]{2,1,0:T(8,128)(2,1)S(1)} %copy-done.2, bf16[2,512,128]{2,1,0:T(8,128)(2,1)S(1)} %collective-permute-done.4.prior_ref, s32[1024,1]{1,0:T(8,128)S(1)} %copy.17.lo_ref), custom_call_target="tpu_custom_call" | custom-call | tf_op jit(solution)/shard_map/attend/pallas_call | solution.py:168
  75.5 11.7 %all_to_all.20.ctx_ref = bf16[4,128,256]{2,1,0:T(8,128)(2,1)S(1)} all-to-all(bf16[4,128,256]{2,1,0:T(8,128)(2,1)} %copy-done.3), channel_id=1, replica_groups=mesh['z'=4,'xh'=2,'core'=2,'xl'=2,'y'=4] {'y'}, dimensions={0} | all-to-all | bytes 524288 | tf_op jit(solution)/shard_map/all_to_all | solution.py:422
  87.2 3.6 %oproj.2 = bf16[128,2048]{1,0:T(8,128)(2,1)S(1)} custom-call(s32[1]{0:T(128)} %bitcast.core_ref, bf16[4,128,256]{2,1,0:T(8,128)(2,1)S(1)} %all_to_all.20.ctx_ref, bf16[4,8,256,128]{3,2,1,0:T(8,128)(2,1)S(1)} %all-to-all-done.2.own_ref, bf16[4,8,256,128]{3,2,1,0:T(8,128)(2,1)S(1)} %collective-permute-done.5.oth_ref), custom_call_target="tpu_custom_call" | custom-call | tf_op jit(solution)/shard_map/oproj/pallas_call | solution.py:207
  90.8 0.6 collective-permute-start.6
  91.4 3.4 %all-to-all-start.3 = ((bf16[4,128,256]{2,1,0:T(8,128)(2,1)}), bf16[4,128,256]{2,1,0:T(8,128)(2,1)S(1)}, u32[]{:S(2)}, u32[]{:S(2)}) async-start(bf16[4,128,256]{2,1,0:T(8,128)(2,1)} %attend.3), calls=%async_computation.3 | async-start | bytes 524288 | tf_op jit(solution)/shard_map/all_to_all | solution.py:422
  94.8 6.6 %all-to-all-done.3.ctx_ref = bf16[4,128,256]{2,1,0:T(8,128)(2,1)S(1)} async-done(((bf16[4,128,256]{2,1,0:T(8,128)(2,1)}), bf16[4,128,256]{2,1,0:T(8,128)(2,1)S(1)}, u32[]{:S(2)}, u32[]{:S(2)}) %all-to-all-start.3) | async-done | bytes 262176 | tf_op jit(solution)/shard_map/all_to_all | solution.py:422
  101.5 1.7 copy-done.1
  103.2 3.6 %oproj.3 = f32[128,2048]{1,0:T(8,128)S(1)} custom-call(s32[1]{0:T(128)} %bitcast.core_ref, bf16[4,128,256]{2,1,0:T(8,128)(2,1)S(1)} %all-to-all-done.3.ctx_ref, bf16[4,8,256,128]{3,2,1,0:T(8,128)(2,1)S(1)} %all-to-all-done.2.own_ref, bf16[4,8,256,128]{3,2,1,0:T(8,128)(2,1)S(1)} %copy-done.1), custom_call_target="tpu_custom_call" | custom-call | tf_op jit(solution)/shard_map/oproj/pallas_call | solution.py:207
  106.8 9.6 %collective-permute-done.6 = bf16[128,2048]{1,0:T(8,128)(2,1)S(1)} collective-permute-done((bf16[128,2048]{1,0:T(8,128)(2,1)S(1)}, bf16[128,2048]{1,0:T(8,128)(2,1)S(1)}, u32[]{:S(2)}, u32[]{:S(2)}) %collective-permute-start.6) | collective-permute-done | bytes 524320 | tf_op jit(solution)/shard_map/ppermute | solution.py:23
  116.4 1.3 add_convert_fusion
  118.1 1.2 collective-permute-start.8
  119.3 0.9 collective-permute-start.7
  120.2 10.5 %collective-permute-done.8.x2_ref = bf16[128,2048]{1,0:T(8,128)(2,1)S(1)} collective-permute-done((bf16[128,2048]{1,0:T(8,128)(2,1)S(1)}, bf16[128,2048]{1,0:T(8,128)(2,1)S(1)}, u32[]{:S(2)}, u32[]{:S(2)}) %collective-permute-start.8) | collective-permute-done | bytes 524320 | tf_op jit(solution)/shard_map/ppermute | solution.py:440
  130.6 2.1 %collective-permute-done.7.x1_ref = bf16[128,2048]{1,0:T(8,128)(2,1)S(1)} collective-permute-done((bf16[128,2048]{1,0:T(8,128)(2,1)S(1)}, bf16[128,2048]{1,0:T(8,128)(2,1)S(1)}, u32[]{:S(2)}, u32[]{:S(2)}) %collective-permute-start.7) | collective-permute-done | bytes 524320 | tf_op jit(solution)/shard_map/ppermute | solution.py:439
  133.1 1.7 collective-permute-start.9
  134.9 6.7 %collective-permute-done.10.x4_ref = bf16[64,2048]{1,0:T(8,128)(2,1)S(1)} collective-permute-done((bf16[64,2048]{1,0:T(8,128)(2,1)S(1)}, bf16[64,2048]{1,0:T(8,128)(2,1)S(1)}, u32[]{:S(2)}, u32[]{:S(2)}) %collective-permute-start.10) | collective-permute-done | bytes 262176 | tf_op jit(solution)/shard_map/ppermute | solution.py:444
  141.6 1.3 collective-permute-done.9.x3_ref
  142.9 6.4 %gate_up.2.hid0_ref = bf16[512,768]{1,0:T(8,128)(2,1)S(1)} custom-call(s32[1]{0:T(128)} %bitcast.2.y_ref, bf16[128,2048]{1,0:T(8,128)(2,1)S(1)} %fusion.2.x0_ref, bf16[128,2048]{1,0:T(8,128)(2,1)S(1)} %collective-permute-done.7.x1_ref, bf16[128,2048]{1,0:T(8,128)(2,1)S(1)} %collective-permute-done.8.x2_ref, ...), custom_call_target="tpu_custom_call" | custom-call | tf_op jit(solution)/shard_map/gate_up/pallas_call | solution.py:293
  149.3 4.7 %gate_up.3.hid1_ref = bf16[512,768]{1,0:T(8,128)(2,1)S(1)} custom-call(s32[1]{0:T(128)} %bitcast.2.y_ref, bf16[128,2048]{1,0:T(8,128)(2,1)S(1)} %fusion.2.x0_ref, bf16[128,2048]{1,0:T(8,128)(2,1)S(1)} %collective-permute-done.7.x1_ref, bf16[128,2048]{1,0:T(8,128)(2,1)S(1)} %collective-permute-done.8.x2_ref, ...), custom_call_target="tpu_custom_call" | custom-call | tf_op jit(solution)/shard_map/gate_up/pallas_call | solution.py:293
  154.0 3.6 %down_far.1 = (bf16[64,2048]{1,0:T(8,128)(2,1)S(1)}, bf16[64,2048]{1,0:T(8,128)(2,1)S(1)}, bf16[1,16,96,2048]{3,2,1,0:T(8,128)(2,1)S(1)}) custom-call(s32[1]{0:T(128)} %bitcast.2.y_ref, bf16[512,768]{1,0:T(8,128)(2,1)S(1)} %gate_up.2.hid0_ref, bf16[512,768]{1,0:T(8,128)(2,1)S(1)} %gate_up.3.hid1_ref, bf16[8,2,4,288,256]{4,3,2,1,0:T(8,128)(2,1)} %bitcast.13, ...), custom_call_target="tpu_custom_call" | custom-call | tf_op jit(solution)/shard_map/down_far/pallas_call | solution.py:311
  158.1 2.8 %collective-permute-start.13 = (bf16[64,2048]{1,0:T(8,128)(2,1)S(1)}, bf16[64,2048]{1,0:T(8,128)(2,1)S(1)}, u32[]{:S(2)}, u32[]{:S(2)}) collective-permute-start(bf16[64,2048]{1,0:T(8,128)(2,1)S(1)} %get-tuple-element.50), channel_id=1, source_target_pairs={{0,3},{1,0},{2,1},{3,2},{4,7},{5,4},{6,5},{7,6},{8,11},{9,8},{10,9... | collective-permute-start | bytes 786440 | tf_op jit(solution)/shard_map/ppermute | solution.py:452
  160.9 3.2 %down.1 = (f32[128,2048]{1,0:T(8,128)S(1)}, bf16[128,2048]{1,0:T(8,128)(2,1)S(1)}, bf16[128,2048]{1,0:T(8,128)(2,1)S(1)}) custom-call(bf16[512,768]{1,0:T(8,128)(2,1)S(1)} %gate_up.2.hid0_ref, bf16[512,768]{1,0:T(8,128)(2,1)S(1)} %gate_up.3.hid1_ref, bf16[1,16,96,2048]{3,2,1,0:T(8,128)(2,1)S(1)} %get-tuple-element.46.w_ref), custom_call_target="tpu_custom_call" | custom-call | tf_op jit(solution)/shard_map/down/pallas_call | solution.py:323
  164.2 2.4 %collective-permute-done.12 = bf16[64,2048]{1,0:T(8,128)(2,1)S(1)} collective-permute-done((bf16[64,2048]{1,0:T(8,128)(2,1)S(1)}, bf16[64,2048]{1,0:T(8,128)(2,1)S(1)}, u32[]{:S(2)}, u32[]{:S(2)}) %collective-permute-start.12) | collective-permute-done | bytes 262176 | tf_op jit(solution)/shard_map/ppermute | solution.py:451
  166.8 3.0 %collective-permute-start.15 = (bf16[128,2048]{1,0:T(8,128)(2,1)S(1)}, bf16[128,2048]{1,0:T(8,128)(2,1)S(1)}, u32[]{:S(2)}, u32[]{:S(2)}) collective-permute-start(bf16[128,2048]{1,0:T(8,128)(2,1)S(1)} %pad_maximum_fusion.2), channel_id=1, source_target_pairs={{0,3},{1,0},{2,1},{3,2},{4,7},{5,4},{6,5},{7,6},{8,11},{9,8},{10,9... | collective-permute-start | bytes 1572872 | tf_op jit(solution)/shard_map/ppermute | solution.py:458
  169.9 9.5 %collective-permute-done.15 = bf16[128,2048]{1,0:T(8,128)(2,1)S(1)} collective-permute-done((bf16[128,2048]{1,0:T(8,128)(2,1)S(1)}, bf16[128,2048]{1,0:T(8,128)(2,1)S(1)}, u32[]{:S(2)}, u32[]{:S(2)}) %collective-permute-start.15) | collective-permute-done | bytes 524320 | tf_op jit(solution)/shard_map/ppermute | solution.py:458
  179.5 3.5 %collective-permute-done.14 = bf16[128,2048]{1,0:T(8,128)(2,1)S(1)} collective-permute-done((bf16[128,2048]{1,0:T(8,128)(2,1)S(1)}, bf16[128,2048]{1,0:T(8,128)(2,1)S(1)}, u32[]{:S(2)}, u32[]{:S(2)}) %collective-permute-start.14) | collective-permute-done | bytes 524320 | tf_op jit(solution)/shard_map/ppermute | solution.py:457
  183.0 1.1 fusion.3
  (49 shorter events, 2.2 us)
Async XLA Ops:
  9.5 15.0 %copy-start.11 = (s32[1024]{0:T(1024)S(1)}, s32[1024]{0:T(1024)}, u32[]{:S(2)}) copy-start(s32[1024]{0:T(1024)} %param.15) | copy-start | bytes 12292
  9.5 28.3 %all-to-all-start = ((bf16[8,768,128]{2,1,0:T(8,128)(2,1)}), bf16[8,768,128]{2,1,0:T(8,128)(2,1)}, u32[]{:S(2)}, u32[]{:S(2)}) async-start(bf16[8,768,128]{2,1,0:T(8,128)(2,1)} %pack.1), calls=%async_computation | async-start | bytes 3145728 | tf_op jit(solution)/shard_map/all_to_all | solution.py:403
  17.5 115.2 %all-gather.3.cloned.1.call-start = ((), (), s32[]{:S(2)}) async-start(), calls=%async_computation.4 | async-start | bytes 10027008 | tf_op jit(solution)/shard_map/all_gather | solution.py:412
  19.9 9.0 %collective-permute-start = (bf16[288,256]{1,0:T(8,128)(2,1)}, bf16[288,256]{1,0:T(8,128)(2,1)S(1)}, u32[]{:S(2)}, u32[]{:S(2)}) collective-permute-start(bf16[288,256]{1,0:T(8,128)(2,1)} %get-tuple-element.29), channel_id=1, source_target_pairs={{0,3},{1,0},{2,1},{3,2},{4,7},{5,4},{6,5},{7,6},{8,11},{9,8},{10,9... | collective-permute-start | bytes 442376 | tf_op jit(solution)/shard_map/ppermute | solution.py:377
  22.9 8.1 %collective-permute-start.1 = (bf16[288,256]{1,0:T(8,128)(2,1)}, bf16[288,256]{1,0:T(8,128)(2,1)S(1)}, u32[]{:S(2)}, u32[]{:S(2)}) collective-permute-start(bf16[288,256]{1,0:T(8,128)(2,1)} %get-tuple-element.30), channel_id=1, source_target_pairs={{0,2},{1,3},{2,0},{3,1},{4,6},{5,7},{6,4},{7,5},{8,10},{9,11},{10,... | collective-permute-start | bytes 442376 | tf_op jit(solution)/shard_map/ppermute | solution.py:377
  23.5 9.0 %collective-permute-start.2 = (bf16[288,256]{1,0:T(8,128)(2,1)}, bf16[288,256]{1,0:T(8,128)(2,1)S(1)}, u32[]{:S(2)}, u32[]{:S(2)}) collective-permute-start(bf16[288,256]{1,0:T(8,128)(2,1)} %get-tuple-element.31), channel_id=1, source_target_pairs={{0,1},{1,2},{2,3},{3,0},{4,5},{5,6},{6,7},{7,4},{8,9},{9,10},{10,1... | collective-permute-start | bytes 442376 | tf_op jit(solution)/shard_map/ppermute | solution.py:377
  28.9 3.6 %copy-start.7 = (bf16[288,256]{1,0:T(8,128)(2,1)}, bf16[288,256]{1,0:T(8,128)(2,1)S(1)}, u32[]{:S(2)}) copy-start(bf16[288,256]{1,0:T(8,128)(2,1)S(1)} %collective-permute-done.p1_ref) | copy-start | bytes 442372
  31.0 1.5 copy-start.8
  32.5 0.7 copy-start.9
  37.8 7.3 %collective-permute-start.3 = (bf16[8,768,128]{2,1,0:T(8,128)(2,1)}, bf16[8,768,128]{2,1,0:T(8,128)(2,1)}, u32[]{:S(2)}, u32[]{:S(2)}) collective-permute-start(bf16[8,768,128]{2,1,0:T(8,128)(2,1)} %all-to-all-done.own_ref.src_ref), channel_id=1, source_target_pairs={{0,8},{8,0},{1,9},{9,1},{2,10},{10,2},{3,11},{11,3},{4,12},{12,4},... | collective-permute-start | bytes 4718600 | tf_op jit(solution)/shard_map/ppermute | solution.py:23
  40.5 4.6 %copy-start.4 = (f32[2048]{0:T(1024)S(1)}, f32[2048]{0:T(1024)}, u32[]{:S(2)}) copy-start(f32[2048]{0:T(1024)} %param.16) | copy-start | bytes 24580
  40.5 4.6 %copy-start.5 = (f32[128]{0:T(128)S(1)}, f32[128]{0:T(128)}, u32[]{:S(2)}) copy-start(f32[128]{0:T(128)} %param.18) | copy-start | bytes 1540
  40.5 4.6 %copy-start.6 = (f32[128]{0:T(128)S(1)}, f32[128]{0:T(128)}, u32[]{:S(2)}) copy-start(f32[128]{0:T(128)} %param.19) | copy-start | bytes 1540
  40.5 35.0 %all-to-all-start.2 = ((bf16[4,8,256,128]{3,2,1,0:T(8,128)(2,1)}), bf16[4,8,256,128]{3,2,1,0:T(8,128)(2,1)S(1)}, u32[]{:S(2)}, u32[]{:S(2)}) async-start(bf16[4,8,256,128]{3,2,1,0:T(8,128)(2,1)} %widen.1), calls=%async_computation.2 | async-start | bytes 4194304 | tf_op jit(solution)/shard_map/all_to_all | solution.py:417
  53.1 12.5 %collective-permute-start.4 = (bf16[2,512,128]{2,1,0:T(8,128)(2,1)}, bf16[2,512,128]{2,1,0:T(8,128)(2,1)S(1)}, u32[]{:S(2)}, u32[]{:S(2)}) collective-permute-start(bf16[2,512,128]{2,1,0:T(8,128)(2,1)} %get-tuple-element.36), channel_id=1, source_target_pairs={{0,8},{8,16},{16,24},{24,32},{32,40},{40,48},{48,56},{56,64},{64,7... | collective-permute-start | bytes 786440 | tf_op jit(solution)/shard_map/ppermute | solution.py:421
  65.6 1.0 copy-start.2
  70.8 0.7 copy-start.3
  75.5 11.7 %collective-permute-start.5 = (bf16[4,8,256,128]{3,2,1,0:T(8,128)(2,1)S(1)}, bf16[4,8,256,128]{3,2,1,0:T(8,128)(2,1)S(1)}, u32[]{:S(2)}, u32[]{:S(2)}) collective-permute-start(bf16[4,8,256,128]{3,2,1,0:T(8,128)(2,1)S(1)} %all-to-all-done.2.own_ref), channel_id=1, source_target_pairs={{0,8},{8,0},{1,9},{9,1},{2,10},{10,2},{3,11},{11,3},{4,12},{12,4},... | collective-permute-start | bytes 6291464 | tf_op jit(solution)/shard_map/ppermute | solution.py:23
  87.2 3.6 %copy-start = (bf16[4,8,256,128]{3,2,1,0:T(8,128)(2,1)}, bf16[4,8,256,128]{3,2,1,0:T(8,128)(2,1)S(1)}, u32[]{:S(2)}) copy-start(bf16[4,8,256,128]{3,2,1,0:T(8,128)(2,1)S(1)} %collective-permute-done.5.oth_ref) | copy-start | bytes 6291460
  90.8 25.6 %collective-permute-start.6 = (bf16[128,2048]{1,0:T(8,128)(2,1)S(1)}, bf16[128,2048]{1,0:T(8,128)(2,1)S(1)}, u32[]{:S(2)}, u32[]{:S(2)}) collective-permute-start(bf16[128,2048]{1,0:T(8,128)(2,1)S(1)} %oproj.2), channel_id=1, source_target_pairs={{0,4},{4,0},{1,5},{5,1},{2,6},{6,2},{3,7},{7,3},{8,12},{12,8},{9,1... | collective-permute-start | bytes 1572872 | tf_op jit(solution)/shard_map/ppermute | solution.py:23
  91.4 10.1 %all-to-all-start.3 = ((bf16[4,128,256]{2,1,0:T(8,128)(2,1)}), bf16[4,128,256]{2,1,0:T(8,128)(2,1)S(1)}, u32[]{:S(2)}, u32[]{:S(2)}) async-start(bf16[4,128,256]{2,1,0:T(8,128)(2,1)} %attend.3), calls=%async_computation.3 | async-start | bytes 524288 | tf_op jit(solution)/shard_map/all_to_all | solution.py:422
  101.5 1.7 copy-start.1
  106.8 11.1 %copy-start.10 = (f32[2048]{0:T(1024)S(1)}, f32[2048]{0:T(1024)}, u32[]{:S(2)}) copy-start(f32[2048]{0:T(1024)} %param.17) | copy-start | bytes 24580
  118.1 12.6 %collective-permute-start.8 = (bf16[128,2048]{1,0:T(8,128)(2,1)S(1)}, bf16[128,2048]{1,0:T(8,128)(2,1)S(1)}, u32[]{:S(2)}, u32[]{:S(2)}) collective-permute-start(bf16[128,2048]{1,0:T(8,128)(2,1)S(1)} %fusion.2.x0_ref), channel_id=1, source_target_pairs={{0,3},{1,0},{2,1},{3,2},{4,7},{5,4},{6,5},{7,6},{8,11},{9,8},{10,9... | collective-permute-start | bytes 1572872 | tf_op jit(solution)/shard_map/ppermute | solution.py:440
  119.3 13.4 %collective-permute-start.7 = (bf16[128,2048]{1,0:T(8,128)(2,1)S(1)}, bf16[128,2048]{1,0:T(8,128)(2,1)S(1)}, u32[]{:S(2)}, u32[]{:S(2)}) collective-permute-start(bf16[128,2048]{1,0:T(8,128)(2,1)S(1)} %fusion.2.x0_ref), channel_id=1, source_target_pairs={{0,1},{1,2},{2,3},{3,0},{4,5},{5,6},{6,7},{7,4},{8,9},{9,10},{10,1... | collective-permute-start | bytes 1572872 | tf_op jit(solution)/shard_map/ppermute | solution.py:439
  132.7 16.5 %collective-permute-start.11 = (bf16[8,2,4,288,256]{4,3,2,1,0:T(8,128)(2,1)}, bf16[8,2,4,288,256]{4,3,2,1,0:T(8,128)(2,1)S(1)}, u32[]{:S(2)}, u32[]{:S(2)}) collective-permute-start(bf16[8,2,4,288,256]{4,3,2,1,0:T(8,128)(2,1)} %bitcast.11), channel_id=1, source_target_pairs={{0,8},{8,0},{1,9},{9,1},{2,10},{10,2},{3,11},{11,3},{4,12},{12,4},... | collective-permute-start | bytes 28311560 | tf_op jit(solution)/shard_map/ppermute | solution.py:23
  132.8 8.8 %collective-permute-start.10 = (bf16[64,2048]{1,0:T(8,128)(2,1)S(1)}, bf16[64,2048]{1,0:T(8,128)(2,1)S(1)}, u32[]{:S(2)}, u32[]{:S(2)}) collective-permute-start(bf16[64,2048]{1,0:T(8,128)(2,1)S(1)} %slice.19), channel_id=1, source_target_pairs={{0,3},{1,0},{2,1},{3,2},{4,7},{5,4},{6,5},{7,6},{8,11},{9,8},{10,9... | collective-permute-start | bytes 786440 | tf_op jit(solution)/shard_map/ppermute | solution.py:444
  133.1 9.7 %collective-permute-start.9 = (bf16[64,2048]{1,0:T(8,128)(2,1)S(1)}, bf16[64,2048]{1,0:T(8,128)(2,1)S(1)}, u32[]{:S(2)}, u32[]{:S(2)}) collective-permute-start(bf16[64,2048]{1,0:T(8,128)(2,1)S(1)} %slice.18), channel_id=1, source_target_pairs={{0,1},{1,2},{2,3},{3,0},{4,5},{5,6},{6,7},{7,4},{8,9},{9,10},{10,1... | collective-permute-start | bytes 786440 | tf_op jit(solution)/shard_map/ppermute | solution.py:443
  157.6 9.0 %collective-permute-start.12 = (bf16[64,2048]{1,0:T(8,128)(2,1)S(1)}, bf16[64,2048]{1,0:T(8,128)(2,1)S(1)}, u32[]{:S(2)}, u32[]{:S(2)}) collective-permute-start(bf16[64,2048]{1,0:T(8,128)(2,1)S(1)} %get-tuple-element.49), channel_id=1, source_target_pairs={{0,1},{1,2},{2,3},{3,0},{4,5},{5,6},{6,7},{7,4},{8,9},{9,10},{10,1... | collective-permute-start | bytes 786440 | tf_op jit(solution)/shard_map/ppermute | solution.py:451
  158.1 8.5 %collective-permute-start.13 = (bf16[64,2048]{1,0:T(8,128)(2,1)S(1)}, bf16[64,2048]{1,0:T(8,128)(2,1)S(1)}, u32[]{:S(2)}, u32[]{:S(2)}) collective-permute-start(bf16[64,2048]{1,0:T(8,128)(2,1)S(1)} %get-tuple-element.50), channel_id=1, source_target_pairs={{0,3},{1,0},{2,1},{3,2},{4,7},{5,4},{6,5},{7,6},{8,11},{9,8},{10,9... | collective-permute-start | bytes 786440 | tf_op jit(solution)/shard_map/ppermute | solution.py:452
  166.8 12.7 %collective-permute-start.15 = (bf16[128,2048]{1,0:T(8,128)(2,1)S(1)}, bf16[128,2048]{1,0:T(8,128)(2,1)S(1)}, u32[]{:S(2)}, u32[]{:S(2)}) collective-permute-start(bf16[128,2048]{1,0:T(8,128)(2,1)S(1)} %pad_maximum_fusion.2), channel_id=1, source_target_pairs={{0,3},{1,0},{2,1},{3,2},{4,7},{5,4},{6,5},{7,6},{8,11},{9,8},{10,9... | collective-permute-start | bytes 1572872 | tf_op jit(solution)/shard_map/ppermute | solution.py:458
  169.9 13.1 %collective-permute-start.14 = (bf16[128,2048]{1,0:T(8,128)(2,1)S(1)}, bf16[128,2048]{1,0:T(8,128)(2,1)S(1)}, u32[]{:S(2)}, u32[]{:S(2)}) collective-permute-start(bf16[128,2048]{1,0:T(8,128)(2,1)S(1)} %pad_maximum_fusion.1), channel_id=1, source_target_pairs={{0,1},{1,2},{2,3},{3,0},{4,5},{5,6},{6,7},{7,4},{8,9},{9,10},{10,1... | collective-permute-start | bytes 1572872 | tf_op jit(solution)/shard_map/ppermute | solution.py:457
Sparse Core Ops, SparseCore 0:
  37.9 86.2 all-gather.2

commit v11 on v10

--- a/solution.py
+++ b/solution.py
@@ -23,7 +23,25 @@
     return lax.ppermute(block, axis, [(0, 1), (1, 0)])
 
 
-def qkv_kernel(core_ref, x_ref, own_ref, oth_ref, gain_ref, qg_ref, kg_ref, cs_ref, q_ref, kv_ref, tail_ref, w_ref):
+def norm_kernel(x_ref, gain_ref, out_ref):
+    x = x_ref[...].astype(F32)
+    scale = lax.rsqrt(jnp.mean(x * x, axis=-1, keepdims=True) + 1e-06)
+    out_ref[...] = (x * scale * gain_ref[...]).astype(BF)
+
+
+def normalise(x, gain):
+    block = pl.BlockSpec((256, 2048), lambda i: (i, 0))
+    return pl.pallas_call(
+        norm_kernel,
+        grid=(x.shape[0] // 256,),
+        in_specs=[block, pl.BlockSpec((1, 2048), lambda i: (0, 0))],
+        out_specs=block,
+        out_shape=jax.ShapeDtypeStruct(x.shape, BF),
+        name="norm",
+    )(x, gain[None])
+
+
+def qkv_kernel(core_ref, x_ref, own_ref, oth_ref, qg_ref, kg_ref, cs_ref, q_ref, kv_ref, tail_ref, w_ref):
     core = core_ref[0]
 
     @pl.when(pl.program_id(0) == 0)
@@ -37,10 +55,7 @@
 
         lax.fori_loop(0, 8, place, 0)
 
-    x = x_ref[...].astype(F32)
-    scale = lax.rsqrt(jnp.mean(x * x, axis=-1, keepdims=True) + 1e-06)
-    normed = (x * scale * gain_ref[...]).astype(BF)
-    raw = jnp.dot(normed, w_ref[...], preferred_element_type=F32)
+    raw = jnp.dot(x_ref[...], w_ref[...], preferred_element_type=F32)
     cs = cs_ref[...]
     turned = pltpu.roll(cs, 64, 1)
     low = lax.broadcasted_iota(jnp.int32, cs.shape, 1) < 64
@@ -64,8 +79,8 @@
         tail_ref[1] = values
 
 
-def project(core, tokens, own, oth, attn_gain, q_gain, key_gain, cs):
-    rows = tokens.shape[0]
+def project(core, normed, own, oth, q_gain, key_gain, cs):
+    rows = normed.shape[0]
     tile = 256
     fixed = lambda *shape: pl.BlockSpec(shape, lambda i, c: (0,) * len(shape))
     return pl.pallas_call(
@@ -77,7 +92,6 @@
                 pl.BlockSpec((tile, 2048), lambda i, c: (i, 0)),
                 fixed(8, 512, 128),
                 fixed(8, 512, 128),
-                fixed(1, 2048),
                 fixed(1, 128),
                 fixed(1, 128),
                 pl.BlockSpec((tile, 128), lambda i, c: (i, 0)),
@@ -96,7 +110,7 @@
         ),
         compiler_params=pltpu.CompilerParams(vmem_limit_bytes=24 << 20),
         name="qkv",
-    )(core, tokens, own, oth, attn_gain[None], q_gain[None], key_gain[None], cs)
+    )(core, normed, own, oth, q_gain[None], key_gain[None], cs)
 
 
 def widen_kernel(src_ref, out_ref):
@@ -408,7 +422,8 @@
     angle = positions.astype(F32)[:, None] * freq[None, :]
     cs = jnp.concatenate([jnp.cos(angle), jnp.sin(angle)], axis=1)
     group = join(parts)
-    cs, at_own, group = hold((cs, at_own, group))
+    normed = normalise(tokens, attn_gain)
+    cs, normed, at_own, group = hold((cs, normed, at_own, group))
     mlp_own = lax.all_gather(group, ("z", "xh", "xl"), axis=0, tiled=False).reshape(8, 2, 4, 288, 256)
     lo = (jnp.arange(rows, dtype=jnp.int32) - positions)[:, None]
 
@@ -416,8 +431,8 @@
 
     o_own = lax.all_to_all(widen(at_own), "y", split_axis=0, concat_axis=0, tiled=True)
 
-    rows_in = pltpu.with_memory_space_constraint(tokens, pltpu.HBM)
-    q, cache, tail = project(core[None], rows_in, at_own, at_oth, attn_gain, q_gain, key_norm_gain, cs)
+    normed = pltpu.with_memory_space_constraint(normed, pltpu.HBM)
+    q, cache, tail = project(core[None], normed, at_own, at_oth, q_gain, key_norm_gain, cs)
     prior = lax.ppermute(tail, REQ, [(i - 1, i) for i in range(1, 16)])
     turn = lambda part: lax.all_to_all(part, "y", split_axis=0, concat_axis=0, tiled=True)
     theirs = attend(1 - xl[None], q, cache, prior, lo)

time: 192 us -> 193 us (level)
  Pallas kernels: 50.6 us -> 55.4 us
  waiting for transfers between devices: 70.9 us -> 66.2 us
    ppermute x3, waiting for transfers between devices: 5.89 us -> 0.44 us  [trade(): lax.ppermute(parts[4 - k], 'y', ring(4 - k))]
    pallas_call x0 -> x1, Pallas kernels: none -> 5.42 us  [normalise(): pl.pallas_call(norm_kernel, grid=(x.shape[0] // 256,), in_specs=[block, p...]
    unnamed x24 -> x22, local copies, waits for them, and re-layouts: 4.09 us -> 5.31 us
  transfers between devices with their start and end apart: 20 -> 20, of which waited for: 14 -> 12; matrix products, arithmetic and copies ran while one was open for 2% -> 2% of each run, Pallas kernels for 21% -> 23%
where the time goes in v11:
time: 193 us; the launch traced here: 192 us
  waiting for transfers between devices  66.2 us (34%)
  Pallas kernels  55.4 us (29%)
  starting transfers between devices  33.7 us (17%)
  between operations  14.3 us (7%)
  blocking collectives  11.6 us (6%)
  local copies, waits for them, and re-layouts  5.61 us (3%)
  other arithmetic  5.06 us (3%)
    all_to_all x1, blocking collectives, per_device(): lax.all_to_all(part, 'y', split_axis=0, concat_axis=0, tiled=True)  11.6 us
    pallas_call x2, Pallas kernels, gate_up(): pl.pallas_call(gate_kernel, in_specs=[pl.BlockSpec(memory_space=pltpu.SME...  11.1 us
    ppermute x1, waiting for transfers between devices, per_device(): prior = lax.ppermute(tail, REQ, [(i - 1, i) for i in range(1, 16)])  10.9 us
    ppermute x1, waiting for transfers between devices, per_device(): right = lax.ppermute(mlp_in, 'y', ring(3))  10.5 us
    ppermute x4, waiting for transfers between devices, swap(): return lax.ppermute(block, axis, [(0, 1), (1, 0)])  9.62 us
    ppermute x1, waiting for transfers between devices, per_device(): from_right = lax.ppermute(to_left, 'y', ring(3))  9.5 us
    pallas_call x2, Pallas kernels, attend(): pl.pallas_call(attend_kernel, in_specs=[pl.BlockSpec(memory_space=pltpu.S...  8.18 us
    all_to_all x1, starting transfers between devices, per_device(): lax.all_to_all(packed, ('z', 'xh'), split_axis=0, concat_axis=0, tiled=True)  7.88 us
  transfers between devices with their start and end apart: 20, of which 12 were waited for; matrix products, arithmetic and copies ran while one was open for 2% of the time, Pallas kernels for 23%

profile of v11, /device:TPU:32, one launch (start us, length us, event | category | flops | bytes accessed | tf_op | source)
XLA Modules:
  0.0 191.9 jit_solution(12782969645081342077)
XLA Ops:
  7.2 2.3 %pack.1 = bf16[8,768,128]{2,1,0:T(8,128)(2,1)} custom-call(f32[128,256]{1,0:T(8,128)} %q_ref.1, f32[128,128]{1,0:T(8,128)} %k_ref.1, f32[128,128]{1,0:T(8,128)} %v_ref.1, f32[256,128]{1,0:T(8,128)} %o_ref.1), custom_call_target="tpu_custom_call" | custom-call | tf_op jit(solution)/shard_map/pack/pallas_call | solution.py:353
  9.5 7.9 %all-to-all-start = ((bf16[8,768,128]{2,1,0:T(8,128)(2,1)}), bf16[8,768,128]{2,1,0:T(8,128)(2,1)}, u32[]{:S(2)}, u32[]{:S(2)}) async-start(bf16[8,768,128]{2,1,0:T(8,128)(2,1)} %pack.1), calls=%async_computation | async-start | bytes 3145728 | tf_op jit(solution)/shard_map/all_to_all | solution.py:417
  17.4 2.4 %prep.1 = (bf16[288,256]{1,0:T(8,128)(2,1)}, bf16[288,256]{1,0:T(8,128)(2,1)}, bf16[288,256]{1,0:T(8,128)(2,1)}, bf16[288,256]{1,0:T(8,128)(2,1)}) custom-call(s32[1]{0:T(128)} %bitcast.3.y_ref, f32[256,384]{1,0:T(8,128)} %gate_ref.1, f32[256,384]{1,0:T(8,128)} %up_ref.1, f32[384,256]{1,0:T(8,128)} %down_ref.1), custom_call_target="tpu_custom_call" | custom-call | tf_op jit(solution)/shard_map/prep/pallas_call | solution.py:372
  19.7 3.0 %collective-permute-start = (bf16[288,256]{1,0:T(8,128)(2,1)}, bf16[288,256]{1,0:T(8,128)(2,1)S(1)}, u32[]{:S(2)}, u32[]{:S(2)}) collective-permute-start(bf16[288,256]{1,0:T(8,128)(2,1)} %get-tuple-element.30), channel_id=1, source_target_pairs={{0,3},{1,0},{2,1},{3,2},{4,7},{5,4},{6,5},{7,6},{8,11},{9,8},{10,9... | collective-permute-start | bytes 442376 | tf_op jit(solution)/shard_map/ppermute | solution.py:391
  22.7 0.6 collective-permute-start.1
  23.4 1.0 collective-permute-start.2
  24.4 1.9 multiply_cosine_fusion
  26.2 5.4 %norm.1.x_ref = bf16[1024,2048]{1,0:T(8,128)(2,1)} custom-call(bf16[1024,2048]{1,0:T(8,128)(2,1)} %x_ref.1, f32[1,2048]{1,0:T(1,128)} %bitcast.14), custom_call_target="tpu_custom_call" | custom-call | tf_op jit(solution)/shard_map/norm/pallas_call | solution.py:34
  31.9 0.4 collective-permute-done.2.p3_ref
  33.0 2.0 %join.1 = bf16[4,288,256]{2,1,0:T(8,128)(2,1)} custom-call(bf16[288,256]{1,0:T(8,128)(2,1)} %get-tuple-element.29.p0_ref, bf16[288,256]{1,0:T(8,128)(2,1)} %copy-done.6, bf16[288,256]{1,0:T(8,128)(2,1)} %copy-done.7, bf16[288,256]{1,0:T(8,128)(2,1)} %copy-done.8), custom_call_target="tpu_custom_call" | custom-call | tf_op jit(solution)/shard_map/join/pallas_call | solution.py:387
  35.0 2.6 %all-to-all-done.own_ref.src_ref = bf16[8,768,128]{2,1,0:T(8,128)(2,1)} async-done(((bf16[8,768,128]{2,1,0:T(8,128)(2,1)}), bf16[8,768,128]{2,1,0:T(8,128)(2,1)}, u32[]{:S(2)}, u32[]{:S(2)}) %all-to-all-start) | async-done | bytes 1572896 | tf_op jit(solution)/shard_map/all_to_all | solution.py:417
  37.7 2.6 %widen.1 = bf16[4,8,256,128]{3,2,1,0:T(8,128)(2,1)} custom-call(bf16[8,768,128]{2,1,0:T(8,128)(2,1)} %all-to-all-done.own_ref.src_ref), custom_call_target="tpu_custom_call" | custom-call | tf_op jit(solution)/shard_map/widen/pallas_call | solution.py:122
  40.4 4.5 %all-to-all-start.2 = ((bf16[4,8,256,128]{3,2,1,0:T(8,128)(2,1)}), bf16[4,8,256,128]{3,2,1,0:T(8,128)(2,1)S(1)}, u32[]{:S(2)}, u32[]{:S(2)}) async-start(bf16[4,8,256,128]{3,2,1,0:T(8,128)(2,1)} %widen.1), calls=%async_computation.2 | async-start | bytes 4194304 | tf_op jit(solution)/shard_map/all_to_all | solution.py:432
  44.8 7.3 %qkv.1 = (bf16[1024,256]{1,0:T(8,128)(2,1)S(1)}, bf16[2,1024,128]{2,1,0:T(8,128)(2,1)}, bf16[2,512,128]{2,1,0:T(8,128)(2,1)}) custom-call(s32[1]{0:T(128)} %bitcast.core_ref, bf16[1024,2048]{1,0:T(8,128)(2,1)} %norm.1.x_ref, bf16[8,768,128]{2,1,0:T(8,128)(2,1)} %all-to-all-done.own_ref.src_ref, bf16[8,768,128]{2,1,0:T(8,128)(2,1)} %collective-permute-done.3.oth_ref, ...), custom_call_target="tpu_custom_call" | custom-call | tf_op jit(solution)/shard_map/qkv/pallas_call | solution.py:86
  52.2 2.1 %collective-permute-start.4 = (bf16[2,512,128]{2,1,0:T(8,128)(2,1)}, bf16[2,512,128]{2,1,0:T(8,128)(2,1)S(1)}, u32[]{:S(2)}, u32[]{:S(2)}) collective-permute-start(bf16[2,512,128]{2,1,0:T(8,128)(2,1)} %get-tuple-element.38), channel_id=1, source_target_pairs={{0,8},{8,16},{16,24},{24,32},{32,40},{40,48},{48,56},{56,64},{64,7... | collective-permute-start | bytes 786440 | tf_op jit(solution)/shard_map/ppermute | solution.py:436
  54.5 10.9 %collective-permute-done.4.prior_ref = bf16[2,512,128]{2,1,0:T(8,128)(2,1)S(1)} collective-permute-done((bf16[2,512,128]{2,1,0:T(8,128)(2,1)}, bf16[2,512,128]{2,1,0:T(8,128)(2,1)S(1)}, u32[]{:S(2)}, u32[]{:S(2)}) %collective-permute-start.4) | collective-permute-done | bytes 262176 | tf_op jit(solution)/shard_map/ppermute | solution.py:436
  65.4 1.0 copy-done.2
  66.5 4.2 %attend.2 = bf16[4,128,256]{2,1,0:T(8,128)(2,1)S(1)} custom-call(s32[1]{0:T(128)S(6)} %sub.6.half_ref, bf16[1024,256]{1,0:T(8,128)(2,1)S(1)} %get-tuple-element.39.q_ref, bf16[2,1024,128]{2,1,0:T(8,128)(2,1)S(1)} %copy-done.2, bf16[2,512,128]{2,1,0:T(8,128)(2,1)S(1)} %collective-permute-done.4.prior_ref, s32[1024,1]{1,0:T(8,128)S(1)} %copy.17.lo_ref), custom_call_target="tpu_custom_call" | custom-call | tf_op jit(solution)/shard_map/attend/pallas_call | solution.py:182
  70.6 0.7 copy-done.3
  71.3 4.0 %attend.3 = bf16[4,128,256]{2,1,0:T(8,128)(2,1)} custom-call(s32[1]{0:T(128)} %bitcast.1.half_ref, bf16[1024,256]{1,0:T(8,128)(2,1)S(1)} %get-tuple-element.39.q_ref, bf16[2,1024,128]{2,1,0:T(8,128)(2,1)S(1)} %copy-done.2, bf16[2,512,128]{2,1,0:T(8,128)(2,1)S(1)} %collective-permute-done.4.prior_ref, s32[1024,1]{1,0:T(8,128)S(1)} %copy.17.lo_ref), custom_call_target="tpu_custom_call" | custom-call | tf_op jit(solution)/shard_map/attend/pallas_call | solution.py:182
  75.3 11.6 %all_to_all.20.ctx_ref = bf16[4,128,256]{2,1,0:T(8,128)(2,1)S(1)} all-to-all(bf16[4,128,256]{2,1,0:T(8,128)(2,1)} %copy-done.3), channel_id=1, replica_groups=mesh['z'=4,'xh'=2,'core'=2,'xl'=2,'y'=4] {'y'}, dimensions={0} | all-to-all | bytes 524288 | tf_op jit(solution)/shard_map/all_to_all | solution.py:437
  87.0 3.6 %oproj.2 = bf16[128,2048]{1,0:T(8,128)(2,1)S(1)} custom-call(s32[1]{0:T(128)} %bitcast.core_ref, bf16[4,128,256]{2,1,0:T(8,128)(2,1)S(1)} %all_to_all.20.ctx_ref, bf16[4,8,256,128]{3,2,1,0:T(8,128)(2,1)S(1)} %all-to-all-done.2.own_ref, bf16[4,8,256,128]{3,2,1,0:T(8,128)(2,1)S(1)} %collective-permute-done.5.oth_ref), custom_call_target="tpu_custom_call" | custom-call | tf_op jit(solution)/shard_map/oproj/pallas_call | solution.py:221
  90.6 1.3 copy-done
  91.9 0.5 collective-permute-start.6
  92.5 3.4 %all-to-all-start.3 = ((bf16[4,128,256]{2,1,0:T(8,128)(2,1)}), bf16[4,128,256]{2,1,0:T(8,128)(2,1)S(1)}, u32[]{:S(2)}, u32[]{:S(2)}) async-start(bf16[4,128,256]{2,1,0:T(8,128)(2,1)} %attend.3), calls=%async_computation.3 | async-start | bytes 524288 | tf_op jit(solution)/shard_map/all_to_all | solution.py:437
  95.9 6.6 %all-to-all-done.3.ctx_ref = bf16[4,128,256]{2,1,0:T(8,128)(2,1)S(1)} async-done(((bf16[4,128,256]{2,1,0:T(8,128)(2,1)}), bf16[4,128,256]{2,1,0:T(8,128)(2,1)S(1)}, u32[]{:S(2)}, u32[]{:S(2)}) %all-to-all-start.3) | async-done | bytes 262176 | tf_op jit(solution)/shard_map/all_to_all | solution.py:437
  102.5 1.6 copy-done.1
  104.1 3.6 %oproj.3 = f32[128,2048]{1,0:T(8,128)S(1)} custom-call(s32[1]{0:T(128)} %bitcast.core_ref, bf16[4,128,256]{2,1,0:T(8,128)(2,1)S(1)} %all-to-all-done.3.ctx_ref, bf16[4,8,256,128]{3,2,1,0:T(8,128)(2,1)S(1)} %all-to-all-done.2.own_ref, bf16[4,8,256,128]{3,2,1,0:T(8,128)(2,1)S(1)} %copy-done.1), custom_call_target="tpu_custom_call" | custom-call | tf_op jit(solution)/shard_map/oproj/pallas_call | solution.py:221
  107.8 9.6 %collective-permute-done.6 = bf16[128,2048]{1,0:T(8,128)(2,1)S(1)} collective-permute-done((bf16[128,2048]{1,0:T(8,128)(2,1)S(1)}, bf16[128,2048]{1,0:T(8,128)(2,1)S(1)}, u32[]{:S(2)}, u32[]{:S(2)}) %collective-permute-start.6) | collective-permute-done | bytes 524320 | tf_op jit(solution)/shard_map/ppermute | solution.py:23
  117.4 1.3 add_convert_fusion
  119.1 1.2 collective-permute-start.8
  120.3 0.9 collective-permute-start.7
  121.1 10.5 %collective-permute-done.8.x2_ref = bf16[128,2048]{1,0:T(8,128)(2,1)S(1)} collective-permute-done((bf16[128,2048]{1,0:T(8,128)(2,1)S(1)}, bf16[128,2048]{1,0:T(8,128)(2,1)S(1)}, u32[]{:S(2)}, u32[]{:S(2)}) %collective-permute-start.8) | collective-permute-done | bytes 524320 | tf_op jit(solution)/shard_map/ppermute | solution.py:455
  131.6 2.1 %collective-permute-done.7.x1_ref = bf16[128,2048]{1,0:T(8,128)(2,1)S(1)} collective-permute-done((bf16[128,2048]{1,0:T(8,128)(2,1)S(1)}, bf16[128,2048]{1,0:T(8,128)(2,1)S(1)}, u32[]{:S(2)}, u32[]{:S(2)}) %collective-permute-start.7) | collective-permute-done | bytes 524320 | tf_op jit(solution)/shard_map/ppermute | solution.py:454
  134.1 1.7 collective-permute-start.9
  135.9 6.7 %collective-permute-done.10.x4_ref = bf16[64,2048]{1,0:T(8,128)(2,1)S(1)} collective-permute-done((bf16[64,2048]{1,0:T(8,128)(2,1)S(1)}, bf16[64,2048]{1,0:T(8,128)(2,1)S(1)}, u32[]{:S(2)}, u32[]{:S(2)}) %collective-permute-start.10) | collective-permute-done | bytes 262176 | tf_op jit(solution)/shard_map/ppermute | solution.py:459
  142.6 1.3 collective-permute-done.9.x3_ref
  143.9 6.4 %gate_up.2.hid0_ref = bf16[512,768]{1,0:T(8,128)(2,1)S(1)} custom-call(s32[1]{0:T(128)} %bitcast.3.y_ref, bf16[128,2048]{1,0:T(8,128)(2,1)S(1)} %fusion.2.x0_ref, bf16[128,2048]{1,0:T(8,128)(2,1)S(1)} %collective-permute-done.7.x1_ref, bf16[128,2048]{1,0:T(8,128)(2,1)S(1)} %collective-permute-done.8.x2_ref, ...), custom_call_target="tpu_custom_call" | custom-call | tf_op jit(solution)/shard_map/gate_up/pallas_call | solution.py:307
  150.3 4.7 %gate_up.3.hid1_ref = bf16[512,768]{1,0:T(8,128)(2,1)S(1)} custom-call(s32[1]{0:T(128)} %bitcast.3.y_ref, bf16[128,2048]{1,0:T(8,128)(2,1)S(1)} %fusion.2.x0_ref, bf16[128,2048]{1,0:T(8,128)(2,1)S(1)} %collective-permute-done.7.x1_ref, bf16[128,2048]{1,0:T(8,128)(2,1)S(1)} %collective-permute-done.8.x2_ref, ...), custom_call_target="tpu_custom_call" | custom-call | tf_op jit(solution)/shard_map/gate_up/pallas_call | solution.py:307
  155.0 3.6 %down_far.1 = (bf16[64,2048]{1,0:T(8,128)(2,1)S(1)}, bf16[64,2048]{1,0:T(8,128)(2,1)S(1)}, bf16[1,16,96,2048]{3,2,1,0:T(8,128)(2,1)S(1)}) custom-call(s32[1]{0:T(128)} %bitcast.3.y_ref, bf16[512,768]{1,0:T(8,128)(2,1)S(1)} %gate_up.2.hid0_ref, bf16[512,768]{1,0:T(8,128)(2,1)S(1)} %gate_up.3.hid1_ref, bf16[8,2,4,288,256]{4,3,2,1,0:T(8,128)(2,1)} %bitcast.12, ...), custom_call_target="tpu_custom_call" | custom-call | tf_op jit(solution)/shard_map/down_far/pallas_call | solution.py:325
  158.6 0.5 collective-permute-start.12
  159.1 2.8 %collective-permute-start.13 = (bf16[64,2048]{1,0:T(8,128)(2,1)S(1)}, bf16[64,2048]{1,0:T(8,128)(2,1)S(1)}, u32[]{:S(2)}, u32[]{:S(2)}) collective-permute-start(bf16[64,2048]{1,0:T(8,128)(2,1)S(1)} %get-tuple-element.52), channel_id=1, source_target_pairs={{0,3},{1,0},{2,1},{3,2},{4,7},{5,4},{6,5},{7,6},{8,11},{9,8},{10,9... | collective-permute-start | bytes 786440 | tf_op jit(solution)/shard_map/ppermute | solution.py:467
  161.9 3.2 %down.1 = (f32[128,2048]{1,0:T(8,128)S(1)}, bf16[128,2048]{1,0:T(8,128)(2,1)S(1)}, bf16[128,2048]{1,0:T(8,128)(2,1)S(1)}) custom-call(bf16[512,768]{1,0:T(8,128)(2,1)S(1)} %gate_up.2.hid0_ref, bf16[512,768]{1,0:T(8,128)(2,1)S(1)} %gate_up.3.hid1_ref, bf16[1,16,96,2048]{3,2,1,0:T(8,128)(2,1)S(1)} %get-tuple-element.48.w_ref), custom_call_target="tpu_custom_call" | custom-call | tf_op jit(solution)/shard_map/down/pallas_call | solution.py:337
  165.2 2.4 %collective-permute-done.12 = bf16[64,2048]{1,0:T(8,128)(2,1)S(1)} collective-permute-done((bf16[64,2048]{1,0:T(8,128)(2,1)S(1)}, bf16[64,2048]{1,0:T(8,128)(2,1)S(1)}, u32[]{:S(2)}, u32[]{:S(2)}) %collective-permute-start.12) | collective-permute-done | bytes 262176 | tf_op jit(solution)/shard_map/ppermute | solution.py:466
  167.8 3.0 %collective-permute-start.15 = (bf16[128,2048]{1,0:T(8,128)(2,1)S(1)}, bf16[128,2048]{1,0:T(8,128)(2,1)S(1)}, u32[]{:S(2)}, u32[]{:S(2)}) collective-permute-start(bf16[128,2048]{1,0:T(8,128)(2,1)S(1)} %pad_maximum_fusion.2), channel_id=1, source_target_pairs={{0,3},{1,0},{2,1},{3,2},{4,7},{5,4},{6,5},{7,6},{8,11},{9,8},{10,9... | collective-permute-start | bytes 1572872 | tf_op jit(solution)/shard_map/ppermute | solution.py:473
  170.9 9.5 %collective-permute-done.15 = bf16[128,2048]{1,0:T(8,128)(2,1)S(1)} collective-permute-done((bf16[128,2048]{1,0:T(8,128)(2,1)S(1)}, bf16[128,2048]{1,0:T(8,128)(2,1)S(1)}, u32[]{:S(2)}, u32[]{:S(2)}) %collective-permute-start.15) | collective-permute-done | bytes 524320 | tf_op jit(solution)/shard_map/ppermute | solution.py:473
  180.4 3.5 %collective-permute-done.14 = bf16[128,2048]{1,0:T(8,128)(2,1)S(1)} collective-permute-done((bf16[128,2048]{1,0:T(8,128)(2,1)S(1)}, bf16[128,2048]{1,0:T(8,128)(2,1)S(1)}, u32[]{:S(2)}, u32[]{:S(2)}) %collective-permute-start.14) | collective-permute-done | bytes 524320 | tf_op jit(solution)/shard_map/ppermute | solution.py:472
  184.0 1.1 fusion.3
  (48 shorter events, 2.4 us)
Async XLA Ops:
  7.2 17.2 %copy-start.10 = (s32[1024]{0:T(1024)S(1)}, s32[1024]{0:T(1024)}, u32[]{:S(2)}) copy-start(s32[1024]{0:T(1024)} %param.15) | copy-start | bytes 12292
  9.5 28.1 %all-to-all-start = ((bf16[8,768,128]{2,1,0:T(8,128)(2,1)}), bf16[8,768,128]{2,1,0:T(8,128)(2,1)}, u32[]{:S(2)}, u32[]{:S(2)}) async-start(bf16[8,768,128]{2,1,0:T(8,128)(2,1)} %pack.1), calls=%async_computation | async-start | bytes 3145728 | tf_op jit(solution)/shard_map/all_to_all | solution.py:417
  17.4 116.4 %all-gather.3.cloned.1.call-start = ((), (), s32[]{:S(2)}) async-start(), calls=%async_computation.4 | async-start | bytes 10027008 | tf_op jit(solution)/shard_map/all_gather | solution.py:427
  19.7 12.2 %collective-permute-start = (bf16[288,256]{1,0:T(8,128)(2,1)}, bf16[288,256]{1,0:T(8,128)(2,1)S(1)}, u32[]{:S(2)}, u32[]{:S(2)}) collective-permute-start(bf16[288,256]{1,0:T(8,128)(2,1)} %get-tuple-element.30), channel_id=1, source_target_pairs={{0,3},{1,0},{2,1},{3,2},{4,7},{5,4},{6,5},{7,6},{8,11},{9,8},{10,9... | collective-permute-start | bytes 442376 | tf_op jit(solution)/shard_map/ppermute | solution.py:391
  22.7 9.2 %collective-permute-start.1 = (bf16[288,256]{1,0:T(8,128)(2,1)}, bf16[288,256]{1,0:T(8,128)(2,1)S(1)}, u32[]{:S(2)}, u32[]{:S(2)}) collective-permute-start(bf16[288,256]{1,0:T(8,128)(2,1)} %get-tuple-element.31), channel_id=1, source_target_pairs={{0,2},{1,3},{2,0},{3,1},{4,6},{5,7},{6,4},{7,5},{8,10},{9,11},{10,... | collective-permute-start | bytes 442376 | tf_op jit(solution)/shard_map/ppermute | solution.py:391
  23.4 9.0 %collective-permute-start.2 = (bf16[288,256]{1,0:T(8,128)(2,1)}, bf16[288,256]{1,0:T(8,128)(2,1)S(1)}, u32[]{:S(2)}, u32[]{:S(2)}) collective-permute-start(bf16[288,256]{1,0:T(8,128)(2,1)} %get-tuple-element.32), channel_id=1, source_target_pairs={{0,1},{1,2},{2,3},{3,0},{4,5},{5,6},{6,7},{7,4},{8,9},{9,10},{10,1... | collective-permute-start | bytes 442376 | tf_op jit(solution)/shard_map/ppermute | solution.py:391
  31.9 0.7 copy-start.6
  31.9 0.7 copy-start.7
  32.4 0.7 copy-start.8
  35.0 9.8 %copy-start.4 = (f32[128]{0:T(128)S(1)}, f32[128]{0:T(128)}, u32[]{:S(2)}) copy-start(f32[128]{0:T(128)} %param.18) | copy-start | bytes 1540
  35.0 9.8 %copy-start.5 = (f32[128]{0:T(128)S(1)}, f32[128]{0:T(128)}, u32[]{:S(2)}) copy-start(f32[128]{0:T(128)} %param.19) | copy-start | bytes 1540
  37.6 7.2 %collective-permute-start.3 = (bf16[8,768,128]{2,1,0:T(8,128)(2,1)}, bf16[8,768,128]{2,1,0:T(8,128)(2,1)}, u32[]{:S(2)}, u32[]{:S(2)}) collective-permute-start(bf16[8,768,128]{2,1,0:T(8,128)(2,1)} %all-to-all-done.own_ref.src_ref), channel_id=1, source_target_pairs={{0,8},{8,0},{1,9},{9,1},{2,10},{10,2},{3,11},{11,3},{4,12},{12,4},... | collective-permute-start | bytes 4718600 | tf_op jit(solution)/shard_map/ppermute | solution.py:23
  40.4 35.0 %all-to-all-start.2 = ((bf16[4,8,256,128]{3,2,1,0:T(8,128)(2,1)}), bf16[4,8,256,128]{3,2,1,0:T(8,128)(2,1)S(1)}, u32[]{:S(2)}, u32[]{:S(2)}) async-start(bf16[4,8,256,128]{3,2,1,0:T(8,128)(2,1)} %widen.1), calls=%async_computation.2 | async-start | bytes 4194304 | tf_op jit(solution)/shard_map/all_to_all | solution.py:432
  52.2 13.2 %collective-permute-start.4 = (bf16[2,512,128]{2,1,0:T(8,128)(2,1)}, bf16[2,512,128]{2,1,0:T(8,128)(2,1)S(1)}, u32[]{:S(2)}, u32[]{:S(2)}) collective-permute-start(bf16[2,512,128]{2,1,0:T(8,128)(2,1)} %get-tuple-element.38), channel_id=1, source_target_pairs={{0,8},{8,16},{16,24},{24,32},{32,40},{40,48},{48,56},{56,64},{64,7... | collective-permute-start | bytes 786440 | tf_op jit(solution)/shard_map/ppermute | solution.py:436
  65.4 1.0 copy-start.2
  70.6 0.7 copy-start.3
  75.3 11.6 %collective-permute-start.5 = (bf16[4,8,256,128]{3,2,1,0:T(8,128)(2,1)S(1)}, bf16[4,8,256,128]{3,2,1,0:T(8,128)(2,1)S(1)}, u32[]{:S(2)}, u32[]{:S(2)}) collective-permute-start(bf16[4,8,256,128]{3,2,1,0:T(8,128)(2,1)S(1)} %all-to-all-done.2.own_ref), channel_id=1, source_target_pairs={{0,8},{8,0},{1,9},{9,1},{2,10},{10,2},{3,11},{11,3},{4,12},{12,4},... | collective-permute-start | bytes 6291464 | tf_op jit(solution)/shard_map/ppermute | solution.py:23
  90.6 1.3 copy-start
  91.9 25.5 %collective-permute-start.6 = (bf16[128,2048]{1,0:T(8,128)(2,1)S(1)}, bf16[128,2048]{1,0:T(8,128)(2,1)S(1)}, u32[]{:S(2)}, u32[]{:S(2)}) collective-permute-start(bf16[128,2048]{1,0:T(8,128)(2,1)S(1)} %oproj.2), channel_id=1, source_target_pairs={{0,4},{4,0},{1,5},{5,1},{2,6},{6,2},{3,7},{7,3},{8,12},{12,8},{9,1... | collective-permute-start | bytes 1572872 | tf_op jit(solution)/shard_map/ppermute | solution.py:23
  92.5 10.1 %all-to-all-start.3 = ((bf16[4,128,256]{2,1,0:T(8,128)(2,1)}), bf16[4,128,256]{2,1,0:T(8,128)(2,1)S(1)}, u32[]{:S(2)}, u32[]{:S(2)}) async-start(bf16[4,128,256]{2,1,0:T(8,128)(2,1)} %attend.3), calls=%async_computation.3 | async-start | bytes 524288 | tf_op jit(solution)/shard_map/all_to_all | solution.py:437
  102.5 1.6 copy-start.1
  104.1 14.7 %copy-start.9 = (f32[2048]{0:T(1024)S(1)}, f32[2048]{0:T(1024)}, u32[]{:S(2)}) copy-start(f32[2048]{0:T(1024)} %param.17) | copy-start | bytes 24580
  119.1 12.6 %collective-permute-start.8 = (bf16[128,2048]{1,0:T(8,128)(2,1)S(1)}, bf16[128,2048]{1,0:T(8,128)(2,1)S(1)}, u32[]{:S(2)}, u32[]{:S(2)}) collective-permute-start(bf16[128,2048]{1,0:T(8,128)(2,1)S(1)} %fusion.2.x0_ref), channel_id=1, source_target_pairs={{0,3},{1,0},{2,1},{3,2},{4,7},{5,4},{6,5},{7,6},{8,11},{9,8},{10,9... | collective-permute-start | bytes 1572872 | tf_op jit(solution)/shard_map/ppermute | solution.py:455
  120.3 13.4 %collective-permute-start.7 = (bf16[128,2048]{1,0:T(8,128)(2,1)S(1)}, bf16[128,2048]{1,0:T(8,128)(2,1)S(1)}, u32[]{:S(2)}, u32[]{:S(2)}) collective-permute-start(bf16[128,2048]{1,0:T(8,128)(2,1)S(1)} %fusion.2.x0_ref), channel_id=1, source_target_pairs={{0,1},{1,2},{2,3},{3,0},{4,5},{5,6},{6,7},{7,4},{8,9},{9,10},{10,1... | collective-permute-start | bytes 1572872 | tf_op jit(solution)/shard_map/ppermute | solution.py:454
  133.7 16.5 %collective-permute-start.11 = (bf16[8,2,4,288,256]{4,3,2,1,0:T(8,128)(2,1)}, bf16[8,2,4,288,256]{4,3,2,1,0:T(8,128)(2,1)S(1)}, u32[]{:S(2)}, u32[]{:S(2)}) collective-permute-start(bf16[8,2,4,288,256]{4,3,2,1,0:T(8,128)(2,1)} %bitcast.10), channel_id=1, source_target_pairs={{0,8},{8,0},{1,9},{9,1},{2,10},{10,2},{3,11},{11,3},{4,12},{12,4},... | collective-permute-start | bytes 28311560 | tf_op jit(solution)/shard_map/ppermute | solution.py:23
  133.8 8.8 %collective-permute-start.10 = (bf16[64,2048]{1,0:T(8,128)(2,1)S(1)}, bf16[64,2048]{1,0:T(8,128)(2,1)S(1)}, u32[]{:S(2)}, u32[]{:S(2)}) collective-permute-start(bf16[64,2048]{1,0:T(8,128)(2,1)S(1)} %slice.19), channel_id=1, source_target_pairs={{0,3},{1,0},{2,1},{3,2},{4,7},{5,4},{6,5},{7,6},{8,11},{9,8},{10,9... | collective-permute-start | bytes 786440 | tf_op jit(solution)/shard_map/ppermute | solution.py:459
  134.1 9.7 %collective-permute-start.9 = (bf16[64,2048]{1,0:T(8,128)(2,1)S(1)}, bf16[64,2048]{1,0:T(8,128)(2,1)S(1)}, u32[]{:S(2)}, u32[]{:S(2)}) collective-permute-start(bf16[64,2048]{1,0:T(8,128)(2,1)S(1)} %slice.18), channel_id=1, source_target_pairs={{0,1},{1,2},{2,3},{3,0},{4,5},{5,6},{6,7},{7,4},{8,9},{9,10},{10,1... | collective-permute-start | bytes 786440 | tf_op jit(solution)/shard_map/ppermute | solution.py:458
  158.6 9.0 %collective-permute-start.12 = (bf16[64,2048]{1,0:T(8,128)(2,1)S(1)}, bf16[64,2048]{1,0:T(8,128)(2,1)S(1)}, u32[]{:S(2)}, u32[]{:S(2)}) collective-permute-start(bf16[64,2048]{1,0:T(8,128)(2,1)S(1)} %get-tuple-element.51), channel_id=1, source_target_pairs={{0,1},{1,2},{2,3},{3,0},{4,5},{5,6},{6,7},{7,4},{8,9},{9,10},{10,1... | collective-permute-start | bytes 786440 | tf_op jit(solution)/shard_map/ppermute | solution.py:466
  159.1 8.5 %collective-permute-start.13 = (bf16[64,2048]{1,0:T(8,128)(2,1)S(1)}, bf16[64,2048]{1,0:T(8,128)(2,1)S(1)}, u32[]{:S(2)}, u32[]{:S(2)}) collective-permute-start(bf16[64,2048]{1,0:T(8,128)(2,1)S(1)} %get-tuple-element.52), channel_id=1, source_target_pairs={{0,3},{1,0},{2,1},{3,2},{4,7},{5,4},{6,5},{7,6},{8,11},{9,8},{10,9... | collective-permute-start | bytes 786440 | tf_op jit(solution)/shard_map/ppermute | solution.py:467
  167.8 12.7 %collective-permute-start.15 = (bf16[128,2048]{1,0:T(8,128)(2,1)S(1)}, bf16[128,2048]{1,0:T(8,128)(2,1)S(1)}, u32[]{:S(2)}, u32[]{:S(2)}) collective-permute-start(bf16[128,2048]{1,0:T(8,128)(2,1)S(1)} %pad_maximum_fusion.2), channel_id=1, source_target_pairs={{0,3},{1,0},{2,1},{3,2},{4,7},{5,4},{6,5},{7,6},{8,11},{9,8},{10,9... | collective-permute-start | bytes 1572872 | tf_op jit(solution)/shard_map/ppermute | solution.py:473
  170.8 13.1 %collective-permute-start.14 = (bf16[128,2048]{1,0:T(8,128)(2,1)S(1)}, bf16[128,2048]{1,0:T(8,128)(2,1)S(1)}, u32[]{:S(2)}, u32[]{:S(2)}) collective-permute-start(bf16[128,2048]{1,0:T(8,128)(2,1)S(1)} %pad_maximum_fusion.1), channel_id=1, source_target_pairs={{0,1},{1,2},{2,3},{3,0},{4,5},{5,6},{6,7},{7,4},{8,9},{9,10},{10,1... | collective-permute-start | bytes 1572872 | tf_op jit(solution)/shard_map/ppermute | solution.py:472
Sparse Core Ops, SparseCore 0:
  37.7 86.4 all-gather.2

commit v12 on v10

--- a/solution.py
+++ b/solution.py
@@ -174,7 +174,7 @@
     )(half, q, kv, prior, lo)
 
 
-def out_kernel(core_ref, ctx_ref, own_ref, oth_ref, out_ref, w_ref, sems):
+def lay_kernel(core_ref, own_ref, oth_ref, w_ref, sems):
     core = core_ref[0]
 
     def each(act):
@@ -190,8 +190,23 @@
         lax.fori_loop(0, 32, step, 0)
 
     each(lambda c: c.start())
+    each(lambda c: c.wait())
+
+
+def lay(core, own, oth):
+    anywhere = pl.BlockSpec(memory_space=pl.ANY)
+    return pl.pallas_call(
+        lay_kernel,
+        in_specs=[pl.BlockSpec(memory_space=pltpu.SMEM), anywhere, anywhere],
+        out_shape=jax.ShapeDtypeStruct((1024, 2048), BF),
+        scratch_shapes=[pltpu.SemaphoreType.DMA((2, 4, 8))],
+        compiler_params=pltpu.CompilerParams(vmem_limit_bytes=6 << 20),
+        name="lay",
+    )(core, own, oth)
+
+
+def out_kernel(ctx_ref, w_ref, out_ref):
     x = jnp.concatenate([ctx_ref[s] for s in range(4)], axis=1)
-    each(lambda c: c.wait())
 
     def column(n, carry):
         at = pl.ds(pl.multiple_of(n * 512, 512), 512)
@@ -201,17 +216,13 @@
     lax.fori_loop(0, 4, column, 0)
 
 
-def out_project(core, ctx, own, oth, dtype):
-    vm = pl.BlockSpec(memory_space=pltpu.VMEM)
-    anywhere = pl.BlockSpec(memory_space=pl.ANY)
+def out_project(ctx, weight, dtype):
     return pl.pallas_call(
         out_kernel,
-        in_specs=[pl.BlockSpec(memory_space=pltpu.SMEM), vm, anywhere, anywhere],
         out_shape=jax.ShapeDtypeStruct((128, 2048), dtype),
-        scratch_shapes=[pltpu.VMEM((1024, 2048), BF), pltpu.SemaphoreType.DMA((2, 4, 8))],
-        compiler_params=pltpu.CompilerParams(vmem_limit_bytes=14 << 20),
+        compiler_params=pltpu.CompilerParams(vmem_limit_bytes=10 << 20),
         name="oproj",
-    )(core, ctx, own, oth)
+    )(ctx, weight)
 
 
 def fetcher(own_ref, oth_ref, w_ref, sems, y, first):
@@ -425,10 +436,11 @@
     mine = attend(xl[None], q, cache, prior, lo)
     _, o_own = hold((mine, o_own))
     o_oth = swap(o_own, "core")
-    send = out_project(core[None], turn(theirs), o_own, o_oth, BF)
+    o_whole = lay(core[None], o_own, o_oth)
+    send = out_project(turn(theirs), o_whole, BF)
     got = swap(send, "xl")
     _, mine = hold((send, mine))
-    keep = out_project(core[None], turn(mine), o_own, o_oth, F32)
+    keep = out_project(turn(mine), o_whole, F32)
 
     own_rows = lax.dynamic_slice_in_dim(tokens, (xl * 4 + y) * 128, 128, 0).astype(F32)
     resid = (own_rows + (keep + got.astype(F32))).astype(BF)

time: 192 us -> 191 us (level)
  blocking collectives: 11.7 us -> 0 us
  local copies, waits for them, and re-layouts: 4.38 us -> 9.36 us
  waiting for transfers between devices: 70.9 us -> 75.2 us
  starting transfers between devices: 34 us -> 38 us
  Pallas kernels: 50.6 us -> 48.4 us
    all_to_all x1 -> x0, blocking collectives: 11.7 us -> none  [per_device(): lax.all_to_all(part, 'y', split_axis=0, concat_axis=0, tiled=True)]
    unnamed x24 -> x26, local copies, waits for them, and re-layouts: 4.09 us -> 9.06 us
    all_to_all x1 -> x2, starting transfers between devices: 3.41 us -> 7.7 us  [per_device(): lax.all_to_all(part, 'y', split_axis=0, concat_axis=0, tiled=True)]
    all_to_all x1 -> x2, waiting for transfers between devices: 6.64 us -> 9.42 us  [per_device(): lax.all_to_all(part, 'y', split_axis=0, concat_axis=0, tiled=True)]
    pallas_call x2 -> x3, Pallas kernels: 7.28 us -> 5.03 us  [the longest x2 2.54 us: out_project(): pl.pallas_call(out_kernel, out_shape=jax.ShapeDtypeStruct((128, 2048), dt...]
  transfers between devices with their start and end apart: 20 -> 21, of which waited for: 14 -> 15; matrix products, arithmetic and copies ran while one was open for 2% -> 2% of each run, Pallas kernels for 21% -> 20%
where the time goes in v12:
time: 191 us; the launch traced here: 190 us
  waiting for transfers between devices  75.2 us (39%)
  Pallas kernels  48.4 us (25%)
  starting transfers between devices  38 us (20%)
  between operations  14.3 us (7%)
  local copies, waits for them, and re-layouts  9.36 us (5%)
  other arithmetic  5.04 us (3%)
    ppermute x4, waiting for transfers between devices, swap(): return lax.ppermute(block, axis, [(0, 1), (1, 0)])  11.2 us
    pallas_call x2, Pallas kernels, gate_up(): pl.pallas_call(gate_kernel, in_specs=[pl.BlockSpec(memory_space=pltpu.SME...  11.1 us
    ppermute x1, waiting for transfers between devices, per_device(): prior = lax.ppermute(tail, REQ, [(i - 1, i) for i in range(1, 16)])  10.3 us
    ppermute x1, waiting for transfers between devices, per_device(): right = lax.ppermute(mlp_in, 'y', ring(3))  10.2 us
    ppermute x1, waiting for transfers between devices, per_device(): from_right = lax.ppermute(to_left, 'y', ring(3))  9.49 us
    all_to_all x2, waiting for transfers between devices, per_device(): lax.all_to_all(part, 'y', split_axis=0, concat_axis=0, tiled=True)  9.42 us
    unnamed x26, local copies, waits for them, and re-layouts  9.06 us
    pallas_call x2, Pallas kernels, attend(): pl.pallas_call(attend_kernel, in_specs=[pl.BlockSpec(memory_space=pltpu.S...  8.18 us
  transfers between devices with their start and end apart: 21, of which 15 were waited for; matrix products, arithmetic and copies ran while one was open for 2% of the time, Pallas kernels for 20%

profile of v12, /device:TPU:32, one launch (start us, length us, event | category | flops | bytes accessed | tf_op | source)
XLA Modules:
  0.0 190.3 jit_solution(13944479774725222595)
XLA Ops:
  7.2 2.3 %pack.1 = bf16[8,768,128]{2,1,0:T(8,128)(2,1)} custom-call(f32[128,256]{1,0:T(8,128)} %q_ref.1, f32[128,128]{1,0:T(8,128)} %k_ref.1, f32[128,128]{1,0:T(8,128)} %v_ref.1, f32[256,128]{1,0:T(8,128)} %o_ref.1), custom_call_target="tpu_custom_call" | custom-call | tf_op jit(solution)/shard_map/pack/pallas_call | solution.py:350
  9.5 7.9 %all-to-all-start = ((bf16[8,768,128]{2,1,0:T(8,128)(2,1)}), bf16[8,768,128]{2,1,0:T(8,128)(2,1)}, u32[]{:S(2)}, u32[]{:S(2)}) async-start(bf16[8,768,128]{2,1,0:T(8,128)(2,1)} %pack.1), calls=%async_computation | async-start | bytes 3145728 | tf_op jit(solution)/shard_map/all_to_all | solution.py:414
  17.4 2.3 %prep.1 = (bf16[288,256]{1,0:T(8,128)(2,1)}, bf16[288,256]{1,0:T(8,128)(2,1)}, bf16[288,256]{1,0:T(8,128)(2,1)}, bf16[288,256]{1,0:T(8,128)(2,1)}) custom-call(s32[1]{0:T(128)} %bitcast.2.y_ref, f32[256,384]{1,0:T(8,128)} %gate_ref.1, f32[256,384]{1,0:T(8,128)} %up_ref.1, f32[384,256]{1,0:T(8,128)} %down_ref.1), custom_call_target="tpu_custom_call" | custom-call | tf_op jit(solution)/shard_map/prep/pallas_call | solution.py:369
  19.7 3.0 %collective-permute-start = (bf16[288,256]{1,0:T(8,128)(2,1)}, bf16[288,256]{1,0:T(8,128)(2,1)S(1)}, u32[]{:S(2)}, u32[]{:S(2)}) collective-permute-start(bf16[288,256]{1,0:T(8,128)(2,1)} %get-tuple-element.29), channel_id=1, source_target_pairs={{0,3},{1,0},{2,1},{3,2},{4,7},{5,4},{6,5},{7,6},{8,11},{9,8},{10,9... | collective-permute-start | bytes 442376 | tf_op jit(solution)/shard_map/ppermute | solution.py:388
  23.4 1.0 collective-permute-start.2
  24.4 1.9 multiply_cosine_fusion
  26.5 2.3 %collective-permute-done.p1_ref = bf16[288,256]{1,0:T(8,128)(2,1)S(1)} collective-permute-done((bf16[288,256]{1,0:T(8,128)(2,1)}, bf16[288,256]{1,0:T(8,128)(2,1)S(1)}, u32[]{:S(2)}, u32[]{:S(2)}) %collective-permute-start) | collective-permute-done | bytes 147488 | tf_op jit(solution)/shard_map/ppermute | solution.py:388
  28.8 2.1 %collective-permute-done.1.p2_ref = bf16[288,256]{1,0:T(8,128)(2,1)S(1)} collective-permute-done((bf16[288,256]{1,0:T(8,128)(2,1)}, bf16[288,256]{1,0:T(8,128)(2,1)S(1)}, u32[]{:S(2)}, u32[]{:S(2)}) %collective-permute-start.1) | collective-permute-done | bytes 147488 | tf_op jit(solution)/shard_map/ppermute | solution.py:388
  30.8 1.5 collective-permute-done.2.p3_ref
  33.0 2.0 %join.1 = bf16[4,288,256]{2,1,0:T(8,128)(2,1)} custom-call(bf16[288,256]{1,0:T(8,128)(2,1)} %get-tuple-element.28.p0_ref, bf16[288,256]{1,0:T(8,128)(2,1)} %copy-done.8, bf16[288,256]{1,0:T(8,128)(2,1)} %copy-done.9, bf16[288,256]{1,0:T(8,128)(2,1)} %copy-done.10), custom_call_target="tpu_custom_call" | custom-call | tf_op jit(solution)/shard_map/join/pallas_call | solution.py:384
  35.0 2.6 %all-to-all-done.own_ref.src_ref = bf16[8,768,128]{2,1,0:T(8,128)(2,1)} async-done(((bf16[8,768,128]{2,1,0:T(8,128)(2,1)}), bf16[8,768,128]{2,1,0:T(8,128)(2,1)}, u32[]{:S(2)}, u32[]{:S(2)}) %all-to-all-start) | async-done | bytes 1572896 | tf_op jit(solution)/shard_map/all_to_all | solution.py:414
  37.7 2.6 %widen.1 = bf16[4,8,256,128]{3,2,1,0:T(8,128)(2,1)} custom-call(bf16[8,768,128]{2,1,0:T(8,128)(2,1)} %all-to-all-done.own_ref.src_ref), custom_call_target="tpu_custom_call" | custom-call | tf_op jit(solution)/shard_map/widen/pallas_call | solution.py:108
  40.4 4.5 %all-to-all-start.2 = ((bf16[4,8,256,128]{3,2,1,0:T(8,128)(2,1)}), bf16[4,8,256,128]{3,2,1,0:T(8,128)(2,1)S(1)}, u32[]{:S(2)}, u32[]{:S(2)}) async-start(bf16[4,8,256,128]{3,2,1,0:T(8,128)(2,1)} %widen.1), calls=%async_computation.2 | async-start | bytes 4194304 | tf_op jit(solution)/shard_map/all_to_all | solution.py:428
  44.9 7.9 %qkv.1 = (bf16[1024,256]{1,0:T(8,128)(2,1)S(1)}, bf16[2,1024,128]{2,1,0:T(8,128)(2,1)}, bf16[2,512,128]{2,1,0:T(8,128)(2,1)}) custom-call(s32[1]{0:T(128)} %bitcast.1.core_ref, bf16[1024,2048]{1,0:T(8,128)(2,1)} %x_ref.1, bf16[8,768,128]{2,1,0:T(8,128)(2,1)} %all-to-all-done.own_ref.src_ref, bf16[8,768,128]{2,1,0:T(8,128)(2,1)} %collective-permute-done.3.oth_ref, ...), custom_call_target="tpu_custom_call" | custom-call | tf_op jit(solution)/shard_map/qkv/pallas_call | solution.py:71
  52.8 2.1 %collective-permute-start.4 = (bf16[2,512,128]{2,1,0:T(8,128)(2,1)}, bf16[2,512,128]{2,1,0:T(8,128)(2,1)S(1)}, u32[]{:S(2)}, u32[]{:S(2)}) collective-permute-start(bf16[2,512,128]{2,1,0:T(8,128)(2,1)} %get-tuple-element.36), channel_id=1, source_target_pairs={{0,8},{8,16},{16,24},{24,32},{32,40},{40,48},{48,56},{56,64},{64,7... | collective-permute-start | bytes 786440 | tf_op jit(solution)/shard_map/ppermute | solution.py:432
  55.1 10.3 %collective-permute-done.4.prior_ref = bf16[2,512,128]{2,1,0:T(8,128)(2,1)S(1)} collective-permute-done((bf16[2,512,128]{2,1,0:T(8,128)(2,1)}, bf16[2,512,128]{2,1,0:T(8,128)(2,1)S(1)}, u32[]{:S(2)}, u32[]{:S(2)}) %collective-permute-start.4) | collective-permute-done | bytes 262176 | tf_op jit(solution)/shard_map/ppermute | solution.py:432
  65.4 1.0 copy-done.3
  66.5 4.2 %attend.2 = bf16[4,128,256]{2,1,0:T(8,128)(2,1)S(1)} custom-call(s32[1]{0:T(128)S(6)} %sub.6.half_ref, bf16[1024,256]{1,0:T(8,128)(2,1)S(1)} %get-tuple-element.37.q_ref, bf16[2,1024,128]{2,1,0:T(8,128)(2,1)S(1)} %copy-done.3, bf16[2,512,128]{2,1,0:T(8,128)(2,1)S(1)} %collective-permute-done.4.prior_ref, s32[1024,1]{1,0:T(8,128)S(1)} %copy.17.lo_ref), custom_call_target="tpu_custom_call" | custom-call | tf_op jit(solution)/shard_map/attend/pallas_call | solution.py:168
  71.3 4.0 %attend.3 = bf16[4,128,256]{2,1,0:T(8,128)(2,1)} custom-call(s32[1]{0:T(128)} %bitcast.half_ref, bf16[1024,256]{1,0:T(8,128)(2,1)S(1)} %get-tuple-element.37.q_ref, bf16[2,1024,128]{2,1,0:T(8,128)(2,1)S(1)} %copy-done.3, bf16[2,512,128]{2,1,0:T(8,128)(2,1)S(1)} %collective-permute-done.4.prior_ref, s32[1024,1]{1,0:T(8,128)S(1)} %copy.17.lo_ref), custom_call_target="tpu_custom_call" | custom-call | tf_op jit(solution)/shard_map/attend/pallas_call | solution.py:168
  75.4 4.3 %all-to-all-start.1 = ((bf16[4,128,256]{2,1,0:T(8,128)(2,1)}), bf16[4,128,256]{2,1,0:T(8,128)(2,1)S(1)}, u32[]{:S(2)}, u32[]{:S(2)}) async-start(bf16[4,128,256]{2,1,0:T(8,128)(2,1)} %copy-done.4), calls=%async_computation.1 | async-start | bytes 524288 | tf_op jit(solution)/shard_map/all_to_all | solution.py:433
  79.7 2.5 %lay.1.w_ref = bf16[1024,2048]{1,0:T(8,128)(2,1)S(1)} custom-call(s32[1]{0:T(128)} %bitcast.1.core_ref, bf16[4,8,256,128]{3,2,1,0:T(8,128)(2,1)S(1)} %all-to-all-done.2.own_ref, bf16[4,8,256,128]{3,2,1,0:T(8,128)(2,1)} %collective-permute-done.5.oth_ref), custom_call_target="tpu_custom_call" | custom-call | tf_op jit(solution)/shard_map/lay/pallas_call | solution.py:198
  82.2 2.0 %copy-done = bf16[1024,2048]{1,0:T(8,128)(2,1)} copy-done((bf16[1024,2048]{1,0:T(8,128)(2,1)}, bf16[1024,2048]{1,0:T(8,128)(2,1)S(1)}, u32[]{:S(2)}) %copy-start) | copy-done | bytes 4194328
  84.2 2.8 %all-to-all-done.1.ctx_ref = bf16[4,128,256]{2,1,0:T(8,128)(2,1)S(1)} async-done(((bf16[4,128,256]{2,1,0:T(8,128)(2,1)}), bf16[4,128,256]{2,1,0:T(8,128)(2,1)S(1)}, u32[]{:S(2)}, u32[]{:S(2)}) %all-to-all-start.1) | async-done | bytes 262176 | tf_op jit(solution)/shard_map/all_to_all | solution.py:433
  87.0 2.3 %copy-done.1 = bf16[1024,2048]{1,0:T(8,128)(2,1)S(1)} copy-done((bf16[1024,2048]{1,0:T(8,128)(2,1)S(1)}, bf16[1024,2048]{1,0:T(8,128)(2,1)}, u32[]{:S(2)}) %copy-start.1) | copy-done | bytes 4194328
  89.3 1.3 oproj.2
  91.1 3.4 %all-to-all-start.3 = ((bf16[4,128,256]{2,1,0:T(8,128)(2,1)}), bf16[4,128,256]{2,1,0:T(8,128)(2,1)S(1)}, u32[]{:S(2)}, u32[]{:S(2)}) async-start(bf16[4,128,256]{2,1,0:T(8,128)(2,1)} %attend.3), calls=%async_computation.3 | async-start | bytes 524288 | tf_op jit(solution)/shard_map/all_to_all | solution.py:433
  94.6 6.6 %all-to-all-done.3.ctx_ref = bf16[4,128,256]{2,1,0:T(8,128)(2,1)S(1)} async-done(((bf16[4,128,256]{2,1,0:T(8,128)(2,1)}), bf16[4,128,256]{2,1,0:T(8,128)(2,1)S(1)}, u32[]{:S(2)}, u32[]{:S(2)}) %all-to-all-start.3) | async-done | bytes 262176 | tf_op jit(solution)/shard_map/all_to_all | solution.py:433
  101.2 2.3 %copy-done.2 = bf16[1024,2048]{1,0:T(8,128)(2,1)S(1)} copy-done((bf16[1024,2048]{1,0:T(8,128)(2,1)S(1)}, bf16[1024,2048]{1,0:T(8,128)(2,1)}, u32[]{:S(2)}) %copy-start.2) | copy-done | bytes 4194328
  103.5 1.3 oproj.3
  104.8 11.2 %collective-permute-done.6 = bf16[128,2048]{1,0:T(8,128)(2,1)S(1)} collective-permute-done((bf16[128,2048]{1,0:T(8,128)(2,1)S(1)}, bf16[128,2048]{1,0:T(8,128)(2,1)S(1)}, u32[]{:S(2)}, u32[]{:S(2)}) %collective-permute-start.6) | collective-permute-done | bytes 524320 | tf_op jit(solution)/shard_map/ppermute | solution.py:23
  116.0 1.2 add_convert_fusion
  117.7 1.2 collective-permute-start.8
  118.9 0.8 collective-permute-start.7
  119.8 10.2 %collective-permute-done.8.x2_ref = bf16[128,2048]{1,0:T(8,128)(2,1)S(1)} collective-permute-done((bf16[128,2048]{1,0:T(8,128)(2,1)S(1)}, bf16[128,2048]{1,0:T(8,128)(2,1)S(1)}, u32[]{:S(2)}, u32[]{:S(2)}) %collective-permute-start.8) | collective-permute-done | bytes 524320 | tf_op jit(solution)/shard_map/ppermute | solution.py:452
  130.0 2.2 %collective-permute-done.7.x1_ref = bf16[128,2048]{1,0:T(8,128)(2,1)S(1)} collective-permute-done((bf16[128,2048]{1,0:T(8,128)(2,1)S(1)}, bf16[128,2048]{1,0:T(8,128)(2,1)S(1)}, u32[]{:S(2)}, u32[]{:S(2)}) %collective-permute-start.7) | collective-permute-done | bytes 524320 | tf_op jit(solution)/shard_map/ppermute | solution.py:451
  132.6 1.7 collective-permute-start.9
  134.3 6.7 %collective-permute-done.10.x4_ref = bf16[64,2048]{1,0:T(8,128)(2,1)S(1)} collective-permute-done((bf16[64,2048]{1,0:T(8,128)(2,1)S(1)}, bf16[64,2048]{1,0:T(8,128)(2,1)S(1)}, u32[]{:S(2)}, u32[]{:S(2)}) %collective-permute-start.10) | collective-permute-done | bytes 262176 | tf_op jit(solution)/shard_map/ppermute | solution.py:456
  141.0 1.3 collective-permute-done.9.x3_ref
  142.3 6.4 %gate_up.2.hid0_ref = bf16[512,768]{1,0:T(8,128)(2,1)S(1)} custom-call(s32[1]{0:T(128)} %bitcast.2.y_ref, bf16[128,2048]{1,0:T(8,128)(2,1)S(1)} %fusion.2.x0_ref, bf16[128,2048]{1,0:T(8,128)(2,1)S(1)} %collective-permute-done.7.x1_ref, bf16[128,2048]{1,0:T(8,128)(2,1)S(1)} %collective-permute-done.8.x2_ref, ...), custom_call_target="tpu_custom_call" | custom-call | tf_op jit(solution)/shard_map/gate_up/pallas_call | solution.py:304
  148.7 4.7 %gate_up.3.hid1_ref = bf16[512,768]{1,0:T(8,128)(2,1)S(1)} custom-call(s32[1]{0:T(128)} %bitcast.2.y_ref, bf16[128,2048]{1,0:T(8,128)(2,1)S(1)} %fusion.2.x0_ref, bf16[128,2048]{1,0:T(8,128)(2,1)S(1)} %collective-permute-done.7.x1_ref, bf16[128,2048]{1,0:T(8,128)(2,1)S(1)} %collective-permute-done.8.x2_ref, ...), custom_call_target="tpu_custom_call" | custom-call | tf_op jit(solution)/shard_map/gate_up/pallas_call | solution.py:304
  153.4 3.6 %down_far.1 = (bf16[64,2048]{1,0:T(8,128)(2,1)S(1)}, bf16[64,2048]{1,0:T(8,128)(2,1)S(1)}, bf16[1,16,96,2048]{3,2,1,0:T(8,128)(2,1)S(1)}) custom-call(s32[1]{0:T(128)} %bitcast.2.y_ref, bf16[512,768]{1,0:T(8,128)(2,1)S(1)} %gate_up.2.hid0_ref, bf16[512,768]{1,0:T(8,128)(2,1)S(1)} %gate_up.3.hid1_ref, bf16[8,2,4,288,256]{4,3,2,1,0:T(8,128)(2,1)} %bitcast.13, ...), custom_call_target="tpu_custom_call" | custom-call | tf_op jit(solution)/shard_map/down_far/pallas_call | solution.py:322
  157.6 2.8 %collective-permute-start.13 = (bf16[64,2048]{1,0:T(8,128)(2,1)S(1)}, bf16[64,2048]{1,0:T(8,128)(2,1)S(1)}, u32[]{:S(2)}, u32[]{:S(2)}) collective-permute-start(bf16[64,2048]{1,0:T(8,128)(2,1)S(1)} %get-tuple-element.50), channel_id=1, source_target_pairs={{0,3},{1,0},{2,1},{3,2},{4,7},{5,4},{6,5},{7,6},{8,11},{9,8},{10,9... | collective-permute-start | bytes 786440 | tf_op jit(solution)/shard_map/ppermute | solution.py:464
  160.4 3.2 %down.1 = (f32[128,2048]{1,0:T(8,128)S(1)}, bf16[128,2048]{1,0:T(8,128)(2,1)S(1)}, bf16[128,2048]{1,0:T(8,128)(2,1)S(1)}) custom-call(bf16[512,768]{1,0:T(8,128)(2,1)S(1)} %gate_up.2.hid0_ref, bf16[512,768]{1,0:T(8,128)(2,1)S(1)} %gate_up.3.hid1_ref, bf16[1,16,96,2048]{3,2,1,0:T(8,128)(2,1)S(1)} %get-tuple-element.46.w_ref), custom_call_target="tpu_custom_call" | custom-call | tf_op jit(solution)/shard_map/down/pallas_call | solution.py:334
  163.6 2.4 %collective-permute-done.12 = bf16[64,2048]{1,0:T(8,128)(2,1)S(1)} collective-permute-done((bf16[64,2048]{1,0:T(8,128)(2,1)S(1)}, bf16[64,2048]{1,0:T(8,128)(2,1)S(1)}, u32[]{:S(2)}, u32[]{:S(2)}) %collective-permute-start.12) | collective-permute-done | bytes 262176 | tf_op jit(solution)/shard_map/ppermute | solution.py:463
  166.2 3.0 %collective-permute-start.15 = (bf16[128,2048]{1,0:T(8,128)(2,1)S(1)}, bf16[128,2048]{1,0:T(8,128)(2,1)S(1)}, u32[]{:S(2)}, u32[]{:S(2)}) collective-permute-start(bf16[128,2048]{1,0:T(8,128)(2,1)S(1)} %pad_maximum_fusion.2), channel_id=1, source_target_pairs={{0,3},{1,0},{2,1},{3,2},{4,7},{5,4},{6,5},{7,6},{8,11},{9,8},{10,9... | collective-permute-start | bytes 1572872 | tf_op jit(solution)/shard_map/ppermute | solution.py:470
  169.4 9.5 %collective-permute-done.15 = bf16[128,2048]{1,0:T(8,128)(2,1)S(1)} collective-permute-done((bf16[128,2048]{1,0:T(8,128)(2,1)S(1)}, bf16[128,2048]{1,0:T(8,128)(2,1)S(1)}, u32[]{:S(2)}, u32[]{:S(2)}) %collective-permute-start.15) | collective-permute-done | bytes 524320 | tf_op jit(solution)/shard_map/ppermute | solution.py:470
  178.9 3.5 %collective-permute-done.14 = bf16[128,2048]{1,0:T(8,128)(2,1)S(1)} collective-permute-done((bf16[128,2048]{1,0:T(8,128)(2,1)S(1)}, bf16[128,2048]{1,0:T(8,128)(2,1)S(1)}, u32[]{:S(2)}, u32[]{:S(2)}) %collective-permute-start.14) | collective-permute-done | bytes 524320 | tf_op jit(solution)/shard_map/ppermute | solution.py:469
  182.4 1.1 fusion.3
  (53 shorter events, 4.8 us)
Async XLA Ops:
  7.2 17.2 %copy-start.12 = (s32[1024]{0:T(1024)S(1)}, s32[1024]{0:T(1024)}, u32[]{:S(2)}) copy-start(s32[1024]{0:T(1024)} %param.15) | copy-start | bytes 12292
  9.5 28.1 %all-to-all-start = ((bf16[8,768,128]{2,1,0:T(8,128)(2,1)}), bf16[8,768,128]{2,1,0:T(8,128)(2,1)}, u32[]{:S(2)}, u32[]{:S(2)}) async-start(bf16[8,768,128]{2,1,0:T(8,128)(2,1)} %pack.1), calls=%async_computation | async-start | bytes 3145728 | tf_op jit(solution)/shard_map/all_to_all | solution.py:414
  17.4 114.8 %all-gather.3.cloned.1.call-start = ((), (), s32[]{:S(2)}) async-start(), calls=%async_computation.4 | async-start | bytes 10027008 | tf_op jit(solution)/shard_map/all_gather | solution.py:423
  19.7 9.0 %collective-permute-start = (bf16[288,256]{1,0:T(8,128)(2,1)}, bf16[288,256]{1,0:T(8,128)(2,1)S(1)}, u32[]{:S(2)}, u32[]{:S(2)}) collective-permute-start(bf16[288,256]{1,0:T(8,128)(2,1)} %get-tuple-element.29), channel_id=1, source_target_pairs={{0,3},{1,0},{2,1},{3,2},{4,7},{5,4},{6,5},{7,6},{8,11},{9,8},{10,9... | collective-permute-start | bytes 442376 | tf_op jit(solution)/shard_map/ppermute | solution.py:388
  22.7 8.1 %collective-permute-start.1 = (bf16[288,256]{1,0:T(8,128)(2,1)}, bf16[288,256]{1,0:T(8,128)(2,1)S(1)}, u32[]{:S(2)}, u32[]{:S(2)}) collective-permute-start(bf16[288,256]{1,0:T(8,128)(2,1)} %get-tuple-element.30), channel_id=1, source_target_pairs={{0,2},{1,3},{2,0},{3,1},{4,6},{5,7},{6,4},{7,5},{8,10},{9,11},{10,... | collective-permute-start | bytes 442376 | tf_op jit(solution)/shard_map/ppermute | solution.py:388
  23.4 9.0 %collective-permute-start.2 = (bf16[288,256]{1,0:T(8,128)(2,1)}, bf16[288,256]{1,0:T(8,128)(2,1)S(1)}, u32[]{:S(2)}, u32[]{:S(2)}) collective-permute-start(bf16[288,256]{1,0:T(8,128)(2,1)} %get-tuple-element.31), channel_id=1, source_target_pairs={{0,1},{1,2},{2,3},{3,0},{4,5},{5,6},{6,7},{7,4},{8,9},{9,10},{10,1... | collective-permute-start | bytes 442376 | tf_op jit(solution)/shard_map/ppermute | solution.py:388
  28.8 3.6 %copy-start.8 = (bf16[288,256]{1,0:T(8,128)(2,1)}, bf16[288,256]{1,0:T(8,128)(2,1)S(1)}, u32[]{:S(2)}) copy-start(bf16[288,256]{1,0:T(8,128)(2,1)S(1)} %collective-permute-done.p1_ref) | copy-start | bytes 442372
  30.8 1.5 copy-start.9
  32.4 0.7 copy-start.10
  35.0 9.8 %copy-start.5 = (f32[2048]{0:T(1024)S(1)}, f32[2048]{0:T(1024)}, u32[]{:S(2)}) copy-start(f32[2048]{0:T(1024)} %param.16) | copy-start | bytes 24580
  35.0 9.8 %copy-start.6 = (f32[128]{0:T(128)S(1)}, f32[128]{0:T(128)}, u32[]{:S(2)}) copy-start(f32[128]{0:T(128)} %param.18) | copy-start | bytes 1540
  35.0 9.8 %copy-start.7 = (f32[128]{0:T(128)S(1)}, f32[128]{0:T(128)}, u32[]{:S(2)}) copy-start(f32[128]{0:T(128)} %param.19) | copy-start | bytes 1540
  37.7 7.2 %collective-permute-start.3 = (bf16[8,768,128]{2,1,0:T(8,128)(2,1)}, bf16[8,768,128]{2,1,0:T(8,128)(2,1)}, u32[]{:S(2)}, u32[]{:S(2)}) collective-permute-start(bf16[8,768,128]{2,1,0:T(8,128)(2,1)} %all-to-all-done.own_ref.src_ref), channel_id=1, source_target_pairs={{0,8},{8,0},{1,9},{9,1},{2,10},{10,2},{3,11},{11,3},{4,12},{12,4},... | collective-permute-start | bytes 4718600 | tf_op jit(solution)/shard_map/ppermute | solution.py:23
  40.4 35.0 %all-to-all-start.2 = ((bf16[4,8,256,128]{3,2,1,0:T(8,128)(2,1)}), bf16[4,8,256,128]{3,2,1,0:T(8,128)(2,1)S(1)}, u32[]{:S(2)}, u32[]{:S(2)}) async-start(bf16[4,8,256,128]{3,2,1,0:T(8,128)(2,1)} %widen.1), calls=%async_computation.2 | async-start | bytes 4194304 | tf_op jit(solution)/shard_map/all_to_all | solution.py:428
  52.8 12.6 %collective-permute-start.4 = (bf16[2,512,128]{2,1,0:T(8,128)(2,1)}, bf16[2,512,128]{2,1,0:T(8,128)(2,1)S(1)}, u32[]{:S(2)}, u32[]{:S(2)}) collective-permute-start(bf16[2,512,128]{2,1,0:T(8,128)(2,1)} %get-tuple-element.36), channel_id=1, source_target_pairs={{0,8},{8,16},{16,24},{24,32},{32,40},{40,48},{48,56},{56,64},{64,7... | collective-permute-start | bytes 786440 | tf_op jit(solution)/shard_map/ppermute | solution.py:432
  65.4 1.0 copy-start.3
  70.6 0.7 copy-start.4
  75.4 4.3 %collective-permute-start.5 = (bf16[4,8,256,128]{3,2,1,0:T(8,128)(2,1)S(1)}, bf16[4,8,256,128]{3,2,1,0:T(8,128)(2,1)}, u32[]{:S(2)}, u32[]{:S(2)}) collective-permute-start(bf16[4,8,256,128]{3,2,1,0:T(8,128)(2,1)S(1)} %all-to-all-done.2.own_ref), channel_id=1, source_target_pairs={{0,8},{8,0},{1,9},{9,1},{2,10},{10,2},{3,11},{11,3},{4,12},{12,4},... | collective-permute-start | bytes 6291464 | tf_op jit(solution)/shard_map/ppermute | solution.py:23
  75.4 11.6 %all-to-all-start.1 = ((bf16[4,128,256]{2,1,0:T(8,128)(2,1)}), bf16[4,128,256]{2,1,0:T(8,128)(2,1)S(1)}, u32[]{:S(2)}, u32[]{:S(2)}) async-start(bf16[4,128,256]{2,1,0:T(8,128)(2,1)} %copy-done.4), calls=%async_computation.1 | async-start | bytes 524288 | tf_op jit(solution)/shard_map/all_to_all | solution.py:433
  82.2 2.1 %copy-start = (bf16[1024,2048]{1,0:T(8,128)(2,1)}, bf16[1024,2048]{1,0:T(8,128)(2,1)S(1)}, u32[]{:S(2)}) copy-start(bf16[1024,2048]{1,0:T(8,128)(2,1)S(1)} %lay.1.w_ref) | copy-start | bytes 12582916
  87.0 2.3 %copy-start.1 = (bf16[1024,2048]{1,0:T(8,128)(2,1)S(1)}, bf16[1024,2048]{1,0:T(8,128)(2,1)}, u32[]{:S(2)}) copy-start(bf16[1024,2048]{1,0:T(8,128)(2,1)} %copy-done) | copy-start | bytes 12582916
  90.6 25.5 %collective-permute-start.6 = (bf16[128,2048]{1,0:T(8,128)(2,1)S(1)}, bf16[128,2048]{1,0:T(8,128)(2,1)S(1)}, u32[]{:S(2)}, u32[]{:S(2)}) collective-permute-start(bf16[128,2048]{1,0:T(8,128)(2,1)S(1)} %oproj.2), channel_id=1, source_target_pairs={{0,4},{4,0},{1,5},{5,1},{2,6},{6,2},{3,7},{7,3},{8,12},{12,8},{9,1... | collective-permute-start | bytes 1572872 | tf_op jit(solution)/shard_map/ppermute | solution.py:23
  91.1 10.1 %all-to-all-start.3 = ((bf16[4,128,256]{2,1,0:T(8,128)(2,1)}), bf16[4,128,256]{2,1,0:T(8,128)(2,1)S(1)}, u32[]{:S(2)}, u32[]{:S(2)}) async-start(bf16[4,128,256]{2,1,0:T(8,128)(2,1)} %attend.3), calls=%async_computation.3 | async-start | bytes 524288 | tf_op jit(solution)/shard_map/all_to_all | solution.py:433
  101.2 2.3 %copy-start.2 = (bf16[1024,2048]{1,0:T(8,128)(2,1)S(1)}, bf16[1024,2048]{1,0:T(8,128)(2,1)}, u32[]{:S(2)}) copy-start(bf16[1024,2048]{1,0:T(8,128)(2,1)} %copy-done) | copy-start | bytes 12582916
  103.5 13.9 %copy-start.11 = (f32[2048]{0:T(1024)S(1)}, f32[2048]{0:T(1024)}, u32[]{:S(2)}) copy-start(f32[2048]{0:T(1024)} %param.17) | copy-start | bytes 24580
  117.7 12.3 %collective-permute-start.8 = (bf16[128,2048]{1,0:T(8,128)(2,1)S(1)}, bf16[128,2048]{1,0:T(8,128)(2,1)S(1)}, u32[]{:S(2)}, u32[]{:S(2)}) collective-permute-start(bf16[128,2048]{1,0:T(8,128)(2,1)S(1)} %fusion.2.x0_ref), channel_id=1, source_target_pairs={{0,3},{1,0},{2,1},{3,2},{4,7},{5,4},{6,5},{7,6},{8,11},{9,8},{10,9... | collective-permute-start | bytes 1572872 | tf_op jit(solution)/shard_map/ppermute | solution.py:452
  118.9 13.2 %collective-permute-start.7 = (bf16[128,2048]{1,0:T(8,128)(2,1)S(1)}, bf16[128,2048]{1,0:T(8,128)(2,1)S(1)}, u32[]{:S(2)}, u32[]{:S(2)}) collective-permute-start(bf16[128,2048]{1,0:T(8,128)(2,1)S(1)} %fusion.2.x0_ref), channel_id=1, source_target_pairs={{0,1},{1,2},{2,3},{3,0},{4,5},{5,6},{6,7},{7,4},{8,9},{9,10},{10,1... | collective-permute-start | bytes 1572872 | tf_op jit(solution)/shard_map/ppermute | solution.py:451
  132.2 16.5 %collective-permute-start.11 = (bf16[8,2,4,288,256]{4,3,2,1,0:T(8,128)(2,1)}, bf16[8,2,4,288,256]{4,3,2,1,0:T(8,128)(2,1)S(1)}, u32[]{:S(2)}, u32[]{:S(2)}) collective-permute-start(bf16[8,2,4,288,256]{4,3,2,1,0:T(8,128)(2,1)} %bitcast.11), channel_id=1, source_target_pairs={{0,8},{8,0},{1,9},{9,1},{2,10},{10,2},{3,11},{11,3},{4,12},{12,4},... | collective-permute-start | bytes 28311560 | tf_op jit(solution)/shard_map/ppermute | solution.py:23
  132.2 8.8 %collective-permute-start.10 = (bf16[64,2048]{1,0:T(8,128)(2,1)S(1)}, bf16[64,2048]{1,0:T(8,128)(2,1)S(1)}, u32[]{:S(2)}, u32[]{:S(2)}) collective-permute-start(bf16[64,2048]{1,0:T(8,128)(2,1)S(1)} %slice.19), channel_id=1, source_target_pairs={{0,3},{1,0},{2,1},{3,2},{4,7},{5,4},{6,5},{7,6},{8,11},{9,8},{10,9... | collective-permute-start | bytes 786440 | tf_op jit(solution)/shard_map/ppermute | solution.py:456
  132.6 9.7 %collective-permute-start.9 = (bf16[64,2048]{1,0:T(8,128)(2,1)S(1)}, bf16[64,2048]{1,0:T(8,128)(2,1)S(1)}, u32[]{:S(2)}, u32[]{:S(2)}) collective-permute-start(bf16[64,2048]{1,0:T(8,128)(2,1)S(1)} %slice.18), channel_id=1, source_target_pairs={{0,1},{1,2},{2,3},{3,0},{4,5},{5,6},{6,7},{7,4},{8,9},{9,10},{10,1... | collective-permute-start | bytes 786440 | tf_op jit(solution)/shard_map/ppermute | solution.py:455
  157.1 9.0 %collective-permute-start.12 = (bf16[64,2048]{1,0:T(8,128)(2,1)S(1)}, bf16[64,2048]{1,0:T(8,128)(2,1)S(1)}, u32[]{:S(2)}, u32[]{:S(2)}) collective-permute-start(bf16[64,2048]{1,0:T(8,128)(2,1)S(1)} %get-tuple-element.49), channel_id=1, source_target_pairs={{0,1},{1,2},{2,3},{3,0},{4,5},{5,6},{6,7},{7,4},{8,9},{9,10},{10,1... | collective-permute-start | bytes 786440 | tf_op jit(solution)/shard_map/ppermute | solution.py:463
  157.6 8.4 %collective-permute-start.13 = (bf16[64,2048]{1,0:T(8,128)(2,1)S(1)}, bf16[64,2048]{1,0:T(8,128)(2,1)S(1)}, u32[]{:S(2)}, u32[]{:S(2)}) collective-permute-start(bf16[64,2048]{1,0:T(8,128)(2,1)S(1)} %get-tuple-element.50), channel_id=1, source_target_pairs={{0,3},{1,0},{2,1},{3,2},{4,7},{5,4},{6,5},{7,6},{8,11},{9,8},{10,9... | collective-permute-start | bytes 786440 | tf_op jit(solution)/shard_map/ppermute | solution.py:464
  166.2 12.6 %collective-permute-start.15 = (bf16[128,2048]{1,0:T(8,128)(2,1)S(1)}, bf16[128,2048]{1,0:T(8,128)(2,1)S(1)}, u32[]{:S(2)}, u32[]{:S(2)}) collective-permute-start(bf16[128,2048]{1,0:T(8,128)(2,1)S(1)} %pad_maximum_fusion.2), channel_id=1, source_target_pairs={{0,3},{1,0},{2,1},{3,2},{4,7},{5,4},{6,5},{7,6},{8,11},{9,8},{10,9... | collective-permute-start | bytes 1572872 | tf_op jit(solution)/shard_map/ppermute | solution.py:470
  169.3 13.1 %collective-permute-start.14 = (bf16[128,2048]{1,0:T(8,128)(2,1)S(1)}, bf16[128,2048]{1,0:T(8,128)(2,1)S(1)}, u32[]{:S(2)}, u32[]{:S(2)}) collective-permute-start(bf16[128,2048]{1,0:T(8,128)(2,1)S(1)} %pad_maximum_fusion.1), channel_id=1, source_target_pairs={{0,1},{1,2},{2,3},{3,0},{4,5},{5,6},{6,7},{7,4},{8,9},{9,10},{10,1... | collective-permute-start | bytes 1572872 | tf_op jit(solution)/shard_map/ppermute | solution.py:469
Sparse Core Ops, SparseCore 0:
  37.8 86.4 all-gather.2

commit v13 on v12

--- a/solution.py
+++ b/solution.py
@@ -207,20 +207,17 @@
 
 def out_kernel(ctx_ref, w_ref, out_ref):
     x = jnp.concatenate([ctx_ref[s] for s in range(4)], axis=1)
-
-    def column(n, carry):
-        at = pl.ds(pl.multiple_of(n * 512, 512), 512)
-        out_ref[:, at] = jnp.dot(x, w_ref[:, at], preferred_element_type=F32).astype(out_ref.dtype)
-        return carry
-
-    lax.fori_loop(0, 4, column, 0)
+    out_ref[...] = jnp.dot(x, w_ref[...], preferred_element_type=F32).astype(out_ref.dtype)
 
 
 def out_project(ctx, weight, dtype):
     return pl.pallas_call(
         out_kernel,
+        grid=(4,),
+        in_specs=[pl.BlockSpec((4, 128, 256), lambda n: (0, 0, 0)), pl.BlockSpec((1024, 512), lambda n: (0, n))],
+        out_specs=pl.BlockSpec((128, 512), lambda n: (0, n)),
         out_shape=jax.ShapeDtypeStruct((128, 2048), dtype),
-        compiler_params=pltpu.CompilerParams(vmem_limit_bytes=10 << 20),
+        compiler_params=pltpu.CompilerParams(vmem_limit_bytes=14 << 20),
         name="oproj",
     )(ctx, weight)
 
@@ -436,7 +433,7 @@
     mine = attend(xl[None], q, cache, prior, lo)
     _, o_own = hold((mine, o_own))
     o_oth = swap(o_own, "core")
-    o_whole = lay(core[None], o_own, o_oth)
+    o_whole = pltpu.with_memory_space_constraint(lay(core[None], o_own, o_oth), pltpu.HBM)
     send = out_project(turn(theirs), o_whole, BF)
     got = swap(send, "xl")
     _, mine = hold((send, mine))

time: 191 us -> 191 us (level)
  Pallas kernels: 48.4 us -> 53 us
  local copies, waits for them, and re-layouts: 9.36 us -> 4.76 us
    pallas_call x2, Pallas kernels: 2.54 us -> 7.17 us  [out_project(): pl.pallas_call(out_kernel, grid=(4,), in_specs=[pl.BlockSpec((4, 128, 256...]
    unnamed x26 -> x22, local copies, waits for them, and re-layouts: 9.06 us -> 4.46 us
  transfers between devices with their start and end apart: 21 -> 21, of which waited for: 15 -> 15; matrix products, arithmetic and copies ran while one was open for 2% -> 2% of each run, Pallas kernels for 20% -> 22%
where the time goes in v13:
time: 191 us; the launch traced here: 190 us
  waiting for transfers between devices  75.2 us (39%)
  Pallas kernels  53 us (28%)
  starting transfers between devices  38.1 us (20%)
  between operations  14.3 us (7%)
  other arithmetic  5.04 us (3%)
  local copies, waits for them, and re-layouts  4.76 us (2%)
    ppermute x4, waiting for transfers between devices, swap(): return lax.ppermute(block, axis, [(0, 1), (1, 0)])  11.2 us
    pallas_call x2, Pallas kernels, gate_up(): pl.pallas_call(gate_kernel, in_specs=[pl.BlockSpec(memory_space=pltpu.SME...  11.1 us
    ppermute x1, waiting for transfers between devices, per_device(): prior = lax.ppermute(tail, REQ, [(i - 1, i) for i in range(1, 16)])  10.3 us
    ppermute x1, waiting for transfers between devices, per_device(): right = lax.ppermute(mlp_in, 'y', ring(3))  10.2 us
    ppermute x1, waiting for transfers between devices, per_device(): from_right = lax.ppermute(to_left, 'y', ring(3))  9.5 us
    all_to_all x2, waiting for transfers between devices, per_device(): lax.all_to_all(part, 'y', split_axis=0, concat_axis=0, tiled=True)  9.4 us
    pallas_call x2, Pallas kernels, attend(): pl.pallas_call(attend_kernel, in_specs=[pl.BlockSpec(memory_space=pltpu.S...  8.18 us
    pallas_call x1, Pallas kernels, project(): pl.pallas_call(qkv_kernel, grid_spec=pltpu.PrefetchScalarGridSpec(num_sca...  7.91 us
  transfers between devices with their start and end apart: 21, of which 15 were waited for; matrix products, arithmetic and copies ran while one was open for 2% of the time, Pallas kernels for 22%

profile of v13, /device:TPU:32, one launch (start us, length us, event | category | flops | bytes accessed | tf_op | source)
XLA Modules:
  0.0 190.4 jit_solution(9871091114000380215)
XLA Ops:
  7.2 2.3 %pack.1 = bf16[8,768,128]{2,1,0:T(8,128)(2,1)} custom-call(f32[128,256]{1,0:T(8,128)} %q_ref.1, f32[128,128]{1,0:T(8,128)} %k_ref.1, f32[128,128]{1,0:T(8,128)} %v_ref.1, f32[256,128]{1,0:T(8,128)} %o_ref.1), custom_call_target="tpu_custom_call" | custom-call | tf_op jit(solution)/shard_map/pack/pallas_call | solution.py:347
  9.5 7.9 %all-to-all-start = ((bf16[8,768,128]{2,1,0:T(8,128)(2,1)}), bf16[8,768,128]{2,1,0:T(8,128)(2,1)}, u32[]{:S(2)}, u32[]{:S(2)}) async-start(bf16[8,768,128]{2,1,0:T(8,128)(2,1)} %pack.1), calls=%async_computation | async-start | bytes 3145728 | tf_op jit(solution)/shard_map/all_to_all | solution.py:411
  17.4 2.3 %prep.1 = (bf16[288,256]{1,0:T(8,128)(2,1)}, bf16[288,256]{1,0:T(8,128)(2,1)}, bf16[288,256]{1,0:T(8,128)(2,1)}, bf16[288,256]{1,0:T(8,128)(2,1)}) custom-call(s32[1]{0:T(128)} %bitcast.2.y_ref, f32[256,384]{1,0:T(8,128)} %gate_ref.1, f32[256,384]{1,0:T(8,128)} %up_ref.1, f32[384,256]{1,0:T(8,128)} %down_ref.1), custom_call_target="tpu_custom_call" | custom-call | tf_op jit(solution)/shard_map/prep/pallas_call | solution.py:366
  19.7 3.0 %collective-permute-start = (bf16[288,256]{1,0:T(8,128)(2,1)}, bf16[288,256]{1,0:T(8,128)(2,1)S(1)}, u32[]{:S(2)}, u32[]{:S(2)}) collective-permute-start(bf16[288,256]{1,0:T(8,128)(2,1)} %get-tuple-element.29), channel_id=1, source_target_pairs={{0,3},{1,0},{2,1},{3,2},{4,7},{5,4},{6,5},{7,6},{8,11},{9,8},{10,9... | collective-permute-start | bytes 442376 | tf_op jit(solution)/shard_map/ppermute | solution.py:385
  23.4 1.0 collective-permute-start.2
  24.4 1.9 multiply_cosine_fusion
  26.5 2.3 %collective-permute-done.p1_ref = bf16[288,256]{1,0:T(8,128)(2,1)S(1)} collective-permute-done((bf16[288,256]{1,0:T(8,128)(2,1)}, bf16[288,256]{1,0:T(8,128)(2,1)S(1)}, u32[]{:S(2)}, u32[]{:S(2)}) %collective-permute-start) | collective-permute-done | bytes 147488 | tf_op jit(solution)/shard_map/ppermute | solution.py:385
  28.8 2.1 %collective-permute-done.1.p2_ref = bf16[288,256]{1,0:T(8,128)(2,1)S(1)} collective-permute-done((bf16[288,256]{1,0:T(8,128)(2,1)}, bf16[288,256]{1,0:T(8,128)(2,1)S(1)}, u32[]{:S(2)}, u32[]{:S(2)}) %collective-permute-start.1) | collective-permute-done | bytes 147488 | tf_op jit(solution)/shard_map/ppermute | solution.py:385
  30.8 1.5 collective-permute-done.2.p3_ref
  32.4 0.7 copy-done.8
  33.0 2.0 %join.1 = bf16[4,288,256]{2,1,0:T(8,128)(2,1)} custom-call(bf16[288,256]{1,0:T(8,128)(2,1)} %get-tuple-element.28.p0_ref, bf16[288,256]{1,0:T(8,128)(2,1)} %copy-done.6, bf16[288,256]{1,0:T(8,128)(2,1)} %copy-done.7, bf16[288,256]{1,0:T(8,128)(2,1)} %copy-done.8), custom_call_target="tpu_custom_call" | custom-call | tf_op jit(solution)/shard_map/join/pallas_call | solution.py:381
  35.0 2.6 %all-to-all-done.own_ref.src_ref = bf16[8,768,128]{2,1,0:T(8,128)(2,1)} async-done(((bf16[8,768,128]{2,1,0:T(8,128)(2,1)}), bf16[8,768,128]{2,1,0:T(8,128)(2,1)}, u32[]{:S(2)}, u32[]{:S(2)}) %all-to-all-start) | async-done | bytes 1572896 | tf_op jit(solution)/shard_map/all_to_all | solution.py:411
  37.8 2.6 %widen.1 = bf16[4,8,256,128]{3,2,1,0:T(8,128)(2,1)} custom-call(bf16[8,768,128]{2,1,0:T(8,128)(2,1)} %all-to-all-done.own_ref.src_ref), custom_call_target="tpu_custom_call" | custom-call | tf_op jit(solution)/shard_map/widen/pallas_call | solution.py:108
  40.4 4.5 %all-to-all-start.2 = ((bf16[4,8,256,128]{3,2,1,0:T(8,128)(2,1)}), bf16[4,8,256,128]{3,2,1,0:T(8,128)(2,1)S(1)}, u32[]{:S(2)}, u32[]{:S(2)}) async-start(bf16[4,8,256,128]{3,2,1,0:T(8,128)(2,1)} %widen.1), calls=%async_computation.2 | async-start | bytes 4194304 | tf_op jit(solution)/shard_map/all_to_all | solution.py:425
  44.9 7.9 %qkv.1 = (bf16[1024,256]{1,0:T(8,128)(2,1)S(1)}, bf16[2,1024,128]{2,1,0:T(8,128)(2,1)}, bf16[2,512,128]{2,1,0:T(8,128)(2,1)}) custom-call(s32[1]{0:T(128)} %bitcast.1.core_ref, bf16[1024,2048]{1,0:T(8,128)(2,1)} %x_ref.1, bf16[8,768,128]{2,1,0:T(8,128)(2,1)} %all-to-all-done.own_ref.src_ref, bf16[8,768,128]{2,1,0:T(8,128)(2,1)} %collective-permute-done.3.oth_ref, ...), custom_call_target="tpu_custom_call" | custom-call | tf_op jit(solution)/shard_map/qkv/pallas_call | solution.py:71
  52.8 2.1 %collective-permute-start.4 = (bf16[2,512,128]{2,1,0:T(8,128)(2,1)}, bf16[2,512,128]{2,1,0:T(8,128)(2,1)S(1)}, u32[]{:S(2)}, u32[]{:S(2)}) collective-permute-start(bf16[2,512,128]{2,1,0:T(8,128)(2,1)} %get-tuple-element.36), channel_id=1, source_target_pairs={{0,8},{8,16},{16,24},{24,32},{32,40},{40,48},{48,56},{56,64},{64,7... | collective-permute-start | bytes 786440 | tf_op jit(solution)/shard_map/ppermute | solution.py:429
  55.2 10.3 %collective-permute-done.4.prior_ref = bf16[2,512,128]{2,1,0:T(8,128)(2,1)S(1)} collective-permute-done((bf16[2,512,128]{2,1,0:T(8,128)(2,1)}, bf16[2,512,128]{2,1,0:T(8,128)(2,1)S(1)}, u32[]{:S(2)}, u32[]{:S(2)}) %collective-permute-start.4) | collective-permute-done | bytes 262176 | tf_op jit(solution)/shard_map/ppermute | solution.py:429
  65.4 1.0 copy-done.1
  66.5 4.2 %attend.2 = bf16[4,128,256]{2,1,0:T(8,128)(2,1)S(1)} custom-call(s32[1]{0:T(128)S(6)} %sub.6.half_ref, bf16[1024,256]{1,0:T(8,128)(2,1)S(1)} %get-tuple-element.37.q_ref, bf16[2,1024,128]{2,1,0:T(8,128)(2,1)S(1)} %copy-done.1, bf16[2,512,128]{2,1,0:T(8,128)(2,1)S(1)} %collective-permute-done.4.prior_ref, s32[1024,1]{1,0:T(8,128)S(1)} %copy.17.lo_ref), custom_call_target="tpu_custom_call" | custom-call | tf_op jit(solution)/shard_map/attend/pallas_call | solution.py:168
  70.7 0.7 copy-done.2
  71.3 4.0 %attend.3 = bf16[4,128,256]{2,1,0:T(8,128)(2,1)} custom-call(s32[1]{0:T(128)} %bitcast.half_ref, bf16[1024,256]{1,0:T(8,128)(2,1)S(1)} %get-tuple-element.37.q_ref, bf16[2,1024,128]{2,1,0:T(8,128)(2,1)S(1)} %copy-done.1, bf16[2,512,128]{2,1,0:T(8,128)(2,1)S(1)} %collective-permute-done.4.prior_ref, s32[1024,1]{1,0:T(8,128)S(1)} %copy.17.lo_ref), custom_call_target="tpu_custom_call" | custom-call | tf_op jit(solution)/shard_map/attend/pallas_call | solution.py:168
  75.4 4.3 %all-to-all-start.1 = ((bf16[4,128,256]{2,1,0:T(8,128)(2,1)}), bf16[4,128,256]{2,1,0:T(8,128)(2,1)S(1)}, u32[]{:S(2)}, u32[]{:S(2)}) async-start(bf16[4,128,256]{2,1,0:T(8,128)(2,1)} %copy-done.2), calls=%async_computation.1 | async-start | bytes 524288 | tf_op jit(solution)/shard_map/all_to_all | solution.py:430
  79.7 2.5 %lay.1.w_ref = bf16[1024,2048]{1,0:T(8,128)(2,1)S(1)} custom-call(s32[1]{0:T(128)} %bitcast.1.core_ref, bf16[4,8,256,128]{3,2,1,0:T(8,128)(2,1)S(1)} %all-to-all-done.2.own_ref, bf16[4,8,256,128]{3,2,1,0:T(8,128)(2,1)} %collective-permute-done.5.oth_ref), custom_call_target="tpu_custom_call" | custom-call | tf_op jit(solution)/shard_map/lay/pallas_call | solution.py:198
  82.2 2.1 %copy-done = bf16[1024,2048]{1,0:T(8,128)(2,1)} copy-done((bf16[1024,2048]{1,0:T(8,128)(2,1)}, bf16[1024,2048]{1,0:T(8,128)(2,1)S(1)}, u32[]{:S(2)}) %copy-start) | copy-done | bytes 4194328
  84.2 2.8 %all-to-all-done.1.ctx_ref = bf16[4,128,256]{2,1,0:T(8,128)(2,1)S(1)} async-done(((bf16[4,128,256]{2,1,0:T(8,128)(2,1)}), bf16[4,128,256]{2,1,0:T(8,128)(2,1)S(1)}, u32[]{:S(2)}, u32[]{:S(2)}) %all-to-all-start.1) | async-done | bytes 262176 | tf_op jit(solution)/shard_map/all_to_all | solution.py:430
  87.0 3.6 %oproj.2 = bf16[128,2048]{1,0:T(8,128)(2,1)S(1)} custom-call(bf16[4,128,256]{2,1,0:T(8,128)(2,1)S(1)} %all-to-all-done.1.ctx_ref, bf16[1024,2048]{1,0:T(8,128)(2,1)} %copy-done), custom_call_target="tpu_custom_call" | custom-call | tf_op jit(solution)/shard_map/oproj/pallas_call | solution.py:214
  91.2 3.4 %all-to-all-start.3 = ((bf16[4,128,256]{2,1,0:T(8,128)(2,1)}), bf16[4,128,256]{2,1,0:T(8,128)(2,1)S(1)}, u32[]{:S(2)}, u32[]{:S(2)}) async-start(bf16[4,128,256]{2,1,0:T(8,128)(2,1)} %attend.3), calls=%async_computation.3 | async-start | bytes 524288 | tf_op jit(solution)/shard_map/all_to_all | solution.py:430
  94.7 6.6 %all-to-all-done.3.ctx_ref = bf16[4,128,256]{2,1,0:T(8,128)(2,1)S(1)} async-done(((bf16[4,128,256]{2,1,0:T(8,128)(2,1)}), bf16[4,128,256]{2,1,0:T(8,128)(2,1)S(1)}, u32[]{:S(2)}, u32[]{:S(2)}) %all-to-all-start.3) | async-done | bytes 262176 | tf_op jit(solution)/shard_map/all_to_all | solution.py:430
  101.3 3.6 %oproj.3 = f32[128,2048]{1,0:T(8,128)S(1)} custom-call(bf16[4,128,256]{2,1,0:T(8,128)(2,1)S(1)} %all-to-all-done.3.ctx_ref, bf16[1024,2048]{1,0:T(8,128)(2,1)} %copy-done), custom_call_target="tpu_custom_call" | custom-call | tf_op jit(solution)/shard_map/oproj/pallas_call | solution.py:214
  104.9 11.2 %collective-permute-done.6 = bf16[128,2048]{1,0:T(8,128)(2,1)S(1)} collective-permute-done((bf16[128,2048]{1,0:T(8,128)(2,1)S(1)}, bf16[128,2048]{1,0:T(8,128)(2,1)S(1)}, u32[]{:S(2)}, u32[]{:S(2)}) %collective-permute-start.6) | collective-permute-done | bytes 524320 | tf_op jit(solution)/shard_map/ppermute | solution.py:23
  116.1 1.2 add_convert_fusion
  117.7 1.3 collective-permute-start.8
  119.0 0.8 collective-permute-start.7
  119.8 10.2 %collective-permute-done.8.x2_ref = bf16[128,2048]{1,0:T(8,128)(2,1)S(1)} collective-permute-done((bf16[128,2048]{1,0:T(8,128)(2,1)S(1)}, bf16[128,2048]{1,0:T(8,128)(2,1)S(1)}, u32[]{:S(2)}, u32[]{:S(2)}) %collective-permute-start.8) | collective-permute-done | bytes 524320 | tf_op jit(solution)/shard_map/ppermute | solution.py:449
  130.0 2.2 %collective-permute-done.7.x1_ref = bf16[128,2048]{1,0:T(8,128)(2,1)S(1)} collective-permute-done((bf16[128,2048]{1,0:T(8,128)(2,1)S(1)}, bf16[128,2048]{1,0:T(8,128)(2,1)S(1)}, u32[]{:S(2)}, u32[]{:S(2)}) %collective-permute-start.7) | collective-permute-done | bytes 524320 | tf_op jit(solution)/shard_map/ppermute | solution.py:448
  132.6 1.7 collective-permute-start.9
  134.4 6.7 %collective-permute-done.10.x4_ref = bf16[64,2048]{1,0:T(8,128)(2,1)S(1)} collective-permute-done((bf16[64,2048]{1,0:T(8,128)(2,1)S(1)}, bf16[64,2048]{1,0:T(8,128)(2,1)S(1)}, u32[]{:S(2)}, u32[]{:S(2)}) %collective-permute-start.10) | collective-permute-done | bytes 262176 | tf_op jit(solution)/shard_map/ppermute | solution.py:453
  141.1 1.3 collective-permute-done.9.x3_ref
  142.4 6.4 %gate_up.2.hid0_ref = bf16[512,768]{1,0:T(8,128)(2,1)S(1)} custom-call(s32[1]{0:T(128)} %bitcast.2.y_ref, bf16[128,2048]{1,0:T(8,128)(2,1)S(1)} %fusion.2.x0_ref, bf16[128,2048]{1,0:T(8,128)(2,1)S(1)} %collective-permute-done.7.x1_ref, bf16[128,2048]{1,0:T(8,128)(2,1)S(1)} %collective-permute-done.8.x2_ref, ...), custom_call_target="tpu_custom_call" | custom-call | tf_op jit(solution)/shard_map/gate_up/pallas_call | solution.py:301
  148.8 4.7 %gate_up.3.hid1_ref = bf16[512,768]{1,0:T(8,128)(2,1)S(1)} custom-call(s32[1]{0:T(128)} %bitcast.2.y_ref, bf16[128,2048]{1,0:T(8,128)(2,1)S(1)} %fusion.2.x0_ref, bf16[128,2048]{1,0:T(8,128)(2,1)S(1)} %collective-permute-done.7.x1_ref, bf16[128,2048]{1,0:T(8,128)(2,1)S(1)} %collective-permute-done.8.x2_ref, ...), custom_call_target="tpu_custom_call" | custom-call | tf_op jit(solution)/shard_map/gate_up/pallas_call | solution.py:301
  153.5 3.6 %down_far.1 = (bf16[64,2048]{1,0:T(8,128)(2,1)S(1)}, bf16[64,2048]{1,0:T(8,128)(2,1)S(1)}, bf16[1,16,96,2048]{3,2,1,0:T(8,128)(2,1)S(1)}) custom-call(s32[1]{0:T(128)} %bitcast.2.y_ref, bf16[512,768]{1,0:T(8,128)(2,1)S(1)} %gate_up.2.hid0_ref, bf16[512,768]{1,0:T(8,128)(2,1)S(1)} %gate_up.3.hid1_ref, bf16[8,2,4,288,256]{4,3,2,1,0:T(8,128)(2,1)} %bitcast.13, ...), custom_call_target="tpu_custom_call" | custom-call | tf_op jit(solution)/shard_map/down_far/pallas_call | solution.py:319
  157.6 2.8 %collective-permute-start.13 = (bf16[64,2048]{1,0:T(8,128)(2,1)S(1)}, bf16[64,2048]{1,0:T(8,128)(2,1)S(1)}, u32[]{:S(2)}, u32[]{:S(2)}) collective-permute-start(bf16[64,2048]{1,0:T(8,128)(2,1)S(1)} %get-tuple-element.50), channel_id=1, source_target_pairs={{0,3},{1,0},{2,1},{3,2},{4,7},{5,4},{6,5},{7,6},{8,11},{9,8},{10,9... | collective-permute-start | bytes 786440 | tf_op jit(solution)/shard_map/ppermute | solution.py:461
  160.4 3.2 %down.1 = (f32[128,2048]{1,0:T(8,128)S(1)}, bf16[128,2048]{1,0:T(8,128)(2,1)S(1)}, bf16[128,2048]{1,0:T(8,128)(2,1)S(1)}) custom-call(bf16[512,768]{1,0:T(8,128)(2,1)S(1)} %gate_up.2.hid0_ref, bf16[512,768]{1,0:T(8,128)(2,1)S(1)} %gate_up.3.hid1_ref, bf16[1,16,96,2048]{3,2,1,0:T(8,128)(2,1)S(1)} %get-tuple-element.46.w_ref), custom_call_target="tpu_custom_call" | custom-call | tf_op jit(solution)/shard_map/down/pallas_call | solution.py:331
  163.7 2.4 %collective-permute-done.12 = bf16[64,2048]{1,0:T(8,128)(2,1)S(1)} collective-permute-done((bf16[64,2048]{1,0:T(8,128)(2,1)S(1)}, bf16[64,2048]{1,0:T(8,128)(2,1)S(1)}, u32[]{:S(2)}, u32[]{:S(2)}) %collective-permute-start.12) | collective-permute-done | bytes 262176 | tf_op jit(solution)/shard_map/ppermute | solution.py:460
  166.3 3.0 %collective-permute-start.15 = (bf16[128,2048]{1,0:T(8,128)(2,1)S(1)}, bf16[128,2048]{1,0:T(8,128)(2,1)S(1)}, u32[]{:S(2)}, u32[]{:S(2)}) collective-permute-start(bf16[128,2048]{1,0:T(8,128)(2,1)S(1)} %pad_maximum_fusion.2), channel_id=1, source_target_pairs={{0,3},{1,0},{2,1},{3,2},{4,7},{5,4},{6,5},{7,6},{8,11},{9,8},{10,9... | collective-permute-start | bytes 1572872 | tf_op jit(solution)/shard_map/ppermute | solution.py:467
  169.4 9.5 %collective-permute-done.15 = bf16[128,2048]{1,0:T(8,128)(2,1)S(1)} collective-permute-done((bf16[128,2048]{1,0:T(8,128)(2,1)S(1)}, bf16[128,2048]{1,0:T(8,128)(2,1)S(1)}, u32[]{:S(2)}, u32[]{:S(2)}) %collective-permute-start.15) | collective-permute-done | bytes 524320 | tf_op jit(solution)/shard_map/ppermute | solution.py:467
  178.9 3.5 %collective-permute-done.14 = bf16[128,2048]{1,0:T(8,128)(2,1)S(1)} collective-permute-done((bf16[128,2048]{1,0:T(8,128)(2,1)S(1)}, bf16[128,2048]{1,0:T(8,128)(2,1)S(1)}, u32[]{:S(2)}, u32[]{:S(2)}) %collective-permute-start.14) | collective-permute-done | bytes 524320 | tf_op jit(solution)/shard_map/ppermute | solution.py:466
  182.5 1.1 fusion.3
  (49 shorter events, 3.5 us)
Async XLA Ops:
  7.2 17.2 %copy-start.10 = (s32[1024]{0:T(1024)S(1)}, s32[1024]{0:T(1024)}, u32[]{:S(2)}) copy-start(s32[1024]{0:T(1024)} %param.15) | copy-start | bytes 12292
  9.5 28.1 %all-to-all-start = ((bf16[8,768,128]{2,1,0:T(8,128)(2,1)}), bf16[8,768,128]{2,1,0:T(8,128)(2,1)}, u32[]{:S(2)}, u32[]{:S(2)}) async-start(bf16[8,768,128]{2,1,0:T(8,128)(2,1)} %pack.1), calls=%async_computation | async-start | bytes 3145728 | tf_op jit(solution)/shard_map/all_to_all | solution.py:411
  17.4 114.8 %all-gather.3.cloned.1.call-start = ((), (), s32[]{:S(2)}) async-start(), calls=%async_computation.4 | async-start | bytes 10027008 | tf_op jit(solution)/shard_map/all_gather | solution.py:420
  19.7 9.0 %collective-permute-start = (bf16[288,256]{1,0:T(8,128)(2,1)}, bf16[288,256]{1,0:T(8,128)(2,1)S(1)}, u32[]{:S(2)}, u32[]{:S(2)}) collective-permute-start(bf16[288,256]{1,0:T(8,128)(2,1)} %get-tuple-element.29), channel_id=1, source_target_pairs={{0,3},{1,0},{2,1},{3,2},{4,7},{5,4},{6,5},{7,6},{8,11},{9,8},{10,9... | collective-permute-start | bytes 442376 | tf_op jit(solution)/shard_map/ppermute | solution.py:385
  22.7 8.1 %collective-permute-start.1 = (bf16[288,256]{1,0:T(8,128)(2,1)}, bf16[288,256]{1,0:T(8,128)(2,1)S(1)}, u32[]{:S(2)}, u32[]{:S(2)}) collective-permute-start(bf16[288,256]{1,0:T(8,128)(2,1)} %get-tuple-element.30), channel_id=1, source_target_pairs={{0,2},{1,3},{2,0},{3,1},{4,6},{5,7},{6,4},{7,5},{8,10},{9,11},{10,... | collective-permute-start | bytes 442376 | tf_op jit(solution)/shard_map/ppermute | solution.py:385
  23.4 9.0 %collective-permute-start.2 = (bf16[288,256]{1,0:T(8,128)(2,1)}, bf16[288,256]{1,0:T(8,128)(2,1)S(1)}, u32[]{:S(2)}, u32[]{:S(2)}) collective-permute-start(bf16[288,256]{1,0:T(8,128)(2,1)} %get-tuple-element.31), channel_id=1, source_target_pairs={{0,1},{1,2},{2,3},{3,0},{4,5},{5,6},{6,7},{7,4},{8,9},{9,10},{10,1... | collective-permute-start | bytes 442376 | tf_op jit(solution)/shard_map/ppermute | solution.py:385
  28.8 3.6 %copy-start.6 = (bf16[288,256]{1,0:T(8,128)(2,1)}, bf16[288,256]{1,0:T(8,128)(2,1)S(1)}, u32[]{:S(2)}) copy-start(bf16[288,256]{1,0:T(8,128)(2,1)S(1)} %collective-permute-done.p1_ref) | copy-start | bytes 442372
  30.8 1.5 copy-start.7
  32.4 0.7 copy-start.8
  35.0 9.8 %copy-start.3 = (f32[2048]{0:T(1024)S(1)}, f32[2048]{0:T(1024)}, u32[]{:S(2)}) copy-start(f32[2048]{0:T(1024)} %param.16) | copy-start | bytes 24580
  35.0 9.8 %copy-start.4 = (f32[128]{0:T(128)S(1)}, f32[128]{0:T(128)}, u32[]{:S(2)}) copy-start(f32[128]{0:T(128)} %param.18) | copy-start | bytes 1540
  35.0 9.8 %copy-start.5 = (f32[128]{0:T(128)S(1)}, f32[128]{0:T(128)}, u32[]{:S(2)}) copy-start(f32[128]{0:T(128)} %param.19) | copy-start | bytes 1540
  37.7 7.2 %collective-permute-start.3 = (bf16[8,768,128]{2,1,0:T(8,128)(2,1)}, bf16[8,768,128]{2,1,0:T(8,128)(2,1)}, u32[]{:S(2)}, u32[]{:S(2)}) collective-permute-start(bf16[8,768,128]{2,1,0:T(8,128)(2,1)} %all-to-all-done.own_ref.src_ref), channel_id=1, source_target_pairs={{0,8},{8,0},{1,9},{9,1},{2,10},{10,2},{3,11},{11,3},{4,12},{12,4},... | collective-permute-start | bytes 4718600 | tf_op jit(solution)/shard_map/ppermute | solution.py:23
  40.4 35.0 %all-to-all-start.2 = ((bf16[4,8,256,128]{3,2,1,0:T(8,128)(2,1)}), bf16[4,8,256,128]{3,2,1,0:T(8,128)(2,1)S(1)}, u32[]{:S(2)}, u32[]{:S(2)}) async-start(bf16[4,8,256,128]{3,2,1,0:T(8,128)(2,1)} %widen.1), calls=%async_computation.2 | async-start | bytes 4194304 | tf_op jit(solution)/shard_map/all_to_all | solution.py:425
  52.8 12.7 %collective-permute-start.4 = (bf16[2,512,128]{2,1,0:T(8,128)(2,1)}, bf16[2,512,128]{2,1,0:T(8,128)(2,1)S(1)}, u32[]{:S(2)}, u32[]{:S(2)}) collective-permute-start(bf16[2,512,128]{2,1,0:T(8,128)(2,1)} %get-tuple-element.36), channel_id=1, source_target_pairs={{0,8},{8,16},{16,24},{24,32},{32,40},{40,48},{48,56},{56,64},{64,7... | collective-permute-start | bytes 786440 | tf_op jit(solution)/shard_map/ppermute | solution.py:429
  65.4 1.0 copy-start.1
  70.7 0.7 copy-start.2
  75.4 4.3 %collective-permute-start.5 = (bf16[4,8,256,128]{3,2,1,0:T(8,128)(2,1)S(1)}, bf16[4,8,256,128]{3,2,1,0:T(8,128)(2,1)}, u32[]{:S(2)}, u32[]{:S(2)}) collective-permute-start(bf16[4,8,256,128]{3,2,1,0:T(8,128)(2,1)S(1)} %all-to-all-done.2.own_ref), channel_id=1, source_target_pairs={{0,8},{8,0},{1,9},{9,1},{2,10},{10,2},{3,11},{11,3},{4,12},{12,4},... | collective-permute-start | bytes 6291464 | tf_op jit(solution)/shard_map/ppermute | solution.py:23
  75.4 11.6 %all-to-all-start.1 = ((bf16[4,128,256]{2,1,0:T(8,128)(2,1)}), bf16[4,128,256]{2,1,0:T(8,128)(2,1)S(1)}, u32[]{:S(2)}, u32[]{:S(2)}) async-start(bf16[4,128,256]{2,1,0:T(8,128)(2,1)} %copy-done.2), calls=%async_computation.1 | async-start | bytes 524288 | tf_op jit(solution)/shard_map/all_to_all | solution.py:430
  82.2 2.1 %copy-start = (bf16[1024,2048]{1,0:T(8,128)(2,1)}, bf16[1024,2048]{1,0:T(8,128)(2,1)S(1)}, u32[]{:S(2)}) copy-start(bf16[1024,2048]{1,0:T(8,128)(2,1)S(1)} %lay.1.w_ref) | copy-start | bytes 12582916
  90.6 25.5 %collective-permute-start.6 = (bf16[128,2048]{1,0:T(8,128)(2,1)S(1)}, bf16[128,2048]{1,0:T(8,128)(2,1)S(1)}, u32[]{:S(2)}, u32[]{:S(2)}) collective-permute-start(bf16[128,2048]{1,0:T(8,128)(2,1)S(1)} %oproj.2), channel_id=1, source_target_pairs={{0,4},{4,0},{1,5},{5,1},{2,6},{6,2},{3,7},{7,3},{8,12},{12,8},{9,1... | collective-permute-start | bytes 1572872 | tf_op jit(solution)/shard_map/ppermute | solution.py:23
  91.2 10.1 %all-to-all-start.3 = ((bf16[4,128,256]{2,1,0:T(8,128)(2,1)}), bf16[4,128,256]{2,1,0:T(8,128)(2,1)S(1)}, u32[]{:S(2)}, u32[]{:S(2)}) async-start(bf16[4,128,256]{2,1,0:T(8,128)(2,1)} %attend.3), calls=%async_computation.3 | async-start | bytes 524288 | tf_op jit(solution)/shard_map/all_to_all | solution.py:430
  94.7 22.9 %copy-start.9 = (f32[2048]{0:T(1024)S(1)}, f32[2048]{0:T(1024)}, u32[]{:S(2)}) copy-start(f32[2048]{0:T(1024)} %param.17) | copy-start | bytes 24580
  117.7 12.3 %collective-permute-start.8 = (bf16[128,2048]{1,0:T(8,128)(2,1)S(1)}, bf16[128,2048]{1,0:T(8,128)(2,1)S(1)}, u32[]{:S(2)}, u32[]{:S(2)}) collective-permute-start(bf16[128,2048]{1,0:T(8,128)(2,1)S(1)} %fusion.2.x0_ref), channel_id=1, source_target_pairs={{0,3},{1,0},{2,1},{3,2},{4,7},{5,4},{6,5},{7,6},{8,11},{9,8},{10,9... | collective-permute-start | bytes 1572872 | tf_op jit(solution)/shard_map/ppermute | solution.py:449
  119.0 13.3 %collective-permute-start.7 = (bf16[128,2048]{1,0:T(8,128)(2,1)S(1)}, bf16[128,2048]{1,0:T(8,128)(2,1)S(1)}, u32[]{:S(2)}, u32[]{:S(2)}) collective-permute-start(bf16[128,2048]{1,0:T(8,128)(2,1)S(1)} %fusion.2.x0_ref), channel_id=1, source_target_pairs={{0,1},{1,2},{2,3},{3,0},{4,5},{5,6},{6,7},{7,4},{8,9},{9,10},{10,1... | collective-permute-start | bytes 1572872 | tf_op jit(solution)/shard_map/ppermute | solution.py:448
  132.2 16.5 %collective-permute-start.11 = (bf16[8,2,4,288,256]{4,3,2,1,0:T(8,128)(2,1)}, bf16[8,2,4,288,256]{4,3,2,1,0:T(8,128)(2,1)S(1)}, u32[]{:S(2)}, u32[]{:S(2)}) collective-permute-start(bf16[8,2,4,288,256]{4,3,2,1,0:T(8,128)(2,1)} %bitcast.11), channel_id=1, source_target_pairs={{0,8},{8,0},{1,9},{9,1},{2,10},{10,2},{3,11},{11,3},{4,12},{12,4},... | collective-permute-start | bytes 28311560 | tf_op jit(solution)/shard_map/ppermute | solution.py:23
  132.3 8.8 %collective-permute-start.10 = (bf16[64,2048]{1,0:T(8,128)(2,1)S(1)}, bf16[64,2048]{1,0:T(8,128)(2,1)S(1)}, u32[]{:S(2)}, u32[]{:S(2)}) collective-permute-start(bf16[64,2048]{1,0:T(8,128)(2,1)S(1)} %slice.19), channel_id=1, source_target_pairs={{0,3},{1,0},{2,1},{3,2},{4,7},{5,4},{6,5},{7,6},{8,11},{9,8},{10,9... | collective-permute-start | bytes 786440 | tf_op jit(solution)/shard_map/ppermute | solution.py:453
  132.6 9.7 %collective-permute-start.9 = (bf16[64,2048]{1,0:T(8,128)(2,1)S(1)}, bf16[64,2048]{1,0:T(8,128)(2,1)S(1)}, u32[]{:S(2)}, u32[]{:S(2)}) collective-permute-start(bf16[64,2048]{1,0:T(8,128)(2,1)S(1)} %slice.18), channel_id=1, source_target_pairs={{0,1},{1,2},{2,3},{3,0},{4,5},{5,6},{6,7},{7,4},{8,9},{9,10},{10,1... | collective-permute-start | bytes 786440 | tf_op jit(solution)/shard_map/ppermute | solution.py:452
  157.1 9.0 %collective-permute-start.12 = (bf16[64,2048]{1,0:T(8,128)(2,1)S(1)}, bf16[64,2048]{1,0:T(8,128)(2,1)S(1)}, u32[]{:S(2)}, u32[]{:S(2)}) collective-permute-start(bf16[64,2048]{1,0:T(8,128)(2,1)S(1)} %get-tuple-element.49), channel_id=1, source_target_pairs={{0,1},{1,2},{2,3},{3,0},{4,5},{5,6},{6,7},{7,4},{8,9},{9,10},{10,1... | collective-permute-start | bytes 786440 | tf_op jit(solution)/shard_map/ppermute | solution.py:460
  157.6 8.5 %collective-permute-start.13 = (bf16[64,2048]{1,0:T(8,128)(2,1)S(1)}, bf16[64,2048]{1,0:T(8,128)(2,1)S(1)}, u32[]{:S(2)}, u32[]{:S(2)}) collective-permute-start(bf16[64,2048]{1,0:T(8,128)(2,1)S(1)} %get-tuple-element.50), channel_id=1, source_target_pairs={{0,3},{1,0},{2,1},{3,2},{4,7},{5,4},{6,5},{7,6},{8,11},{9,8},{10,9... | collective-permute-start | bytes 786440 | tf_op jit(solution)/shard_map/ppermute | solution.py:461
  166.3 12.7 %collective-permute-start.15 = (bf16[128,2048]{1,0:T(8,128)(2,1)S(1)}, bf16[128,2048]{1,0:T(8,128)(2,1)S(1)}, u32[]{:S(2)}, u32[]{:S(2)}) collective-permute-start(bf16[128,2048]{1,0:T(8,128)(2,1)S(1)} %pad_maximum_fusion.2), channel_id=1, source_target_pairs={{0,3},{1,0},{2,1},{3,2},{4,7},{5,4},{6,5},{7,6},{8,11},{9,8},{10,9... | collective-permute-start | bytes 1572872 | tf_op jit(solution)/shard_map/ppermute | solution.py:467
  169.4 13.1 %collective-permute-start.14 = (bf16[128,2048]{1,0:T(8,128)(2,1)S(1)}, bf16[128,2048]{1,0:T(8,128)(2,1)S(1)}, u32[]{:S(2)}, u32[]{:S(2)}) collective-permute-start(bf16[128,2048]{1,0:T(8,128)(2,1)S(1)} %pad_maximum_fusion.1), channel_id=1, source_target_pairs={{0,1},{1,2},{2,3},{3,0},{4,5},{5,6},{6,7},{7,4},{8,9},{9,10},{10,1... | collective-permute-start | bytes 1572872 | tf_op jit(solution)/shard_map/ppermute | solution.py:466
Sparse Core Ops, SparseCore 0:
  37.8 86.4 all-gather.2
